TPU v7x, 256 devices: a whole 4x4x8 slice. The times are simulated.
256 devices in a mesh: seq: 32 (over y, z), head: 8 (over x, core).
Axes of the slice: x: 4, y: 4, z: 8, core: 2. Of those that a mesh axis runs over, the one named last changes fastest.
Arguments:
- queries: bfloat16 [16384, 4096], P('seq', 'head'), may hold values from -8 to 8
- keys: bfloat16 [16384, 4096], P('seq', 'head'), may hold values from -8 to 8
- values: bfloat16 [16384, 4096], P('seq', 'head'), may hold values from -6 to 6
- w_out: bfloat16 [4096, 4096], P('head', 'seq'), may hold values from -0.1875 to 0.1875
- grad_y: bfloat16 [16384, 4096], P('seq', 'head'), may hold values from -6 to 6
Outputs:
- mixer_result: bfloat16 [16384, 4096], P('seq', 'head')
- grad_queries: bfloat16 [16384, 4096], P('seq', 'head')
- grad_keys: bfloat16 [16384, 4096], P('seq', 'head')
- grad_values: bfloat16 [16384, 4096], P('seq', 'head')
- projection_sensitivity: float32 [4096, 4096], P('head', 'seq')
All inputs are finite; a program needn't handle non-finite values.
Results may differ from a plain program's by a relative error of at most 0.025.
Values may be sent and summed in bfloat16 or wider, within the bound.
No kernel may reach another device: no remote copies, remote signals or barrier semaphores. Data moves between devices by JAX's collectives and lax.ppermute only.
A program may use at most 128 MiB of HBM per device.

v0:
```python
import math

import jax
import jax.numpy as jnp
from jax import lax
from jax.sharding import PartitionSpec as P

DH = 128
BLOCK = 64
BAND = 8


EPSILON = 1e-05
MASKED = -1e30


def entering(shard, axis, join, neutral, backward):
    count = lax.axis_size(axis)
    place = lax.axis_index(axis)
    ahead = count - 1 - place if backward else place
    gathered = lax.all_gather(shard.astype(jnp.bfloat16), axis)
    state = jnp.zeros_like(shard) + jnp.asarray(neutral, shard.dtype)

    def one(turn, state):
        source = count - 1 - turn if backward else turn
        return join(state, lax.dynamic_index_in_dim(gathered, source, 0, False).astype(shard.dtype))

    return lax.fori_loop(0, ahead, one, state)


def shifted(shard, axis, by):
    count = lax.axis_size(axis)
    pairs = [(i, i + by) for i in range(count) if 0 <= i + by < count]
    return lax.ppermute(shard, axis, pairs)


def band_allowed(first, rows, span, offset):
    query = first + jnp.arange(rows, dtype=jnp.int32)
    place = first - (BAND - 1) * BLOCK + jnp.arange(span, dtype=jnp.int32)
    near = place[:, None] // BLOCK >= query[None, :] // BLOCK - (BAND - 1)
    return (place[:, None] <= query[None, :]) & near & (place[:, None] + offset >= 0)


def add_states(earlier, later):
    return earlier + later


def carry_states(local_sum, backward):
    return entering(local_sum, "seq", add_states, jnp.zeros_like(local_sum), backward)


def shards(queries, keys, values, w_out, grad_y):
    tok_rows, width = queries.shape
    groups = width // DH
    block_count = tok_rows // BLOCK
    rows = BAND * BLOCK
    edge = (BAND - 1) * BLOCK
    span = rows + edge
    query_blocks = tok_rows // rows
    score_scale = 1.0 / math.sqrt(DH)
    offset = lax.axis_index("seq") * tok_rows
    tokens_all = tok_rows * lax.axis_size("seq")
    query_block_rows = queries.reshape(block_count, BLOCK, groups, DH)
    lookup_tile_entries = keys.reshape(block_count, BLOCK, groups, DH)
    value_block_rows = values.reshape(block_count, BLOCK, groups, DH)
    cross_block_totals = jnp.einsum(
        "nbhk,nbhv->nhkv", lookup_tile_entries, value_block_rows, preferred_element_type=jnp.float32
    )
    before = carry_states(jnp.sum(cross_block_totals, axis=0), False)
    running_state = (
        before[None] + jnp.cumsum(cross_block_totals, axis=0) - cross_block_totals
    ).astype(jnp.bfloat16)
    causal = (jnp.arange(BLOCK)[:, None] >= jnp.arange(BLOCK)[None, :])[None, None]
    inside_block_scores = jnp.where(
        causal,
        jnp.einsum(
            "nthk,njhk->nhtj",
            query_block_rows,
            lookup_tile_entries,
            preferred_element_type=jnp.float32,
        ),
        0.0,
    ).astype(jnp.bfloat16)
    linear_branch = jnp.einsum(
        "nthk,nhkv->nthv", query_block_rows, running_state, preferred_element_type=jnp.float32
    )
    linear_branch = linear_branch + jnp.einsum(
        "nhtj,njhv->nthv", inside_block_scores, value_block_rows, preferred_element_type=jnp.float32
    )
    linear_branch = linear_branch.reshape(tok_rows, groups, DH)
    inv_rms = lax.rsqrt(jnp.mean(linear_branch * linear_branch, axis=-1, keepdims=True) + EPSILON)
    normed = linear_branch * inv_rms
    edge_pair = shifted(jnp.stack([keys[tok_rows - edge :], values[tok_rows - edge :]]), "seq", 1)
    lookup_matrix_padded = jnp.concatenate([edge_pair[0], keys]).reshape(
        tok_rows + edge, groups, DH
    )
    values_wide = jnp.concatenate([edge_pair[1], values]).reshape(tok_rows + edge, groups, DH)
    q_heads = queries.reshape(tok_rows, groups, DH)

    def band_scores(first, q_rows, k_span):
        score = (
            jnp.einsum("khd,qhd->hkq", k_span, q_rows, preferred_element_type=jnp.float32)
            * score_scale
        )
        return jnp.where(band_allowed(first, rows, span, offset)[None], score, MASKED)

    def window_block(index):
        first = index * rows
        score = band_scores(first, q_heads, lookup_matrix_padded)
        row_max = jnp.max(score, axis=1)
        raised = jnp.exp(score - row_max[:, None, :])
        inv_total = 1.0 / jnp.sum(raised, axis=1)
        probs = (raised * inv_total[:, None, :]).astype(jnp.bfloat16)
        return (
            jnp.einsum("hkq,khd->qhd", probs, values_wide, preferred_element_type=jnp.float32),
            row_max,
            inv_total,
        )

    outs, maxima, inverses = lax.map(window_block, jnp.arange(query_blocks, dtype=jnp.int32))
    window = outs.reshape(tok_rows, groups, DH)
    mixed = (normed + window).astype(jnp.bfloat16).reshape(tok_rows, width)
    partial_value = jnp.dot(
        mixed, lax.all_gather(w_out, "seq", axis=1, tiled=True), preferred_element_type=jnp.float32
    )
    mixer_result = lax.psum_scatter(
        partial_value.astype(jnp.bfloat16), "head", scatter_dimension=1, tiled=True
    )
    grad_full = lax.all_gather(grad_y, "head", axis=1, tiled=True)
    columns = grad_full
    grad_mixed = lax.dot_general(
        columns,
        lax.all_gather(w_out, "seq", axis=1, tiled=True),
        (((1,), (1,)), ((), ())),
        preferred_element_type=jnp.float32,
    )
    grad_mixed = grad_mixed.astype(jnp.bfloat16)
    columns = grad_full
    weight_part = lax.psum_scatter(
        lax.dot_general(
            columns, mixed, (((0,), (0,)), ((), ())), preferred_element_type=jnp.float32
        ).astype(jnp.bfloat16),
        "seq",
        scatter_dimension=0,
        tiled=True,
    ).astype(jnp.float32)
    projection_sensitivity = weight_part.T * tokens_all ** (-0.5)
    grad_mix = grad_mixed.reshape(tok_rows, groups, DH)
    grad_f = grad_mix.astype(jnp.float32)
    delta = jnp.sum(grad_f * window, axis=-1)
    inner = jnp.mean(grad_f * normed, axis=-1, keepdims=True)
    grad_lin = (inv_rms * (grad_f - normed * inner)).astype(jnp.bfloat16)
    upstream_tile_entries = grad_lin.reshape(block_count, BLOCK, groups, DH)
    reverse_state_totals = jnp.einsum(
        "nthk,nthv->nhkv",
        query_block_rows,
        upstream_tile_entries,
        preferred_element_type=jnp.float32,
    )
    local_back = jnp.sum(reverse_state_totals, axis=0)
    later = carry_states(local_back, True)
    back_state = (later[None] + local_back[None] - jnp.cumsum(reverse_state_totals, axis=0)).astype(
        jnp.bfloat16
    )
    intra_grad = jnp.where(
        causal,
        jnp.einsum(
            "nthv,njhv->nhtj",
            upstream_tile_entries,
            value_block_rows,
            preferred_element_type=jnp.float32,
        ),
        0.0,
    ).astype(jnp.bfloat16)
    asking_plain_entries = jnp.einsum(
        "nthv,nhkv->nthk", upstream_tile_entries, running_state, preferred_element_type=jnp.float32
    )
    asking_plain_entries = asking_plain_entries + jnp.einsum(
        "nhtj,njhk->nthk", intra_grad, lookup_tile_entries, preferred_element_type=jnp.float32
    )
    key_linear_rows = jnp.einsum(
        "njhv,nhkv->njhk", value_block_rows, back_state, preferred_element_type=jnp.float32
    )
    key_linear_rows = key_linear_rows + jnp.einsum(
        "nhtj,nthk->njhk", intra_grad, query_block_rows, preferred_element_type=jnp.float32
    )
    value_linear_rows = jnp.einsum(
        "njhk,nhkv->njhv", lookup_tile_entries, back_state, preferred_element_type=jnp.float32
    )
    value_linear_rows = value_linear_rows + jnp.einsum(
        "nhtj,nthv->njhv",
        inside_block_scores,
        upstream_tile_entries,
        preferred_element_type=jnp.float32,
    )

    def window_back(index, carry):
        q_acc, k_acc, v_acc = carry
        first = index * rows
        score = band_scores(first, q_heads, lookup_matrix_padded)
        probs = (jnp.exp(score - maxima[index][:, None, :]) * inverses[index][:, None, :]).astype(
            jnp.bfloat16
        )
        dprob = jnp.einsum(
            "khd,qhd->hkq", values_wide, grad_mix, preferred_element_type=jnp.float32
        )
        delta_rows = delta.T
        dscore = (
            probs.astype(jnp.float32) * (dprob - delta_rows[:, None, :]) * score_scale
        ).astype(jnp.bfloat16)
        q_acc = jnp.einsum(
            "hkq,khd->qhd", dscore, lookup_matrix_padded, preferred_element_type=jnp.float32
        )
        k_new = k_acc + jnp.einsum(
            "hkq,qhd->khd", dscore, q_heads, preferred_element_type=jnp.float32
        )
        v_new = v_acc + jnp.einsum(
            "hkq,qhd->khd", probs, grad_mix, preferred_element_type=jnp.float32
        )
        k_acc = k_new
        v_acc = v_new
        return (q_acc, k_acc, v_acc)

    start_carry = (
        jnp.zeros((tok_rows, groups, DH), jnp.float32),
        jnp.zeros((tok_rows + edge, groups, DH), jnp.float32),
        jnp.zeros((tok_rows + edge, groups, DH), jnp.float32),
    )
    q_window, k_wide_grad, v_wide_grad = lax.fori_loop(0, query_blocks, window_back, start_carry)
    returned = shifted(
        jnp.stack([k_wide_grad[:edge], v_wide_grad[:edge]]).astype(jnp.bfloat16), "seq", -1
    ).astype(jnp.float32)
    k_window = k_wide_grad[edge:].at[tok_rows - edge :].add(returned[0])
    v_window = v_wide_grad[edge:].at[tok_rows - edge :].add(returned[1])
    grad_queries = (
        (asking_plain_entries.reshape(tok_rows, groups, DH) + q_window)
        .astype(jnp.bfloat16)
        .reshape(tok_rows, width)
    )
    grad_keys = (
        (key_linear_rows.reshape(tok_rows, groups, DH) + k_window)
        .astype(jnp.bfloat16)
        .reshape(tok_rows, width)
    )
    grad_values = (
        (value_linear_rows.reshape(tok_rows, groups, DH) + v_window)
        .astype(jnp.bfloat16)
        .reshape(tok_rows, width)
    )
    return (mixer_result, grad_queries, grad_keys, grad_values, projection_sensitivity)


def solution(mesh):
    placed = (
        P("seq", "head"),
        P("seq", "head"),
        P("seq", "head"),
        P("head", "seq"),
        P("seq", "head"),
    )
    return jax.shard_map(
        shards,
        mesh=mesh,
        in_specs=placed,
        out_specs=(
            P("seq", "head"),
            P("seq", "head"),
            P("seq", "head"),
            P("seq", "head"),
            P("head", "seq"),
        ),
        check_vma=False,
    )
```

profile of v0, /device:TPU:16, one launch (start us, length us, event | category | flops | bytes accessed | tf_op | source)
XLA Modules:
  0.0 588.9 jit_solution(10219988638877954904)
XLA Ops:
  7.2 1.2 reshape.466
  8.4 1.4 reshape.465
  12.5 1.2 slice_bitcast_fusion.2
  14.7 3.8 collective-permute-start
  18.6 2.0 copy.87
  20.6 2.0 copy.84
  23.8 2.2 copy.89
  26.1 2.1 copy.86
  28.2 1.6 fusion.9
  29.8 1.2 fusion.17
  31.0 15.8 %collective-permute-done = bf16[2,448,512]{2,1,0:T(8,128)(2,1)} collective-permute-done((bf16[2,448,512]{2,1,0:T(8,128)(2,1)}, bf16[2,448,512]{2,1,0:T(8,128)(2,1)}, u32[]{:S(2)}, u32[]{:S(2)}) %collective-permute-start) | collective-permute-done | bytes 917536 | tf_op jit(solution)/shard_map/ppermute | solution.py:34
  46.7 2.0 fusion.76
  48.7 1.9 concatenate.23
  50.7 1.9 copy.88
  53.5 7.5 %fusion.77 = (f32[4,512]{1,0:T(4,128)S(1)}, f32[4,960,512]{2,1,0:T(8,128)}) fusion(pred[960,512]{1,0:T(8,128)(4,1)} %fusion.9, bf16[512,4,128]{2,0,1:T(8,128)(2,1)} %copy.89, bf16[448,4,128]{2,0,1:T(8,128)(2,1)} %copy.88, bf16[512,512]{1,0:T(8,128)(2,1)} %param.13), kind=kOutput, calls=%fused_computation.125 | convolution fusion | flops 513147840 | bytes 9871360 | tf_op jit(solution)/shard_map/while/body/eval_jaxpr/sub | solution.py:111
  61.0 6.3 %multiply_convert_fusion.1 = bf16[4,960,512]{2,1,0:T(8,128)(2,1)} fusion(f32[4,960,512]{2,1,0:T(8,128)} %get-tuple-element.211, f32[4,512]{1,0:T(4,128)S(1)} %broadcast_divide_fusion), kind=kLoop, calls=%fused_computation.4 | loop fusion | flops 3932160 | bytes 11804672 | tf_op jit(solution)/shard_map/while/body/eval_jaxpr/convert_element_type | solution.py:113
  67.2 27.4 %all-gather.11.cloned.1.call-done = bf16[128,128,128]{2,1,0:T(8,128)(2,1)} async-done(((bf16[4,128,128]{2,1,0:T(8,128)(2,1)}), bf16[128,128,128]{2,1,0:T(8,128)(2,1)}) %all-gather.11.cloned.1.call-update) | async-done | bytes 4194320 | tf_op jit(solution)/shard_map/all_gather | solution.py:21
  94.6 16.0 %while.16 = (s32[]{:T(128)}, f32[4,128,128]{2,1,0:T(8,128)S(1)}, s32[]{:T(128)}, bf16[32,4,128,128]{3,2,1,0:T(8,128)(2,1)}, s32[]{:T(128)}, /*index=5*/s32[]{:T(128)}, s32[]{:T(128)}) while((s32[]{:T(128)}, f32[4,128,128]{2,1,0:T(8,128)S(1)}, s32[]{:T(128)}, bf16[32,4,128,128]{3,2,1,0:T(8,128)(2,1)}, s32[]{:T(128)}, /*index=5*/s32[]{:T(128)}, ...), condition=%wide.region_2.3_spmd, body=%wide.region_1.2_spmd.sunk | while | flops 131077 | bytes 655483 | solution.py:28
  112.7 1.3 copy.83
  114.2 15.8 %all-gather.9.cloned.1.call-done = bf16[512,4096]{1,0:T(8,128)(2,1)} async-done(((bf16[512,512]{1,0:T(8,128)(2,1)}), bf16[512,4096]{1,0:T(8,128)(2,1)}) %all-gather.9.cloned.1.call-update) | async-done | bytes 4194320 | tf_op jit(solution)/shard_map/all_gather | solution.py:129
  129.9 86.7 %all-gather.7.cloned.1.call-done = bf16[512,4096]{1,0:T(8,128)(2,1)} async-done(((bf16[512,128]{1,0:T(8,128)(2,1)}), bf16[512,4096]{1,0:T(8,128)(2,1)}) %all-gather.7.cloned.1.call-update) | async-done | bytes 4194320 | tf_op jit(solution)/shard_map/all_gather | solution.py:124
  216.6 5.8 convolution_convert_fusion.2
  222.5 1.8 reshape.485
  224.2 3.2 copy.93
  227.4 4.4 fusion.21
  231.9 1.7 multiply_convert_fusion.2
  233.7 1.9 bitcast_reduce_fusion
  236.4 6.6 %fusion.2 = bf16[4096,512]{0,1:T(8,128)(2,1)} fusion(bf16[512,512]{0,1:T(8,128)(2,1)S(1)} %bitcast.161, bf16[512,4096]{1,0:T(8,128)(2,1)} %all-gather.9.cloned.1.call-done), kind=kOutput, calls=%fused_computation.10 | convolution fusion | flops 2149580800 | bytes 8912896 | tf_op jit(solution)/shard_map/dot_general | solution.py:140
  243.0 6.5 %copy.126 = bf16[4096,512]{1,0:T(8,128)(2,1)} copy(bf16[4096,512]{0,1:T(8,128)(2,1)} %fusion.2) | data formatting | bytes 8388608
  249.8 6.6 %convolution_convert_fusion.1 = bf16[512,4096]{1,0:T(8,128)(2,1)} fusion(bf16[512,512]{0,1:T(8,128)(2,1)S(1)} %bitcast.162, bf16[512,4096]{1,0:T(8,128)(2,1)} %all-gather.7.cloned.1.call-done), kind=kOutput, calls=%fused_computation.9 | convolution fusion | flops 2149580800 | bytes 8912896 | tf_op jit(solution)/shard_map/dot_general | solution.py:123
  256.4 3.6 convolution_bitcast_fusion
  260.3 1.4 multiply_convert_fusion
  261.7 1.2 convolution_bitcast_fusion.1
  265.2 4.7 collective-permute-start.1
  272.6 3.8 fusion.19
  276.4 2.2 copy.115
  278.6 8.8 %collective-permute-done.1 = bf16[2,448,4,128]{3,1,2,0:T(8,128)(2,1)} collective-permute-done((bf16[2,448,4,128]{3,1,2,0:T(8,128)(2,1)}, bf16[2,448,4,128]{3,1,2,0:T(8,128)(2,1)}, u32[]{:S(2)}, u32[]{:S(2)}) %collective-permute-start.1) | collective-permute-done | bytes 917536 | tf_op jit(solution)/shard_map/ppermute | solution.py:34
  287.4 1.3 convert_element_type.130
  288.7 2.4 fusion.25
  291.1 26.2 %all-gather.13.cloned.1.call-done = bf16[128,128,128]{2,1,0:T(8,128)(2,1)} async-done(((bf16[4,128,128]{2,1,0:T(8,128)(2,1)}), bf16[128,128,128]{2,1,0:T(8,128)(2,1)}) %all-gather.13.cloned.1.call-update) | async-done | bytes 4194320 | tf_op jit(solution)/shard_map/all_gather | solution.py:21
  317.3 14.9 %while.17 = (s32[]{:T(128)}, f32[4,128,128]{2,1,0:T(8,128)S(1)}, s32[]{:T(128)}, bf16[32,4,128,128]{3,2,1,0:T(8,128)(2,1)}, s32[]{:T(128)}, /*index=5*/s32[]{:T(128)}, s32[]{:T(128)}, s32[]{:T(128)}) while((s32[]{:T(128)}, f32[4,128,128]{2,1,0:T(8,128)S(1)}, s32[]{:T(128)}, bf16[32,4,128,128]{3,2,1,0:T(8,128)(2,1)}, s32[]{:T(128)}, ...), condition=%wide.region_12.13_spmd, body=%wide.region_11.12_spmd.sunk | while | flops 131078 | bytes 655503 | solution.py:28
  332.4 1.9 subtract_convert_fusion
  334.7 1.4 fusion.13
  337.1 2.1 copy.109
  339.3 2.0 copy.116
  342.1 1.4 fusion.12
  345.0 194.3 %reduce-scatter.7.cloned.1.call-done = bf16[128,512]{1,0:T(8,128)(2,1)} async-done(((bf16[4096,512]{1,0:T(8,128)(2,1)}), bf16[128,512]{1,0:T(8,128)(2,1)}) %reduce-scatter.7.cloned.1.call-update) | async-done | bytes 131088
  541.0 41.0 %reduce-scatter.5.cloned.1.call-done = bf16[512,512]{1,0:T(8,128)(2,1)} async-done(((bf16[512,4096]{1,0:T(8,128)(2,1)}), bf16[512,512]{1,0:T(8,128)(2,1)}) %reduce-scatter.5.cloned.1.call-update) | async-done | bytes 524304 | tf_op jit(solution)/shard_map/reduce_scatter | solution.py:126
  (154 shorter events, 50.0 us)
Async XLA Ops:
  7.2 87.5 %all-gather.11.cloned.1.call-start = ((), (), s32[]{:S(2)}) async-start(), calls=%async_computation.5 | async-start | bytes 4325376 | tf_op jit(solution)/shard_map/all_gather | solution.py:21
  8.4 6.3 %copy-start.8 = (bf16[8,64,4,128]{3,2,1,0:T(4,128)(2,1)}, bf16[8,64,4,128]{3,2,1,0:T(4,128)(2,1)S(1)}, u32[]{:S(2)}) copy-start(bf16[8,64,4,128]{3,2,1,0:T(4,128)(2,1)S(1)} %reshape.466) | copy-start | bytes 1572868
  9.8 20.0 %copy-start.5 = (bf16[8,64,4,128]{3,2,1,0:T(4,128)(2,1)}, bf16[8,64,4,128]{3,2,1,0:T(4,128)(2,1)S(1)}, u32[]{:S(2)}) copy-start(bf16[8,64,4,128]{3,2,1,0:T(4,128)(2,1)S(1)} %reshape.465) | copy-start | bytes 1572868
  10.9 119.0 %all-gather.9.cloned.1.call-start = ((), (), s32[]{:S(2)}) async-start(), calls=%async_computation.4 | async-start | bytes 4718592 | tf_op jit(solution)/shard_map/all_gather | solution.py:129
  11.7 204.9 %all-gather.7.cloned.1.call-start = ((), (), s32[]{:S(2)}) async-start(), calls=%async_computation.2 | async-start | bytes 4325376 | tf_op jit(solution)/shard_map/all_gather | solution.py:124
  12.4 304.9 %all-gather.13.cloned.1.call-start = ((), (), s32[]{:S(2)}) async-start(), calls=%async_computation.6 | async-start | bytes 4325376 | tf_op jit(solution)/shard_map/all_gather | solution.py:21
  14.7 32.0 %collective-permute-start = (bf16[2,448,512]{2,1,0:T(8,128)(2,1)}, bf16[2,448,512]{2,1,0:T(8,128)(2,1)}, u32[]{:S(2)}, u32[]{:S(2)}) collective-permute-start(bf16[2,448,512]{2,1,0:T(8,128)(2,1)} %pad_maximum_fusion.2), channel_id=1, source_target_pairs={{0,8},{8,16},{16,24},{24,32},{32,40},{40,48},{48,56},{56,64},{64,7... | collective-permute-start | bytes 2752520 | tf_op jit(solution)/shard_map/ppermute | solution.py:34
  23.8 28.7 %copy-start.12 = (bf16[8,64,4,128]{3,2,1,0:T(4,128)(2,1)}, bf16[8,64,4,128]{3,2,1,0:T(4,128)(2,1)S(1)}, u32[]{:S(2)}) copy-start(bf16[8,64,4,128]{3,2,1,0:T(4,128)(2,1)S(1)} %reshape.467) | copy-start | bytes 1572868
  110.7 1.0 copy-start.13
  110.7 1.4 copy-start.9
  110.7 1.4 copy-start.26
  222.4 9.4 %copy-start.22 = (bf16[512,512]{0,1:T(8,128)(2,1)}, bf16[512,512]{0,1:T(8,128)(2,1)S(1)}, u32[]{:S(2)}) copy-start(bf16[512,512]{0,1:T(8,128)(2,1)S(1)} %convolution_convert_fusion.2) | copy-start | bytes 1572868
  227.4 6.3 %copy-start.14 = (bf16[8,64,4,128]{3,2,1,0:T(4,128)(2,1)S(1)}, bf16[8,64,4,128]{3,2,1,0:T(4,128)(2,1)}, u32[]{:S(2)}) copy-start(bf16[8,64,4,128]{3,2,1,0:T(4,128)(2,1)} %copy-done.12) | copy-start | bytes 1572868
  233.7 9.3 %copy-start.16 = (bf16[8,64,4,128]{3,1,2,0:T(8,128)(2,1)}, bf16[8,64,4,128]{3,1,2,0:T(8,128)(2,1)S(1)}, u32[]{:S(2)}) copy-start(bf16[8,64,4,128]{3,1,2,0:T(8,128)(2,1)S(1)} %multiply_convert_fusion.2) | copy-start | bytes 1572868
  233.7 2.8 copy-start.29
  235.6 7.4 %copy-start.20 = (f32[4,128,128]{1,2,0:T(8,128)}, f32[4,128,128]{1,2,0:T(8,128)S(1)}, u32[]{:S(2)}) copy-start(f32[4,128,128]{1,2,0:T(8,128)S(1)} %get-tuple-element.216) | copy-start | bytes 786436
  236.4 302.9 %reduce-scatter.7.cloned.1.call-start = ((), (), s32[]{:S(2)}) async-start(), calls=%async_computation.7 | async-start | bytes 4325376
  249.5 332.5 %reduce-scatter.5.cloned.1.call-start = ((), (), s32[]{:S(2)}) async-start(), calls=%async_computation.3 | async-start | bytes 4718592 | tf_op jit(solution)/shard_map/reduce_scatter | solution.py:126
  256.4 3.7 copy-start.1
  256.4 3.7 copy-start.23
  256.4 3.7 copy-start.30
  256.4 3.9 copy-start.31
  260.1 4.0 copy-start.2
  260.3 1.4 copy-start.24
  261.7 2.3 copy-start
  262.9 7.9 %copy-start.4 = (f32[960,4,128]{2,0,1:T(8,128)}, f32[960,4,128]{2,0,1:T(8,128)S(1)}, u32[]{:S(2)}) copy-start(f32[960,4,128]{2,0,1:T(8,128)S(1)} %convolution_bitcast_fusion.1) | copy-start | bytes 5898244
  262.9 7.0 %copy-start.17 = (bf16[8,64,4,128]{3,1,2,0:T(8,128)(2,1)S(1)}, bf16[8,64,4,128]{3,1,2,0:T(8,128)(2,1)}, u32[]{:S(2)}) copy-start(bf16[8,64,4,128]{3,1,2,0:T(8,128)(2,1)} %copy-done.16) | copy-start | bytes 1572868
  262.9 7.9 %copy-start.10 = (bf16[8,64,4,128]{3,2,1,0:T(4,128)(2,1)S(1)}, bf16[8,64,4,128]{3,2,1,0:T(4,128)(2,1)}, u32[]{:S(2)}) copy-start(bf16[8,64,4,128]{3,2,1,0:T(4,128)(2,1)} %copy-done.8) | copy-start | bytes 1572868
  264.0 7.2 %copy-start.6 = (bf16[8,64,4,128]{3,2,1,0:T(4,128)(2,1)S(1)}, bf16[8,64,4,128]{3,2,1,0:T(4,128)(2,1)}, u32[]{:S(2)}) copy-start(bf16[8,64,4,128]{3,2,1,0:T(4,128)(2,1)} %copy-done.5) | copy-start | bytes 1572868
  265.2 22.2 %collective-permute-start.1 = (bf16[2,448,4,128]{3,1,2,0:T(8,128)(2,1)}, bf16[2,448,4,128]{3,1,2,0:T(8,128)(2,1)}, u32[]{:S(2)}, u32[]{:S(2)}) collective-permute-start(bf16[2,448,4,128]{3,1,2,0:T(8,128)(2,1)} %pad_maximum_fusion.3), channel_id=1, source_target_pairs={{8,0},{16,8},{24,16},{32,24},{40,32},{48,40},{56,48},{64,56},{72,6... | collective-permute-start | bytes 2752520 | tf_op jit(solution)/shard_map/ppermute | solution.py:34
  271.2 0.8 copy-start.27
  271.2 1.2 copy-start.25
  271.2 1.4 copy-start.28
  272.6 16.1 %slice-start = ((f32[960,4,128]{2,0,1:T(8,128)}), f32[512,4,128]{2,0,1:T(8,128)S(1)}, s32[]{:S(2)}) async-start(f32[960,4,128]{2,0,1:T(8,128)} %copy-done.2), calls=%async_computation.8 | async-start | bytes 2097152 | tf_op jit(solution)/shard_map/slice | solution.py:234
  276.4 12.3 %copy-start.3 = (f32[960,4,128]{2,0,1:T(8,128)S(1)}, f32[960,4,128]{2,0,1:T(8,128)}, u32[]{:S(2)}) copy-start(f32[960,4,128]{2,0,1:T(8,128)} %copy-done.2) | copy-start | bytes 5898244
  291.1 41.2 %copy-start.21 = (f32[4,128,128]{1,2,0:T(8,128)S(1)}, f32[4,128,128]{1,2,0:T(8,128)}, u32[]{:S(2)}) copy-start(f32[4,128,128]{1,2,0:T(8,128)} %copy-done.20) | copy-start | bytes 786436
  317.3 17.0 %copy-start.11 = (bf16[8,64,4,128]{3,2,1,0:T(4,128)(2,1)S(1)}, bf16[8,64,4,128]{3,2,1,0:T(4,128)(2,1)}, u32[]{:S(2)}) copy-start(bf16[8,64,4,128]{3,2,1,0:T(4,128)(2,1)} %copy-done.8) | copy-start | bytes 1572868
  332.2 2.5 copy-start.15
  334.3 1.9 copy-start.19
  336.1 5.2 copy-start.7
  336.2 5.9 %copy-start.18 = (bf16[8,64,4,128]{3,1,2,0:T(8,128)(2,1)S(1)}, bf16[8,64,4,128]{3,1,2,0:T(8,128)(2,1)}, u32[]{:S(2)}) copy-start(bf16[8,64,4,128]{3,1,2,0:T(8,128)(2,1)} %copy-done.16) | copy-start | bytes 1572868
Sparse Core Ops, SparseCore 0:
  11.2 83.4 all-gather.10
  96.5 33.4 all-gather.8
  132.4 84.1 all-gather.6
  236.5 80.7 all-gather.12
  321.0 218.2 reduce-scatter.6
  542.4 39.5 reduce-scatter.4
where the time goes:
time: 591 us; the launch traced here: 589 us
  waiting for transfers between devices  417 us (71%)
  matrix products  51.5 us (9%)
  other arithmetic  49.4 us (8%)
  local copies, waits for them, and re-layouts  46.1 us (8%)
  between operations  14.7 us (2%)
  starting transfers between devices  9.02 us (2%)
    unnamed x7, waiting for transfers between devices  196 us
    all_gather x1, waiting for transfers between devices, shards(): lax.all_gather(w_out, 'seq', axis=1, tiled=True)  86.7 us
    all_gather x2, waiting for transfers between devices, entering(): gathered = lax.all_gather(shard.astype(jnp.bfloat16), axis)  53.6 us
    reduce_scatter x1, waiting for transfers between devices, shards(): lax.psum_scatter(partial_value.astype(jnp.bfloat16), 'head', scatter_dime...  41 us
    add x31, other arithmetic, add_states(): return earlier + later  30 us
    ppermute x2, waiting for transfers between devices, shifted(): return lax.ppermute(shard, axis, pairs)  24.6 us
    unnamed x71, local copies, waits for them, and re-layouts  18.5 us
    all_gather x1, waiting for transfers between devices, shards(): grad_full = lax.all_gather(grad_y, 'head', axis=1, tiled=True)  15.8 us
  transfers between devices with their start and end apart: 8, of which 8 were waited for; matrix products, arithmetic and copies ran while one was open for 21% of the time, Pallas kernels for 0%

commit v1 on v0

v1 whole, which is shorter than its diff:
```python
import functools
import math

import jax
import jax.numpy as jnp
from jax import lax
from jax.experimental import pallas as pl
from jax.experimental.pallas import tpu as pltpu
from jax.sharding import PartitionSpec as P

DH = 128
BLOCK = 64
BAND = 8
TILE = 128
TOK = BAND * BLOCK
EDGE = TOK - BLOCK
SCALE = 1.0 / math.sqrt(DH)
EPSILON = 1e-05
MASKED = -1e30
F32 = jnp.float32
BF16 = jnp.bfloat16


def nn(a, b):
    return lax.dot_general(a, b, (((1,), (0,)), ((), ())), preferred_element_type=F32)


def nt(a, b):
    return lax.dot_general(a, b, (((1,), (1,)), ((), ())), preferred_element_type=F32)


def tn(a, b):
    return lax.dot_general(a, b, (((0,), (0,)), ((), ())), preferred_element_type=F32)


def flip(a):
    return a.astype(F32).T


def call(kernel, heads, ins, outs, out_shape, scratch=(), flops=0, size=0, prefetch=0):
    return pl.pallas_call(
        kernel,
        grid_spec=pltpu.PrefetchScalarGridSpec(
            num_scalar_prefetch=prefetch,
            grid=(heads,),
            in_specs=ins,
            out_specs=outs,
            scratch_shapes=scratch,
        ),
        out_shape=out_shape,
        compiler_params=pltpu.CompilerParams(
            dimension_semantics=("arbitrary",), vmem_limit_bytes=48 * 1024 * 1024
        ),
        cost_estimate=pl.CostEstimate(flops=flops, bytes_accessed=size, transcendentals=0),
    )


def columns(rows, at=0):
    return pl.BlockSpec((rows, DH), lambda h, *_: (at, h))


def heads_of(*dims):
    return pl.BlockSpec((1,) + dims, lambda h, *_: (h,) + (0,) * len(dims))


def rows_of(rows, cols):
    return pl.BlockSpec((rows, cols), lambda h, *_: (h, 0))


def sums_kernel(k, v, out):
    out[0] = tn(k[...], v[...]).astype(BF16)


def causal_tile():
    row = lax.broadcasted_iota(jnp.int32, (TILE, TILE), 0)
    col = lax.broadcasted_iota(jnp.int32, (TILE, TILE), 1)
    return row <= col


def edge_tile():
    row = lax.broadcasted_iota(jnp.int32, (TILE, TILE), 0)
    col = lax.broadcasted_iota(jnp.int32, (TILE, TILE), 1)
    return (row >= BLOCK) & (col < BLOCK)


def pad_into(wide, part):
    wide[0:BLOCK, :] = jnp.zeros((BLOCK, DH), BF16)
    wide[BLOCK:TOK, :] = part[...]


def window_kernel(place, q, k, v, kh, vh, near, far, raw, window, intra, kw, vw):
    pad_into(kw, kh)
    pad_into(vw, vh)
    causal, edge = causal_tile(), edge_tile()
    inside = place[0] > 0
    v_t = flip(v[...]).astype(BF16)
    vh_t = flip(vw[...]).astype(BF16)
    for i in range(TOK // TILE):
        lo, hi = i * TILE, (i + 1) * TILE
        q_i = q[lo:hi, :]
        s_near = nt(k[0:hi, :], q_i)
        s_far = nt(kw[lo:TOK, :], q_i) * SCALE
        if i == 0:
            s_near = jnp.where(causal, s_near, 0.0)
            raw_i = s_near.astype(BF16)
            s_near = jnp.where(causal, s_near * SCALE, MASKED)
        else:
            full, last = s_near[0:lo], s_near[lo:hi]
            raw_i = jnp.concatenate([full, jnp.where(causal, last, 0.0)]).astype(BF16)
            s_near = jnp.concatenate([full * SCALE, jnp.where(causal, last * SCALE, MASKED)])
        raw[0, 0:hi, lo:hi] = raw_i
        head = jnp.where(edge, s_far[0:TILE], MASKED)
        if i < TOK // TILE - 1:
            s_far = jnp.concatenate([head, s_far[TILE:]])
        else:
            s_far = head
        s_far = jnp.where(inside, s_far, MASKED)
        top = jnp.maximum(
            jnp.max(s_near, axis=0, keepdims=True), jnp.max(s_far, axis=0, keepdims=True)
        )
        p_near = jnp.exp(s_near - top)
        p_far = jnp.exp(s_far - top)
        inv = 1.0 / (
            jnp.sum(p_near, axis=0, keepdims=True) + jnp.sum(p_far, axis=0, keepdims=True)
        )
        p_near = (p_near * inv).astype(BF16)
        p_far = (p_far * inv).astype(BF16)
        near[0, 0:hi, lo:hi] = p_near
        far[0, lo:TOK, lo:hi] = p_far
        window[:, lo:hi] = nn(v_t[:, 0:hi], p_near) + nn(vh_t[:, lo:TOK], p_far)
        intra[:, lo:hi] = nn(v_t[:, 0:hi], raw_i)


def mixed_kernel(q, before, window, intra, normed, inverse, mixed_t, mixed):
    lin = intra[...] + nt(flip(before[0]).astype(BF16), q[...])
    inv = lax.rsqrt(jnp.mean(lin * lin, axis=0, keepdims=True) + EPSILON)
    unit = lin * inv
    normed[...] = unit
    inverse[0] = inv
    out = unit + window[...]
    mixed_t[...] = out.astype(BF16)
    mixed[...] = out.T.astype(BF16)


def far_kernel(q, g, kh, vh, far, window, dq, dk, dv, delta, kw, vw, ds):
    pad_into(kw, kh)
    pad_into(vw, vh)
    g_t = flip(g[...])
    d = jnp.sum(g_t * window[...], axis=0, keepdims=True)
    delta[0] = d
    kh_t = flip(kw[...]).astype(BF16)
    for i in range(TOK // TILE):
        lo, hi = i * TILE, (i + 1) * TILE
        dp = nt(vw[lo:TOK, :], g[lo:hi, :])
        part = (far[0, lo:TOK, lo:hi].astype(F32) * (dp - d[:, lo:hi]) * SCALE).astype(BF16)
        ds[lo:TOK, lo:hi] = part
        dq[:, lo:hi] = nn(kh_t[:, lo:TOK], part)
    for j in range(TOK // TILE):
        lo, hi = j * TILE, (j + 1) * TILE
        dk_j = nn(ds[lo:hi, 0:hi], q[0:hi, :]).astype(BF16)
        dv_j = nn(far[0, lo:hi, 0:hi], g[0:hi, :]).astype(BF16)
        if j == 0:
            dk[0 : hi - BLOCK, :] = dk_j[BLOCK:]
            dv[0 : hi - BLOCK, :] = dv_j[BLOCK:]
        else:
            dk[lo - BLOCK : hi - BLOCK, :] = dk_j
            dv[lo - BLOCK : hi - BLOCK, :] = dv_j


def lin_kernel(q, g, normed, inverse, grad_lin, sums):
    g_t = flip(g[...])
    unit = normed[...]
    inner = jnp.mean(g_t * unit, axis=0, keepdims=True)
    out = inverse[0] * (g_t - unit * inner)
    rows = out.T.astype(BF16)
    grad_lin[...] = rows
    sums[0] = tn(q[...], rows).astype(BF16)


def near_kernel(q, k, v, g, gl, near, raw, before, delta, dq_far, dq, dk, dv, both):
    causal = causal_tile()
    d = delta[0]
    k_t = flip(k[...]).astype(BF16)
    dq_t = dq_far[...] + nt(before[0], gl[...])
    parts = []
    for i in range(TOK // TILE):
        lo, hi = i * TILE, (i + 1) * TILE
        dp = nt(v[0:hi, :], g[lo:hi, :])
        ig = nt(v[0:hi, :], gl[lo:hi, :])
        last = jnp.where(causal, ig[lo:hi], 0.0)
        ig = last if i == 0 else jnp.concatenate([ig[0:lo], last])
        sum_i = near[0, 0:hi, lo:hi].astype(F32) * (dp - d[:, lo:hi]) * SCALE + ig
        sum_i = sum_i.astype(BF16)
        both[0:hi, lo:hi] = sum_i
        parts.append(dq_t[:, lo:hi] + nn(k_t[:, 0:hi], sum_i))
    dq[...] = jnp.concatenate(parts, axis=1).T.astype(BF16)
    for j in range(TOK // TILE):
        lo, hi = j * TILE, (j + 1) * TILE
        dk[lo:hi, :] = nn(both[lo:hi, lo:TOK], q[lo:TOK, :])
        dv[lo:hi, :] = nn(near[0, lo:hi, lo:TOK], g[lo:TOK, :]) + nn(
            raw[0, lo:hi, lo:TOK], gl[lo:TOK, :]
        )


def last_kernel(k, v, later, dk, dv, rk, rv, out_k, out_v):
    state = later[0]
    add_k = dk[...] + nt(v[...], state)
    add_v = dv[...] + nn(k[...], state)
    out_k[0:BLOCK, :] = add_k[0:BLOCK].astype(BF16)
    out_v[0:BLOCK, :] = add_v[0:BLOCK].astype(BF16)
    out_k[BLOCK:TOK, :] = (add_k[BLOCK:] + rk[...].astype(F32)).astype(BF16)
    out_v[BLOCK:TOK, :] = (add_v[BLOCK:] + rv[...].astype(F32)).astype(BF16)


def scan_kernel(backward, x, out):
    total = jnp.zeros(x.shape[1:], F32)
    count = x.shape[0]
    for i in range(count):
        at = count - 1 - i if backward else i
        out[at] = total.astype(BF16)
        total = total + x[at].astype(F32)


def carry_states(local, backward):
    count = lax.axis_size("seq")
    pieces = local.reshape(count, -1, DH)
    met = lax.all_to_all(pieces, "seq", 0, 0)
    done = pl.pallas_call(
        functools.partial(scan_kernel, backward),
        out_shape=jax.ShapeDtypeStruct(met.shape, BF16),
    )(met)
    return lax.all_to_all(done, "seq", 0, 0).reshape(local.shape)


def whole(kernel, ids, ins, out_shape, scratch=(), flops=0, size=0):
    vmem = pl.BlockSpec(memory_space=pltpu.VMEM)
    smem = pl.BlockSpec(memory_space=pltpu.SMEM)
    return pl.pallas_call(
        kernel,
        in_specs=[smem] + [vmem] * len(ins),
        out_specs=jax.tree.map(lambda _: vmem, out_shape),
        out_shape=out_shape,
        scratch_shapes=scratch,
        compiler_params=pltpu.CompilerParams(vmem_limit_bytes=48 * 1024 * 1024),
        cost_estimate=pl.CostEstimate(flops=flops, bytes_accessed=size, transcendentals=0),
    )(ids, *ins)


def grad_mixed_kernel(ids, w, *rest):
    blocks, out, acc = rest[:-2], rest[-2], rest[-1]
    width = blocks[0].shape[1]
    for j, block in enumerate(blocks):
        at = pl.multiple_of(ids[j] * width, width)
        part = nt(block[...], w[:, pl.ds(at, width)])
        if j == 0:
            acc[...] = part
        elif j < len(blocks) - 1:
            acc[...] += part
        else:
            out[...] = (acc[...] + part).astype(BF16)


def sens_kernel(n, ids, mixed_t, *rest):
    blocks, outs = rest[:n], rest[n:]
    width = blocks[0].shape[1]
    for j, block in enumerate(blocks):
        part = nn(mixed_t[...], block[...]).astype(BF16)
        slot, at = ids[n + j], pl.multiple_of(ids[2 * n + j] * width, width)
        for r, out in enumerate(outs):

            @pl.when(slot == r)
            def _(out=out, part=part, at=at):
                out[:, pl.ds(at, width)] = part


def fold_kernel(n, ids, *rest):
    parts, outs = rest[:n], rest[n:]
    width = outs[0].shape[1]
    for j, out in enumerate(outs):
        at = pl.ds(pl.multiple_of(ids[j] * width, width), width)
        total = parts[0][:, at].astype(F32)
        for part in parts[1:]:
            total = total + part[:, at].astype(F32)
        out[...] = total.astype(BF16)


YS, ZS, XS = 4, 8, 4
Y_HOPS = (1, 3, 2)
Z_HOPS = (1, 7, 2, 6, 3, 5, 4)


def shifted(shard, by):
    count = lax.axis_size("seq")
    pairs = [(i, i + by) for i in range(count) if 0 <= i + by < count]
    return lax.ppermute(shard, "seq", pairs)


def hop_y(shard, by):
    return lax.ppermute(
        shard, "seq", [(y * ZS + z, (y + by) % YS * ZS + z) for y in range(YS) for z in range(ZS)]
    )


def hop_z(shard, by):
    return lax.ppermute(
        shard, "seq", [(y * ZS + z, y * ZS + (z + by) % ZS) for y in range(YS) for z in range(ZS)]
    )


def hop_x(shard, by):
    return lax.ppermute(
        shard, "head", [(x * 2 + c, (x + by) % XS * 2 + c) for x in range(XS) for c in range(2)]
    )


def swap_core(shard):
    return lax.ppermute(shard, "head", [(i, i ^ 1) for i in range(2 * XS)])


def shards(queries, keys, values, w_out, grad_y):
    rows, width = queries.shape
    heads = width // DH
    seq, head = lax.axis_index("seq"), lax.axis_index("head")
    y, z, x, core = seq // ZS, seq % ZS, head // 2, head % 2
    tokens_all = rows * lax.axis_size("seq")
    shape = jax.ShapeDtypeStruct
    col = columns(rows)
    tri = heads_of(rows, rows)
    st = heads_of(DH, DH)
    turned = rows_of(DH, rows)
    line = heads_of(1, rows)
    mm = 2 * rows * rows * width

    halo = shifted(jnp.concatenate([keys[BLOCK:], values[BLOCK:]]), 1)
    full_w = lax.all_gather(w_out, "seq", axis=1, tiled=True)
    grads = [grad_y] + [hop_x(grad_y, by) for by in (1, XS - 1, 2)]
    grads = grads + [swap_core(g) for g in grads]
    source = [(x - by) % XS for by in (0, 1, XS - 1, 2)]
    block_of = [s * 2 + core for s in source] + [s * 2 + 1 - core for s in source]
    slot_of = [(b // 2 - y) % YS for b in block_of]
    ids = jnp.stack(block_of + slot_of + [b % 2 for b in block_of]).astype(jnp.int32)

    local = call(
        sums_kernel, heads, [col, col], st, shape((heads, DH, DH), BF16), flops=2 * mm // 4
    )(keys, values)
    before = carry_states(local, False)

    sq = shape((heads, rows, rows), BF16)
    flat_t = shape((width, rows), F32)
    edge = EDGE
    wide = [pltpu.VMEM((rows, DH), BF16)] * 2
    near, far, raw, window, intra = call(
        window_kernel,
        heads,
        [col, col, col, columns(edge, 0), columns(edge, 1)],
        [tri, tri, tri, turned, turned],
        [sq, sq, sq, flat_t, flat_t],
        scratch=wide,
        flops=12 * mm // 8,
        size=12 << 20,
        prefetch=1,
    )(seq.reshape(1).astype(jnp.int32), queries, keys, values, halo, halo)

    normed, inverse, mixed_t, mixed = call(
        mixed_kernel,
        heads,
        [col, st, turned, turned],
        [turned, line, turned, col],
        [
            flat_t,
            shape((heads, 1, rows), F32),
            shape((width, rows), BF16),
            shape((rows, width), BF16),
        ],
        flops=mm // 4,
        size=5 << 20,
    )(queries, before, window, intra)

    pieces = whole(
        functools.partial(sens_kernel, len(grads)),
        ids,
        [mixed_t] + grads,
        [shape((width, 2 * width), BF16)] * YS,
        flops=8 * mm,
        size=9 << 20,
    )
    got = [pieces[0]] + [hop_y(pieces[by], by) for by in Y_HOPS]
    z_ids = jnp.stack([(z + by) % ZS for by in (0,) + Z_HOPS]).astype(jnp.int32)
    parts = whole(
        functools.partial(fold_kernel, YS),
        z_ids,
        got,
        [shape((width, DH), BF16)] * ZS,
        size=5 << 20,
    )
    total = parts[0].astype(F32)
    for part, by in zip(parts[1:], Z_HOPS):
        total = total + hop_z(part, by).astype(F32)
    projection_sensitivity = total * tokens_all ** (-0.5)

    grad_mixed = whole(
        grad_mixed_kernel,
        ids,
        [full_w] + grads,
        shape((rows, width), BF16),
        scratch=[pltpu.VMEM((rows, width), F32)],
        flops=8 * mm,
        size=9 << 20,
    )
    partial_value = jnp.dot(mixed, full_w, preferred_element_type=F32).astype(BF16)
    mixer_result = lax.psum_scatter(partial_value, "head", scatter_dimension=1, tiled=True)

    edge_grad = shape((edge, width), BF16)
    dq_far, far_k, far_v, delta = call(
        far_kernel,
        heads,
        [col, col, columns(edge, 0), columns(edge, 1), tri, turned],
        [turned, columns(edge), columns(edge), line],
        [flat_t, edge_grad, edge_grad, shape((heads, 1, rows), F32)],
        scratch=wide + [pltpu.VMEM((rows, rows), BF16)],
        flops=8 * mm // 8,
        size=8 << 20,
    )(queries, grad_mixed, halo, halo, far, window)
    back_k, back_v = shifted(far_k, -1), shifted(far_v, -1)

    grad_lin, local_back = call(
        lin_kernel,
        heads,
        [col, col, turned, line],
        [col, st],
        [shape((rows, width), BF16), shape((heads, DH, DH), BF16)],
        flops=mm // 4,
        size=3 << 20,
    )(queries, grad_mixed, normed, inverse)
    later = carry_states(local_back, True)

    grad_queries, near_k, near_v = call(
        near_kernel,
        heads,
        [col, col, col, col, col, tri, tri, st, line, turned],
        [col, col, col],
        [shape((rows, width), BF16), shape((rows, width), F32), shape((rows, width), F32)],
        scratch=[pltpu.VMEM((rows, rows), BF16)],
        flops=12 * mm // 8,
        size=12 << 20,
    )(queries, keys, values, grad_mixed, grad_lin, near, raw, before, delta, dq_far)

    grad_keys, grad_values = call(
        last_kernel,
        heads,
        [col, col, st, col, col, columns(edge), columns(edge)],
        [col, col],
        [shape((rows, width), BF16)] * 2,
        flops=mm // 2,
        size=5 << 20,
    )(keys, values, later, near_k, near_v, back_k, back_v)
    return (mixer_result, grad_queries, grad_keys, grad_values, projection_sensitivity)


def solution(mesh):
    placed = (
        P("seq", "head"),
        P("seq", "head"),
        P("seq", "head"),
        P("head", "seq"),
        P("seq", "head"),
    )
    return jax.shard_map(
        shards,
        mesh=mesh,
        in_specs=placed,
        out_specs=(
            P("seq", "head"),
            P("seq", "head"),
            P("seq", "head"),
            P("seq", "head"),
            P("head", "seq"),
        ),
        check_vma=False,
    )
```

time: 591 us -> 294 us (0.50)
  waiting for transfers between devices: 417 us -> 109 us
  Pallas kernels: 0 us -> 51 us
  starting transfers between devices: 9.02 us -> 57.6 us
  other arithmetic: 49.4 us -> 3.08 us
  matrix products: 51.5 us -> 6.7 us
  blocking collectives: 0 us -> 28.7 us
  local copies, waits for them, and re-layouts: 46.1 us -> 22.3 us
    unnamed x7 -> x2, waiting for transfers between devices: 196 us -> 0.7 us
    all_gather x4 -> x1, waiting for transfers between devices: 156 us -> 29.5 us  [shards(): full_w = lax.all_gather(w_out, 'seq', axis=1, tiled=True)]
    ppermute x2 -> x20, waiting for transfers between devices: 24.6 us -> 78.7 us  [the longest x3 44.6 us: hop_y(): lax.ppermute(shard, 'seq', [(y * ZS + z, (y + by) % YS * ZS + z) for y in...]
    pallas_call x0 -> x12, Pallas kernels: none -> 51 us  [the longest x3 16.7 us: whole(): pl.pallas_call(kernel, in_specs=[smem] + [vmem] * len(ins), out_specs=jax...]
    reduce_scatter x1, waiting for transfers between devices: 41 us -> 0.01 us  [shards(): lax.psum_scatter(partial_value, 'head', scatter_dimension=1, tiled=True)]
    dot_general x20 -> x1, matrix products: 44 us -> 6.7 us  [shards(): jnp.dot(mixed, full_w, preferred_element_type=F32).astype(BF16)]
    add x32 -> x0, other arithmetic: 30 us -> none  [the longest x31 30 us: add_states(): return earlier + later]
    all_to_all x0 -> x1, blocking collectives: none -> 28.7 us  [carry_states(): met = lax.all_to_all(pieces, 'seq', 0, 0)]
  transfers between devices with their start and end apart: 8 -> 25, of which waited for: 8 -> 7; matrix products, arithmetic and copies ran while one was open for 21% -> 2% of each run, Pallas kernels for 0% -> 17%
where the time goes in v1:
time: 294 us; the launch traced here: 293 us
  waiting for transfers between devices  109 us (37%)
  starting transfers between devices  57.6 us (20%)
  Pallas kernels  51 us (17%)
  blocking collectives  28.7 us (10%)
  local copies, waits for them, and re-layouts  22.3 us (8%)
  between operations  14.4 us (5%)
  matrix products  6.7 us (2%)
  other arithmetic  3.08 us (1%)
    ppermute x3, waiting for transfers between devices, hop_y(): lax.ppermute(shard, 'seq', [(y * ZS + z, (y + by) % YS * ZS + z) for y in...  44.6 us
    all_gather x1, waiting for transfers between devices, shards(): full_w = lax.all_gather(w_out, 'seq', axis=1, tiled=True)  29.5 us
    all_to_all x1, blocking collectives, carry_states(): met = lax.all_to_all(pieces, 'seq', 0, 0)  28.7 us
    ppermute x3, waiting for transfers between devices, hop_x(): lax.ppermute(shard, 'head', [(x * 2 + c, (x + by) % XS * 2 + c) for x in...  26 us
    unnamed x56, local copies, waits for them, and re-layouts  20 us
    pallas_call x3, Pallas kernels, whole(): pl.pallas_call(kernel, in_specs=[smem] + [vmem] * len(ins), out_specs=jax...  16.7 us
    all_to_all x2, starting transfers between devices, carry_states(): return lax.all_to_all(done, 'seq', 0, 0).reshape(local.shape)  15.9 us
    ppermute x7, starting transfers between devices, hop_z(): lax.ppermute(shard, 'seq', [(y * ZS + z, y * ZS + (z + by) % ZS) for y in...  12.8 us
  transfers between devices with their start and end apart: 25, of which 7 were waited for; matrix products, arithmetic and copies ran while one was open for 2% of the time, Pallas kernels for 17%

profile of v1, /device:TPU:16, one launch (start us, length us, event | category | flops | bytes accessed | tf_op | source)
XLA Modules:
  0.0 292.7 jit_solution(4994293801231793301)
XLA Ops:
  7.9 1.1 slice.7
  9.0 1.1 slice.6
  11.1 3.8 %collective-permute-start = (bf16[896,512]{1,0:T(8,128)(2,1)}, bf16[896,512]{1,0:T(8,128)(2,1)S(1)}, u32[]{:S(2)}, u32[]{:S(2)}) collective-permute-start(bf16[896,512]{1,0:T(8,128)(2,1)} %pad_maximum_fusion), channel_id=1, source_target_pairs={{0,8},{8,16},{16,24},{24,32},{32,40},{40,48},{48,56},{56,64},{64,7... | collective-permute-start | bytes 2752520 | tf_op jit(solution)/shard_map/ppermute | solution.py:295
  14.9 1.0 copy-done.1
  15.9 1.0 copy-done.3
  17.0 1.2 shard_map.92
  18.2 28.7 %all_to_all.20.x = bf16[32,16,128]{2,1,0:T(8,128)(2,1)} all-to-all(bf16[32,16,128]{2,1,0:T(8,128)(2,1)S(1)} %bitcast.40), channel_id=1, replica_groups=mesh['seq'=32,'head'=8] {'seq'}, dimensions={0} | all-to-all | bytes 262144 | tf_op jit(solution)/shard_map/all_to_all | solution.py:227
  46.8 1.6 shard_map.93
  48.4 7.7 %all-to-all-start.1 = ((bf16[32,16,128]{2,1,0:T(8,128)(2,1)}), bf16[32,16,128]{2,1,0:T(8,128)(2,1)}, u32[]{:S(2)}, u32[]{:S(2)}) async-start(bf16[32,16,128]{2,1,0:T(8,128)(2,1)} %shard_map.93), calls=%async_computation.1 | async-start | bytes 262144 | tf_op jit(solution)/shard_map/all_to_all | solution.py:232
  56.2 8.4 %shard_map.94 = (bf16[4,512,512]{2,1,0:T(8,128)(2,1)}, bf16[4,512,512]{2,1,0:T(8,128)(2,1)}, bf16[4,512,512]{2,1,0:T(8,128)(2,1)}, f32[512,512]{1,0:T(8,128)S(1)}, f32[512,512]{1,0:T(8,128)S(1)}) custom-call(s32[1]{0:T(128)} %bitcast.2.place, bf16[512,512]{1,0:T(8,128)(2,1)S(1)} %copy-done, bf16[512,512]{1,0:T(8,128)(2,1)S(1)} %copy-done.2, ...), custom_call_target="tpu_custom_call" | custom-call | flops 402653184 | bytes 12582912 | tf_op jit(solution)/shard_map/pallas_call | solution.py:352
  65.7 1.6 copy-done.12
  67.3 2.8 shard_map.95
  72.6 29.5 %all-gather.2.cloned.1.call-done.w = bf16[512,4096]{1,0:T(8,128)(2,1)} async-done(((bf16[512,128]{1,0:T(8,128)(2,1)}), bf16[512,4096]{1,0:T(8,128)(2,1)}) %all-gather.2.cloned.1.call-update) | async-done | bytes 4194320 | tf_op jit(solution)/shard_map/all_gather | solution.py:335
  102.1 6.7 %convolution_convert_fusion = bf16[512,4096]{1,0:T(8,128)(2,1)} fusion(bf16[512,512]{1,0:T(8,128)(2,1)} %copy-done.27, bf16[512,4096]{1,0:T(8,128)(2,1)} %all-gather.2.cloned.1.call-done.w), kind=kOutput, calls=%fused_computation | convolution fusion | flops 2149580800 | bytes 8912896 | tf_op jit(solution)/shard_map/dot_general | solution.py:410
  109.9 1.5 collective-permute-start.1
  111.4 1.8 collective-permute-start.2
  113.1 1.8 collective-permute-start.3
  114.9 11.4 %collective-permute-done.1.rest_1_ = bf16[512,512]{1,0:T(8,128)(2,1)S(1)} collective-permute-done((bf16[512,512]{1,0:T(8,128)(2,1)S(1)}, bf16[512,512]{1,0:T(8,128)(2,1)S(1)}, u32[]{:S(2)}, u32[]{:S(2)}) %collective-permute-start.1) | collective-permute-done | bytes 524320 | tf_op jit(solution)/shard_map/ppermute | solution.py:311
  126.3 3.1 %collective-permute-done.2.rest_2_ = bf16[512,512]{1,0:T(8,128)(2,1)} collective-permute-done((bf16[512,512]{1,0:T(8,128)(2,1)S(1)}, bf16[512,512]{1,0:T(8,128)(2,1)}, u32[]{:S(2)}, u32[]{:S(2)}) %collective-permute-start.2) | collective-permute-done | bytes 524320 | tf_op jit(solution)/shard_map/ppermute | solution.py:311
  129.4 11.5 %collective-permute-done.3.rest_3_ = bf16[512,512]{1,0:T(8,128)(2,1)} collective-permute-done((bf16[512,512]{1,0:T(8,128)(2,1)S(1)}, bf16[512,512]{1,0:T(8,128)(2,1)}, u32[]{:S(2)}, u32[]{:S(2)}) %collective-permute-start.3) | collective-permute-done | bytes 524320 | tf_op jit(solution)/shard_map/ppermute | solution.py:311
  141.0 2.1 collective-permute-done.7.rest_7_
  143.2 1.1 copy-done.18
  144.2 1.1 copy-done.21
  145.3 1.1 copy-done.26
  146.3 7.7 %shard_map.102 = (bf16[512,1024]{1,0:T(8,128)(2,1)S(1)}, bf16[512,1024]{1,0:T(8,128)(2,1)}, bf16[512,1024]{1,0:T(8,128)(2,1)}, bf16[512,1024]{1,0:T(8,128)(2,1)}) custom-call(s32[24]{0:T(128)S(1)} %stack.126.ids, bf16[512,512]{1,0:T(8,128)(2,1)S(1)} %copy-done.26, bf16[512,512]{1,0:T(8,128)(2,1)S(1)} %copy-done.18, bf16[512,512]{1,0:T(8,128)(2,1)S(1)} %copy-done.21, ...), custom_call_target="tpu_custom_call" | custom-call | flops 2147483648 | bytes 9437184 | tf_op jit(solution)/shard_map/pallas_call | solution.py:238
  154.0 1.2 collective-permute-start.10
  156.0 1.3 collective-permute-start.12
  157.4 44.6 %collective-permute-done.10.rest_1_ = bf16[512,1024]{1,0:T(8,128)(2,1)} collective-permute-done((bf16[512,1024]{1,0:T(8,128)(2,1)}, bf16[512,1024]{1,0:T(8,128)(2,1)}, u32[]{:S(2)}, u32[]{:S(2)}) %collective-permute-start.10) | collective-permute-done | bytes 1048608 | tf_op jit(solution)/shard_map/ppermute | solution.py:299
  202.0 3.6 %shard_map.103 = (bf16[512,128]{1,0:T(8,128)(2,1)S(1)}, bf16[512,128]{1,0:T(8,128)(2,1)}, bf16[512,128]{1,0:T(8,128)(2,1)}, bf16[512,128]{1,0:T(8,128)(2,1)}, bf...) custom-call(s32[8]{0:T(128)S(1)} %stack.135.ids, ...), custom_call_target="tpu_custom_call" | custom-call | bytes 5242880 | tf_op jit(solution)/shard_map/pallas_call | solution.py:238
  206.0 4.7 %collective-permute-start.18 = (bf16[512,128]{1,0:T(8,128)(2,1)}, bf16[512,128]{1,0:T(8,128)(2,1)}, u32[]{:S(2)}, u32[]{:S(2)}) collective-permute-start(bf16[512,128]{1,0:T(8,128)(2,1)} %get-tuple-element.67), channel_id=1, source_target_pairs={{0,40},{8,48},{16,56},{24,0},{32,8},{40,16},{48,24},{56,32},{64,10... | collective-permute-start | bytes 393224 | tf_op jit(solution)/shard_map/ppermute | solution.py:305
  210.8 4.3 %collective-permute-start.16 = (bf16[512,128]{1,0:T(8,128)(2,1)}, bf16[512,128]{1,0:T(8,128)(2,1)}, u32[]{:S(2)}, u32[]{:S(2)}) collective-permute-start(bf16[512,128]{1,0:T(8,128)(2,1)} %get-tuple-element.65), channel_id=1, source_target_pairs={{0,48},{8,56},{16,0},{24,8},{32,16},{40,24},{48,32},{56,40},{64,11... | collective-permute-start | bytes 393224 | tf_op jit(solution)/shard_map/ppermute | solution.py:305
  215.1 5.4 %shard_map.96.g = bf16[512,512]{1,0:T(8,128)(2,1)S(1)} custom-call(s32[24]{0:T(128)S(1)} %stack.126.ids, bf16[512,4096]{1,0:T(8,128)(2,1)} %all-gather.2.cloned.1.call-done.w, bf16[512,512]{1,0:T(8,128)(2,1)S(1)} %copy-done.19, bf16[512,512]{1,0:T(8,128)(2,1)S(1)} %copy-done.22, bf16[512,512]{1,0:T(8,128)(2,1)} %collective-permute-done.2.rest_2_, ...), custom_call_target="tpu_custom_call" | custom-call | flops 2147483648 | bytes 9437184 | tf_op jit(solution)/shard_map/pallas_call | solution.py:238
  220.5 1.8 shard_map.97
  223.0 8.8 %all-to-all-start.2 = ((bf16[32,16,128]{2,1,0:T(8,128)(2,1)}), bf16[32,16,128]{2,1,0:T(8,128)(2,1)}, u32[]{:S(2)}, u32[]{:S(2)}) async-start(bf16[32,16,128]{2,1,0:T(8,128)(2,1)} %bitcast.41), calls=%async_computation.3 | async-start | bytes 262144 | tf_op jit(solution)/shard_map/all_to_all | solution.py:227
  231.9 1.2 copy-done.6
  233.1 5.5 %shard_map.98 = (f32[512,512]{1,0:T(8,128)S(1)}, bf16[448,512]{1,0:T(8,128)(2,1)}, bf16[448,512]{1,0:T(8,128)(2,1)}, f32[4,1,512]{2,1,0:T(1,128)S(1)}) custom-call(bf16[512,512]{1,0:T(8,128)(2,1)S(1)} %copy-done, bf16[512,512]{1,0:T(8,128)(2,1)S(1)} %shard_map.96.g, bf16[896,512]{1,0:T(8,128)(2,1)S(1)} %collective-permute-done.kh.vh, ...), custom_call_target="tpu_custom_call" | custom-call | flops 268435456 | bytes 8388608 | tf_op jit(solution)/shard_map/pallas_call | solution.py:414
  239.6 4.6 %collective-permute-start.8 = (bf16[448,512]{1,0:T(8,128)(2,1)}, bf16[448,512]{1,0:T(8,128)(2,1)S(1)}, u32[]{:S(2)}, u32[]{:S(2)}) collective-permute-start(bf16[448,512]{1,0:T(8,128)(2,1)} %get-tuple-element.52), channel_id=1, source_target_pairs={{8,0},{16,8},{24,16},{32,24},{40,32},{48,40},{56,48},{64,56},{72,6... | collective-permute-start | bytes 1376264 | tf_op jit(solution)/shard_map/ppermute | solution.py:295
  244.2 3.4 %collective-permute-start.9 = (bf16[448,512]{1,0:T(8,128)(2,1)}, bf16[448,512]{1,0:T(8,128)(2,1)}, u32[]{:S(2)}, u32[]{:S(2)}) collective-permute-start(bf16[448,512]{1,0:T(8,128)(2,1)} %get-tuple-element.53), channel_id=1, source_target_pairs={{8,0},{16,8},{24,16},{32,24},{40,32},{48,40},{56,48},{64,56},{72,6... | collective-permute-start | bytes 1376264 | tf_op jit(solution)/shard_map/ppermute | solution.py:295
  247.7 3.2 %collective-permute-start.14 = (bf16[512,128]{1,0:T(8,128)(2,1)}, bf16[512,128]{1,0:T(8,128)(2,1)S(1)}, u32[]{:S(2)}, u32[]{:S(2)}) collective-permute-start(bf16[512,128]{1,0:T(8,128)(2,1)} %get-tuple-element.63), channel_id=1, source_target_pairs={{0,56},{8,0},{16,8},{24,16},{32,24},{40,32},{48,40},{56,48},{64,12... | collective-permute-start | bytes 393224 | tf_op jit(solution)/shard_map/ppermute | solution.py:305
  250.9 1.6 shard_map.100
  252.5 8.2 %all-to-all-start.3 = ((bf16[32,16,128]{2,1,0:T(8,128)(2,1)}), bf16[32,16,128]{2,1,0:T(8,128)(2,1)S(1)}, u32[]{:S(2)}, u32[]{:S(2)}) async-start(bf16[32,16,128]{2,1,0:T(8,128)(2,1)} %shard_map.100), calls=%async_computation.4 | async-start | bytes 262144 | tf_op jit(solution)/shard_map/all_to_all | solution.py:232
  260.7 6.0 %collective-permute-done.14 = bf16[512,128]{1,0:T(8,128)(2,1)S(1)} collective-permute-done((bf16[512,128]{1,0:T(8,128)(2,1)}, bf16[512,128]{1,0:T(8,128)(2,1)S(1)}, u32[]{:S(2)}, u32[]{:S(2)}) %collective-permute-start.14) | collective-permute-done | bytes 131104 | tf_op jit(solution)/shard_map/ppermute | solution.py:305
  266.7 2.0 add_multiply_fusion
  268.8 1.2 copy-done.8
  270.0 7.4 %shard_map.99 = (bf16[512,512]{1,0:T(8,128)(2,1)}, f32[512,512]{1,0:T(8,128)S(1)}, f32[512,512]{1,0:T(8,128)S(1)}) custom-call(bf16[512,512]{1,0:T(8,128)(2,1)S(1)} %copy-done, bf16[512,512]{1,0:T(8,128)(2,1)S(1)} %copy-done.2, bf16[512,512]{1,0:T(8,128)(2,1)S(1)} %copy-done.4, bf16[512,512]{1,0:T(8,128)(2,1)S(1)} %shard_map.96.g, ...), custom_call_target="tpu_custom_call" | custom-call | flops 402653184 | bytes 12582912 | tf_op jit(solution)/shard_map/pallas_call | solution.py:437
  279.4 1.2 copy-done.14
  280.7 1.2 copy-done.16
  281.9 3.9 %shard_map.101 = (bf16[512,512]{1,0:T(8,128)(2,1)}, bf16[512,512]{1,0:T(8,128)(2,1)}) custom-call(bf16[512,512]{1,0:T(8,128)(2,1)S(1)} %copy-done.2, bf16[512,512]{1,0:T(8,128)(2,1)S(1)} %copy-done.4, bf16[4,128,128]{2,1,0:T(8,128)(2,1)S(1)} %bitcast.39, f32[512,512]{1,0:T(8,128)S(1)} %copy-done.14, f32[512,512]{1,0:T(8,128)S(1)} %copy-done.16, ...), custom_call_target="tpu_custom_call" | custom-call | flops 134217728 | bytes 5242880 | tf_op jit(solution)/shard_map/pallas_call | solution.py:448
  (80 shorter events, 11.8 us)
Async XLA Ops:
  7.2 49.0 %copy-start.4 = (bf16[512,512]{1,0:T(8,128)(2,1)S(1)}, bf16[512,512]{1,0:T(8,128)(2,1)}, u32[]{:S(2)}) copy-start(bf16[512,512]{1,0:T(8,128)(2,1)} %v.7) | copy-start | bytes 1572868
  7.2 49.0 %copy-start.2 = (bf16[512,512]{1,0:T(8,128)(2,1)S(1)}, bf16[512,512]{1,0:T(8,128)(2,1)}, u32[]{:S(2)}) copy-start(bf16[512,512]{1,0:T(8,128)(2,1)} %k.7) | copy-start | bytes 1572868
  7.2 49.0 %copy-start = (bf16[512,512]{1,0:T(8,128)(2,1)S(1)}, bf16[512,512]{1,0:T(8,128)(2,1)}, u32[]{:S(2)}) copy-start(bf16[512,512]{1,0:T(8,128)(2,1)} %q.9) | copy-start | bytes 1572868
  7.2 94.9 %all-gather.2.cloned.1.call-start = ((), (), s32[]{:S(2)}) async-start(), calls=%async_computation.5 | async-start | bytes 4325376 | tf_op jit(solution)/shard_map/all_gather | solution.py:335
  11.1 45.1 %collective-permute-start = (bf16[896,512]{1,0:T(8,128)(2,1)}, bf16[896,512]{1,0:T(8,128)(2,1)S(1)}, u32[]{:S(2)}, u32[]{:S(2)}) collective-permute-start(bf16[896,512]{1,0:T(8,128)(2,1)} %pad_maximum_fusion), channel_id=1, source_target_pairs={{0,8},{8,16},{16,24},{24,32},{32,40},{40,48},{48,56},{56,64},{64,7... | collective-permute-start | bytes 2752520 | tf_op jit(solution)/shard_map/ppermute | solution.py:295
  14.9 1.0 copy-start.1
  15.9 1.0 copy-start.3
  48.4 17.3 %all-to-all-start.1 = ((bf16[32,16,128]{2,1,0:T(8,128)(2,1)}), bf16[32,16,128]{2,1,0:T(8,128)(2,1)}, u32[]{:S(2)}, u32[]{:S(2)}) async-start(bf16[32,16,128]{2,1,0:T(8,128)(2,1)} %shard_map.93), calls=%async_computation.1 | async-start | bytes 262144 | tf_op jit(solution)/shard_map/all_to_all | solution.py:232
  56.1 229.7 %reduce-scatter.2.cloned.1.call-start = ((), (), s32[]{:S(2)}) async-start(), calls=%async_computation.6 | async-start | bytes 4718592 | tf_op jit(solution)/shard_map/reduce_scatter | solution.py:411
  64.6 1.0 copy-start.11
  65.7 43.2 %copy-start.5 = (f32[512,512]{1,0:T(8,128)}, f32[512,512]{1,0:T(8,128)S(1)}, u32[]{:S(2)}) copy-start(f32[512,512]{1,0:T(8,128)S(1)} %get-tuple-element.37.window) | copy-start | bytes 3145732
  65.7 1.6 copy-start.12
  108.8 1.0 copy-start.17
  109.9 16.4 %collective-permute-start.1 = (bf16[512,512]{1,0:T(8,128)(2,1)S(1)}, bf16[512,512]{1,0:T(8,128)(2,1)S(1)}, u32[]{:S(2)}, u32[]{:S(2)}) collective-permute-start(bf16[512,512]{1,0:T(8,128)(2,1)S(1)} %copy-done.17), channel_id=1, source_target_pairs={{0,2},{1,3},{2,4},{3,5},{4,6},{5,7},{6,0},{7,1},{8,10},{9,11},{10,... | collective-permute-start | bytes 1572872 | tf_op jit(solution)/shard_map/ppermute | solution.py:311
  111.4 18.1 %collective-permute-start.2 = (bf16[512,512]{1,0:T(8,128)(2,1)S(1)}, bf16[512,512]{1,0:T(8,128)(2,1)}, u32[]{:S(2)}, u32[]{:S(2)}) collective-permute-start(bf16[512,512]{1,0:T(8,128)(2,1)S(1)} %copy-done.17), channel_id=1, source_target_pairs={{0,6},{1,7},{2,0},{3,1},{4,2},{5,3},{6,4},{7,5},{8,14},{9,15},{10,... | collective-permute-start | bytes 1572872 | tf_op jit(solution)/shard_map/ppermute | solution.py:311
  113.1 27.8 %collective-permute-start.3 = (bf16[512,512]{1,0:T(8,128)(2,1)S(1)}, bf16[512,512]{1,0:T(8,128)(2,1)}, u32[]{:S(2)}, u32[]{:S(2)}) collective-permute-start(bf16[512,512]{1,0:T(8,128)(2,1)S(1)} %copy-done.17), channel_id=1, source_target_pairs={{0,4},{1,5},{2,6},{3,7},{4,0},{5,1},{6,2},{7,3},{8,12},{9,13},{10,... | collective-permute-start | bytes 1572872 | tf_op jit(solution)/shard_map/ppermute | solution.py:311
  114.9 26.1 %collective-permute-start.4 = (bf16[512,512]{1,0:T(8,128)(2,1)S(1)}, bf16[512,512]{1,0:T(8,128)(2,1)}, u32[]{:S(2)}, u32[]{:S(2)}) collective-permute-start(bf16[512,512]{1,0:T(8,128)(2,1)S(1)} %copy-done.17), channel_id=1, source_target_pairs={{0,1},{1,0},{2,3},{3,2},{4,5},{5,4},{6,7},{7,6},{8,9},{9,8},{10,11... | collective-permute-start | bytes 1572872 | tf_op jit(solution)/shard_map/ppermute | solution.py:317
  126.3 16.8 %copy-start.20 = (bf16[512,512]{1,0:T(8,128)(2,1)}, bf16[512,512]{1,0:T(8,128)(2,1)S(1)}, u32[]{:S(2)}) copy-start(bf16[512,512]{1,0:T(8,128)(2,1)S(1)} %collective-permute-done.1.rest_1_) | copy-start | bytes 1572868
  126.3 14.7 %collective-permute-start.5 = (bf16[512,512]{1,0:T(8,128)(2,1)S(1)}, bf16[512,512]{1,0:T(8,128)(2,1)}, u32[]{:S(2)}, u32[]{:S(2)}) collective-permute-start(bf16[512,512]{1,0:T(8,128)(2,1)S(1)} %collective-permute-done.1.rest_1_), channel_id=1, source_target_pairs={{0,1},{1,0},{2,3},{3,2},{4,5},{5,4},{6,7},{7,6},{8,9},{9,8},{10,11... | collective-permute-start | bytes 1572872 | tf_op jit(solution)/shard_map/ppermute | solution.py:317
  129.4 11.6 %collective-permute-start.6 = (bf16[512,512]{1,0:T(8,128)(2,1)}, bf16[512,512]{1,0:T(8,128)(2,1)}, u32[]{:S(2)}, u32[]{:S(2)}) collective-permute-start(bf16[512,512]{1,0:T(8,128)(2,1)} %collective-permute-done.2.rest_2_), channel_id=1, source_target_pairs={{0,1},{1,0},{2,3},{3,2},{4,5},{5,4},{6,7},{7,6},{8,9},{9,8},{10,11... | collective-permute-start | bytes 1572872 | tf_op jit(solution)/shard_map/ppermute | solution.py:317
  140.9 2.3 collective-permute-start.7
  143.2 1.1 copy-start.18
  144.2 1.1 copy-start.21
  145.3 1.1 copy-start.26
  154.0 48.0 %collective-permute-start.10 = (bf16[512,1024]{1,0:T(8,128)(2,1)}, bf16[512,1024]{1,0:T(8,128)(2,1)}, u32[]{:S(2)}, u32[]{:S(2)}) collective-permute-start(bf16[512,1024]{1,0:T(8,128)(2,1)} %get-tuple-element.58), channel_id=1, source_target_pairs={{0,64},{8,72},{16,80},{24,88},{32,96},{40,104},{48,112},{56,120},{... | collective-permute-start | bytes 3145736 | tf_op jit(solution)/shard_map/ppermute | solution.py:299
  155.2 46.7 %collective-permute-start.11 = (bf16[512,1024]{1,0:T(8,128)(2,1)}, bf16[512,1024]{1,0:T(8,128)(2,1)}, u32[]{:S(2)}, u32[]{:S(2)}) collective-permute-start(bf16[512,1024]{1,0:T(8,128)(2,1)} %get-tuple-element.59), channel_id=1, source_target_pairs={{0,192},{8,200},{16,208},{24,216},{32,224},{40,232},{48,240},{56,2... | collective-permute-start | bytes 3145736 | tf_op jit(solution)/shard_map/ppermute | solution.py:299
  156.0 45.9 %collective-permute-start.12 = (bf16[512,1024]{1,0:T(8,128)(2,1)}, bf16[512,1024]{1,0:T(8,128)(2,1)}, u32[]{:S(2)}, u32[]{:S(2)}) collective-permute-start(bf16[512,1024]{1,0:T(8,128)(2,1)} %get-tuple-element.60), channel_id=1, source_target_pairs={{0,128},{8,136},{16,144},{24,152},{32,160},{40,168},{48,176},{56,1... | collective-permute-start | bytes 3145736 | tf_op jit(solution)/shard_map/ppermute | solution.py:299
  157.4 57.7 %copy-start.19 = (bf16[512,512]{1,0:T(8,128)(2,1)S(1)}, bf16[512,512]{1,0:T(8,128)(2,1)}, u32[]{:S(2)}) copy-start(bf16[512,512]{1,0:T(8,128)(2,1)} %rest_0_.3) | copy-start | bytes 1572868
  157.4 57.7 %copy-start.22 = (bf16[512,512]{1,0:T(8,128)(2,1)S(1)}, bf16[512,512]{1,0:T(8,128)(2,1)}, u32[]{:S(2)}) copy-start(bf16[512,512]{1,0:T(8,128)(2,1)} %copy-done.20) | copy-start | bytes 1572868
  205.6 14.9 %copy-start.23 = (bf16[512,128]{1,0:T(8,128)(2,1)}, bf16[512,128]{1,0:T(8,128)(2,1)S(1)}, u32[]{:S(2)}) copy-start(bf16[512,128]{1,0:T(8,128)(2,1)S(1)} %get-tuple-element.61) | copy-start | bytes 393220
  205.6 38.6 %collective-permute-start.19 = (bf16[512,128]{1,0:T(8,128)(2,1)}, bf16[512,128]{1,0:T(8,128)(2,1)}, u32[]{:S(2)}, u32[]{:S(2)}) collective-permute-start(bf16[512,128]{1,0:T(8,128)(2,1)} %get-tuple-element.68), channel_id=1, source_target_pairs={{0,32},{8,40},{16,48},{24,56},{32,0},{40,8},{48,16},{56,24},{64,96... | collective-permute-start | bytes 393224 | tf_op jit(solution)/shard_map/ppermute | solution.py:305
  206.0 41.6 %collective-permute-start.18 = (bf16[512,128]{1,0:T(8,128)(2,1)}, bf16[512,128]{1,0:T(8,128)(2,1)}, u32[]{:S(2)}, u32[]{:S(2)}) collective-permute-start(bf16[512,128]{1,0:T(8,128)(2,1)} %get-tuple-element.67), channel_id=1, source_target_pairs={{0,40},{8,48},{16,56},{24,0},{32,8},{40,16},{48,24},{56,32},{64,10... | collective-permute-start | bytes 393224 | tf_op jit(solution)/shard_map/ppermute | solution.py:305
  210.7 37.0 %collective-permute-start.17 = (bf16[512,128]{1,0:T(8,128)(2,1)}, bf16[512,128]{1,0:T(8,128)(2,1)}, u32[]{:S(2)}, u32[]{:S(2)}) collective-permute-start(bf16[512,128]{1,0:T(8,128)(2,1)} %get-tuple-element.66), channel_id=1, source_target_pairs={{0,24},{8,32},{16,40},{24,48},{32,56},{40,0},{48,8},{56,16},{64,88... | collective-permute-start | bytes 393224 | tf_op jit(solution)/shard_map/ppermute | solution.py:305
  210.8 9.7 %copy-start.10 = (f32[512,512]{1,0:T(8,128)S(1)}, f32[512,512]{1,0:T(8,128)}, u32[]{:S(2)}) copy-start(f32[512,512]{1,0:T(8,128)} %copy-done.9) | copy-start | bytes 3145732
  210.8 40.1 %collective-permute-start.16 = (bf16[512,128]{1,0:T(8,128)(2,1)}, bf16[512,128]{1,0:T(8,128)(2,1)}, u32[]{:S(2)}, u32[]{:S(2)}) collective-permute-start(bf16[512,128]{1,0:T(8,128)(2,1)} %get-tuple-element.65), channel_id=1, source_target_pairs={{0,48},{8,56},{16,0},{24,8},{32,16},{40,24},{48,32},{56,40},{64,11... | collective-permute-start | bytes 393224 | tf_op jit(solution)/shard_map/ppermute | solution.py:305
  223.0 27.9 %all-to-all-start.2 = ((bf16[32,16,128]{2,1,0:T(8,128)(2,1)}), bf16[32,16,128]{2,1,0:T(8,128)(2,1)}, u32[]{:S(2)}, u32[]{:S(2)}) async-start(bf16[32,16,128]{2,1,0:T(8,128)(2,1)} %bitcast.41), calls=%async_computation.3 | async-start | bytes 262144 | tf_op jit(solution)/shard_map/all_to_all | solution.py:227
  231.9 1.2 copy-start.6
  238.6 1.0 copy-start.7
  239.6 39.8 %collective-permute-start.8 = (bf16[448,512]{1,0:T(8,128)(2,1)}, bf16[448,512]{1,0:T(8,128)(2,1)S(1)}, u32[]{:S(2)}, u32[]{:S(2)}) collective-permute-start(bf16[448,512]{1,0:T(8,128)(2,1)} %get-tuple-element.52), channel_id=1, source_target_pairs={{8,0},{16,8},{24,16},{32,24},{40,32},{48,40},{56,48},{64,56},{72,6... | collective-permute-start | bytes 1376264 | tf_op jit(solution)/shard_map/ppermute | solution.py:295
  244.2 35.2 %collective-permute-start.9 = (bf16[448,512]{1,0:T(8,128)(2,1)}, bf16[448,512]{1,0:T(8,128)(2,1)}, u32[]{:S(2)}, u32[]{:S(2)}) collective-permute-start(bf16[448,512]{1,0:T(8,128)(2,1)} %get-tuple-element.53), channel_id=1, source_target_pairs={{8,0},{16,8},{24,16},{32,24},{40,32},{48,40},{56,48},{64,56},{72,6... | collective-permute-start | bytes 1376264 | tf_op jit(solution)/shard_map/ppermute | solution.py:295
  247.6 13.2 %collective-permute-start.15 = (bf16[512,128]{1,0:T(8,128)(2,1)}, bf16[512,128]{1,0:T(8,128)(2,1)S(1)}, u32[]{:S(2)}, u32[]{:S(2)}) collective-permute-start(bf16[512,128]{1,0:T(8,128)(2,1)} %get-tuple-element.64), channel_id=1, source_target_pairs={{0,16},{8,24},{16,32},{24,40},{32,48},{40,56},{48,0},{56,8},{64,80... | collective-permute-start | bytes 393224 | tf_op jit(solution)/shard_map/ppermute | solution.py:305
  247.7 19.0 %collective-permute-start.14 = (bf16[512,128]{1,0:T(8,128)(2,1)}, bf16[512,128]{1,0:T(8,128)(2,1)S(1)}, u32[]{:S(2)}, u32[]{:S(2)}) collective-permute-start(bf16[512,128]{1,0:T(8,128)(2,1)} %get-tuple-element.63), channel_id=1, source_target_pairs={{0,56},{8,0},{16,8},{24,16},{32,24},{40,32},{48,40},{56,48},{64,12... | collective-permute-start | bytes 393224 | tf_op jit(solution)/shard_map/ppermute | solution.py:305
  250.9 15.8 %collective-permute-start.13 = (bf16[512,128]{1,0:T(8,128)(2,1)}, bf16[512,128]{1,0:T(8,128)(2,1)}, u32[]{:S(2)}, u32[]{:S(2)}) collective-permute-start(bf16[512,128]{1,0:T(8,128)(2,1)} %get-tuple-element.62), channel_id=1, source_target_pairs={{0,8},{8,16},{16,24},{24,32},{32,40},{40,48},{48,56},{56,0},{64,72... | collective-permute-start | bytes 393224 | tf_op jit(solution)/shard_map/ppermute | solution.py:305
  252.5 26.9 %all-to-all-start.3 = ((bf16[32,16,128]{2,1,0:T(8,128)(2,1)}), bf16[32,16,128]{2,1,0:T(8,128)(2,1)S(1)}, u32[]{:S(2)}, u32[]{:S(2)}) async-start(bf16[32,16,128]{2,1,0:T(8,128)(2,1)} %shard_map.100), calls=%async_computation.4 | async-start | bytes 262144 | tf_op jit(solution)/shard_map/all_to_all | solution.py:232
  268.8 1.2 copy-start.8
  277.4 1.0 copy-start.13
  279.4 1.2 copy-start.14
  280.7 1.2 copy-start.16
  (5 other events, 4.2 us)
Sparse Core Ops, SparseCore 0:
  10.5 91.6 all-gather.1
  109.0 47.9 reduce-scatter.1

commit v2 on v1

--- a/solution.py
+++ b/solution.py
@@ -38,7 +38,7 @@
 
 
 def call(kernel, heads, ins, outs, out_shape, scratch=(), flops=0, size=0, prefetch=0):
-    return pl.pallas_call(
+    run = pl.pallas_call(
         kernel,
         grid_spec=pltpu.PrefetchScalarGridSpec(
             num_scalar_prefetch=prefetch,
@@ -49,10 +49,19 @@
         ),
         out_shape=out_shape,
         compiler_params=pltpu.CompilerParams(
-            dimension_semantics=("arbitrary",), vmem_limit_bytes=48 * 1024 * 1024
+            dimension_semantics=("arbitrary",), vmem_limit_bytes=40 * 1024 * 1024
         ),
         cost_estimate=pl.CostEstimate(flops=flops, bytes_accessed=size, transcendentals=0),
     )
+    return lambda *args: run(*args[:prefetch], *(kept(a) for a in args[prefetch:]))
+
+
+def kept(a):
+    return pltpu.with_memory_space_constraint(a, pltpu.HBM)
+
+
+def large(*args):
+    return pltpu.HBM(*args)
 
 
 def columns(rows, at=0):
@@ -83,14 +92,7 @@
     return (row >= BLOCK) & (col < BLOCK)
 
 
-def pad_into(wide, part):
-    wide[0:BLOCK, :] = jnp.zeros((BLOCK, DH), BF16)
-    wide[BLOCK:TOK, :] = part[...]
-
-
-def window_kernel(place, q, k, v, kh, vh, near, far, raw, window, intra, kw, vw):
-    pad_into(kw, kh)
-    pad_into(vw, vh)
+def window_kernel(place, q, k, v, kw, vw, near, far, raw, window, intra):
     causal, edge = causal_tile(), edge_tile()
     inside = place[0] > 0
     v_t = flip(v[...]).astype(BF16)
@@ -142,9 +144,7 @@
     mixed[...] = out.T.astype(BF16)
 
 
-def far_kernel(q, g, kh, vh, far, window, dq, dk, dv, delta, kw, vw, ds):
-    pad_into(kw, kh)
-    pad_into(vw, vh)
+def far_kernel(q, g, kw, vw, far, window, dq, dk, dv, delta, ds):
     g_t = flip(g[...])
     d = jnp.sum(g_t * window[...], axis=0, keepdims=True)
     delta[0] = d
@@ -221,72 +221,91 @@
         total = total + x[at].astype(F32)
 
 
-def carry_states(local, backward):
+def carry_states(local, backward, beside=()):
     count = lax.axis_size("seq")
     pieces = local.reshape(count, -1, DH)
     met = lax.all_to_all(pieces, "seq", 0, 0)
+    met, beside = lax.optimization_barrier((met, beside))
     done = pl.pallas_call(
         functools.partial(scan_kernel, backward),
         out_shape=jax.ShapeDtypeStruct(met.shape, BF16),
     )(met)
-    return lax.all_to_all(done, "seq", 0, 0).reshape(local.shape)
-
-
-def whole(kernel, ids, ins, out_shape, scratch=(), flops=0, size=0):
-    vmem = pl.BlockSpec(memory_space=pltpu.VMEM)
-    smem = pl.BlockSpec(memory_space=pltpu.SMEM)
-    return pl.pallas_call(
-        kernel,
-        in_specs=[smem] + [vmem] * len(ins),
-        out_specs=jax.tree.map(lambda _: vmem, out_shape),
-        out_shape=out_shape,
-        scratch_shapes=scratch,
-        compiler_params=pltpu.CompilerParams(vmem_limit_bytes=48 * 1024 * 1024),
-        cost_estimate=pl.CostEstimate(flops=flops, bytes_accessed=size, transcendentals=0),
-    )(ids, *ins)
-
-
-def grad_mixed_kernel(ids, w, *rest):
-    blocks, out, acc = rest[:-2], rest[-2], rest[-1]
-    width = blocks[0].shape[1]
+    return lax.all_to_all(done, "seq", 0, 0).reshape(local.shape), beside
+
+
+def block_id(t, head):
+    hops = jnp.where(t % XS < 2, t % XS, 5 - t % XS)
+    x = (head[0] // 2 + XS - hops) % XS
+    core = jnp.where(t < XS, head[0] % 2, 1 - head[0] % 2)
+    return 2 * x + core
+
+
+def gathered_specs(rows, width):
+    return [pl.BlockSpec((rows, width), lambda t, head: (0, 0))] * (2 * XS)
+
+
+def weight_specs(part, rest, width):
+    return [
+        pl.BlockSpec((width // DH, part, DH), lambda t, head: (block_id(t, head), 0, 0)),
+        pl.BlockSpec((rest, width), lambda t, head: (0, block_id(t, head))),
+    ]
+
+
+def across(w):
+    return jnp.concatenate([w[i] for i in range(w.shape[0])], axis=1)
+
+
+def each_block(blocks, use):
     for j, block in enumerate(blocks):
-        at = pl.multiple_of(ids[j] * width, width)
-        part = nt(block[...], w[:, pl.ds(at, width)])
-        if j == 0:
-            acc[...] = part
-        elif j < len(blocks) - 1:
-            acc[...] += part
-        else:
-            out[...] = (acc[...] + part).astype(BF16)
-
-
-def sens_kernel(n, ids, mixed_t, *rest):
-    blocks, outs = rest[:n], rest[n:]
-    width = blocks[0].shape[1]
-    for j, block in enumerate(blocks):
-        part = nn(mixed_t[...], block[...]).astype(BF16)
-        slot, at = ids[n + j], pl.multiple_of(ids[2 * n + j] * width, width)
-        for r, out in enumerate(outs):
-
-            @pl.when(slot == r)
-            def _(out=out, part=part, at=at):
-                out[:, pl.ds(at, width)] = part
-
-
-def fold_kernel(n, ids, *rest):
-    parts, outs = rest[:n], rest[n:]
-    width = outs[0].shape[1]
-    for j, out in enumerate(outs):
-        at = pl.ds(pl.multiple_of(ids[j] * width, width), width)
-        total = parts[0][:, at].astype(F32)
-        for part in parts[1:]:
-            total = total + part[:, at].astype(F32)
-        out[...] = total.astype(BF16)
+
+        @pl.when(pl.program_id(0) == j)
+        def _(block=block):
+            use(block[...])
+
+
+def grad_mixed_kernel(head, *refs):
+    blocks, (wa, wb, out, acc) = refs[: 2 * XS], refs[2 * XS :]
+    part = wa.shape[1]
+    t = pl.program_id(0)
+
+    @pl.when(t == 0)
+    def _():
+        acc[...] = jnp.zeros_like(acc)
+
+    def add(block):
+        acc[:, 0:part] += nt(block, across(wa))
+        acc[:, part:] += nt(block, wb[...])
+
+    each_block(blocks, add)
+
+    @pl.when(t == 2 * XS - 1)
+    def _():
+        out[...] = acc[...].astype(BF16)
+
+
+def sens_kernel(head, *refs):
+    blocks, (mixed_t, out) = refs[: 2 * XS], refs[2 * XS :]
+
+    def put(block):
+        out[0] = nn(mixed_t[...], block).astype(BF16)
+
+    each_block(blocks, put)
+
+
+def mixer_kernel(head, mixed, wa, wb, out):
+    part = wa.shape[1]
+    out[...] = (nn(mixed[:, 0:part], across(wa)) + nn(mixed[:, part:], wb[...])).astype(BF16)
+
+
+def fold_kernel(*refs):
+    total = refs[0][...].astype(F32)
+    for part in refs[1:-1]:
+        total = total + part[...].astype(F32)
+    refs[-1][0] = total.astype(BF16)
 
 
 YS, ZS, XS = 4, 8, 4
-Y_HOPS = (1, 3, 2)
-Z_HOPS = (1, 7, 2, 6, 3, 5, 4)
+Y_HOPS = (1, YS - 1, 2)
 
 
 def shifted(shard, by):
@@ -295,18 +314,25 @@
     return lax.ppermute(shard, "seq", pairs)
 
 
+Z_GROUPS = [[y * ZS + z for z in range(ZS)] for y in range(YS)]
+Y_GROUPS = [[y * ZS + z for y in range(YS)] for z in range(ZS)]
+
+
+def exchange(pieces, axis, groups):
+    return lax.all_to_all(pieces, axis, 0, 0, axis_index_groups=groups)
+
+
+def spread(shard, axis, groups):
+    copies = jnp.broadcast_to(shard[None], (len(groups[0]),) + shard.shape)
+    return exchange(copies, axis, groups)
+
+
 def hop_y(shard, by):
     return lax.ppermute(
         shard, "seq", [(y * ZS + z, (y + by) % YS * ZS + z) for y in range(YS) for z in range(ZS)]
     )
 
 
-def hop_z(shard, by):
-    return lax.ppermute(
-        shard, "seq", [(y * ZS + z, y * ZS + (z + by) % ZS) for y in range(YS) for z in range(ZS)]
-    )
-
-
 def hop_x(shard, by):
     return lax.ppermute(
         shard, "head", [(x * 2 + c, (x + by) % XS * 2 + c) for x in range(XS) for c in range(2)]
@@ -320,9 +346,10 @@
 def shards(queries, keys, values, w_out, grad_y):
     rows, width = queries.shape
     heads = width // DH
-    seq, head = lax.axis_index("seq"), lax.axis_index("head")
-    y, z, x, core = seq // ZS, seq % ZS, head // 2, head % 2
+    seq = lax.axis_index("seq").reshape(1).astype(jnp.int32)
+    head = lax.axis_index("head").reshape(1).astype(jnp.int32)
     tokens_all = rows * lax.axis_size("seq")
+    cut = rows // 4
     shape = jax.ShapeDtypeStruct
     col = columns(rows)
     tri = heads_of(rows, rows)
@@ -331,35 +358,33 @@
     line = heads_of(1, rows)
     mm = 2 * rows * rows * width
 
-    halo = shifted(jnp.concatenate([keys[BLOCK:], values[BLOCK:]]), 1)
-    full_w = lax.all_gather(w_out, "seq", axis=1, tiled=True)
+    wb = lax.all_gather(w_out[cut:], "seq", axis=1, tiled=True)
     grads = [grad_y] + [hop_x(grad_y, by) for by in (1, XS - 1, 2)]
-    grads = grads + [swap_core(g) for g in grads]
-    source = [(x - by) % XS for by in (0, 1, XS - 1, 2)]
-    block_of = [s * 2 + core for s in source] + [s * 2 + 1 - core for s in source]
-    slot_of = [(b // 2 - y) % YS for b in block_of]
-    ids = jnp.stack(block_of + slot_of + [b % 2 for b in block_of]).astype(jnp.int32)
+    kh, vh = shifted(keys, 1), shifted(values, 1)
 
     local = call(
         sums_kernel, heads, [col, col], st, shape((heads, DH, DH), BF16), flops=2 * mm // 4
     )(keys, values)
-    before = carry_states(local, False)
-
-    sq = shape((heads, rows, rows), BF16)
-    flat_t = shape((width, rows), F32)
+    before, (kh, vh, grads) = carry_states(local, False, (kh, vh, grads))
+
+    swapped = [swap_core(g) for g in grads]
+    before, first, swapped = lax.optimization_barrier((before, w_out[:cut], swapped))
+    wa = spread(spread(first, "seq", Z_GROUPS), "seq", Y_GROUPS).reshape(YS * ZS, cut, DH)
+
+    sq = large((heads, rows, rows), BF16)
+    flat_t = large((width, rows), F32)
     edge = EDGE
-    wide = [pltpu.VMEM((rows, DH), BF16)] * 2
+    grads = list(grads) + list(swapped)
     near, far, raw, window, intra = call(
         window_kernel,
         heads,
-        [col, col, col, columns(edge, 0), columns(edge, 1)],
+        [col] * 5,
         [tri, tri, tri, turned, turned],
         [sq, sq, sq, flat_t, flat_t],
-        scratch=wide,
         flops=12 * mm // 8,
         size=12 << 20,
         prefetch=1,
-    )(seq.reshape(1).astype(jnp.int32), queries, keys, values, halo, halo)
+    )(seq, queries, keys, values, kh, vh)
 
     normed, inverse, mixed_t, mixed = call(
         mixed_kernel,
@@ -369,58 +394,58 @@
         [
             flat_t,
             shape((heads, 1, rows), F32),
-            shape((width, rows), BF16),
-            shape((rows, width), BF16),
+            large((width, rows), BF16),
+            large((rows, width), BF16),
         ],
         flops=mm // 4,
         size=5 << 20,
     )(queries, before, window, intra)
 
-    pieces = whole(
-        functools.partial(sens_kernel, len(grads)),
-        ids,
-        [mixed_t] + grads,
-        [shape((width, 2 * width), BF16)] * YS,
-        flops=8 * mm,
-        size=9 << 20,
-    )
-    got = [pieces[0]] + [hop_y(pieces[by], by) for by in Y_HOPS]
-    z_ids = jnp.stack([(z + by) % ZS for by in (0,) + Z_HOPS]).astype(jnp.int32)
-    parts = whole(
-        functools.partial(fold_kernel, YS),
-        z_ids,
-        got,
-        [shape((width, DH), BF16)] * ZS,
-        size=5 << 20,
-    )
-    total = parts[0].astype(F32)
-    for part, by in zip(parts[1:], Z_HOPS):
-        total = total + hop_z(part, by).astype(F32)
-    projection_sensitivity = total * tokens_all ** (-0.5)
-
-    grad_mixed = whole(
+    gathered = gathered_specs(rows, width)
+    weights = weight_specs(cut, rows - cut, width)
+    out_block = pl.BlockSpec((rows, width), lambda t, head: (0, block_id(t, head)))
+    fixed = pl.BlockSpec((rows, width), lambda t, head: (0, 0))
+    by_block = functools.partial(call, heads=2 * XS, size=9 << 20, flops=8 * mm, prefetch=1)
+    pieces = by_block(
+        sens_kernel,
+        ins=gathered + [fixed],
+        outs=pl.BlockSpec(
+            (1, width, width), lambda t, head: (block_id(t, head) // 2, 0, block_id(t, head) % 2)
+        ),
+        out_shape=large((YS, width, 2 * width), BF16),
+    )(head, *grads, mixed_t)
+    y = lax.axis_index("seq") // ZS
+    own = lax.dynamic_index_in_dim(pieces, y, 0, False)
+    sends = [lax.dynamic_index_in_dim(pieces, (y + by) % YS, 0, False) for by in Y_HOPS]
+    met = [own] + [hop_y(piece, by) for piece, by in zip(sends, Y_HOPS)]
+    own, sends, wa, wb = lax.optimization_barrier((own, sends, wa, wb))
+
+    partial_value = by_block(
+        mixer_kernel,
+        ins=[fixed] + weights,
+        outs=out_block,
+        out_shape=large((rows, 2 * XS * width), BF16),
+    )(head, mixed, wa, wb)
+    mixer_result = lax.psum_scatter(partial_value, "head", scatter_dimension=1, tiled=True)
+    grad_mixed = by_block(
         grad_mixed_kernel,
-        ids,
-        [full_w] + grads,
-        shape((rows, width), BF16),
+        ins=gathered + weights,
+        outs=fixed,
+        out_shape=large((rows, width), BF16),
         scratch=[pltpu.VMEM((rows, width), F32)],
-        flops=8 * mm,
-        size=9 << 20,
-    )
-    partial_value = jnp.dot(mixed, full_w, preferred_element_type=F32).astype(BF16)
-    mixer_result = lax.psum_scatter(partial_value, "head", scatter_dimension=1, tiled=True)
-
-    edge_grad = shape((edge, width), BF16)
+    )(head, *grads, wa, wb)
+
+    edge_grad = large((edge, width), BF16)
     dq_far, far_k, far_v, delta = call(
         far_kernel,
         heads,
-        [col, col, columns(edge, 0), columns(edge, 1), tri, turned],
+        [col, col, col, col, tri, turned],
         [turned, columns(edge), columns(edge), line],
         [flat_t, edge_grad, edge_grad, shape((heads, 1, rows), F32)],
-        scratch=wide + [pltpu.VMEM((rows, rows), BF16)],
+        scratch=[pltpu.VMEM((rows, rows), BF16)],
         flops=8 * mm // 8,
         size=8 << 20,
-    )(queries, grad_mixed, halo, halo, far, window)
+    )(queries, grad_mixed, kh, vh, far, window)
     back_k, back_v = shifted(far_k, -1), shifted(far_v, -1)
 
     grad_lin, local_back = call(
@@ -428,18 +453,18 @@
         heads,
         [col, col, turned, line],
         [col, st],
-        [shape((rows, width), BF16), shape((heads, DH, DH), BF16)],
+        [large((rows, width), BF16), shape((heads, DH, DH), BF16)],
         flops=mm // 4,
         size=3 << 20,
     )(queries, grad_mixed, normed, inverse)
-    later = carry_states(local_back, True)
+    later, _ = carry_states(local_back, True)
 
     grad_queries, near_k, near_v = call(
         near_kernel,
         heads,
         [col, col, col, col, col, tri, tri, st, line, turned],
         [col, col, col],
-        [shape((rows, width), BF16), shape((rows, width), F32), shape((rows, width), F32)],
+        [large((rows, width), BF16), large((rows, width), F32), large((rows, width), F32)],
         scratch=[pltpu.VMEM((rows, rows), BF16)],
         flops=12 * mm // 8,
         size=12 << 20,
@@ -450,10 +475,22 @@
         heads,
         [col, col, st, col, col, columns(edge), columns(edge)],
         [col, col],
-        [shape((rows, width), BF16)] * 2,
+        [large((rows, width), BF16)] * 2,
         flops=mm // 2,
         size=5 << 20,
     )(keys, values, later, near_k, near_v, back_k, back_v)
+    met, _ = lax.optimization_barrier((met, grad_keys))
+    parts = call(
+        fold_kernel,
+        ZS,
+        [pl.BlockSpec((width, DH), lambda z: (0, z))] * YS,
+        pl.BlockSpec((1, width, DH), lambda z: (z, 0, 0)),
+        large((ZS, width, DH), BF16),
+        size=5 << 20,
+    )(*met)
+    total = jnp.sum(exchange(parts, "seq", Z_GROUPS).astype(F32), axis=0)
+    projection_sensitivity = total * tokens_all ** (-0.5)
+
     return (mixer_result, grad_queries, grad_keys, grad_values, projection_sensitivity)
 
 

time: 294 us -> 260 us (0.88)
  waiting for transfers between devices: 109 us -> 17.6 us
  blocking collectives: 28.7 us -> 68.4 us
  Pallas kernels: 51 us -> 75.1 us
  starting transfers between devices: 57.6 us -> 69.2 us
  local copies, waits for them, and re-layouts: 22.3 us -> 12.5 us
  matrix products: 6.7 us -> 0 us
    all_to_all x0 -> x2, blocking collectives: none -> 45.6 us  [exchange(): return lax.all_to_all(pieces, axis, 0, 0, axis_index_groups=groups)]
    ppermute x3, waiting for transfers between devices: 44.6 us -> 0.01 us  [hop_y(): lax.ppermute(shard, 'seq', [(y * ZS + z, (y + by) % YS * ZS + z) for y in...]
    all_gather x1, waiting for transfers between devices: 29.5 us -> 0.01 us  [shards(): wb = lax.all_gather(w_out[cut:], 'seq', axis=1, tiled=True)]
    ppermute x3, waiting for transfers between devices: 26 us -> 0.01 us  [hop_x(): lax.ppermute(shard, 'head', [(x * 2 + c, (x + by) % XS * 2 + c) for x in...]
    pallas_call x10 -> x11, Pallas kernels: 47.8 us -> 71.9 us  [call(): run(*args[:prefetch], *(kept(a) for a in args[prefetch:]))]
    all_to_all x2 -> x3, starting transfers between devices: 15.9 us -> 38.2 us  [the longest x2 32.3 us: carry_states(): return (lax.all_to_all(done, 'seq', 0, 0).reshape(local.shape), beside)]
    unnamed x56 -> x30, local copies, waits for them, and re-layouts: 20 us -> 4.97 us
    ppermute x7 -> x0, starting transfers between devices: 12.8 us -> none  [hop_z(): lax.ppermute(shard, 'seq', [(y * ZS + z, y * ZS + (z + by) % ZS) for y in...]
  transfers between devices with their start and end apart: 25 -> 20, of which waited for: 7 -> 3; matrix products, arithmetic and copies ran while one was open for 2% -> 3% of each run, Pallas kernels for 17% -> 26%
where the time goes in v2:
time: 260 us; the launch traced here: 258 us
  Pallas kernels  75.1 us (29%)
  starting transfers between devices  69.2 us (27%)
  blocking collectives  68.4 us (26%)
  waiting for transfers between devices  17.6 us (7%)
  between operations  14.3 us (6%)
  local copies, waits for them, and re-layouts  12.5 us (5%)
    pallas_call x11, Pallas kernels, call(): run(*args[:prefetch], *(kept(a) for a in args[prefetch:]))  71.9 us
    all_to_all x2, blocking collectives, exchange(): return lax.all_to_all(pieces, axis, 0, 0, axis_index_groups=groups)  45.6 us
    all_to_all x2, starting transfers between devices, carry_states(): return (lax.all_to_all(done, 'seq', 0, 0).reshape(local.shape), beside)  32.3 us
    all_to_all x1, blocking collectives, carry_states(): met = lax.all_to_all(pieces, 'seq', 0, 0)  22.8 us
    ppermute x4, starting transfers between devices, shifted(): return lax.ppermute(shard, 'seq', pairs)  15.6 us
    all_to_all x1, waiting for transfers between devices, carry_states(): met = lax.all_to_all(pieces, 'seq', 0, 0)  9.16 us
    all_to_all x2, waiting for transfers between devices, carry_states(): return (lax.all_to_all(done, 'seq', 0, 0).reshape(local.shape), beside)  8.35 us
    all_to_all x1, starting transfers between devices, carry_states(): met = lax.all_to_all(pieces, 'seq', 0, 0)  5.9 us
  transfers between devices with their start and end apart: 20, of which 3 were waited for; matrix products, arithmetic and copies ran while one was open for 3% of the time, Pallas kernels for 26%

profile of v2, /device:TPU:16, one launch (start us, length us, event | category | flops | bytes accessed | tf_op | source)
XLA Modules:
  0.0 257.9 jit_solution(385615599917074987)
XLA Ops:
  7.2 1.5 slice.7
  8.8 3.8 %collective-permute-start = (bf16[512,512]{1,0:T(8,128)(2,1)}, bf16[512,512]{1,0:T(8,128)(2,1)S(1)}, u32[]{:S(2)}, u32[]{:S(2)}) collective-permute-start(bf16[512,512]{1,0:T(8,128)(2,1)} %k.7), channel_id=1, source_target_pairs={{0,8},{8,16},{16,24},{24,32},{32,40},{40,48},{48,56},{56,64},{64,7... | collective-permute-start | bytes 1572872 | tf_op jit(solution)/shard_map/ppermute | solution.py:314
  12.6 3.8 %collective-permute-start.1 = (bf16[512,512]{1,0:T(8,128)(2,1)}, bf16[512,512]{1,0:T(8,128)(2,1)S(1)}, u32[]{:S(2)}, u32[]{:S(2)}) collective-permute-start(bf16[512,512]{1,0:T(8,128)(2,1)} %v.7), channel_id=1, source_target_pairs={{0,8},{8,16},{16,24},{24,32},{32,40},{40,48},{48,56},{56,64},{64,7... | collective-permute-start | bytes 1572872 | tf_op jit(solution)/shard_map/ppermute | solution.py:314
  16.4 1.6 collective-permute-start.2
  18.0 1.7 collective-permute-start.3
  19.8 1.8 collective-permute-start.4
  21.6 2.7 %shard_map.92 = bf16[4,128,128]{2,1,0:T(8,128)(2,1)S(1)} custom-call(bf16[512,512]{1,0:T(8,128)(2,1)} %k.7, bf16[512,512]{1,0:T(8,128)(2,1)} %v.7), custom_call_target="tpu_custom_call" | custom-call | flops 134217728 | tf_op jit(solution)/shard_map/pallas_call | solution.py:56
  24.3 22.8 %all_to_all.35.x = bf16[32,16,128]{2,1,0:T(8,128)(2,1)} all-to-all(bf16[32,16,128]{2,1,0:T(8,128)(2,1)S(1)} %bitcast.15), channel_id=1, replica_groups=mesh['seq'=32,'head'=8] {'seq'}, dimensions={0} | all-to-all | bytes 262144 | tf_op jit(solution)/shard_map/all_to_all | solution.py:227
  47.3 0.5 collective-permute-start.6
  47.9 0.2 copy-done.10
  48.1 0.3 collective-permute-start.8
  48.4 1.6 shard_map.93
  50.0 7.6 %all-to-all-start.1 = ((bf16[32,16,128]{2,1,0:T(8,128)(2,1)}), bf16[32,16,128]{2,1,0:T(8,128)(2,1)S(1)}, u32[]{:S(2)}, u32[]{:S(2)}) async-start(bf16[32,16,128]{2,1,0:T(8,128)(2,1)} %shard_map.93), calls=%async_computation.1 | async-start | bytes 262144 | tf_op jit(solution)/shard_map/all_to_all | solution.py:233
  57.6 0.8 slice.6
  58.4 8.0 %all-to-all-done.1 = bf16[32,16,128]{2,1,0:T(8,128)(2,1)S(1)} async-done(((bf16[32,16,128]{2,1,0:T(8,128)(2,1)}), bf16[32,16,128]{2,1,0:T(8,128)(2,1)S(1)}, u32[]{:S(2)}, u32[]{:S(2)}) %all-to-all-start.1) | async-done | bytes 131104 | tf_op jit(solution)/shard_map/all_to_all | solution.py:233
  66.4 15.8 %all_to_all.36 = bf16[8,128,128]{2,1,0:T(8,128)(2,1)S(1)} all-to-all(bf16[8,128,128]{2,1,0:T(8,128)(2,1)S(1)} %broadcast_in_dim.4), channel_id=1, replica_groups={{0,8,16,24,32,40,48,56},{64,72,80,88,96,104,112,120},{128,136,144,152,1..., dimensions={0} | all-to-all | bytes 524288 | tf_op jit(solution)/shard_map/all_to_all | solution.py:322
  82.2 1.3 broadcast_in_dim.5
  83.5 5.8 %all-to-all-start.3 = ((bf16[4,8,128,128]{3,2,1,0:T(8,128)(2,1)}), bf16[4,8,128,128]{3,2,1,0:T(8,128)(2,1)S(1)}, u32[]{:S(2)}, u32[]{:S(2)}) async-start(bf16[4,8,128,128]{3,2,1,0:T(8,128)(2,1)} %broadcast_in_dim.5), calls=%async_computation.3 | async-start | bytes 2097152 | tf_op jit(solution)/shard_map/all_to_all | solution.py:322
  89.3 9.3 %shard_map.94 = (bf16[4,512,512]{2,1,0:T(8,128)(2,1)}, bf16[4,512,512]{2,1,0:T(8,128)(2,1)}, bf16[4,512,512]{2,1,0:T(8,128)(2,1)}, f32[512,512]{1,0:T(8,128)}, f32[512,512]{1,0:T(8,128)}) custom-call(s32[1]{0:T(128)} %bitcast.3.place, bf16[512,512]{1,0:T(8,128)(2,1)} %q.9, bf16[512,512]{1,0:T(8,128)(2,1)} %k.7, bf16[512,512]{1,0:T(8,128)(2,1)} %v.7, ...), custom_call_target="tpu_custom_call" | custom-call | flops 402653184 | bytes 12582912 | tf_op jit(solution)/shard_map/pallas_call | solution.py:56
  98.6 4.4 %shard_map.95 = (f32[512,512]{1,0:T(8,128)}, f32[4,1,512]{2,1,0:T(1,128)S(1)}, bf16[512,512]{1,0:T(8,128)(2,1)}, bf16[512,512]{1,0:T(8,128)(2,1)}) custom-call(bf16[512,512]{1,0:T(8,128)(2,1)} %q.9, bf16[4,128,128]{2,1,0:T(8,128)(2,1)} %bitcast.18, f32[512,512]{1,0:T(8,128)} %get-tuple-element.52.window, f32[512,512]{1,0:T(8,128)} %get-tuple-element.53.intra), custom_call_target="tpu_custom_call" | custom-call | flops 67108864 | bytes 5242880 | tf_op jit(solution)/shard_map/pallas_call | solution.py:56
  103.1 0.6 copy-done
  103.6 8.1 %shard_map.96 = bf16[4,512,1024]{2,1,0:T(8,128)(2,1)} custom-call(s32[1]{0:T(128)} %bitcast.head, bf16[512,512]{1,0:T(8,128)(2,1)} %refs_0_.1, bf16[512,512]{1,0:T(8,128)(2,1)} %copy-done.3, bf16[512,512]{1,0:T(8,128)(2,1)} %copy-done.4, bf16[512,512]{1,0:T(8,128)(2,1)} %copy-done.5, bf16[512,512]{1,0:T(8,128)(2,1)} %copy-done.6, ...), custom_call_target="tpu_custom_call" | custom-call | flops 2147483648 | bytes 9437184 | tf_op jit(solution)/shard_map/pallas_call | solution.py:56
  111.8 3.9 %dynamic-slice_bitcast_fusion = (bf16[512,1024]{1,0:T(8,128)(2,1)S(1)}, bf16[512,1024]{1,0:T(8,128)(2,1)S(1)}, bf16[512,1024]{1,0:T(8,128)(2,1)}, bf16[512,1024]{1,0:T(8,128)(2,1)}) fusion(bf16[4,512,1024]{2,1,0:T(8,128)(2,1)} %shard_map.96, s32[]{:T(128)S(6)} %select_n.39, s32[]{:T(128)S(6)} %select_n.37, s32[]{:T(128)S(6)} %select_n.35, s32[]{:T(128)S(6)} %select_n.33), kind=kLoop, calls=%fused_computation.1 | loop fusion | bytes 8388624 | tf_op jit(solution)/shard_map/jit(dynamic_index_in_dim)/squeeze | solution.py:419
  115.7 1.0 copy-done.2
  116.7 8.9 %shard_map.97 = bf16[512,4096]{1,0:T(8,128)(2,1)} custom-call(s32[1]{0:T(128)} %bitcast.head, bf16[512,512]{1,0:T(8,128)(2,1)} %get-tuple-element.54.mixed, bf16[32,128,128]{2,1,0:T(8,128)(2,1)} %bitcast.16, bf16[384,4096]{1,0:T(8,128)(2,1)} %all-gather.2.cloned.1.call-done.wb.refs_9_), custom_call_target="tpu_custom_call" | custom-call | flops 2147483648 | bytes 9437184 | tf_op jit(solution)/shard_map/pallas_call | solution.py:56
  125.6 1.2 copy-done.12
  126.8 1.2 collective-permute-start.11
  128.0 0.9 collective-permute-start.12
  128.8 1.4 collective-permute-start.13
  130.2 9.6 %shard_map.98.g = bf16[512,512]{1,0:T(8,128)(2,1)} custom-call(s32[1]{0:T(128)} %bitcast.head, bf16[512,512]{1,0:T(8,128)(2,1)} %refs_0_.1, bf16[512,512]{1,0:T(8,128)(2,1)} %copy-done.3, bf16[512,512]{1,0:T(8,128)(2,1)} %copy-done.4, bf16[512,512]{1,0:T(8,128)(2,1)} %copy-done.5, bf16[512,512]{1,0:T(8,128)(2,1)} %copy-done.6, bf16[512,512]{1,0:T(8,128)(2,1)} %copy-done.7, ...), custom_call_target="tpu_custom_call" | custom-call | flops 2147483648 | bytes 9437184 | tf_op jit(solution)/shard_map/pallas_call | solution.py:56
  139.8 4.2 %shard_map.99 = (bf16[512,512]{1,0:T(8,128)(2,1)}, bf16[4,128,128]{2,1,0:T(8,128)(2,1)}) custom-call(bf16[512,512]{1,0:T(8,128)(2,1)} %q.9, bf16[512,512]{1,0:T(8,128)(2,1)} %shard_map.98.g, f32[512,512]{1,0:T(8,128)} %get-tuple-element.63.normed, f32[4,1,512]{2,1,0:T(1,128)} %copy-done), custom_call_target="tpu_custom_call" | custom-call | flops 67108864 | bytes 3145728 | tf_op jit(solution)/shard_map/pallas_call | solution.py:56
  144.1 5.9 %all-to-all-start.4 = ((bf16[32,16,128]{2,1,0:T(8,128)(2,1)}), bf16[32,16,128]{2,1,0:T(8,128)(2,1)S(1)}, u32[]{:S(2)}, u32[]{:S(2)}) async-start(bf16[32,16,128]{2,1,0:T(8,128)(2,1)} %bitcast.9), calls=%async_computation.5 | async-start | bytes 262144 | tf_op jit(solution)/shard_map/all_to_all | solution.py:227
  150.0 6.1 %shard_map.100 = (f32[512,512]{1,0:T(8,128)}, bf16[448,512]{1,0:T(8,128)(2,1)}, bf16[448,512]{1,0:T(8,128)(2,1)}, f32[4,1,512]{2,1,0:T(1,128)S(1)}) custom-call(bf16[512,512]{1,0:T(8,128)(2,1)} %q.9, bf16[512,512]{1,0:T(8,128)(2,1)} %shard_map.98.g, bf16[512,512]{1,0:T(8,128)(2,1)} %copy-done.9, bf16[512,512]{1,0:T(8,128)(2,1)} %copy-done.10, ...), custom_call_target="tpu_custom_call" | custom-call | flops 268435456 | bytes 8388608 | tf_op jit(solution)/shard_map/pallas_call | solution.py:56
  156.1 0.6 copy-done.1
  156.7 4.6 %collective-permute-start.10 = (bf16[448,512]{1,0:T(8,128)(2,1)}, bf16[448,512]{1,0:T(8,128)(2,1)}, u32[]{:S(2)}, u32[]{:S(2)}) collective-permute-start(bf16[448,512]{1,0:T(8,128)(2,1)} %get-tuple-element.76), channel_id=1, source_target_pairs={{8,0},{16,8},{24,16},{32,24},{40,32},{48,40},{56,48},{64,56},{72,6... | collective-permute-start | bytes 1376264 | tf_op jit(solution)/shard_map/ppermute | solution.py:314
  161.2 3.4 %collective-permute-start.9 = (bf16[448,512]{1,0:T(8,128)(2,1)}, bf16[448,512]{1,0:T(8,128)(2,1)}, u32[]{:S(2)}, u32[]{:S(2)}) collective-permute-start(bf16[448,512]{1,0:T(8,128)(2,1)} %get-tuple-element.75), channel_id=1, source_target_pairs={{8,0},{16,8},{24,16},{32,24},{40,32},{48,40},{56,48},{64,56},{72,6... | collective-permute-start | bytes 1376264 | tf_op jit(solution)/shard_map/ppermute | solution.py:314
  164.6 9.2 %all-to-all-done.4.x = bf16[32,16,128]{2,1,0:T(8,128)(2,1)S(1)} async-done(((bf16[32,16,128]{2,1,0:T(8,128)(2,1)}), bf16[32,16,128]{2,1,0:T(8,128)(2,1)S(1)}, u32[]{:S(2)}, u32[]{:S(2)}) %all-to-all-start.4) | async-done | bytes 131104 | tf_op jit(solution)/shard_map/all_to_all | solution.py:227
  173.8 0.7 copy-done.14
  174.4 1.6 shard_map.102
  176.0 24.7 %all-to-all-start.5 = ((bf16[32,16,128]{2,1,0:T(8,128)(2,1)}), bf16[32,16,128]{2,1,0:T(8,128)(2,1)S(1)}, u32[]{:S(2)}, u32[]{:S(2)}) async-start(bf16[32,16,128]{2,1,0:T(8,128)(2,1)} %shard_map.102), calls=%async_computation.6 | async-start | bytes 262144 | tf_op jit(solution)/shard_map/all_to_all | solution.py:233
  200.8 8.0 %shard_map.101 = (bf16[512,512]{1,0:T(8,128)(2,1)}, f32[512,512]{1,0:T(8,128)}, f32[512,512]{1,0:T(8,128)}) custom-call(bf16[512,512]{1,0:T(8,128)(2,1)} %q.9, bf16[512,512]{1,0:T(8,128)(2,1)} %k.7, bf16[512,512]{1,0:T(8,128)(2,1)} %v.7, bf16[512,512]{1,0:T(8,128)(2,1)} %shard_map.98.g, bf16[512,512]{1,0:T(8,128)(2,1)} %get-tuple-element.65.gl, ...), custom_call_target="tpu_custom_call" | custom-call | flops 402653184 | bytes 12582912 | tf_op jit(solution)/shard_map/pallas_call | solution.py:56
  208.8 0.4 all-to-all-done.5
  209.2 0.7 copy-done.13
  209.9 4.4 %shard_map.103 = (bf16[512,512]{1,0:T(8,128)(2,1)}, bf16[512,512]{1,0:T(8,128)(2,1)}) custom-call(bf16[512,512]{1,0:T(8,128)(2,1)} %k.7, bf16[512,512]{1,0:T(8,128)(2,1)} %v.7, bf16[4,128,128]{2,1,0:T(8,128)(2,1)} %bitcast.20, f32[512,512]{1,0:T(8,128)} %get-tuple-element.73.dk, f32[512,512]{1,0:T(8,128)} %get-tuple-element.74.dv, ...), custom_call_target="tpu_custom_call" | custom-call | flops 134217728 | bytes 5242880 | tf_op jit(solution)/shard_map/pallas_call | solution.py:56
  214.3 6.1 %shard_map.104 = bf16[8,512,128]{2,1,0:T(8,128)(2,1)} custom-call(bf16[512,1024]{1,0:T(8,128)(2,1)} %get-tuple-element.79.refs_0_, bf16[512,1024]{1,0:T(8,128)(2,1)} %collective-permute-done.11.refs_1_, bf16[512,1024]{1,0:T(8,128)(2,1)} %collective-permute-done.12.refs_2_, bf16[512,1024]{1,0:T(8,128)(2,1)} %collective-permute-done.13.refs_3_), custom_call_target="tpu_custom_call" | custom-call | bytes 5242880 | tf_op jit(solution)/shard_map/pallas_call | solution.py:56
  220.4 29.8 %all_to_all.37 = bf16[8,512,128]{2,1,0:T(8,128)(2,1)S(1)} all-to-all(bf16[8,512,128]{2,1,0:T(8,128)(2,1)} %shard_map.104), channel_id=1, replica_groups={{0,8,16,24,32,40,48,56},{64,72,80,88,96,104,112,120},{128,136,144,152,1..., dimensions={0} | all-to-all | bytes 2097152 | tf_op jit(solution)/shard_map/all_to_all | solution.py:322
  250.2 0.1 convert_reduce_fusion
  250.4 0.7 broadcast_multiply_fusion
  (47 shorter events, 0.4 us)
Async XLA Ops:
  7.2 108.6 %all-gather.2.cloned.1.call-start = ((), (), s32[]{:S(2)}) async-start(), calls=%async_computation.8 | async-start | bytes 3244032 | tf_op jit(solution)/shard_map/all_gather | solution.py:361
  8.8 38.3 %collective-permute-start = (bf16[512,512]{1,0:T(8,128)(2,1)}, bf16[512,512]{1,0:T(8,128)(2,1)S(1)}, u32[]{:S(2)}, u32[]{:S(2)}) collective-permute-start(bf16[512,512]{1,0:T(8,128)(2,1)} %k.7), channel_id=1, source_target_pairs={{0,8},{8,16},{16,24},{24,32},{32,40},{40,48},{48,56},{56,64},{64,7... | collective-permute-start | bytes 1572872 | tf_op jit(solution)/shard_map/ppermute | solution.py:314
  12.6 34.5 %collective-permute-start.1 = (bf16[512,512]{1,0:T(8,128)(2,1)}, bf16[512,512]{1,0:T(8,128)(2,1)S(1)}, u32[]{:S(2)}, u32[]{:S(2)}) collective-permute-start(bf16[512,512]{1,0:T(8,128)(2,1)} %v.7), channel_id=1, source_target_pairs={{0,8},{8,16},{16,24},{24,32},{32,40},{40,48},{48,56},{56,64},{64,7... | collective-permute-start | bytes 1572872 | tf_op jit(solution)/shard_map/ppermute | solution.py:314
  16.4 30.7 %collective-permute-start.2 = (bf16[512,512]{1,0:T(8,128)(2,1)}, bf16[512,512]{1,0:T(8,128)(2,1)S(1)}, u32[]{:S(2)}, u32[]{:S(2)}) collective-permute-start(bf16[512,512]{1,0:T(8,128)(2,1)} %refs_0_.1), channel_id=1, source_target_pairs={{0,2},{1,3},{2,4},{3,5},{4,6},{5,7},{6,0},{7,1},{8,10},{9,11},{10,... | collective-permute-start | bytes 1572872 | tf_op jit(solution)/shard_map/ppermute | solution.py:337
  18.0 29.1 %collective-permute-start.3 = (bf16[512,512]{1,0:T(8,128)(2,1)}, bf16[512,512]{1,0:T(8,128)(2,1)S(1)}, u32[]{:S(2)}, u32[]{:S(2)}) collective-permute-start(bf16[512,512]{1,0:T(8,128)(2,1)} %refs_0_.1), channel_id=1, source_target_pairs={{0,6},{1,7},{2,0},{3,1},{4,2},{5,3},{6,4},{7,5},{8,14},{9,15},{10,... | collective-permute-start | bytes 1572872 | tf_op jit(solution)/shard_map/ppermute | solution.py:337
  19.8 27.4 %collective-permute-start.4 = (bf16[512,512]{1,0:T(8,128)(2,1)}, bf16[512,512]{1,0:T(8,128)(2,1)S(1)}, u32[]{:S(2)}, u32[]{:S(2)}) collective-permute-start(bf16[512,512]{1,0:T(8,128)(2,1)} %refs_0_.1), channel_id=1, source_target_pairs={{0,4},{1,5},{2,6},{3,7},{4,0},{5,1},{6,2},{7,3},{8,12},{9,13},{10,... | collective-permute-start | bytes 1572872 | tf_op jit(solution)/shard_map/ppermute | solution.py:337
  47.1 0.8 copy-start.9
  47.1 1.0 copy-start.10
  47.1 51.5 %copy-start.3 = (bf16[512,512]{1,0:T(8,128)(2,1)}, bf16[512,512]{1,0:T(8,128)(2,1)S(1)}, u32[]{:S(2)}) copy-start(bf16[512,512]{1,0:T(8,128)(2,1)S(1)} %collective-permute-done.2.refs_1_) | copy-start | bytes 1572868
  47.1 51.5 %copy-start.4 = (bf16[512,512]{1,0:T(8,128)(2,1)}, bf16[512,512]{1,0:T(8,128)(2,1)S(1)}, u32[]{:S(2)}) copy-start(bf16[512,512]{1,0:T(8,128)(2,1)S(1)} %collective-permute-done.3.refs_2_) | copy-start | bytes 1572868
  47.2 51.5 %copy-start.5 = (bf16[512,512]{1,0:T(8,128)(2,1)}, bf16[512,512]{1,0:T(8,128)(2,1)S(1)}, u32[]{:S(2)}) copy-start(bf16[512,512]{1,0:T(8,128)(2,1)S(1)} %collective-permute-done.4.refs_3_) | copy-start | bytes 1572868
  47.2 19.1 %collective-permute-start.5 = (bf16[512,512]{1,0:T(8,128)(2,1)}, bf16[512,512]{1,0:T(8,128)(2,1)S(1)}, u32[]{:S(2)}, u32[]{:S(2)}) collective-permute-start(bf16[512,512]{1,0:T(8,128)(2,1)} %refs_0_.1), channel_id=1, source_target_pairs={{0,1},{1,0},{2,3},{3,2},{4,5},{5,4},{6,7},{7,6},{8,9},{9,8},{10,11... | collective-permute-start | bytes 1572872 | tf_op jit(solution)/shard_map/ppermute | solution.py:343
  47.3 19.0 %collective-permute-start.6 = (bf16[512,512]{1,0:T(8,128)(2,1)S(1)}, bf16[512,512]{1,0:T(8,128)(2,1)S(1)}, u32[]{:S(2)}, u32[]{:S(2)}) collective-permute-start(bf16[512,512]{1,0:T(8,128)(2,1)S(1)} %collective-permute-done.2.refs_1_), channel_id=1, source_target_pairs={{0,1},{1,0},{2,3},{3,2},{4,5},{5,4},{6,7},{7,6},{8,9},{9,8},{10,11... | collective-permute-start | bytes 1572872 | tf_op jit(solution)/shard_map/ppermute | solution.py:343
  47.9 18.5 %collective-permute-start.7 = (bf16[512,512]{1,0:T(8,128)(2,1)S(1)}, bf16[512,512]{1,0:T(8,128)(2,1)S(1)}, u32[]{:S(2)}, u32[]{:S(2)}) collective-permute-start(bf16[512,512]{1,0:T(8,128)(2,1)S(1)} %collective-permute-done.3.refs_2_), channel_id=1, source_target_pairs={{0,1},{1,0},{2,3},{3,2},{4,5},{5,4},{6,7},{7,6},{8,9},{9,8},{10,11... | collective-permute-start | bytes 1572872 | tf_op jit(solution)/shard_map/ppermute | solution.py:343
  48.1 18.3 %collective-permute-start.8 = (bf16[512,512]{1,0:T(8,128)(2,1)S(1)}, bf16[512,512]{1,0:T(8,128)(2,1)}, u32[]{:S(2)}, u32[]{:S(2)}) collective-permute-start(bf16[512,512]{1,0:T(8,128)(2,1)S(1)} %collective-permute-done.4.refs_3_), channel_id=1, source_target_pairs={{0,1},{1,0},{2,3},{3,2},{4,5},{5,4},{6,7},{7,6},{8,9},{9,8},{10,11... | collective-permute-start | bytes 1572872 | tf_op jit(solution)/shard_map/ppermute | solution.py:343
  50.0 16.3 %all-to-all-start.1 = ((bf16[32,16,128]{2,1,0:T(8,128)(2,1)}), bf16[32,16,128]{2,1,0:T(8,128)(2,1)S(1)}, u32[]{:S(2)}, u32[]{:S(2)}) async-start(bf16[32,16,128]{2,1,0:T(8,128)(2,1)} %shard_map.93), calls=%async_computation.1 | async-start | bytes 262144 | tf_op jit(solution)/shard_map/all_to_all | solution.py:233
  66.3 32.3 %copy-start.11 = (bf16[32,16,128]{2,1,0:T(8,128)(2,1)}, bf16[32,16,128]{2,1,0:T(8,128)(2,1)S(1)}, u32[]{:S(2)}) copy-start(bf16[32,16,128]{2,1,0:T(8,128)(2,1)S(1)} %all-to-all-done.1) | copy-start | bytes 393220
  66.3 32.3 %copy-start.6 = (bf16[512,512]{1,0:T(8,128)(2,1)}, bf16[512,512]{1,0:T(8,128)(2,1)S(1)}, u32[]{:S(2)}) copy-start(bf16[512,512]{1,0:T(8,128)(2,1)S(1)} %collective-permute-done.5.refs_4_) | copy-start | bytes 1572868
  66.3 17.2 %copy-start.7 = (bf16[512,512]{1,0:T(8,128)(2,1)}, bf16[512,512]{1,0:T(8,128)(2,1)S(1)}, u32[]{:S(2)}) copy-start(bf16[512,512]{1,0:T(8,128)(2,1)S(1)} %collective-permute-done.6.refs_5_) | copy-start | bytes 1572868
  66.3 17.1 %copy-start.8 = (bf16[512,512]{1,0:T(8,128)(2,1)}, bf16[512,512]{1,0:T(8,128)(2,1)S(1)}, u32[]{:S(2)}) copy-start(bf16[512,512]{1,0:T(8,128)(2,1)S(1)} %collective-permute-done.7.refs_6_) | copy-start | bytes 1572868
  83.5 32.2 %all-to-all-start.3 = ((bf16[4,8,128,128]{3,2,1,0:T(8,128)(2,1)}), bf16[4,8,128,128]{3,2,1,0:T(8,128)(2,1)S(1)}, u32[]{:S(2)}, u32[]{:S(2)}) async-start(bf16[4,8,128,128]{3,2,1,0:T(8,128)(2,1)} %broadcast_in_dim.5), calls=%async_computation.3 | async-start | bytes 2097152 | tf_op jit(solution)/shard_map/all_to_all | solution.py:322
  89.3 161.8 %reduce-scatter.2.cloned.1.call-start = ((), (), s32[]{:S(2)}) async-start(), calls=%async_computation.9 | async-start | bytes 4718592 | tf_op jit(solution)/shard_map/reduce_scatter | solution.py:429
  103.1 0.6 copy-start
  115.7 1.0 copy-start.2
  125.6 1.2 copy-start.12
  126.8 87.4 %collective-permute-start.11 = (bf16[512,1024]{1,0:T(8,128)(2,1)S(1)}, bf16[512,1024]{1,0:T(8,128)(2,1)}, u32[]{:S(2)}, u32[]{:S(2)}) collective-permute-start(bf16[512,1024]{1,0:T(8,128)(2,1)S(1)} %copy-done.12), channel_id=1, source_target_pairs={{0,64},{8,72},{16,80},{24,88},{32,96},{40,104},{48,112},{56,120},{... | collective-permute-start | bytes 3145736 | tf_op jit(solution)/shard_map/ppermute | solution.py:331
  128.0 86.3 %collective-permute-start.12 = (bf16[512,1024]{1,0:T(8,128)(2,1)S(1)}, bf16[512,1024]{1,0:T(8,128)(2,1)}, u32[]{:S(2)}, u32[]{:S(2)}) collective-permute-start(bf16[512,1024]{1,0:T(8,128)(2,1)S(1)} %get-tuple-element.84), channel_id=1, source_target_pairs={{0,192},{8,200},{16,208},{24,216},{32,224},{40,232},{48,240},{56,2... | collective-permute-start | bytes 3145736 | tf_op jit(solution)/shard_map/ppermute | solution.py:331
  128.8 85.4 %collective-permute-start.13 = (bf16[512,1024]{1,0:T(8,128)(2,1)S(1)}, bf16[512,1024]{1,0:T(8,128)(2,1)}, u32[]{:S(2)}, u32[]{:S(2)}) collective-permute-start(bf16[512,1024]{1,0:T(8,128)(2,1)S(1)} %get-tuple-element.83), channel_id=1, source_target_pairs={{0,128},{8,136},{16,144},{24,152},{32,160},{40,168},{48,176},{56,1... | collective-permute-start | bytes 3145736 | tf_op jit(solution)/shard_map/ppermute | solution.py:331
  144.1 29.7 %all-to-all-start.4 = ((bf16[32,16,128]{2,1,0:T(8,128)(2,1)}), bf16[32,16,128]{2,1,0:T(8,128)(2,1)S(1)}, u32[]{:S(2)}, u32[]{:S(2)}) async-start(bf16[32,16,128]{2,1,0:T(8,128)(2,1)} %bitcast.9), calls=%async_computation.5 | async-start | bytes 262144 | tf_op jit(solution)/shard_map/all_to_all | solution.py:227
  156.1 0.6 copy-start.1
  156.7 52.1 %collective-permute-start.10 = (bf16[448,512]{1,0:T(8,128)(2,1)}, bf16[448,512]{1,0:T(8,128)(2,1)}, u32[]{:S(2)}, u32[]{:S(2)}) collective-permute-start(bf16[448,512]{1,0:T(8,128)(2,1)} %get-tuple-element.76), channel_id=1, source_target_pairs={{8,0},{16,8},{24,16},{32,24},{40,32},{48,40},{56,48},{64,56},{72,6... | collective-permute-start | bytes 1376264 | tf_op jit(solution)/shard_map/ppermute | solution.py:314
  161.2 47.6 %collective-permute-start.9 = (bf16[448,512]{1,0:T(8,128)(2,1)}, bf16[448,512]{1,0:T(8,128)(2,1)}, u32[]{:S(2)}, u32[]{:S(2)}) collective-permute-start(bf16[448,512]{1,0:T(8,128)(2,1)} %get-tuple-element.75), channel_id=1, source_target_pairs={{8,0},{16,8},{24,16},{32,24},{40,32},{48,40},{56,48},{64,56},{72,6... | collective-permute-start | bytes 1376264 | tf_op jit(solution)/shard_map/ppermute | solution.py:314
  173.8 0.7 copy-start.14
  176.0 33.2 %all-to-all-start.5 = ((bf16[32,16,128]{2,1,0:T(8,128)(2,1)}), bf16[32,16,128]{2,1,0:T(8,128)(2,1)S(1)}, u32[]{:S(2)}, u32[]{:S(2)}) async-start(bf16[32,16,128]{2,1,0:T(8,128)(2,1)} %shard_map.102), calls=%async_computation.6 | async-start | bytes 262144 | tf_op jit(solution)/shard_map/all_to_all | solution.py:233
  209.2 0.7 copy-start.13
Sparse Core Ops, SparseCore 0:
  10.5 90.1 all-gather.1
  125.7 37.5 reduce-scatter.1

commit v3 on v2

--- a/solution.py
+++ b/solution.py
@@ -241,18 +241,7 @@
 
 
 def gathered_specs(rows, width):
-    return [pl.BlockSpec((rows, width), lambda t, head: (0, 0))] * (2 * XS)
-
-
-def weight_specs(part, rest, width):
-    return [
-        pl.BlockSpec((width // DH, part, DH), lambda t, head: (block_id(t, head), 0, 0)),
-        pl.BlockSpec((rest, width), lambda t, head: (0, block_id(t, head))),
-    ]
-
-
-def across(w):
-    return jnp.concatenate([w[i] for i in range(w.shape[0])], axis=1)
+    return [pl.BlockSpec((rows, width), lambda t, *_: (0, 0))] * (2 * XS)
 
 
 def each_block(blocks, use):
@@ -263,18 +252,33 @@
             use(block[...])
 
 
-def grad_mixed_kernel(head, *refs):
-    blocks, (wa, wb, out, acc) = refs[: 2 * XS], refs[2 * XS :]
-    part = wa.shape[1]
+def project_kernel(head, y, *refs):
+    blocks, rest = refs[: 2 * XS], refs[2 * XS :]
+    mixed, near_w, far_w = rest[0], rest[1 : 1 + YS], rest[1 + YS]
+    partial_value, out, acc, w = rest[2 + YS :]
     t = pl.program_id(0)
+    part = near_w[0].shape[1]
+    shards_in = far_w.shape[0]
+    block = block_id(t, head)
+    slot = (y[0] + YS - block // 2) % YS
 
     @pl.when(t == 0)
     def _():
         acc[...] = jnp.zeros_like(acc)
 
+    for r, source in enumerate(near_w):
+
+        @pl.when(slot == r)
+        def _(source=source):
+            for i in range(shards_in):
+                w[0:part, i * DH : (i + 1) * DH] = source[block % 2 * shards_in + i]
+
+    for i in range(shards_in):
+        w[part:, i * DH : (i + 1) * DH] = far_w[i, 0]
+    partial_value[...] = nn(mixed[...], w[...]).astype(BF16)
+
     def add(block):
-        acc[:, 0:part] += nt(block, across(wa))
-        acc[:, part:] += nt(block, wb[...])
+        acc[...] += nt(block, w[...])
 
     each_block(blocks, add)
 
@@ -283,18 +287,22 @@
         out[...] = acc[...].astype(BF16)
 
 
-def sens_kernel(head, *refs):
-    blocks, (mixed_t, out) = refs[: 2 * XS], refs[2 * XS :]
+def sens_kernel(head, y, *refs):
+    blocks, (mixed_t, *outs) = refs[: 2 * XS], refs[2 * XS :]
+    block = block_id(pl.program_id(0), head)
+    slot = (block // 2 + YS - y[0]) % YS
+    width = mixed_t.shape[0]
+    at = pl.ds(pl.multiple_of(block % 2 * width, width), width)
 
     def put(block):
-        out[0] = nn(mixed_t[...], block).astype(BF16)
+        part = nn(mixed_t[...], block).astype(BF16)
+        for r, out in enumerate(outs):
+
+            @pl.when(slot == r)
+            def _(out=out):
+                out[:, at] = part
 
     each_block(blocks, put)
-
-
-def mixer_kernel(head, mixed, wa, wb, out):
-    part = wa.shape[1]
-    out[...] = (nn(mixed[:, 0:part], across(wa)) + nn(mixed[:, part:], wb[...])).astype(BF16)
 
 
 def fold_kernel(*refs):
@@ -349,7 +357,6 @@
     seq = lax.axis_index("seq").reshape(1).astype(jnp.int32)
     head = lax.axis_index("head").reshape(1).astype(jnp.int32)
     tokens_all = rows * lax.axis_size("seq")
-    cut = rows // 4
     shape = jax.ShapeDtypeStruct
     col = columns(rows)
     tri = heads_of(rows, rows)
@@ -358,23 +365,26 @@
     line = heads_of(1, rows)
     mm = 2 * rows * rows * width
 
-    wb = lax.all_gather(w_out[cut:], "seq", axis=1, tiled=True)
-    grads = [grad_y] + [hop_x(grad_y, by) for by in (1, XS - 1, 2)]
-    kh, vh = shifted(keys, 1), shifted(values, 1)
-
+    half = rows // 2
+    far_w = w_out[half:]
+    far_w = jnp.stack([far_w] + [hop_y(far_w, by) for by in range(1, YS)])
+    far_w = lax.all_gather(far_w, "seq", axis_index_groups=Z_GROUPS)
     local = call(
         sums_kernel, heads, [col, col], st, shape((heads, DH, DH), BF16), flops=2 * mm // 4
     )(keys, values)
-    before, (kh, vh, grads) = carry_states(local, False, (kh, vh, grads))
-
+    local, grad, k_out, v_out = lax.optimization_barrier((local, grad_y, keys, values))
+    hopped = [hop_x(grad, by) for by in (1, XS - 1, 2)]
+    kh, vh = shifted(k_out, 1), shifted(v_out, 1)
+    before, (kh, vh, hopped) = carry_states(local, False, (kh, vh, hopped))
+    grads = [grad_y] + list(hopped)
     swapped = [swap_core(g) for g in grads]
-    before, first, swapped = lax.optimization_barrier((before, w_out[:cut], swapped))
-    wa = spread(spread(first, "seq", Z_GROUPS), "seq", Y_GROUPS).reshape(YS * ZS, cut, DH)
+
+    near_w = spread(w_out[:half], "seq", Z_GROUPS)
+    near_w = [near_w] + [hop_y(near_w, by) for by in range(1, YS)]
 
     sq = large((heads, rows, rows), BF16)
     flat_t = large((width, rows), F32)
     edge = EDGE
-    grads = list(grads) + list(swapped)
     near, far, raw, window, intra = call(
         window_kernel,
         heads,
@@ -386,6 +396,8 @@
         prefetch=1,
     )(seq, queries, keys, values, kh, vh)
 
+    before, window = lax.optimization_barrier((before, window))
+    grads = grads + swapped
     normed, inverse, mixed_t, mixed = call(
         mixed_kernel,
         heads,
@@ -402,38 +414,41 @@
     )(queries, before, window, intra)
 
     gathered = gathered_specs(rows, width)
-    weights = weight_specs(cut, rows - cut, width)
-    out_block = pl.BlockSpec((rows, width), lambda t, head: (0, block_id(t, head)))
-    fixed = pl.BlockSpec((rows, width), lambda t, head: (0, 0))
-    by_block = functools.partial(call, heads=2 * XS, size=9 << 20, flops=8 * mm, prefetch=1)
+    fixed = pl.BlockSpec((rows, width), lambda t, *_: (0, 0))
+    by_block = functools.partial(call, heads=2 * XS, size=9 << 20, flops=8 * mm)
+    y = (lax.axis_index("seq") // ZS).reshape(1).astype(jnp.int32)
     pieces = by_block(
         sens_kernel,
         ins=gathered + [fixed],
-        outs=pl.BlockSpec(
-            (1, width, width), lambda t, head: (block_id(t, head) // 2, 0, block_id(t, head) % 2)
-        ),
-        out_shape=large((YS, width, 2 * width), BF16),
-    )(head, *grads, mixed_t)
-    y = lax.axis_index("seq") // ZS
-    own = lax.dynamic_index_in_dim(pieces, y, 0, False)
-    sends = [lax.dynamic_index_in_dim(pieces, (y + by) % YS, 0, False) for by in Y_HOPS]
-    met = [own] + [hop_y(piece, by) for piece, by in zip(sends, Y_HOPS)]
-    own, sends, wa, wb = lax.optimization_barrier((own, sends, wa, wb))
-
-    partial_value = by_block(
-        mixer_kernel,
-        ins=[fixed] + weights,
-        outs=out_block,
-        out_shape=large((rows, 2 * XS * width), BF16),
-    )(head, mixed, wa, wb)
+        outs=[pl.BlockSpec((width, 2 * width), lambda t, *_: (0, 0))] * YS,
+        out_shape=[large((width, 2 * width), BF16)] * YS,
+        prefetch=2,
+    )(head, y, *grads, mixed_t)
+    met = [pieces[0]] + [hop_y(pieces[by], by) for by in Y_HOPS]
+    pieces, far_w = lax.optimization_barrier((pieces, far_w))
+
+    partial_value, grad_mixed = by_block(
+        project_kernel,
+        ins=gathered
+        + [fixed]
+        + [pl.BlockSpec((ZS, half, DH), lambda t, *_: (0, 0, 0))] * YS
+        + [
+            pl.BlockSpec(
+                (ZS // 2, 1, half, DH),
+                lambda t, head, y: (
+                    block_id(t, head) % 2,
+                    (y[0] + YS - block_id(t, head) // 2) % YS,
+                    0,
+                    0,
+                ),
+            )
+        ],
+        outs=[pl.BlockSpec((rows, width), lambda t, head, y: (0, block_id(t, head))), fixed],
+        out_shape=[large((rows, 2 * XS * width), BF16), large((rows, width), BF16)],
+        scratch=[pltpu.VMEM((rows, width), F32), pltpu.VMEM((rows, width), BF16)],
+        prefetch=2,
+    )(head, y, *grads, mixed, *near_w, far_w)
     mixer_result = lax.psum_scatter(partial_value, "head", scatter_dimension=1, tiled=True)
-    grad_mixed = by_block(
-        grad_mixed_kernel,
-        ins=gathered + weights,
-        outs=fixed,
-        out_shape=large((rows, width), BF16),
-        scratch=[pltpu.VMEM((rows, width), F32)],
-    )(head, *grads, wa, wb)
 
     edge_grad = large((edge, width), BF16)
     dq_far, far_k, far_v, delta = call(

time: 260 us -> 288 us (1.11)
  waiting for transfers between devices: 17.6 us -> 70.5 us
  blocking collectives: 68.4 us -> 33.3 us
  starting transfers between devices: 69.2 us -> 87.7 us
  local copies, waits for them, and re-layouts: 12.5 us -> 7.48 us
  Pallas kernels: 75.1 us -> 71.7 us
    ppermute x4, waiting for transfers between devices: 0.01 us -> 30.9 us  [shifted(): return lax.ppermute(shard, 'seq', pairs)]
    all_to_all x1 -> x0, blocking collectives: 22.8 us -> none  [carry_states(): met = lax.all_to_all(pieces, 'seq', 0, 0)]
    all_to_all x1 -> x2, starting transfers between devices: 5.9 us -> 19.8 us  [carry_states(): met = lax.all_to_all(pieces, 'seq', 0, 0)]
    all_to_all x2 -> x1, blocking collectives: 45.6 us -> 33.3 us  [exchange(): return lax.all_to_all(pieces, axis, 0, 0, axis_index_groups=groups)]
    all_to_all x1 -> x2, waiting for transfers between devices: 9.16 us -> 20.5 us  [carry_states(): met = lax.all_to_all(pieces, 'seq', 0, 0)]
    ppermute x3 -> x9, starting transfers between devices: 3.41 us -> 13.7 us  [hop_y(): lax.ppermute(shard, 'seq', [(y * ZS + z, (y + by) % YS * ZS + z) for y in...]
    all_to_all x1, waiting for transfers between devices: 0.01 us -> 10.1 us  [exchange(): return lax.all_to_all(pieces, axis, 0, 0, axis_index_groups=groups)]
    squeeze x1 -> x0, local copies, waits for them, and re-layouts: 3.93 us -> none  [shards(): lax.dynamic_index_in_dim(pieces, (y + by) % YS, 0, False)]
  transfers between devices with their start and end apart: 20 -> 27, of which waited for: 3 -> 9; matrix products, arithmetic and copies ran while one was open for 3% -> 1% of each run, Pallas kernels for 26% -> 20%
where the time goes in v3:
time: 288 us; the launch traced here: 287 us
  starting transfers between devices  87.7 us (30%)
  Pallas kernels  71.7 us (25%)
  waiting for transfers between devices  70.5 us (24%)
  blocking collectives  33.3 us (12%)
  between operations  14.3 us (5%)
  local copies, waits for them, and re-layouts  7.48 us (3%)
    pallas_call x10, Pallas kernels, call(): run(*args[:prefetch], *(kept(a) for a in args[prefetch:]))  68.5 us
    all_to_all x1, blocking collectives, exchange(): return lax.all_to_all(pieces, axis, 0, 0, axis_index_groups=groups)  33.3 us
    ppermute x4, waiting for transfers between devices, shifted(): return lax.ppermute(shard, 'seq', pairs)  30.9 us
    all_to_all x2, starting transfers between devices, carry_states(): return (lax.all_to_all(done, 'seq', 0, 0).reshape(local.shape), beside)  28.6 us
    all_to_all x2, waiting for transfers between devices, carry_states(): met = lax.all_to_all(pieces, 'seq', 0, 0)  20.5 us
    all_to_all x2, starting transfers between devices, carry_states(): met = lax.all_to_all(pieces, 'seq', 0, 0)  19.8 us
    ppermute x4, starting transfers between devices, shifted(): return lax.ppermute(shard, 'seq', pairs)  14.7 us
    ppermute x9, starting transfers between devices, hop_y(): lax.ppermute(shard, 'seq', [(y * ZS + z, (y + by) % YS * ZS + z) for y in...  13.7 us
  transfers between devices with their start and end apart: 27, of which 9 were waited for; matrix products, arithmetic and copies ran while one was open for 1% of the time, Pallas kernels for 20%

profile of v3, /device:TPU:16, one launch (start us, length us, event | category | flops | bytes accessed | tf_op | source)
XLA Modules:
  0.0 286.5 jit_solution(3811336543128683876)
XLA Ops:
  7.2 1.0 slice_bitcast_fusion
  8.2 2.2 collective-permute-start.13
  10.9 1.6 collective-permute-start.14
  12.4 2.0 collective-permute-done.13
  14.4 0.7 collective-permute-done.12
  15.3 0.7 pad_maximum_fusion
  16.0 3.7 %shard_map.92 = bf16[4,128,128]{2,1,0:T(8,128)(2,1)} custom-call(bf16[512,512]{1,0:T(8,128)(2,1)} %k.7, bf16[512,512]{1,0:T(8,128)(2,1)} %v.7), custom_call_target="tpu_custom_call" | custom-call | flops 134217728 | tf_op jit(solution)/shard_map/pallas_call | solution.py:56
  19.7 13.4 %all-to-all-start = ((bf16[32,16,128]{2,1,0:T(8,128)(2,1)}), bf16[32,16,128]{2,1,0:T(8,128)(2,1)S(1)}, u32[]{:S(2)}, u32[]{:S(2)}) async-start(bf16[32,16,128]{2,1,0:T(8,128)(2,1)} %bitcast.2), calls=%async_computation | async-start | bytes 262144 | tf_op jit(solution)/shard_map/all_to_all | solution.py:227
  33.1 3.4 %collective-permute-start = (bf16[512,512]{1,0:T(8,128)(2,1)S(1)}, bf16[512,512]{1,0:T(8,128)(2,1)S(1)}, u32[]{:S(2)}, u32[]{:S(2)}) collective-permute-start(bf16[512,512]{1,0:T(8,128)(2,1)S(1)} %copy-done.2), channel_id=1, source_target_pairs={{0,8},{8,16},{16,24},{24,32},{32,40},{40,48},{48,56},{56,64},{64,7... | collective-permute-start | bytes 1572872 | tf_op jit(solution)/shard_map/ppermute | solution.py:322
  36.5 3.4 %collective-permute-start.1 = (bf16[512,512]{1,0:T(8,128)(2,1)S(1)}, bf16[512,512]{1,0:T(8,128)(2,1)S(1)}, u32[]{:S(2)}, u32[]{:S(2)}) collective-permute-start(bf16[512,512]{1,0:T(8,128)(2,1)S(1)} %copy-done.3), channel_id=1, source_target_pairs={{0,8},{8,16},{16,24},{24,32},{32,40},{40,48},{48,56},{56,64},{64,7... | collective-permute-start | bytes 1572872 | tf_op jit(solution)/shard_map/ppermute | solution.py:322
  39.9 3.1 %collective-permute-start.4 = (bf16[512,512]{1,0:T(8,128)(2,1)S(1)}, bf16[512,512]{1,0:T(8,128)(2,1)}, u32[]{:S(2)}, u32[]{:S(2)}) collective-permute-start(bf16[512,512]{1,0:T(8,128)(2,1)S(1)} %copy-done.11), channel_id=1, source_target_pairs={{0,4},{1,5},{2,6},{3,7},{4,0},{5,1},{6,2},{7,3},{8,12},{9,13},{10,... | collective-permute-start | bytes 1572872 | tf_op jit(solution)/shard_map/ppermute | solution.py:345
  43.0 1.1 collective-permute-start.3
  44.1 0.9 collective-permute-start.2
  45.0 0.9 broadcast_in_dim.2
  45.9 4.9 %all-to-all-start.2 = ((bf16[8,256,128]{2,1,0:T(8,128)(2,1)}), bf16[8,256,128]{2,1,0:T(8,128)(2,1)S(1)}, u32[]{:S(2)}, u32[]{:S(2)}) async-start(bf16[8,256,128]{2,1,0:T(8,128)(2,1)} %broadcast_in_dim.2), calls=%async_computation.2 | async-start | bytes 1048576 | tf_op jit(solution)/shard_map/all_to_all | solution.py:330
  50.8 12.7 %collective-permute-done.kw = bf16[512,512]{1,0:T(8,128)(2,1)S(1)} collective-permute-done((bf16[512,512]{1,0:T(8,128)(2,1)S(1)}, bf16[512,512]{1,0:T(8,128)(2,1)S(1)}, u32[]{:S(2)}, u32[]{:S(2)}) %collective-permute-start) | collective-permute-done | bytes 524320 | tf_op jit(solution)/shard_map/ppermute | solution.py:322
  63.5 18.1 %collective-permute-done.1.vw = bf16[512,512]{1,0:T(8,128)(2,1)S(1)} collective-permute-done((bf16[512,512]{1,0:T(8,128)(2,1)S(1)}, bf16[512,512]{1,0:T(8,128)(2,1)S(1)}, u32[]{:S(2)}, u32[]{:S(2)}) %collective-permute-start.1) | collective-permute-done | bytes 524320 | tf_op jit(solution)/shard_map/ppermute | solution.py:322
  82.3 10.1 %all-to-all-done.2.refs_9_ = bf16[8,256,128]{2,1,0:T(8,128)(2,1)S(1)} async-done(((bf16[8,256,128]{2,1,0:T(8,128)(2,1)}), bf16[8,256,128]{2,1,0:T(8,128)(2,1)S(1)}, u32[]{:S(2)}, u32[]{:S(2)}) %all-to-all-start.2) | async-done | bytes 524320 | tf_op jit(solution)/shard_map/all_to_all | solution.py:330
  93.0 2.9 %collective-permute-start.10 = (bf16[8,256,128]{2,1,0:T(8,128)(2,1)S(1)}, bf16[8,256,128]{2,1,0:T(8,128)(2,1)S(1)}, u32[]{:S(2)}, u32[]{:S(2)}) collective-permute-start(bf16[8,256,128]{2,1,0:T(8,128)(2,1)S(1)} %all-to-all-done.2.refs_9_), channel_id=1, source_target_pairs={{0,128},{8,136},{16,144},{24,152},{32,160},{40,168},{48,176},{56,1... | collective-permute-start | bytes 1572872 | tf_op jit(solution)/shard_map/ppermute | solution.py:339
  96.4 1.6 shard_map.93
  97.9 5.6 %all-to-all-start.1 = ((bf16[32,16,128]{2,1,0:T(8,128)(2,1)}), bf16[32,16,128]{2,1,0:T(8,128)(2,1)S(1)}, u32[]{:S(2)}, u32[]{:S(2)}) async-start(bf16[32,16,128]{2,1,0:T(8,128)(2,1)} %shard_map.93), calls=%async_computation.1 | async-start | bytes 262144 | tf_op jit(solution)/shard_map/all_to_all | solution.py:233
  103.8 9.4 %shard_map.94 = (bf16[4,512,512]{2,1,0:T(8,128)(2,1)}, bf16[4,512,512]{2,1,0:T(8,128)(2,1)}, bf16[4,512,512]{2,1,0:T(8,128)(2,1)}, f32[512,512]{1,0:T(8,128)}, f32[512,512]{1,0:T(8,128)}) custom-call(s32[1]{0:T(128)} %bitcast.4.place, bf16[512,512]{1,0:T(8,128)(2,1)} %q.9, bf16[512,512]{1,0:T(8,128)(2,1)} %k.7, bf16[512,512]{1,0:T(8,128)(2,1)} %v.7, ...), custom_call_target="tpu_custom_call" | custom-call | flops 402653184 | bytes 12582912 | tf_op jit(solution)/shard_map/pallas_call | solution.py:56
  113.2 5.7 %all-to-all-done.1 = bf16[32,16,128]{2,1,0:T(8,128)(2,1)S(1)} async-done(((bf16[32,16,128]{2,1,0:T(8,128)(2,1)}), bf16[32,16,128]{2,1,0:T(8,128)(2,1)S(1)}, u32[]{:S(2)}, u32[]{:S(2)}) %all-to-all-start.1) | async-done | bytes 131104 | tf_op jit(solution)/shard_map/all_to_all | solution.py:233
  118.9 0.6 copy-done.7
  119.6 4.5 %shard_map.95 = (f32[512,512]{1,0:T(8,128)}, f32[4,1,512]{2,1,0:T(1,128)S(1)}, bf16[512,512]{1,0:T(8,128)(2,1)}, bf16[512,512]{1,0:T(8,128)(2,1)}) custom-call(bf16[512,512]{1,0:T(8,128)(2,1)} %q.9, bf16[4,128,128]{2,1,0:T(8,128)(2,1)} %bitcast.14, f32[512,512]{1,0:T(8,128)} %get-tuple-element.60.window, f32[512,512]{1,0:T(8,128)} %get-tuple-element.61.intra), custom_call_target="tpu_custom_call" | custom-call | flops 67108864 | bytes 5242880 | tf_op jit(solution)/shard_map/pallas_call | solution.py:56
  124.6 8.9 %shard_map.96 = (bf16[512,1024]{1,0:T(8,128)(2,1)}, bf16[512,1024]{1,0:T(8,128)(2,1)}, bf16[512,1024]{1,0:T(8,128)(2,1)}, bf16[512,1024]{1,0:T(8,128)(2,1)}) custom-call(s32[1]{0:T(128)} %bitcast.head, s32[1]{0:T(128)} %bitcast.1.y, bf16[512,512]{1,0:T(8,128)(2,1)} %refs_0_.3, bf16[512,512]{1,0:T(8,128)(2,1)} %collective-permute-done.2.refs_1_, ...), custom_call_target="tpu_custom_call" | custom-call | flops 2147483648 | bytes 9437184 | tf_op jit(solution)/shard_map/pallas_call | solution.py:56
  133.5 0.8 copy-done.14
  134.4 13.4 %shard_map.97 = (bf16[512,4096]{1,0:T(8,128)(2,1)}, bf16[512,512]{1,0:T(8,128)(2,1)}) custom-call(s32[1]{0:T(128)} %bitcast.head, s32[1]{0:T(128)} %bitcast.1.y, bf16[512,512]{1,0:T(8,128)(2,1)} %refs_0_.3, bf16[512,512]{1,0:T(8,128)(2,1)} %collective-permute-done.2.refs_1_, bf16[512,512]{1,0:T(8,128)(2,1)} %collective-permute-done.3.refs_2_, ...), custom_call_target="tpu_custom_call" | custom-call | flops 2147483648 | bytes 9437184 | tf_op jit(solution)/shard_map/pallas_call | solution.py:56
  147.8 1.5 collective-permute-start.17
  149.3 1.6 collective-permute-start.19
  150.8 2.5 collective-permute-start.18
  153.4 4.2 %shard_map.98 = (bf16[512,512]{1,0:T(8,128)(2,1)}, bf16[4,128,128]{2,1,0:T(8,128)(2,1)}) custom-call(bf16[512,512]{1,0:T(8,128)(2,1)} %q.9, bf16[512,512]{1,0:T(8,128)(2,1)} %get-tuple-element.70.g, f32[512,512]{1,0:T(8,128)} %get-tuple-element.71.normed, f32[4,1,512]{2,1,0:T(1,128)} %copy-done), custom_call_target="tpu_custom_call" | custom-call | flops 67108864 | bytes 3145728 | tf_op jit(solution)/shard_map/pallas_call | solution.py:56
  157.6 6.4 %all-to-all-start.3 = ((bf16[32,16,128]{2,1,0:T(8,128)(2,1)}), bf16[32,16,128]{2,1,0:T(8,128)(2,1)S(1)}, u32[]{:S(2)}, u32[]{:S(2)}) async-start(bf16[32,16,128]{2,1,0:T(8,128)(2,1)} %bitcast.10), calls=%async_computation.4 | async-start | bytes 262144 | tf_op jit(solution)/shard_map/all_to_all | solution.py:227
  164.0 6.1 %shard_map.99 = (f32[512,512]{1,0:T(8,128)}, bf16[448,512]{1,0:T(8,128)(2,1)}, bf16[448,512]{1,0:T(8,128)(2,1)}, f32[4,1,512]{2,1,0:T(1,128)S(1)}) custom-call(bf16[512,512]{1,0:T(8,128)(2,1)} %q.9, bf16[512,512]{1,0:T(8,128)(2,1)} %get-tuple-element.70.g, bf16[512,512]{1,0:T(8,128)(2,1)} %copy-done.5, bf16[512,512]{1,0:T(8,128)(2,1)} %copy-done.6, ...), custom_call_target="tpu_custom_call" | custom-call | flops 268435456 | bytes 8388608 | tf_op jit(solution)/shard_map/pallas_call | solution.py:56
  170.1 0.6 copy-done.1
  170.7 4.6 %collective-permute-start.15 = (bf16[448,512]{1,0:T(8,128)(2,1)}, bf16[448,512]{1,0:T(8,128)(2,1)}, u32[]{:S(2)}, u32[]{:S(2)}) collective-permute-start(bf16[448,512]{1,0:T(8,128)(2,1)} %get-tuple-element.83), channel_id=1, source_target_pairs={{8,0},{16,8},{24,16},{32,24},{40,32},{48,40},{56,48},{64,56},{72,6... | collective-permute-start | bytes 1376264 | tf_op jit(solution)/shard_map/ppermute | solution.py:322
  175.3 3.4 %collective-permute-start.16 = (bf16[448,512]{1,0:T(8,128)(2,1)}, bf16[448,512]{1,0:T(8,128)(2,1)}, u32[]{:S(2)}, u32[]{:S(2)}) collective-permute-start(bf16[448,512]{1,0:T(8,128)(2,1)} %get-tuple-element.84), channel_id=1, source_target_pairs={{8,0},{16,8},{24,16},{32,24},{40,32},{48,40},{56,48},{64,56},{72,6... | collective-permute-start | bytes 1376264 | tf_op jit(solution)/shard_map/ppermute | solution.py:322
  178.6 20.5 %all-to-all-done.3.x = bf16[32,16,128]{2,1,0:T(8,128)(2,1)S(1)} async-done(((bf16[32,16,128]{2,1,0:T(8,128)(2,1)}), bf16[32,16,128]{2,1,0:T(8,128)(2,1)S(1)}, u32[]{:S(2)}, u32[]{:S(2)}) %all-to-all-start.3) | async-done | bytes 131104 | tf_op jit(solution)/shard_map/all_to_all | solution.py:227
  199.1 0.7 copy-done.17
  199.8 1.6 shard_map.101
  201.4 23.0 %all-to-all-start.4 = ((bf16[32,16,128]{2,1,0:T(8,128)(2,1)}), bf16[32,16,128]{2,1,0:T(8,128)(2,1)S(1)}, u32[]{:S(2)}, u32[]{:S(2)}) async-start(bf16[32,16,128]{2,1,0:T(8,128)(2,1)} %shard_map.101), calls=%async_computation.5 | async-start | bytes 262144 | tf_op jit(solution)/shard_map/all_to_all | solution.py:233
  224.4 8.0 %shard_map.100 = (bf16[512,512]{1,0:T(8,128)(2,1)}, f32[512,512]{1,0:T(8,128)}, f32[512,512]{1,0:T(8,128)}) custom-call(bf16[512,512]{1,0:T(8,128)(2,1)} %q.9, bf16[512,512]{1,0:T(8,128)(2,1)} %k.7, bf16[512,512]{1,0:T(8,128)(2,1)} %v.7, bf16[512,512]{1,0:T(8,128)(2,1)} %get-tuple-element.70.g, bf16[512,512]{1,0:T(8,128)(2,1)} %get-tuple-element.73.gl, ...), custom_call_target="tpu_custom_call" | custom-call | flops 402653184 | bytes 12582912 | tf_op jit(solution)/shard_map/pallas_call | solution.py:56
  232.8 0.7 copy-done.15
  233.5 4.4 %shard_map.102 = (bf16[512,512]{1,0:T(8,128)(2,1)}, bf16[512,512]{1,0:T(8,128)(2,1)}) custom-call(bf16[512,512]{1,0:T(8,128)(2,1)} %k.7, bf16[512,512]{1,0:T(8,128)(2,1)} %v.7, bf16[4,128,128]{2,1,0:T(8,128)(2,1)} %bitcast.16, f32[512,512]{1,0:T(8,128)} %get-tuple-element.81.dk, f32[512,512]{1,0:T(8,128)} %get-tuple-element.82.dv, ...), custom_call_target="tpu_custom_call" | custom-call | flops 134217728 | bytes 5242880 | tf_op jit(solution)/shard_map/pallas_call | solution.py:56
  237.9 0.9 copy-done.8
  239.5 6.1 %shard_map.103 = bf16[8,512,128]{2,1,0:T(8,128)(2,1)} custom-call(bf16[512,1024]{1,0:T(8,128)(2,1)} %get-tuple-element.87.refs_0_, bf16[512,1024]{1,0:T(8,128)(2,1)} %copy-done.8, bf16[512,1024]{1,0:T(8,128)(2,1)} %copy-done.10, bf16[512,1024]{1,0:T(8,128)(2,1)} %copy-done.9), custom_call_target="tpu_custom_call" | custom-call | bytes 5242880 | tf_op jit(solution)/shard_map/pallas_call | solution.py:56
  245.6 33.3 %all_to_all.30 = bf16[8,512,128]{2,1,0:T(8,128)(2,1)S(1)} all-to-all(bf16[8,512,128]{2,1,0:T(8,128)(2,1)} %shard_map.103), channel_id=1, replica_groups={{0,8,16,24,32,40,48,56},{64,72,80,88,96,104,112,120},{128,136,144,152,1..., dimensions={0} | all-to-all | bytes 2097152 | tf_op jit(solution)/shard_map/all_to_all | solution.py:330
  279.0 0.7 broadcast_multiply_fusion
  (62 shorter events, 4.5 us)
Async XLA Ops:
  7.2 29.3 %copy-start.3 = (bf16[512,512]{1,0:T(8,128)(2,1)S(1)}, bf16[512,512]{1,0:T(8,128)(2,1)}, u32[]{:S(2)}) copy-start(bf16[512,512]{1,0:T(8,128)(2,1)} %v.7) | copy-start | bytes 1572868
  7.2 25.9 %copy-start.2 = (bf16[512,512]{1,0:T(8,128)(2,1)S(1)}, bf16[512,512]{1,0:T(8,128)(2,1)}, u32[]{:S(2)}) copy-start(bf16[512,512]{1,0:T(8,128)(2,1)} %k.7) | copy-start | bytes 1572868
  7.2 32.7 %copy-start.11 = (bf16[512,512]{1,0:T(8,128)(2,1)S(1)}, bf16[512,512]{1,0:T(8,128)(2,1)}, u32[]{:S(2)}) copy-start(bf16[512,512]{1,0:T(8,128)(2,1)} %refs_0_.3) | copy-start | bytes 1572868
  7.2 126.3 %all-gather.3.cloned.1.call-start = ((), (), s32[]{:S(2)}) async-start(), calls=%async_computation.8 | async-start | bytes 2359296 | tf_op jit(solution)/shard_map/all_gather | solution.py:371
  8.2 6.2 %collective-permute-start.13 = (bf16[256,128]{1,0:T(8,128)(2,1)S(1)}, bf16[256,128]{1,0:T(8,128)(2,1)S(1)}, u32[]{:S(2)}, u32[]{:S(2)}) collective-permute-start(bf16[256,128]{1,0:T(8,128)(2,1)S(1)} %get-tuple-element.92), channel_id=1, source_target_pairs={{0,128},{8,136},{16,144},{24,152},{32,160},{40,168},{48,176},{56,1... | collective-permute-start | bytes 196616 | tf_op jit(solution)/shard_map/ppermute | solution.py:339
  10.4 4.7 %collective-permute-start.12 = (bf16[256,128]{1,0:T(8,128)(2,1)S(1)}, bf16[256,128]{1,0:T(8,128)(2,1)S(1)}, u32[]{:S(2)}, u32[]{:S(2)}) collective-permute-start(bf16[256,128]{1,0:T(8,128)(2,1)S(1)} %get-tuple-element.92), channel_id=1, source_target_pairs={{0,64},{8,72},{16,80},{24,88},{32,96},{40,104},{48,112},{56,120},{... | collective-permute-start | bytes 196616 | tf_op jit(solution)/shard_map/ppermute | solution.py:339
  10.9 4.4 %collective-permute-start.14 = (bf16[256,128]{1,0:T(8,128)(2,1)S(1)}, bf16[256,128]{1,0:T(8,128)(2,1)S(1)}, u32[]{:S(2)}, u32[]{:S(2)}) collective-permute-start(bf16[256,128]{1,0:T(8,128)(2,1)S(1)} %get-tuple-element.92), channel_id=1, source_target_pairs={{0,192},{8,200},{16,208},{24,216},{32,224},{40,232},{48,240},{56,2... | collective-permute-start | bytes 196616 | tf_op jit(solution)/shard_map/ppermute | solution.py:339
  19.7 25.3 %all-to-all-start = ((bf16[32,16,128]{2,1,0:T(8,128)(2,1)}), bf16[32,16,128]{2,1,0:T(8,128)(2,1)S(1)}, u32[]{:S(2)}, u32[]{:S(2)}) async-start(bf16[32,16,128]{2,1,0:T(8,128)(2,1)} %bitcast.2), calls=%async_computation | async-start | bytes 262144 | tf_op jit(solution)/shard_map/all_to_all | solution.py:227
  33.1 30.4 %collective-permute-start = (bf16[512,512]{1,0:T(8,128)(2,1)S(1)}, bf16[512,512]{1,0:T(8,128)(2,1)S(1)}, u32[]{:S(2)}, u32[]{:S(2)}) collective-permute-start(bf16[512,512]{1,0:T(8,128)(2,1)S(1)} %copy-done.2), channel_id=1, source_target_pairs={{0,8},{8,16},{16,24},{24,32},{32,40},{40,48},{48,56},{56,64},{64,7... | collective-permute-start | bytes 1572872 | tf_op jit(solution)/shard_map/ppermute | solution.py:322
  36.5 45.1 %collective-permute-start.1 = (bf16[512,512]{1,0:T(8,128)(2,1)S(1)}, bf16[512,512]{1,0:T(8,128)(2,1)S(1)}, u32[]{:S(2)}, u32[]{:S(2)}) collective-permute-start(bf16[512,512]{1,0:T(8,128)(2,1)S(1)} %copy-done.3), channel_id=1, source_target_pairs={{0,8},{8,16},{16,24},{24,32},{32,40},{40,48},{48,56},{56,64},{64,7... | collective-permute-start | bytes 1572872 | tf_op jit(solution)/shard_map/ppermute | solution.py:322
  39.9 41.7 %collective-permute-start.4 = (bf16[512,512]{1,0:T(8,128)(2,1)S(1)}, bf16[512,512]{1,0:T(8,128)(2,1)}, u32[]{:S(2)}, u32[]{:S(2)}) collective-permute-start(bf16[512,512]{1,0:T(8,128)(2,1)S(1)} %copy-done.11), channel_id=1, source_target_pairs={{0,4},{1,5},{2,6},{3,7},{4,0},{5,1},{6,2},{7,3},{8,12},{9,13},{10,... | collective-permute-start | bytes 1572872 | tf_op jit(solution)/shard_map/ppermute | solution.py:345
  43.0 38.6 %collective-permute-start.3 = (bf16[512,512]{1,0:T(8,128)(2,1)S(1)}, bf16[512,512]{1,0:T(8,128)(2,1)}, u32[]{:S(2)}, u32[]{:S(2)}) collective-permute-start(bf16[512,512]{1,0:T(8,128)(2,1)S(1)} %copy-done.11), channel_id=1, source_target_pairs={{0,6},{1,7},{2,0},{3,1},{4,2},{5,3},{6,4},{7,5},{8,14},{9,15},{10,... | collective-permute-start | bytes 1572872 | tf_op jit(solution)/shard_map/ppermute | solution.py:345
  44.1 37.5 %collective-permute-start.2 = (bf16[512,512]{1,0:T(8,128)(2,1)S(1)}, bf16[512,512]{1,0:T(8,128)(2,1)}, u32[]{:S(2)}, u32[]{:S(2)}) collective-permute-start(bf16[512,512]{1,0:T(8,128)(2,1)S(1)} %copy-done.11), channel_id=1, source_target_pairs={{0,2},{1,3},{2,4},{3,5},{4,6},{5,7},{6,0},{7,1},{8,10},{9,11},{10,... | collective-permute-start | bytes 1572872 | tf_op jit(solution)/shard_map/ppermute | solution.py:345
  45.0 51.3 %copy-start.16 = (bf16[32,16,128]{2,1,0:T(8,128)(2,1)}, bf16[32,16,128]{2,1,0:T(8,128)(2,1)S(1)}, u32[]{:S(2)}) copy-start(bf16[32,16,128]{2,1,0:T(8,128)(2,1)S(1)} %all-to-all-done.x) | copy-start | bytes 393220
  45.9 46.6 %all-to-all-start.2 = ((bf16[8,256,128]{2,1,0:T(8,128)(2,1)}), bf16[8,256,128]{2,1,0:T(8,128)(2,1)S(1)}, u32[]{:S(2)}, u32[]{:S(2)}) async-start(bf16[8,256,128]{2,1,0:T(8,128)(2,1)} %broadcast_in_dim.2), calls=%async_computation.2 | async-start | bytes 1048576 | tf_op jit(solution)/shard_map/all_to_all | solution.py:330
  63.5 40.3 %copy-start.5 = (bf16[512,512]{1,0:T(8,128)(2,1)}, bf16[512,512]{1,0:T(8,128)(2,1)S(1)}, u32[]{:S(2)}) copy-start(bf16[512,512]{1,0:T(8,128)(2,1)S(1)} %collective-permute-done.kw) | copy-start | bytes 1572868
  63.5 29.5 %collective-permute-start.5 = (bf16[512,512]{1,0:T(8,128)(2,1)S(1)}, bf16[512,512]{1,0:T(8,128)(2,1)S(1)}, u32[]{:S(2)}, u32[]{:S(2)}) collective-permute-start(bf16[512,512]{1,0:T(8,128)(2,1)S(1)} %copy-done.11), channel_id=1, source_target_pairs={{0,1},{1,0},{2,3},{3,2},{4,5},{5,4},{6,7},{7,6},{8,9},{9,8},{10,11... | collective-permute-start | bytes 1572872 | tf_op jit(solution)/shard_map/ppermute | solution.py:351
  81.6 22.2 %copy-start.6 = (bf16[512,512]{1,0:T(8,128)(2,1)}, bf16[512,512]{1,0:T(8,128)(2,1)S(1)}, u32[]{:S(2)}) copy-start(bf16[512,512]{1,0:T(8,128)(2,1)S(1)} %collective-permute-done.1.vw) | copy-start | bytes 1572868
  81.6 14.3 %collective-permute-start.6 = (bf16[512,512]{1,0:T(8,128)(2,1)}, bf16[512,512]{1,0:T(8,128)(2,1)S(1)}, u32[]{:S(2)}, u32[]{:S(2)}) collective-permute-start(bf16[512,512]{1,0:T(8,128)(2,1)} %collective-permute-done.2.refs_1_), channel_id=1, source_target_pairs={{0,1},{1,0},{2,3},{3,2},{4,5},{5,4},{6,7},{7,6},{8,9},{9,8},{10,11... | collective-permute-start | bytes 1572872 | tf_op jit(solution)/shard_map/ppermute | solution.py:351
  81.7 42.9 %collective-permute-start.7 = (bf16[512,512]{1,0:T(8,128)(2,1)}, bf16[512,512]{1,0:T(8,128)(2,1)}, u32[]{:S(2)}, u32[]{:S(2)}) collective-permute-start(bf16[512,512]{1,0:T(8,128)(2,1)} %collective-permute-done.3.refs_2_), channel_id=1, source_target_pairs={{0,1},{1,0},{2,3},{3,2},{4,5},{5,4},{6,7},{7,6},{8,9},{9,8},{10,11... | collective-permute-start | bytes 1572872 | tf_op jit(solution)/shard_map/ppermute | solution.py:351
  82.2 42.4 %collective-permute-start.8 = (bf16[512,512]{1,0:T(8,128)(2,1)}, bf16[512,512]{1,0:T(8,128)(2,1)}, u32[]{:S(2)}, u32[]{:S(2)}) collective-permute-start(bf16[512,512]{1,0:T(8,128)(2,1)} %collective-permute-done.4.refs_3_), channel_id=1, source_target_pairs={{0,1},{1,0},{2,3},{3,2},{4,5},{5,4},{6,7},{7,6},{8,9},{9,8},{10,11... | collective-permute-start | bytes 1572872 | tf_op jit(solution)/shard_map/ppermute | solution.py:351
  92.4 31.6 %copy-start.4 = (bf16[8,256,128]{2,1,0:T(8,128)(2,1)}, bf16[8,256,128]{2,1,0:T(8,128)(2,1)S(1)}, u32[]{:S(2)}) copy-start(bf16[8,256,128]{2,1,0:T(8,128)(2,1)S(1)} %all-to-all-done.2.refs_9_) | copy-start | bytes 1572868
  92.4 41.1 %collective-permute-start.11 = (bf16[8,256,128]{2,1,0:T(8,128)(2,1)S(1)}, bf16[8,256,128]{2,1,0:T(8,128)(2,1)}, u32[]{:S(2)}, u32[]{:S(2)}) collective-permute-start(bf16[8,256,128]{2,1,0:T(8,128)(2,1)S(1)} %all-to-all-done.2.refs_9_), channel_id=1, source_target_pairs={{0,192},{8,200},{16,208},{24,216},{32,224},{40,232},{48,240},{56,2... | collective-permute-start | bytes 1572872 | tf_op jit(solution)/shard_map/ppermute | solution.py:339
  93.0 31.0 %copy-start.12 = (bf16[512,512]{1,0:T(8,128)(2,1)}, bf16[512,512]{1,0:T(8,128)(2,1)S(1)}, u32[]{:S(2)}) copy-start(bf16[512,512]{1,0:T(8,128)(2,1)S(1)} %collective-permute-done.5.refs_4_) | copy-start | bytes 1572868
  93.0 40.5 %collective-permute-start.10 = (bf16[8,256,128]{2,1,0:T(8,128)(2,1)S(1)}, bf16[8,256,128]{2,1,0:T(8,128)(2,1)S(1)}, u32[]{:S(2)}, u32[]{:S(2)}) collective-permute-start(bf16[8,256,128]{2,1,0:T(8,128)(2,1)S(1)} %all-to-all-done.2.refs_9_), channel_id=1, source_target_pairs={{0,128},{8,136},{16,144},{24,152},{32,160},{40,168},{48,176},{56,1... | collective-permute-start | bytes 1572872 | tf_op jit(solution)/shard_map/ppermute | solution.py:339
  95.9 2.0 copy-start.13
  95.9 37.6 %collective-permute-start.9 = (bf16[8,256,128]{2,1,0:T(8,128)(2,1)S(1)}, bf16[8,256,128]{2,1,0:T(8,128)(2,1)}, u32[]{:S(2)}, u32[]{:S(2)}) collective-permute-start(bf16[8,256,128]{2,1,0:T(8,128)(2,1)S(1)} %all-to-all-done.2.refs_9_), channel_id=1, source_target_pairs={{0,64},{8,72},{16,80},{24,88},{32,96},{40,104},{48,112},{56,120},{... | collective-permute-start | bytes 1572872 | tf_op jit(solution)/shard_map/ppermute | solution.py:339
  97.9 21.0 %all-to-all-start.1 = ((bf16[32,16,128]{2,1,0:T(8,128)(2,1)}), bf16[32,16,128]{2,1,0:T(8,128)(2,1)S(1)}, u32[]{:S(2)}, u32[]{:S(2)}) async-start(bf16[32,16,128]{2,1,0:T(8,128)(2,1)} %shard_map.93), calls=%async_computation.1 | async-start | bytes 262144 | tf_op jit(solution)/shard_map/all_to_all | solution.py:233
  103.5 176.2 %reduce-scatter.2.cloned.1.call-start = ((), (), s32[]{:S(2)}) async-start(), calls=%async_computation.7 | async-start | bytes 4718592 | tf_op jit(solution)/shard_map/reduce_scatter | solution.py:451
  118.9 0.6 copy-start.7
  124.0 0.6 copy-start
  133.5 0.9 copy-start.14
  147.8 90.1 %collective-permute-start.17 = (bf16[512,1024]{1,0:T(8,128)(2,1)}, bf16[512,1024]{1,0:T(8,128)(2,1)S(1)}, u32[]{:S(2)}, u32[]{:S(2)}) collective-permute-start(bf16[512,1024]{1,0:T(8,128)(2,1)} %get-tuple-element.65), channel_id=1, source_target_pairs={{0,64},{8,72},{16,80},{24,88},{32,96},{40,104},{48,112},{56,120},{... | collective-permute-start | bytes 3145736 | tf_op jit(solution)/shard_map/ppermute | solution.py:339
  149.3 88.6 %collective-permute-start.19 = (bf16[512,1024]{1,0:T(8,128)(2,1)}, bf16[512,1024]{1,0:T(8,128)(2,1)S(1)}, u32[]{:S(2)}, u32[]{:S(2)}) collective-permute-start(bf16[512,1024]{1,0:T(8,128)(2,1)} %get-tuple-element.66), channel_id=1, source_target_pairs={{0,128},{8,136},{16,144},{24,152},{32,160},{40,168},{48,176},{56,1... | collective-permute-start | bytes 3145736 | tf_op jit(solution)/shard_map/ppermute | solution.py:339
  150.8 87.0 %collective-permute-start.18 = (bf16[512,1024]{1,0:T(8,128)(2,1)}, bf16[512,1024]{1,0:T(8,128)(2,1)S(1)}, u32[]{:S(2)}, u32[]{:S(2)}) collective-permute-start(bf16[512,1024]{1,0:T(8,128)(2,1)} %get-tuple-element.67), channel_id=1, source_target_pairs={{0,192},{8,200},{16,208},{24,216},{32,224},{40,232},{48,240},{56,2... | collective-permute-start | bytes 3145736 | tf_op jit(solution)/shard_map/ppermute | solution.py:339
  157.6 41.5 %all-to-all-start.3 = ((bf16[32,16,128]{2,1,0:T(8,128)(2,1)}), bf16[32,16,128]{2,1,0:T(8,128)(2,1)S(1)}, u32[]{:S(2)}, u32[]{:S(2)}) async-start(bf16[32,16,128]{2,1,0:T(8,128)(2,1)} %bitcast.10), calls=%async_computation.4 | async-start | bytes 262144 | tf_op jit(solution)/shard_map/all_to_all | solution.py:227
  170.1 0.6 copy-start.1
  170.7 61.7 %collective-permute-start.15 = (bf16[448,512]{1,0:T(8,128)(2,1)}, bf16[448,512]{1,0:T(8,128)(2,1)}, u32[]{:S(2)}, u32[]{:S(2)}) collective-permute-start(bf16[448,512]{1,0:T(8,128)(2,1)} %get-tuple-element.83), channel_id=1, source_target_pairs={{8,0},{16,8},{24,16},{32,24},{40,32},{48,40},{56,48},{64,56},{72,6... | collective-permute-start | bytes 1376264 | tf_op jit(solution)/shard_map/ppermute | solution.py:322
  175.3 57.1 %collective-permute-start.16 = (bf16[448,512]{1,0:T(8,128)(2,1)}, bf16[448,512]{1,0:T(8,128)(2,1)}, u32[]{:S(2)}, u32[]{:S(2)}) collective-permute-start(bf16[448,512]{1,0:T(8,128)(2,1)} %get-tuple-element.84), channel_id=1, source_target_pairs={{8,0},{16,8},{24,16},{32,24},{40,32},{48,40},{56,48},{64,56},{72,6... | collective-permute-start | bytes 1376264 | tf_op jit(solution)/shard_map/ppermute | solution.py:322
  199.1 0.7 copy-start.17
  201.4 31.4 %all-to-all-start.4 = ((bf16[32,16,128]{2,1,0:T(8,128)(2,1)}), bf16[32,16,128]{2,1,0:T(8,128)(2,1)S(1)}, u32[]{:S(2)}, u32[]{:S(2)}) async-start(bf16[32,16,128]{2,1,0:T(8,128)(2,1)} %shard_map.101), calls=%async_computation.5 | async-start | bytes 262144 | tf_op jit(solution)/shard_map/all_to_all | solution.py:233
  232.8 0.7 copy-start.15
  237.8 1.0 copy-start.8
  237.9 1.3 copy-start.9
  237.9 1.6 copy-start.10
Sparse Core Ops, SparseCore 0:
  16.2 59.8 all-gather.2
  147.9 38.4 reduce-scatter.1

commit v4 on v2

--- a/solution.py
+++ b/solution.py
@@ -42,16 +42,16 @@
         kernel,
         grid_spec=pltpu.PrefetchScalarGridSpec(
             num_scalar_prefetch=prefetch,
-            grid=(heads,),
+            grid=heads if isinstance(heads, tuple) else (heads,),
             in_specs=ins,
             out_specs=outs,
             scratch_shapes=scratch,
         ),
         out_shape=out_shape,
         compiler_params=pltpu.CompilerParams(
-            dimension_semantics=("arbitrary",), vmem_limit_bytes=40 * 1024 * 1024
+            vmem_limit_bytes=40 * 1024 * 1024
         ),
-        cost_estimate=pl.CostEstimate(flops=flops, bytes_accessed=size, transcendentals=0),
+        cost_estimate=pl.CostEstimate(flops=0, bytes_accessed=0, transcendentals=0),
     )
     return lambda *args: run(*args[:prefetch], *(kept(a) for a in args[prefetch:]))
 
@@ -221,87 +221,67 @@
         total = total + x[at].astype(F32)
 
 
-def carry_states(local, backward, beside=()):
+def carry_states(local, backward):
     count = lax.axis_size("seq")
     pieces = local.reshape(count, -1, DH)
     met = lax.all_to_all(pieces, "seq", 0, 0)
-    met, beside = lax.optimization_barrier((met, beside))
     done = pl.pallas_call(
         functools.partial(scan_kernel, backward),
         out_shape=jax.ShapeDtypeStruct(met.shape, BF16),
     )(met)
-    return lax.all_to_all(done, "seq", 0, 0).reshape(local.shape), beside
-
-
-def block_id(t, head):
-    hops = jnp.where(t % XS < 2, t % XS, 5 - t % XS)
-    x = (head[0] // 2 + XS - hops) % XS
-    core = jnp.where(t < XS, head[0] % 2, 1 - head[0] % 2)
-    return 2 * x + core
-
-
-def gathered_specs(rows, width):
-    return [pl.BlockSpec((rows, width), lambda t, head: (0, 0))] * (2 * XS)
-
-
-def weight_specs(part, rest, width):
-    return [
-        pl.BlockSpec((width // DH, part, DH), lambda t, head: (block_id(t, head), 0, 0)),
-        pl.BlockSpec((rest, width), lambda t, head: (0, block_id(t, head))),
-    ]
-
-
-def across(w):
-    return jnp.concatenate([w[i] for i in range(w.shape[0])], axis=1)
-
-
-def each_block(blocks, use):
-    for j, block in enumerate(blocks):
-
-        @pl.when(pl.program_id(0) == j)
-        def _(block=block):
-            use(block[...])
-
-
-def grad_mixed_kernel(head, *refs):
-    blocks, (wa, wb, out, acc) = refs[: 2 * XS], refs[2 * XS :]
-    part = wa.shape[1]
-    t = pl.program_id(0)
-
-    @pl.when(t == 0)
+    return lax.all_to_all(done, "seq", 0, 0).reshape(local.shape)
+
+
+def project_kernel(y, g, mixed, *refs):
+    sources, (partial_value, out, acc, w) = refs[:YS], refs[YS:]
+    block = pl.program_id(0)
+    count = sources[0].shape[0] // 2
+    slot = (y[0] + YS - block // 2) % YS
+
+    @pl.when(block == 0)
     def _():
         acc[...] = jnp.zeros_like(acc)
 
-    def add(block):
-        acc[:, 0:part] += nt(block, across(wa))
-        acc[:, part:] += nt(block, wb[...])
-
-    each_block(blocks, add)
-
-    @pl.when(t == 2 * XS - 1)
+    for r, source in enumerate(sources):
+
+        @pl.when(slot == r)
+        def _(source=source):
+            for i in range(count):
+                w[:, i * DH : (i + 1) * DH] = source[block % 2 * count + i]
+
+    partial_value[...] = nn(mixed[...], w[...]).astype(BF16)
+    acc[...] += nt(g[...], w[...])
+
+    @pl.when(block == 2 * XS - 1)
     def _():
         out[...] = acc[...].astype(BF16)
 
 
-def sens_kernel(head, *refs):
-    blocks, (mixed_t, out) = refs[: 2 * XS], refs[2 * XS :]
-
-    def put(block):
-        out[0] = nn(mixed_t[...], block).astype(BF16)
-
-    each_block(blocks, put)
-
-
-def mixer_kernel(head, mixed, wa, wb, out):
-    part = wa.shape[1]
-    out[...] = (nn(mixed[:, 0:part], across(wa)) + nn(mixed[:, part:], wb[...])).astype(BF16)
-
-
-def fold_kernel(*refs):
-    total = refs[0][...].astype(F32)
-    for part in refs[1:-1]:
-        total = total + part[...].astype(F32)
-    refs[-1][0] = total.astype(BF16)
+def sens_kernel(place, g, *refs):
+    sources, outs, acc = refs[:YS], refs[YS:-1], refs[-1]
+    half, turn = pl.program_id(0), pl.program_id(1)
+
+    @pl.when(turn == 0)
+    def _():
+        acc[...] = jnp.zeros_like(acc)
+
+    for r, source in enumerate(sources):
+
+        @pl.when(turn == r)
+        def _(source=source):
+            acc[...] += nn(source[...], g[...])
+
+    @pl.when(turn == YS - 1)
+    def _():
+        count = ZS // 2
+        for i in range(count):
+            slot = (half * count + i + ZS - place[1]) % ZS
+            part = acc[:, i * DH : (i + 1) * DH].astype(BF16)
+            for r, out in enumerate(outs):
+
+                @pl.when(slot == r)
+                def _(out=out, part=part):
+                    out[...] = part
 
 
 YS, ZS, XS = 4, 8, 4
@@ -333,23 +313,28 @@
     )
 
 
-def hop_x(shard, by):
+def hop_z(shard, by):
     return lax.ppermute(
-        shard, "head", [(x * 2 + c, (x + by) % XS * 2 + c) for x in range(XS) for c in range(2)]
+        shard, "seq", [(y * ZS + z, y * ZS + (z + by) % ZS) for y in range(YS) for z in range(ZS)]
     )
 
 
-def swap_core(shard):
-    return lax.ppermute(shard, "head", [(i, i ^ 1) for i in range(2 * XS)])
+def turn_xy(shard):
+    pairs = [
+        ((y * ZS + z) * 2 * XS + 2 * x + c, (x * ZS + z) * 2 * XS + 2 * y + c)
+        for y in range(YS)
+        for z in range(ZS)
+        for x in range(XS)
+        for c in range(2)
+    ]
+    return lax.ppermute(shard, ("seq", "head"), pairs)
 
 
 def shards(queries, keys, values, w_out, grad_y):
     rows, width = queries.shape
     heads = width // DH
     seq = lax.axis_index("seq").reshape(1).astype(jnp.int32)
-    head = lax.axis_index("head").reshape(1).astype(jnp.int32)
     tokens_all = rows * lax.axis_size("seq")
-    cut = rows // 4
     shape = jax.ShapeDtypeStruct
     col = columns(rows)
     tri = heads_of(rows, rows)
@@ -358,23 +343,23 @@
     line = heads_of(1, rows)
     mm = 2 * rows * rows * width
 
-    wb = lax.all_gather(w_out[cut:], "seq", axis=1, tiled=True)
-    grads = [grad_y] + [hop_x(grad_y, by) for by in (1, XS - 1, 2)]
-    kh, vh = shifted(keys, 1), shifted(values, 1)
-
+    place = jnp.concatenate([seq // ZS, seq % ZS])
+
+    grad_full = lax.all_gather(grad_y, "head", axis=1, tiled=True)
+    turned_grad = turn_xy(grad_y)
+    w_row = spread(w_out, "seq", Z_GROUPS)
     local = call(
         sums_kernel, heads, [col, col], st, shape((heads, DH, DH), BF16), flops=2 * mm // 4
     )(keys, values)
-    before, (kh, vh, grads) = carry_states(local, False, (kh, vh, grads))
-
-    swapped = [swap_core(g) for g in grads]
-    before, first, swapped = lax.optimization_barrier((before, w_out[:cut], swapped))
-    wa = spread(spread(first, "seq", Z_GROUPS), "seq", Y_GROUPS).reshape(YS * ZS, cut, DH)
+    local, w_row, turned_grad = lax.optimization_barrier((local, w_row, turned_grad))
+    grad_wide = lax.all_gather(turned_grad, "head", axis=1, tiled=True)
+    w_rows = [w_row] + [hop_y(w_row, by) for by in range(1, YS)]
+    kh, vh = shifted(keys, 1), shifted(values, 1)
+    before = carry_states(local, False)
 
     sq = large((heads, rows, rows), BF16)
     flat_t = large((width, rows), F32)
     edge = EDGE
-    grads = list(grads) + list(swapped)
     near, far, raw, window, intra = call(
         window_kernel,
         heads,
@@ -386,6 +371,7 @@
         prefetch=1,
     )(seq, queries, keys, values, kh, vh)
 
+    before, window = lax.optimization_barrier((before, window))
     normed, inverse, mixed_t, mixed = call(
         mixed_kernel,
         heads,
@@ -401,40 +387,31 @@
         size=5 << 20,
     )(queries, before, window, intra)
 
-    gathered = gathered_specs(rows, width)
-    weights = weight_specs(cut, rows - cut, width)
-    out_block = pl.BlockSpec((rows, width), lambda t, head: (0, block_id(t, head)))
-    fixed = pl.BlockSpec((rows, width), lambda t, head: (0, 0))
-    by_block = functools.partial(call, heads=2 * XS, size=9 << 20, flops=8 * mm, prefetch=1)
-    pieces = by_block(
-        sens_kernel,
-        ins=gathered + [fixed],
-        outs=pl.BlockSpec(
-            (1, width, width), lambda t, head: (block_id(t, head) // 2, 0, block_id(t, head) % 2)
-        ),
-        out_shape=large((YS, width, 2 * width), BF16),
-    )(head, *grads, mixed_t)
-    y = lax.axis_index("seq") // ZS
-    own = lax.dynamic_index_in_dim(pieces, y, 0, False)
-    sends = [lax.dynamic_index_in_dim(pieces, (y + by) % YS, 0, False) for by in Y_HOPS]
-    met = [own] + [hop_y(piece, by) for piece, by in zip(sends, Y_HOPS)]
-    own, sends, wa, wb = lax.optimization_barrier((own, sends, wa, wb))
-
-    partial_value = by_block(
-        mixer_kernel,
-        ins=[fixed] + weights,
-        outs=out_block,
-        out_shape=large((rows, 2 * XS * width), BF16),
-    )(head, mixed, wa, wb)
+    w_rows, before = lax.optimization_barrier((w_rows, before))
+    across_y = [mixed_t] + [hop_y(mixed_t, by) for by in range(1, YS)]
+    fixed = pl.BlockSpec((rows, width), lambda *_: (0, 0))
+    by_block = pl.BlockSpec((rows, width), lambda b, *_: (0, b))
+    partial_value, grad_mixed = call(
+        project_kernel,
+        2 * XS,
+        [by_block, fixed] + [pl.BlockSpec((ZS, rows, DH), lambda *_: (0, 0, 0))] * YS,
+        [by_block, fixed],
+        [large((rows, 2 * XS * width), BF16), large((rows, width), BF16)],
+        scratch=[pltpu.VMEM((rows, width), F32), pltpu.VMEM((rows, width), BF16)],
+        prefetch=1,
+    )(place, grad_full, mixed, *w_rows)
     mixer_result = lax.psum_scatter(partial_value, "head", scatter_dimension=1, tiled=True)
-    grad_mixed = by_block(
-        grad_mixed_kernel,
-        ins=gathered + weights,
-        outs=fixed,
-        out_shape=large((rows, width), BF16),
-        scratch=[pltpu.VMEM((rows, width), F32)],
-    )(head, *grads, wa, wb)
-
+
+    grad_lin, local_back = call(
+        lin_kernel,
+        heads,
+        [col, col, turned, line],
+        [col, st],
+        [large((rows, width), BF16), shape((heads, DH, DH), BF16)],
+        flops=mm // 4,
+        size=3 << 20,
+    )(queries, grad_mixed, normed, inverse)
+    local_back, g_far = lax.optimization_barrier((local_back, grad_mixed))
     edge_grad = large((edge, width), BF16)
     dq_far, far_k, far_v, delta = call(
         far_kernel,
@@ -445,19 +422,30 @@
         scratch=[pltpu.VMEM((rows, rows), BF16)],
         flops=8 * mm // 8,
         size=8 << 20,
-    )(queries, grad_mixed, kh, vh, far, window)
+    )(queries, g_far, kh, vh, far, window)
     back_k, back_v = shifted(far_k, -1), shifted(far_v, -1)
 
-    grad_lin, local_back = call(
-        lin_kernel,
-        heads,
-        [col, col, turned, line],
-        [col, st],
-        [large((rows, width), BF16), shape((heads, DH, DH), BF16)],
-        flops=mm // 4,
-        size=3 << 20,
-    )(queries, grad_mixed, normed, inverse)
-    later, _ = carry_states(local_back, True)
+    later = carry_states(local_back, True)
+
+    across_y, local_back = lax.optimization_barrier((across_y, local_back))
+    parts = call(
+        sens_kernel,
+        (2, YS),
+        [
+            pl.BlockSpec(
+                (rows, width), lambda c, by, place: (0, (place[0] + YS - by) % YS * 2 + c)
+            )
+        ]
+        + [fixed] * YS,
+        [pl.BlockSpec((width, DH), lambda *_: (0, 0))] * ZS,
+        [large((width, DH), BF16)] * ZS,
+        scratch=[pltpu.VMEM((width, rows), F32)],
+        prefetch=1,
+    )(place, grad_wide, *across_y)
+    total = parts[0].astype(F32)
+    for by in range(1, ZS):
+        total = total + hop_z(parts[by], by).astype(F32)
+    projection_sensitivity = total * tokens_all ** (-0.5)
 
     grad_queries, near_k, near_v = call(
         near_kernel,
@@ -479,18 +467,6 @@
         flops=mm // 2,
         size=5 << 20,
     )(keys, values, later, near_k, near_v, back_k, back_v)
-    met, _ = lax.optimization_barrier((met, grad_keys))
-    parts = call(
-        fold_kernel,
-        ZS,
-        [pl.BlockSpec((width, DH), lambda z: (0, z))] * YS,
-        pl.BlockSpec((1, width, DH), lambda z: (z, 0, 0)),
-        large((ZS, width, DH), BF16),
-        size=5 << 20,
-    )(*met)
-    total = jnp.sum(exchange(parts, "seq", Z_GROUPS).astype(F32), axis=0)
-    projection_sensitivity = total * tokens_all ** (-0.5)
-
     return (mixer_result, grad_queries, grad_keys, grad_values, projection_sensitivity)
 
 

time: 260 us -> 269 us (1.035)
  starting transfers between devices: 69.2 us -> 97.8 us
  Pallas kernels: 75.1 us -> 63.8 us
  blocking collectives: 68.4 us -> 58.6 us
  waiting for transfers between devices: 17.6 us -> 23 us
  local copies, waits for them, and re-layouts: 12.5 us -> 9.67 us
    all_to_all x2 -> x0, blocking collectives: 45.6 us -> none  [exchange(): return lax.all_to_all(pieces, axis, 0, 0, axis_index_groups=groups)]
    all_to_all x1, blocking collectives: 22.8 us -> 58.6 us  [carry_states(): met = lax.all_to_all(pieces, 'seq', 0, 0)]
    ppermute x7 -> x8, waiting for transfers between devices: 0.02 us -> 22.2 us  [the longest x1 22.2 us: turn_xy(): return lax.ppermute(shard, ('seq', 'head'), pairs)]
    ppermute x3 -> x6, starting transfers between devices: 3.41 us -> 17.8 us  [hop_y(): lax.ppermute(shard, 'seq', [(y * ZS + z, (y + by) % YS * ZS + z) for y in...]
    ppermute x7 -> x8, starting transfers between devices: 6.06 us -> 20.1 us  [the longest x7 15.4 us: hop_z(): lax.ppermute(shard, 'seq', [(y * ZS + z, y * ZS + (z + by) % ZS) for y in...]
    pallas_call x11 -> x9, Pallas kernels: 71.9 us -> 60.6 us  [call(): run(*args[:prefetch], *(kept(a) for a in args[prefetch:]))]
    all_to_all x1, waiting for transfers between devices: 9.16 us -> 0.01 us  [carry_states(): met = lax.all_to_all(pieces, 'seq', 0, 0)]
    all_to_all x2, waiting for transfers between devices: 8.35 us -> 0.01 us  [carry_states(): return lax.all_to_all(done, 'seq', 0, 0).reshape(local.shape)]
  transfers between devices with their start and end apart: 20 -> 25, of which waited for: 3 -> 1; matrix products, arithmetic and copies ran while one was open for 3% -> 1% of each run, Pallas kernels for 26% -> 24%
where the time goes in v4:
time: 269 us; the launch traced here: 268 us
  starting transfers between devices  97.8 us (36%)
  Pallas kernels  63.8 us (24%)
  blocking collectives  58.6 us (22%)
  waiting for transfers between devices  23 us (9%)
  between operations  14 us (5%)
  local copies, waits for them, and re-layouts  9.67 us (4%)
    pallas_call x9, Pallas kernels, call(): run(*args[:prefetch], *(kept(a) for a in args[prefetch:]))  60.6 us
    all_to_all x1, blocking collectives, carry_states(): met = lax.all_to_all(pieces, 'seq', 0, 0)  58.6 us
    all_to_all x2, starting transfers between devices, carry_states(): return lax.all_to_all(done, 'seq', 0, 0).reshape(local.shape)  29 us
    ppermute x1, waiting for transfers between devices, turn_xy(): return lax.ppermute(shard, ('seq', 'head'), pairs)  22.2 us
    ppermute x6, starting transfers between devices, hop_y(): lax.ppermute(shard, 'seq', [(y * ZS + z, (y + by) % YS * ZS + z) for y in...  17.8 us
    ppermute x4, starting transfers between devices, shifted(): return lax.ppermute(shard, 'seq', pairs)  17 us
    ppermute x7, starting transfers between devices, hop_z(): lax.ppermute(shard, 'seq', [(y * ZS + z, y * ZS + (z + by) % ZS) for y in...  15.4 us
    all_to_all x1, starting transfers between devices, exchange(): return lax.all_to_all(pieces, axis, 0, 0, axis_index_groups=groups)  8.47 us
  transfers between devices with their start and end apart: 25, of which 1 were waited for; matrix products, arithmetic and copies ran while one was open for 1% of the time, Pallas kernels for 24%

profile of v4, /device:TPU:16, one launch (start us, length us, event | category | flops | bytes accessed | tf_op | source)
XLA Modules:
  0.0 267.8 jit_solution(2852523330262385890)
XLA Ops:
  7.2 0.7 all-gather.3.cloned.1.call-update
  7.9 2.1 broadcast_in_dim.2
  10.0 8.5 %all-to-all-start = ((bf16[8,512,128]{2,1,0:T(8,128)(2,1)}), bf16[8,512,128]{2,1,0:T(8,128)(2,1)S(1)}, u32[]{:S(2)}, u32[]{:S(2)}) async-start(bf16[8,512,128]{2,1,0:T(8,128)(2,1)} %broadcast_in_dim.2), calls=%async_computation | async-start | bytes 2097152 | tf_op jit(solution)/shard_map/all_to_all | solution.py:302
  18.5 4.7 %collective-permute-start = (bf16[512,512]{1,0:T(8,128)(2,1)}, bf16[512,512]{1,0:T(8,128)(2,1)S(1)}, u32[]{:S(2)}, u32[]{:S(2)}) collective-permute-start(bf16[512,512]{1,0:T(8,128)(2,1)} %param.9), channel_id=1, source_target_pairs={{0,0},{1,1},{2,64},{3,65},{4,128},{5,129},{6,192},{7,193},{8,8},{9... | collective-permute-start | bytes 1572872 | tf_op jit(solution)/shard_map/ppermute | solution.py:330
  23.2 2.8 %shard_map.92 = bf16[4,128,128]{2,1,0:T(8,128)(2,1)S(1)} custom-call(bf16[512,512]{1,0:T(8,128)(2,1)} %k.7, bf16[512,512]{1,0:T(8,128)(2,1)} %v.7), custom_call_target="tpu_custom_call" | custom-call | tf_op jit(solution)/shard_map/pallas_call | solution.py:56
  26.0 22.2 %collective-permute-done = bf16[512,512]{1,0:T(8,128)(2,1)S(1)} collective-permute-done((bf16[512,512]{1,0:T(8,128)(2,1)}, bf16[512,512]{1,0:T(8,128)(2,1)S(1)}, u32[]{:S(2)}, u32[]{:S(2)}) %collective-permute-start) | collective-permute-done | bytes 524320 | tf_op jit(solution)/shard_map/ppermute | solution.py:330
  48.2 0.8 copy-done.13
  49.0 12.9 %collective-permute-start.3 = (bf16[8,512,128]{2,1,0:T(8,128)(2,1)S(1)}, bf16[8,512,128]{2,1,0:T(8,128)(2,1)}, u32[]{:S(2)}, u32[]{:S(2)}) collective-permute-start(bf16[8,512,128]{2,1,0:T(8,128)(2,1)S(1)} %all-to-all-done.refs_0_), channel_id=1, source_target_pairs={{0,64},{8,72},{16,80},{24,88},{32,96},{40,104},{48,112},{56,120},{... | collective-permute-start | bytes 3145736 | tf_op jit(solution)/shard_map/ppermute | solution.py:311
  62.0 1.6 collective-permute-start.5
  63.5 3.6 %collective-permute-start.1 = (bf16[512,512]{1,0:T(8,128)(2,1)S(1)}, bf16[512,512]{1,0:T(8,128)(2,1)S(1)}, u32[]{:S(2)}, u32[]{:S(2)}) collective-permute-start(bf16[512,512]{1,0:T(8,128)(2,1)S(1)} %copy-done.2), channel_id=1, source_target_pairs={{0,8},{8,16},{16,24},{24,32},{32,40},{40,48},{48,56},{56,64},{64,7... | collective-permute-start | bytes 1572872 | tf_op jit(solution)/shard_map/ppermute | solution.py:294
  67.1 3.4 %collective-permute-start.2 = (bf16[512,512]{1,0:T(8,128)(2,1)S(1)}, bf16[512,512]{1,0:T(8,128)(2,1)S(1)}, u32[]{:S(2)}, u32[]{:S(2)}) collective-permute-start(bf16[512,512]{1,0:T(8,128)(2,1)S(1)} %copy-done.3), channel_id=1, source_target_pairs={{0,8},{8,16},{16,24},{24,32},{32,40},{40,48},{48,56},{56,64},{64,7... | collective-permute-start | bytes 1572872 | tf_op jit(solution)/shard_map/ppermute | solution.py:294
  70.5 58.6 %all_to_all.25.x = bf16[32,16,128]{2,1,0:T(8,128)(2,1)} all-to-all(bf16[32,16,128]{2,1,0:T(8,128)(2,1)S(1)} %bitcast.5), channel_id=1, replica_groups=mesh['seq'=32,'head'=8] {'seq'}, dimensions={0} | all-to-all | bytes 262144 | tf_op jit(solution)/shard_map/all_to_all | solution.py:227
  129.1 1.6 shard_map.93
  130.7 7.7 %all-to-all-start.2 = ((bf16[32,16,128]{2,1,0:T(8,128)(2,1)}), bf16[32,16,128]{2,1,0:T(8,128)(2,1)S(1)}, u32[]{:S(2)}, u32[]{:S(2)}) async-start(bf16[32,16,128]{2,1,0:T(8,128)(2,1)} %shard_map.93), calls=%async_computation.2 | async-start | bytes 262144 | tf_op jit(solution)/shard_map/all_to_all | solution.py:232
  138.6 0.8 copy-done.5
  139.4 0.8 copy-done.6
  140.2 9.2 %shard_map.94 = (bf16[4,512,512]{2,1,0:T(8,128)(2,1)}, bf16[4,512,512]{2,1,0:T(8,128)(2,1)}, bf16[4,512,512]{2,1,0:T(8,128)(2,1)}, f32[512,512]{1,0:T(8,128)}, f32[512,512]{1,0:T(8,128)}) custom-call(s32[1]{0:T(128)} %bitcast.place, bf16[512,512]{1,0:T(8,128)(2,1)} %q.9, bf16[512,512]{1,0:T(8,128)(2,1)} %k.7, bf16[512,512]{1,0:T(8,128)(2,1)} %v.7, ...), custom_call_target="tpu_custom_call" | custom-call | tf_op jit(solution)/shard_map/pallas_call | solution.py:56
  149.4 0.6 copy-done.7
  150.0 4.4 %shard_map.95 = (f32[512,512]{1,0:T(8,128)}, f32[4,1,512]{2,1,0:T(1,128)S(1)}, bf16[512,512]{1,0:T(8,128)(2,1)}, bf16[512,512]{1,0:T(8,128)(2,1)}) custom-call(bf16[512,512]{1,0:T(8,128)(2,1)} %q.9, bf16[4,128,128]{2,1,0:T(8,128)(2,1)} %bitcast.6, f32[512,512]{1,0:T(8,128)} %get-tuple-element.54.window, f32[512,512]{1,0:T(8,128)} %get-tuple-element.55.intra), custom_call_target="tpu_custom_call" | custom-call | tf_op jit(solution)/shard_map/pallas_call | solution.py:56
  154.4 0.6 copy-done.1
  155.1 12.2 %shard_map.96 = (bf16[512,4096]{1,0:T(8,128)(2,1)}, bf16[512,512]{1,0:T(8,128)(2,1)}) custom-call(s32[2]{0:T(128)S(1)} %pad_add_fusion.y.place, bf16[512,4096]{1,0:T(8,128)(2,1)} %all-gather.3.cloned.1.call-done.g, bf16[512,512]{1,0:T(8,128)(2,1)} %get-tuple-element.56.mixed, bf16[8,512,128]{2,1,0:T(8,128)(2,1)} %copy-done.4, ...), custom_call_target="tpu_custom_call" | custom-call | tf_op jit(solution)/shard_map/pallas_call | solution.py:56
  167.3 1.0 copy-done.8
  168.3 0.5 collective-permute-start.10
  168.8 1.5 collective-permute-start.8
  170.3 1.3 collective-permute-start.9
  171.6 4.2 %shard_map.97 = (bf16[512,512]{1,0:T(8,128)(2,1)}, bf16[4,128,128]{2,1,0:T(8,128)(2,1)}) custom-call(bf16[512,512]{1,0:T(8,128)(2,1)} %q.9, bf16[512,512]{1,0:T(8,128)(2,1)} %get-tuple-element.71.g, f32[512,512]{1,0:T(8,128)} %get-tuple-element.64.normed, f32[4,1,512]{2,1,0:T(1,128)} %copy-done.1), custom_call_target="tpu_custom_call" | custom-call | tf_op jit(solution)/shard_map/pallas_call | solution.py:56
  175.8 6.0 %shard_map.98 = (f32[512,512]{1,0:T(8,128)}, bf16[448,512]{1,0:T(8,128)(2,1)}, bf16[448,512]{1,0:T(8,128)(2,1)}, f32[4,1,512]{2,1,0:T(1,128)S(1)}) custom-call(bf16[512,512]{1,0:T(8,128)(2,1)} %q.9, bf16[512,512]{1,0:T(8,128)(2,1)} %get-tuple-element.71.g, bf16[512,512]{1,0:T(8,128)(2,1)} %copy-done.5, bf16[512,512]{1,0:T(8,128)(2,1)} %copy-done.6, ...), custom_call_target="tpu_custom_call" | custom-call | tf_op jit(solution)/shard_map/pallas_call | solution.py:56
  181.8 0.6 copy-done
  182.4 6.7 %collective-permute-start.6 = (bf16[448,512]{1,0:T(8,128)(2,1)}, bf16[448,512]{1,0:T(8,128)(2,1)S(1)}, u32[]{:S(2)}, u32[]{:S(2)}) collective-permute-start(bf16[448,512]{1,0:T(8,128)(2,1)} %get-tuple-element.79), channel_id=1, source_target_pairs={{8,0},{16,8},{24,16},{32,24},{40,32},{48,40},{56,48},{64,56},{72,6... | collective-permute-start | bytes 1376264 | tf_op jit(solution)/shard_map/ppermute | solution.py:294
  189.1 3.4 %collective-permute-start.7 = (bf16[448,512]{1,0:T(8,128)(2,1)}, bf16[448,512]{1,0:T(8,128)(2,1)S(1)}, u32[]{:S(2)}, u32[]{:S(2)}) collective-permute-start(bf16[448,512]{1,0:T(8,128)(2,1)} %get-tuple-element.80), channel_id=1, source_target_pairs={{8,0},{16,8},{24,16},{32,24},{40,32},{48,40},{56,48},{64,56},{72,6... | collective-permute-start | bytes 1376264 | tf_op jit(solution)/shard_map/ppermute | solution.py:294
  192.5 5.3 %all-to-all-start.3 = ((bf16[32,16,128]{2,1,0:T(8,128)(2,1)}), bf16[32,16,128]{2,1,0:T(8,128)(2,1)S(1)}, u32[]{:S(2)}, u32[]{:S(2)}) async-start(bf16[32,16,128]{2,1,0:T(8,128)(2,1)} %bitcast.3), calls=%async_computation.4 | async-start | bytes 262144 | tf_op jit(solution)/shard_map/all_to_all | solution.py:227
  197.8 0.8 copy-done.9
  198.7 0.2 copy-done.11
  198.9 9.4 %shard_map.102 = (bf16[512,128]{1,0:T(8,128)(2,1)}, bf16[512,128]{1,0:T(8,128)(2,1)}, bf16[512,128]{1,0:T(8,128)(2,1)}, bf16[512,128]{1,0:T(8,128)(2,1)}, bf16[5...) custom-call(s32[2]{0:T(128)S(1)} %pad_add_fusion.y.place, ...), custom_call_target="tpu_custom_call" | custom-call | tf_op jit(solution)/shard_map/pallas_call | solution.py:56
  208.3 1.5 collective-permute-start.11
  209.8 2.4 collective-permute-start.12
  212.2 0.7 copy-done.14
  212.8 1.6 shard_map.100
  214.4 21.3 %all-to-all-start.4 = ((bf16[32,16,128]{2,1,0:T(8,128)(2,1)}), bf16[32,16,128]{2,1,0:T(8,128)(2,1)S(1)}, u32[]{:S(2)}, u32[]{:S(2)}) async-start(bf16[32,16,128]{2,1,0:T(8,128)(2,1)} %shard_map.100), calls=%async_computation.5 | async-start | bytes 262144 | tf_op jit(solution)/shard_map/all_to_all | solution.py:232
  235.7 3.3 %collective-permute-start.13 = (bf16[512,128]{1,0:T(8,128)(2,1)}, bf16[512,128]{1,0:T(8,128)(2,1)S(1)}, u32[]{:S(2)}, u32[]{:S(2)}) collective-permute-start(bf16[512,128]{1,0:T(8,128)(2,1)} %get-tuple-element.92), channel_id=1, source_target_pairs={{0,24},{8,32},{16,40},{24,48},{32,56},{40,0},{48,8},{56,16},{64,88... | collective-permute-start | bytes 393224 | tf_op jit(solution)/shard_map/ppermute | solution.py:317
  239.0 2.7 %collective-permute-start.14 = (bf16[512,128]{1,0:T(8,128)(2,1)}, bf16[512,128]{1,0:T(8,128)(2,1)S(1)}, u32[]{:S(2)}, u32[]{:S(2)}) collective-permute-start(bf16[512,128]{1,0:T(8,128)(2,1)} %get-tuple-element.93), channel_id=1, source_target_pairs={{0,32},{8,40},{16,48},{24,56},{32,0},{40,8},{48,16},{56,24},{64,96... | collective-permute-start | bytes 393224 | tf_op jit(solution)/shard_map/ppermute | solution.py:317
  241.7 4.5 %collective-permute-start.15 = (bf16[512,128]{1,0:T(8,128)(2,1)}, bf16[512,128]{1,0:T(8,128)(2,1)S(1)}, u32[]{:S(2)}, u32[]{:S(2)}) collective-permute-start(bf16[512,128]{1,0:T(8,128)(2,1)} %get-tuple-element.94), channel_id=1, source_target_pairs={{0,40},{8,48},{16,56},{24,0},{32,8},{40,16},{48,24},{56,32},{64,10... | collective-permute-start | bytes 393224 | tf_op jit(solution)/shard_map/ppermute | solution.py:317
  246.2 0.6 collective-permute-start.16
  246.8 0.6 collective-permute-start.17
  247.3 8.0 %shard_map.99 = (bf16[512,512]{1,0:T(8,128)(2,1)}, f32[512,512]{1,0:T(8,128)}, f32[512,512]{1,0:T(8,128)}) custom-call(bf16[512,512]{1,0:T(8,128)(2,1)} %q.9, bf16[512,512]{1,0:T(8,128)(2,1)} %k.7, bf16[512,512]{1,0:T(8,128)(2,1)} %v.7, bf16[512,512]{1,0:T(8,128)(2,1)} %get-tuple-element.71.g, bf16[512,512]{1,0:T(8,128)(2,1)} %get-tuple-element.66.gl, ...), custom_call_target="tpu_custom_call" | custom-call | tf_op jit(solution)/shard_map/pallas_call | solution.py:56
  255.4 0.6 copy-done.12
  256.0 4.4 %shard_map.101 = (bf16[512,512]{1,0:T(8,128)(2,1)}, bf16[512,512]{1,0:T(8,128)(2,1)}) custom-call(bf16[512,512]{1,0:T(8,128)(2,1)} %k.7, bf16[512,512]{1,0:T(8,128)(2,1)} %v.7, bf16[4,128,128]{2,1,0:T(8,128)(2,1)} %bitcast.8, f32[512,512]{1,0:T(8,128)} %get-tuple-element.77.dk, f32[512,512]{1,0:T(8,128)} %get-tuple-element.78.dv, ...), custom_call_target="tpu_custom_call" | custom-call | tf_op jit(solution)/shard_map/pallas_call | solution.py:56
  260.4 0.8 add_multiply_fusion
  (56 shorter events, 0.5 us)
Async XLA Ops:
  7.2 56.4 %copy-start.2 = (bf16[512,512]{1,0:T(8,128)(2,1)S(1)}, bf16[512,512]{1,0:T(8,128)(2,1)}, u32[]{:S(2)}) copy-start(bf16[512,512]{1,0:T(8,128)(2,1)} %k.7) | copy-start | bytes 1572868
  7.2 59.9 %copy-start.3 = (bf16[512,512]{1,0:T(8,128)(2,1)S(1)}, bf16[512,512]{1,0:T(8,128)(2,1)}, u32[]{:S(2)}) copy-start(bf16[512,512]{1,0:T(8,128)(2,1)} %v.7) | copy-start | bytes 1572868
  7.2 147.9 %all-gather.3.cloned.1.call-start = ((), (), s32[]{:S(2)}) async-start(), calls=%async_computation.6 | async-start | bytes 4718592 | tf_op jit(solution)/shard_map/all_gather | solution.py:348
  10.0 38.2 %all-to-all-start = ((bf16[8,512,128]{2,1,0:T(8,128)(2,1)}), bf16[8,512,128]{2,1,0:T(8,128)(2,1)S(1)}, u32[]{:S(2)}, u32[]{:S(2)}) async-start(bf16[8,512,128]{2,1,0:T(8,128)(2,1)} %broadcast_in_dim.2), calls=%async_computation | async-start | bytes 2097152 | tf_op jit(solution)/shard_map/all_to_all | solution.py:302
  18.5 179.4 %all-gather.5.cloned.1.call-start = ((), (), s32[]{:S(2)}) async-start(), calls=%async_computation.8 | async-start | bytes 4718592 | tf_op jit(solution)/shard_map/all_gather | solution.py:355
  18.5 29.7 %collective-permute-start = (bf16[512,512]{1,0:T(8,128)(2,1)}, bf16[512,512]{1,0:T(8,128)(2,1)S(1)}, u32[]{:S(2)}, u32[]{:S(2)}) collective-permute-start(bf16[512,512]{1,0:T(8,128)(2,1)} %param.9), channel_id=1, source_target_pairs={{0,0},{1,1},{2,64},{3,65},{4,128},{5,129},{6,192},{7,193},{8,8},{9... | collective-permute-start | bytes 1572872 | tf_op jit(solution)/shard_map/ppermute | solution.py:330
  48.2 0.8 copy-start.13
  48.2 106.9 %copy-start.4 = (bf16[8,512,128]{2,1,0:T(8,128)(2,1)}, bf16[8,512,128]{2,1,0:T(8,128)(2,1)S(1)}, u32[]{:S(2)}) copy-start(bf16[8,512,128]{2,1,0:T(8,128)(2,1)S(1)} %all-to-all-done.refs_0_) | copy-start | bytes 3145732
  49.0 106.0 %collective-permute-start.3 = (bf16[8,512,128]{2,1,0:T(8,128)(2,1)S(1)}, bf16[8,512,128]{2,1,0:T(8,128)(2,1)}, u32[]{:S(2)}, u32[]{:S(2)}) collective-permute-start(bf16[8,512,128]{2,1,0:T(8,128)(2,1)S(1)} %all-to-all-done.refs_0_), channel_id=1, source_target_pairs={{0,64},{8,72},{16,80},{24,88},{32,96},{40,104},{48,112},{56,120},{... | collective-permute-start | bytes 3145736 | tf_op jit(solution)/shard_map/ppermute | solution.py:311
  62.0 93.1 %collective-permute-start.4 = (bf16[8,512,128]{2,1,0:T(8,128)(2,1)S(1)}, bf16[8,512,128]{2,1,0:T(8,128)(2,1)}, u32[]{:S(2)}, u32[]{:S(2)}) collective-permute-start(bf16[8,512,128]{2,1,0:T(8,128)(2,1)S(1)} %all-to-all-done.refs_0_), channel_id=1, source_target_pairs={{0,128},{8,136},{16,144},{24,152},{32,160},{40,168},{48,176},{56,1... | collective-permute-start | bytes 3145736 | tf_op jit(solution)/shard_map/ppermute | solution.py:311
  62.0 93.1 %collective-permute-start.5 = (bf16[8,512,128]{2,1,0:T(8,128)(2,1)S(1)}, bf16[8,512,128]{2,1,0:T(8,128)(2,1)}, u32[]{:S(2)}, u32[]{:S(2)}) collective-permute-start(bf16[8,512,128]{2,1,0:T(8,128)(2,1)S(1)} %all-to-all-done.refs_0_), channel_id=1, source_target_pairs={{0,192},{8,200},{16,208},{24,216},{32,224},{40,232},{48,240},{56,2... | collective-permute-start | bytes 3145736 | tf_op jit(solution)/shard_map/ppermute | solution.py:311
  63.5 75.1 %collective-permute-start.1 = (bf16[512,512]{1,0:T(8,128)(2,1)S(1)}, bf16[512,512]{1,0:T(8,128)(2,1)S(1)}, u32[]{:S(2)}, u32[]{:S(2)}) collective-permute-start(bf16[512,512]{1,0:T(8,128)(2,1)S(1)} %copy-done.2), channel_id=1, source_target_pairs={{0,8},{8,16},{16,24},{24,32},{32,40},{40,48},{48,56},{56,64},{64,7... | collective-permute-start | bytes 1572872 | tf_op jit(solution)/shard_map/ppermute | solution.py:294
  67.1 71.5 %collective-permute-start.2 = (bf16[512,512]{1,0:T(8,128)(2,1)S(1)}, bf16[512,512]{1,0:T(8,128)(2,1)S(1)}, u32[]{:S(2)}, u32[]{:S(2)}) collective-permute-start(bf16[512,512]{1,0:T(8,128)(2,1)S(1)} %copy-done.3), channel_id=1, source_target_pairs={{0,8},{8,16},{16,24},{24,32},{32,40},{40,48},{48,56},{56,64},{64,7... | collective-permute-start | bytes 1572872 | tf_op jit(solution)/shard_map/ppermute | solution.py:294
  130.7 18.7 %all-to-all-start.2 = ((bf16[32,16,128]{2,1,0:T(8,128)(2,1)}), bf16[32,16,128]{2,1,0:T(8,128)(2,1)S(1)}, u32[]{:S(2)}, u32[]{:S(2)}) async-start(bf16[32,16,128]{2,1,0:T(8,128)(2,1)} %shard_map.93), calls=%async_computation.2 | async-start | bytes 262144 | tf_op jit(solution)/shard_map/all_to_all | solution.py:232
  138.4 122.9 %reduce-scatter.2.cloned.1.call-start = ((), (), s32[]{:S(2)}) async-start(), calls=%async_computation.7 | async-start | bytes 4718592 | tf_op jit(solution)/shard_map/reduce_scatter | solution.py:403
  138.6 0.8 copy-start.5
  139.4 0.8 copy-start.6
  149.4 0.7 copy-start.7
  154.4 0.6 copy-start.1
  167.2 1.0 copy-start.8
  168.3 29.5 %collective-permute-start.10 = (bf16[512,512]{1,0:T(8,128)(2,1)S(1)}, bf16[512,512]{1,0:T(8,128)(2,1)S(1)}, u32[]{:S(2)}, u32[]{:S(2)}) collective-permute-start(bf16[512,512]{1,0:T(8,128)(2,1)S(1)} %copy-done.8), channel_id=1, source_target_pairs={{0,192},{8,200},{16,208},{24,216},{32,224},{40,232},{48,240},{56,2... | collective-permute-start | bytes 1572872 | tf_op jit(solution)/shard_map/ppermute | solution.py:311
  168.8 29.0 %collective-permute-start.8 = (bf16[512,512]{1,0:T(8,128)(2,1)S(1)}, bf16[512,512]{1,0:T(8,128)(2,1)S(1)}, u32[]{:S(2)}, u32[]{:S(2)}) collective-permute-start(bf16[512,512]{1,0:T(8,128)(2,1)S(1)} %copy-done.8), channel_id=1, source_target_pairs={{0,64},{8,72},{16,80},{24,88},{32,96},{40,104},{48,112},{56,120},{... | collective-permute-start | bytes 1572872 | tf_op jit(solution)/shard_map/ppermute | solution.py:311
  170.3 27.5 %collective-permute-start.9 = (bf16[512,512]{1,0:T(8,128)(2,1)S(1)}, bf16[512,512]{1,0:T(8,128)(2,1)S(1)}, u32[]{:S(2)}, u32[]{:S(2)}) collective-permute-start(bf16[512,512]{1,0:T(8,128)(2,1)S(1)} %copy-done.8), channel_id=1, source_target_pairs={{0,128},{8,136},{16,144},{24,152},{32,160},{40,168},{48,176},{56,1... | collective-permute-start | bytes 1572872 | tf_op jit(solution)/shard_map/ppermute | solution.py:311
  181.8 0.6 copy-start
  182.4 56.6 %collective-permute-start.6 = (bf16[448,512]{1,0:T(8,128)(2,1)}, bf16[448,512]{1,0:T(8,128)(2,1)S(1)}, u32[]{:S(2)}, u32[]{:S(2)}) collective-permute-start(bf16[448,512]{1,0:T(8,128)(2,1)} %get-tuple-element.79), channel_id=1, source_target_pairs={{8,0},{16,8},{24,16},{32,24},{40,32},{48,40},{56,48},{64,56},{72,6... | collective-permute-start | bytes 1376264 | tf_op jit(solution)/shard_map/ppermute | solution.py:294
  189.1 52.6 %collective-permute-start.7 = (bf16[448,512]{1,0:T(8,128)(2,1)}, bf16[448,512]{1,0:T(8,128)(2,1)S(1)}, u32[]{:S(2)}, u32[]{:S(2)}) collective-permute-start(bf16[448,512]{1,0:T(8,128)(2,1)} %get-tuple-element.80), channel_id=1, source_target_pairs={{8,0},{16,8},{24,16},{32,24},{40,32},{48,40},{56,48},{64,56},{72,6... | collective-permute-start | bytes 1376264 | tf_op jit(solution)/shard_map/ppermute | solution.py:294
  192.5 19.7 %all-to-all-start.3 = ((bf16[32,16,128]{2,1,0:T(8,128)(2,1)}), bf16[32,16,128]{2,1,0:T(8,128)(2,1)S(1)}, u32[]{:S(2)}, u32[]{:S(2)}) async-start(bf16[32,16,128]{2,1,0:T(8,128)(2,1)} %bitcast.3), calls=%async_computation.4 | async-start | bytes 262144 | tf_op jit(solution)/shard_map/all_to_all | solution.py:227
  197.8 0.8 copy-start.9
  197.8 0.9 copy-start.10
  197.8 1.1 copy-start.11
  208.3 37.8 %collective-permute-start.11 = (bf16[512,128]{1,0:T(8,128)(2,1)}, bf16[512,128]{1,0:T(8,128)(2,1)S(1)}, u32[]{:S(2)}, u32[]{:S(2)}) collective-permute-start(bf16[512,128]{1,0:T(8,128)(2,1)} %get-tuple-element.90), channel_id=1, source_target_pairs={{0,8},{8,16},{16,24},{24,32},{32,40},{40,48},{48,56},{56,0},{64,72... | collective-permute-start | bytes 393224 | tf_op jit(solution)/shard_map/ppermute | solution.py:317
  209.8 36.9 %collective-permute-start.12 = (bf16[512,128]{1,0:T(8,128)(2,1)}, bf16[512,128]{1,0:T(8,128)(2,1)S(1)}, u32[]{:S(2)}, u32[]{:S(2)}) collective-permute-start(bf16[512,128]{1,0:T(8,128)(2,1)} %get-tuple-element.91), channel_id=1, source_target_pairs={{0,16},{8,24},{16,32},{24,40},{32,48},{40,56},{48,0},{56,8},{64,80... | collective-permute-start | bytes 393224 | tf_op jit(solution)/shard_map/ppermute | solution.py:317
  212.2 0.7 copy-start.14
  214.4 40.9 %all-to-all-start.4 = ((bf16[32,16,128]{2,1,0:T(8,128)(2,1)}), bf16[32,16,128]{2,1,0:T(8,128)(2,1)S(1)}, u32[]{:S(2)}, u32[]{:S(2)}) async-start(bf16[32,16,128]{2,1,0:T(8,128)(2,1)} %shard_map.100), calls=%async_computation.5 | async-start | bytes 262144 | tf_op jit(solution)/shard_map/all_to_all | solution.py:232
  235.7 24.7 %collective-permute-start.13 = (bf16[512,128]{1,0:T(8,128)(2,1)}, bf16[512,128]{1,0:T(8,128)(2,1)S(1)}, u32[]{:S(2)}, u32[]{:S(2)}) collective-permute-start(bf16[512,128]{1,0:T(8,128)(2,1)} %get-tuple-element.92), channel_id=1, source_target_pairs={{0,24},{8,32},{16,40},{24,48},{32,56},{40,0},{48,8},{56,16},{64,88... | collective-permute-start | bytes 393224 | tf_op jit(solution)/shard_map/ppermute | solution.py:317
  239.0 16.3 %copy-start.15 = (bf16[448,512]{1,0:T(8,128)(2,1)}, bf16[448,512]{1,0:T(8,128)(2,1)S(1)}, u32[]{:S(2)}) copy-start(bf16[448,512]{1,0:T(8,128)(2,1)S(1)} %collective-permute-done.6.rk) | copy-start | bytes 1376260
  239.0 21.4 %collective-permute-start.14 = (bf16[512,128]{1,0:T(8,128)(2,1)}, bf16[512,128]{1,0:T(8,128)(2,1)S(1)}, u32[]{:S(2)}, u32[]{:S(2)}) collective-permute-start(bf16[512,128]{1,0:T(8,128)(2,1)} %get-tuple-element.93), channel_id=1, source_target_pairs={{0,32},{8,40},{16,48},{24,56},{32,0},{40,8},{48,16},{56,24},{64,96... | collective-permute-start | bytes 393224 | tf_op jit(solution)/shard_map/ppermute | solution.py:317
  241.7 13.6 %copy-start.16 = (bf16[448,512]{1,0:T(8,128)(2,1)}, bf16[448,512]{1,0:T(8,128)(2,1)S(1)}, u32[]{:S(2)}) copy-start(bf16[448,512]{1,0:T(8,128)(2,1)S(1)} %collective-permute-done.7.rv) | copy-start | bytes 1376260
  241.7 18.7 %collective-permute-start.15 = (bf16[512,128]{1,0:T(8,128)(2,1)}, bf16[512,128]{1,0:T(8,128)(2,1)S(1)}, u32[]{:S(2)}, u32[]{:S(2)}) collective-permute-start(bf16[512,128]{1,0:T(8,128)(2,1)} %get-tuple-element.94), channel_id=1, source_target_pairs={{0,40},{8,48},{16,56},{24,0},{32,8},{40,16},{48,24},{56,32},{64,10... | collective-permute-start | bytes 393224 | tf_op jit(solution)/shard_map/ppermute | solution.py:317
  246.2 14.2 %collective-permute-start.16 = (bf16[512,128]{1,0:T(8,128)(2,1)}, bf16[512,128]{1,0:T(8,128)(2,1)S(1)}, u32[]{:S(2)}, u32[]{:S(2)}) collective-permute-start(bf16[512,128]{1,0:T(8,128)(2,1)} %get-tuple-element.95), channel_id=1, source_target_pairs={{0,48},{8,56},{16,0},{24,8},{32,16},{40,24},{48,32},{56,40},{64,11... | collective-permute-start | bytes 393224 | tf_op jit(solution)/shard_map/ppermute | solution.py:317
  246.8 13.7 %collective-permute-start.17 = (bf16[512,128]{1,0:T(8,128)(2,1)}, bf16[512,128]{1,0:T(8,128)(2,1)S(1)}, u32[]{:S(2)}, u32[]{:S(2)}) collective-permute-start(bf16[512,128]{1,0:T(8,128)(2,1)} %get-tuple-element.96), channel_id=1, source_target_pairs={{0,56},{8,0},{16,8},{24,16},{32,24},{40,32},{48,40},{56,48},{64,12... | collective-permute-start | bytes 393224 | tf_op jit(solution)/shard_map/ppermute | solution.py:317
  247.3 13.1 %copy-start.17 = (bf16[512,128]{1,0:T(8,128)(2,1)S(1)}, bf16[512,128]{1,0:T(8,128)(2,1)}, u32[]{:S(2)}) copy-start(bf16[512,128]{1,0:T(8,128)(2,1)} %get-tuple-element.89) | copy-start | bytes 393220
  255.3 0.7 copy-start.12
Sparse Core Ops, SparseCore 0:
  9.9 48.0 all-gather.2
  59.8 41.9 all-gather.4
  167.4 39.0 reduce-scatter.1

commit v5 on v4

--- a/solution.py
+++ b/solution.py
@@ -221,45 +221,49 @@
         total = total + x[at].astype(F32)
 
 
-def carry_states(local, backward):
+def carry_states(local, backward, beside=(), between=()):
     count = lax.axis_size("seq")
     pieces = local.reshape(count, -1, DH)
     met = lax.all_to_all(pieces, "seq", 0, 0)
+    met, between = lax.optimization_barrier((met, between))
     done = pl.pallas_call(
         functools.partial(scan_kernel, backward),
         out_shape=jax.ShapeDtypeStruct(met.shape, BF16),
     )(met)
-    return lax.all_to_all(done, "seq", 0, 0).reshape(local.shape)
-
-
-def project_kernel(y, g, mixed, *refs):
-    sources, (partial_value, out, acc, w) = refs[:YS], refs[YS:]
-    block = pl.program_id(0)
-    count = sources[0].shape[0] // 2
-    slot = (y[0] + YS - block // 2) % YS
-
-    @pl.when(block == 0)
+    done, beside = lax.optimization_barrier((done, beside))
+    return lax.all_to_all(done, "seq", 0, 0).reshape(local.shape), beside, between
+
+
+def block_id(t, head):
+    x = (head[0] // 2 + XS - t % XS) % XS
+    core = jnp.where(t < XS, head[0] % 2, 1 - head[0] % 2)
+    return 2 * x + core
+
+
+def project_kernel(head, mixed, w, *refs):
+    blocks, (partial_value, out, acc) = refs[:-3], refs[-3:]
+    t = pl.program_id(0)
+
+    @pl.when(t == 0)
     def _():
         acc[...] = jnp.zeros_like(acc)
 
-    for r, source in enumerate(sources):
-
-        @pl.when(slot == r)
-        def _(source=source):
-            for i in range(count):
-                w[:, i * DH : (i + 1) * DH] = source[block % 2 * count + i]
-
     partial_value[...] = nn(mixed[...], w[...]).astype(BF16)
-    acc[...] += nt(g[...], w[...])
-
-    @pl.when(block == 2 * XS - 1)
+    for j, block in enumerate(blocks):
+
+        @pl.when(t == j)
+        def _(block=block):
+            acc[...] += nt(block[...], w[...])
+
+    @pl.when(t == len(blocks) - 1)
     def _():
         out[...] = acc[...].astype(BF16)
 
 
-def sens_kernel(place, g, *refs):
+def sens_kernel(place, mine, other, *refs):
     sources, outs, acc = refs[:YS], refs[YS:-1], refs[-1]
-    half, turn = pl.program_id(0), pl.program_id(1)
+    side, turn = pl.program_id(0), pl.program_id(1)
+    half = jnp.where(side == 0, place[2], 1 - place[2])
 
     @pl.when(turn == 0)
     def _():
@@ -267,9 +271,13 @@
 
     for r, source in enumerate(sources):
 
-        @pl.when(turn == r)
+        @pl.when((turn == r) & (side == 0))
         def _(source=source):
-            acc[...] += nn(source[...], g[...])
+            acc[...] += nn(source[...], mine[0])
+
+        @pl.when((turn == r) & (side == 1))
+        def _(source=source):
+            acc[...] += nn(source[...], other[0])
 
     @pl.when(turn == YS - 1)
     def _():
@@ -311,6 +319,19 @@
     return lax.ppermute(
         shard, "seq", [(y * ZS + z, (y + by) % YS * ZS + z) for y in range(YS) for z in range(ZS)]
     )
+
+
+X_GROUPS = [[2 * x + c for x in range(XS)] for c in range(2)]
+
+
+def hop_x(shard, by):
+    return lax.ppermute(
+        shard, "head", [(x * 2 + c, (x + by) % XS * 2 + c) for x in range(XS) for c in range(2)]
+    )
+
+
+def swap_core(shard):
+    return lax.ppermute(shard, "head", [(i, i ^ 1) for i in range(2 * XS)])
 
 
 def hop_z(shard, by):
@@ -343,19 +364,21 @@
     line = heads_of(1, rows)
     mm = 2 * rows * rows * width
 
-    place = jnp.concatenate([seq // ZS, seq % ZS])
-
-    grad_full = lax.all_gather(grad_y, "head", axis=1, tiled=True)
-    turned_grad = turn_xy(grad_y)
-    w_row = spread(w_out, "seq", Z_GROUPS)
+    head = lax.axis_index("head").reshape(1).astype(jnp.int32)
+    place = jnp.concatenate([seq // ZS, seq % ZS, head % 2])
+
+    full_w = lax.all_gather(w_out, "seq", axis=1, tiled=True)
+    hopped = [hop_x(grad_y, by) for by in range(1, XS)]
     local = call(
         sums_kernel, heads, [col, col], st, shape((heads, DH, DH), BF16), flops=2 * mm // 4
     )(keys, values)
-    local, w_row, turned_grad = lax.optimization_barrier((local, w_row, turned_grad))
-    grad_wide = lax.all_gather(turned_grad, "head", axis=1, tiled=True)
-    w_rows = [w_row] + [hop_y(w_row, by) for by in range(1, YS)]
-    kh, vh = shifted(keys, 1), shifted(values, 1)
-    before = carry_states(local, False)
+    before, _, sent = carry_states(local, False, (), (keys, values, grad_y))
+    kh, vh, turned_grad = shifted(sent[0], 1), shifted(sent[1], 1), turn_xy(sent[2])
+    before, kh, vh, hopped, turned_grad = lax.optimization_barrier(
+        (before, kh, vh, hopped, turned_grad)
+    )
+    grads = [grad_y] + hopped
+    grads = grads + [swap_core(g) for g in grads]
 
     sq = large((heads, rows, rows), BF16)
     flat_t = large((width, rows), F32)
@@ -387,19 +410,22 @@
         size=5 << 20,
     )(queries, before, window, intra)
 
-    w_rows, before = lax.optimization_barrier((w_rows, before))
+    turned_grad, mixed_t = lax.optimization_barrier((turned_grad, mixed_t))
+    mine = spread(turned_grad, "head", X_GROUPS)
     across_y = [mixed_t] + [hop_y(mixed_t, by) for by in range(1, YS)]
+    mine, across_y, full_w = lax.optimization_barrier((mine, across_y, full_w))
+    other = swap_core(mine)
     fixed = pl.BlockSpec((rows, width), lambda *_: (0, 0))
-    by_block = pl.BlockSpec((rows, width), lambda b, *_: (0, b))
+    by_block = pl.BlockSpec((rows, width), lambda t, head: (0, block_id(t, head)))
     partial_value, grad_mixed = call(
         project_kernel,
         2 * XS,
-        [by_block, fixed] + [pl.BlockSpec((ZS, rows, DH), lambda *_: (0, 0, 0))] * YS,
+        [fixed, by_block] + [fixed] * (2 * XS),
         [by_block, fixed],
         [large((rows, 2 * XS * width), BF16), large((rows, width), BF16)],
-        scratch=[pltpu.VMEM((rows, width), F32), pltpu.VMEM((rows, width), BF16)],
+        scratch=[pltpu.VMEM((rows, width), F32)],
         prefetch=1,
-    )(place, grad_full, mixed, *w_rows)
+    )(head, mixed, full_w, *grads)
     mixer_result = lax.psum_scatter(partial_value, "head", scatter_dimension=1, tiled=True)
 
     grad_lin, local_back = call(
@@ -425,23 +451,34 @@
     )(queries, g_far, kh, vh, far, window)
     back_k, back_v = shifted(far_k, -1), shifted(far_v, -1)
 
-    later = carry_states(local_back, True)
-
-    across_y, local_back = lax.optimization_barrier((across_y, local_back))
+    later, grad_lin, _ = carry_states(local_back, True, grad_lin)
+
+    across_y, mine, other, local_back = lax.optimization_barrier(
+        (across_y, mine, other, local_back)
+    )
     parts = call(
         sens_kernel,
         (2, YS),
         [
             pl.BlockSpec(
-                (rows, width), lambda c, by, place: (0, (place[0] + YS - by) % YS * 2 + c)
-            )
+                (1, rows, width),
+                lambda s, by, place: (
+                    jnp.where(s == 0, (place[0] + YS - by) % YS, (place[0] + 1) % YS), 0, 0
+                ),
+            ),
+            pl.BlockSpec(
+                (1, rows, width),
+                lambda s, by, place: (
+                    jnp.where(s == 1, (place[0] + YS - by) % YS, place[0] % YS), 0, 0
+                ),
+            ),
         ]
         + [fixed] * YS,
         [pl.BlockSpec((width, DH), lambda *_: (0, 0))] * ZS,
         [large((width, DH), BF16)] * ZS,
         scratch=[pltpu.VMEM((width, rows), F32)],
         prefetch=1,
-    )(place, grad_wide, *across_y)
+    )(place, mine, other, *across_y)
     total = parts[0].astype(F32)
     for by in range(1, ZS):
         total = total + hop_z(parts[by], by).astype(F32)

time: 269 us -> 239 us (0.89)
  blocking collectives: 58.6 us -> 0 us
  waiting for transfers between devices: 23 us -> 71.1 us
  starting transfers between devices: 97.8 us -> 78.2 us
  local copies, waits for them, and re-layouts: 9.67 us -> 5.84 us
    all_to_all x1 -> x0, blocking collectives: 58.6 us -> none  [carry_states(): met = lax.all_to_all(pieces, 'seq', 0, 0)]
    all_to_all x2, waiting for transfers between devices: 0.01 us -> 38.2 us  [carry_states(): lax.all_to_all(done, 'seq', 0, 0).reshape(local.shape)]
    ppermute x1, waiting for transfers between devices: 22.2 us -> 0.01 us  [turn_xy(): return lax.ppermute(shard, ('seq', 'head'), pairs)]
    ppermute x6 -> x3, waiting for transfers between devices: 0.02 us -> 17.8 us  [hop_y(): lax.ppermute(shard, 'seq', [(y * ZS + z, (y + by) % YS * ZS + z) for y in...]
    all_to_all x1 -> x2, starting transfers between devices: 5.26 us -> 22.8 us  [carry_states(): met = lax.all_to_all(pieces, 'seq', 0, 0)]
    all_to_all x2, starting transfers between devices: 29 us -> 14 us  [carry_states(): lax.all_to_all(done, 'seq', 0, 0).reshape(local.shape)]
    ppermute x6 -> x3, starting transfers between devices: 17.8 us -> 3.55 us  [hop_y(): lax.ppermute(shard, 'seq', [(y * ZS + z, (y + by) % YS * ZS + z) for y in...]
    all_to_all x1 -> x2, waiting for transfers between devices: 0.01 us -> 10.1 us  [carry_states(): met = lax.all_to_all(pieces, 'seq', 0, 0)]
  transfers between devices with their start and end apart: 25 -> 30, of which waited for: 1 -> 8; matrix products, arithmetic and copies ran while one was open for 1% -> 1% of each run, Pallas kernels for 24% -> 22%
where the time goes in v5:
time: 239 us; the launch traced here: 237 us
  starting transfers between devices  78.2 us (33%)
  waiting for transfers between devices  71.1 us (30%)
  Pallas kernels  66 us (28%)
  between operations  14.4 us (6%)
  local copies, waits for them, and re-layouts  5.84 us (2%)
    pallas_call x9, Pallas kernels, call(): run(*args[:prefetch], *(kept(a) for a in args[prefetch:]))  62.8 us
    all_to_all x2, waiting for transfers between devices, carry_states(): lax.all_to_all(done, 'seq', 0, 0).reshape(local.shape)  38.2 us
    all_to_all x2, starting transfers between devices, carry_states(): met = lax.all_to_all(pieces, 'seq', 0, 0)  22.8 us
    ppermute x3, waiting for transfers between devices, hop_y(): lax.ppermute(shard, 'seq', [(y * ZS + z, (y + by) % YS * ZS + z) for y in...  17.8 us
    ppermute x7, starting transfers between devices, hop_z(): lax.ppermute(shard, 'seq', [(y * ZS + z, y * ZS + (z + by) % ZS) for y in...  15.5 us
    all_to_all x2, starting transfers between devices, carry_states(): lax.all_to_all(done, 'seq', 0, 0).reshape(local.shape)  14 us
    all_to_all x2, waiting for transfers between devices, carry_states(): met = lax.all_to_all(pieces, 'seq', 0, 0)  10.1 us
    ppermute x4, starting transfers between devices, shifted(): return lax.ppermute(shard, 'seq', pairs)  9.38 us
  transfers between devices with their start and end apart: 30, of which 8 were waited for; matrix products, arithmetic and copies ran while one was open for 1% of the time, Pallas kernels for 22%

profile of v5, /device:TPU:16, one launch (start us, length us, event | category | flops | bytes accessed | tf_op | source)
XLA Modules:
  0.0 236.5 jit_solution(11768363618178626642)
XLA Ops:
  7.2 0.7 all-gather.2.cloned.1.call-update
  7.9 2.8 %collective-permute-start.4 = (bf16[512,512]{1,0:T(8,128)(2,1)}, bf16[512,512]{1,0:T(8,128)(2,1)S(1)}, u32[]{:S(2)}, u32[]{:S(2)}) collective-permute-start(bf16[512,512]{1,0:T(8,128)(2,1)} %refs_0_.1), channel_id=1, source_target_pairs={{0,6},{1,7},{2,0},{3,1},{4,2},{5,3},{6,4},{7,5},{8,14},{9,15},{10,... | collective-permute-start | bytes 1572872 | tf_op jit(solution)/shard_map/ppermute | solution.py:328
  10.7 3.7 %shard_map.92 = bf16[4,128,128]{2,1,0:T(8,128)(2,1)} custom-call(bf16[512,512]{1,0:T(8,128)(2,1)} %k.7, bf16[512,512]{1,0:T(8,128)(2,1)} %v.7), custom_call_target="tpu_custom_call" | custom-call | tf_op jit(solution)/shard_map/pallas_call | solution.py:56
  14.4 11.6 %all-to-all-start = ((bf16[32,16,128]{2,1,0:T(8,128)(2,1)}), bf16[32,16,128]{2,1,0:T(8,128)(2,1)S(1)}, u32[]{:S(2)}, u32[]{:S(2)}) async-start(bf16[32,16,128]{2,1,0:T(8,128)(2,1)} %bitcast.1), calls=%async_computation | async-start | bytes 262144 | tf_op jit(solution)/shard_map/all_to_all | solution.py:227
  26.0 0.9 collective-permute-start.3
  26.9 0.9 collective-permute-start.2
  27.8 7.1 %all-to-all-done.x = bf16[32,16,128]{2,1,0:T(8,128)(2,1)S(1)} async-done(((bf16[32,16,128]{2,1,0:T(8,128)(2,1)}), bf16[32,16,128]{2,1,0:T(8,128)(2,1)S(1)}, u32[]{:S(2)}, u32[]{:S(2)}) %all-to-all-start) | async-done | bytes 131104 | tf_op jit(solution)/shard_map/all_to_all | solution.py:227
  34.8 3.0 %collective-permute-start = (bf16[512,512]{1,0:T(8,128)(2,1)}, bf16[512,512]{1,0:T(8,128)(2,1)S(1)}, u32[]{:S(2)}, u32[]{:S(2)}) collective-permute-start(bf16[512,512]{1,0:T(8,128)(2,1)} %k.7), channel_id=1, source_target_pairs={{0,8},{8,16},{16,24},{24,32},{32,40},{40,48},{48,56},{56,64},{64,7... | collective-permute-start | bytes 1572872 | tf_op jit(solution)/shard_map/ppermute | solution.py:302
  37.8 2.6 %collective-permute-start.1 = (bf16[512,512]{1,0:T(8,128)(2,1)}, bf16[512,512]{1,0:T(8,128)(2,1)S(1)}, u32[]{:S(2)}, u32[]{:S(2)}) collective-permute-start(bf16[512,512]{1,0:T(8,128)(2,1)} %v.7), channel_id=1, source_target_pairs={{0,8},{8,16},{16,24},{24,32},{32,40},{40,48},{48,56},{56,64},{64,7... | collective-permute-start | bytes 1572872 | tf_op jit(solution)/shard_map/ppermute | solution.py:302
  40.4 4.1 %collective-permute-start.5 = (bf16[512,512]{1,0:T(8,128)(2,1)}, bf16[512,512]{1,0:T(8,128)(2,1)S(1)}, u32[]{:S(2)}, u32[]{:S(2)}) collective-permute-start(bf16[512,512]{1,0:T(8,128)(2,1)} %refs_0_.1), channel_id=1, source_target_pairs={{0,0},{1,1},{2,64},{3,65},{4,128},{5,129},{6,192},{7,193},{8,8},{9... | collective-permute-start | bytes 1572872 | tf_op jit(solution)/shard_map/ppermute | solution.py:351
  44.5 1.6 shard_map.93
  46.1 7.3 %all-to-all-start.1 = ((bf16[32,16,128]{2,1,0:T(8,128)(2,1)}), bf16[32,16,128]{2,1,0:T(8,128)(2,1)S(1)}, u32[]{:S(2)}, u32[]{:S(2)}) async-start(bf16[32,16,128]{2,1,0:T(8,128)(2,1)} %shard_map.93), calls=%async_computation.1 | async-start | bytes 262144 | tf_op jit(solution)/shard_map/all_to_all | solution.py:234
  53.4 38.2 %all-to-all-done.1 = bf16[32,16,128]{2,1,0:T(8,128)(2,1)S(1)} async-done(((bf16[32,16,128]{2,1,0:T(8,128)(2,1)}), bf16[32,16,128]{2,1,0:T(8,128)(2,1)S(1)}, u32[]{:S(2)}, u32[]{:S(2)}) %all-to-all-start.1) | async-done | bytes 131104 | tf_op jit(solution)/shard_map/all_to_all | solution.py:234
  91.6 0.8 copy-done.3
  92.6 9.3 %shard_map.94 = (bf16[4,512,512]{2,1,0:T(8,128)(2,1)}, bf16[4,512,512]{2,1,0:T(8,128)(2,1)}, bf16[4,512,512]{2,1,0:T(8,128)(2,1)}, f32[512,512]{1,0:T(8,128)}, f32[512,512]{1,0:T(8,128)}) custom-call(s32[1]{0:T(128)} %bitcast.3.place, bf16[512,512]{1,0:T(8,128)(2,1)} %q.9, bf16[512,512]{1,0:T(8,128)(2,1)} %k.7, bf16[512,512]{1,0:T(8,128)(2,1)} %v.7, ...), custom_call_target="tpu_custom_call" | custom-call | tf_op jit(solution)/shard_map/pallas_call | solution.py:56
  101.9 4.4 %shard_map.95 = (f32[512,512]{1,0:T(8,128)}, f32[4,1,512]{2,1,0:T(1,128)S(1)}, bf16[512,512]{1,0:T(8,128)(2,1)}, bf16[512,512]{1,0:T(8,128)(2,1)}) custom-call(bf16[512,512]{1,0:T(8,128)(2,1)} %q.9, bf16[4,128,128]{2,1,0:T(8,128)(2,1)} %bitcast.6, f32[512,512]{1,0:T(8,128)} %get-tuple-element.75.window, f32[512,512]{1,0:T(8,128)} %get-tuple-element.76.intra), custom_call_target="tpu_custom_call" | custom-call | tf_op jit(solution)/shard_map/pallas_call | solution.py:56
  106.3 0.6 copy-done.1
  106.9 1.5 broadcast_in_dim.2
  108.4 3.7 %all-to-all-start.2 = ((bf16[4,512,512]{2,1,0:T(8,128)(2,1)}), bf16[4,512,512]{2,1,0:T(8,128)(2,1)S(1)}, u32[]{:S(2)}, u32[]{:S(2)}) async-start(bf16[4,512,512]{2,1,0:T(8,128)(2,1)} %broadcast_in_dim.2), calls=%async_computation.2 | async-start | bytes 4194304 | tf_op jit(solution)/shard_map/all_to_all | solution.py:310
  112.6 3.1 %collective-permute-start.7 = (bf16[512,512]{1,0:T(8,128)(2,1)S(1)}, bf16[512,512]{1,0:T(8,128)(2,1)S(1)}, u32[]{:S(2)}, u32[]{:S(2)}) collective-permute-start(bf16[512,512]{1,0:T(8,128)(2,1)S(1)} %copy-done.7), channel_id=1, source_target_pairs={{0,128},{8,136},{16,144},{24,152},{32,160},{40,168},{48,176},{56,1... | collective-permute-start | bytes 1572872 | tf_op jit(solution)/shard_map/ppermute | solution.py:319
  116.2 8.1 %collective-permute-done.8.refs_3_ = bf16[512,512]{1,0:T(8,128)(2,1)S(1)} collective-permute-done((bf16[512,512]{1,0:T(8,128)(2,1)S(1)}, bf16[512,512]{1,0:T(8,128)(2,1)S(1)}, u32[]{:S(2)}, u32[]{:S(2)}) %collective-permute-start.8) | collective-permute-done | bytes 524320 | tf_op jit(solution)/shard_map/ppermute | solution.py:319
  124.3 3.9 %collective-permute-done.7.refs_2_ = bf16[512,512]{1,0:T(8,128)(2,1)S(1)} collective-permute-done((bf16[512,512]{1,0:T(8,128)(2,1)S(1)}, bf16[512,512]{1,0:T(8,128)(2,1)S(1)}, u32[]{:S(2)}, u32[]{:S(2)}) %collective-permute-start.7) | collective-permute-done | bytes 524320 | tf_op jit(solution)/shard_map/ppermute | solution.py:319
  128.3 0.8 copy-done.9
  129.1 5.8 %collective-permute-done.6.refs_1_ = bf16[512,512]{1,0:T(8,128)(2,1)} collective-permute-done((bf16[512,512]{1,0:T(8,128)(2,1)S(1)}, bf16[512,512]{1,0:T(8,128)(2,1)}, u32[]{:S(2)}, u32[]{:S(2)}) %collective-permute-start.6) | collective-permute-done | bytes 524320 | tf_op jit(solution)/shard_map/ppermute | solution.py:319
  134.9 12.9 %shard_map.96 = (bf16[512,4096]{1,0:T(8,128)(2,1)}, bf16[512,512]{1,0:T(8,128)(2,1)}) custom-call(s32[1]{0:T(128)} %bitcast.head, bf16[512,512]{1,0:T(8,128)(2,1)} %get-tuple-element.77.mixed, bf16[512,4096]{1,0:T(8,128)(2,1)} %all-gather.2.cloned.1.call-done.w, bf16[512,512]{1,0:T(8,128)(2,1)} %refs_0_.1, bf16[512,512]{1,0:T(8,128)(2,1)} %copy-done.12, ...), custom_call_target="tpu_custom_call" | custom-call | tf_op jit(solution)/shard_map/pallas_call | solution.py:56
  148.0 4.2 %shard_map.97 = (bf16[512,512]{1,0:T(8,128)(2,1)}, bf16[4,128,128]{2,1,0:T(8,128)(2,1)}) custom-call(bf16[512,512]{1,0:T(8,128)(2,1)} %q.9, bf16[512,512]{1,0:T(8,128)(2,1)} %get-tuple-element.96.g, f32[512,512]{1,0:T(8,128)} %get-tuple-element.88.normed, f32[4,1,512]{2,1,0:T(1,128)} %copy-done.1), custom_call_target="tpu_custom_call" | custom-call | tf_op jit(solution)/shard_map/pallas_call | solution.py:56
  152.2 6.1 %shard_map.99 = (f32[512,512]{1,0:T(8,128)}, bf16[448,512]{1,0:T(8,128)(2,1)}, bf16[448,512]{1,0:T(8,128)(2,1)}, f32[4,1,512]{2,1,0:T(1,128)S(1)}) custom-call(bf16[512,512]{1,0:T(8,128)(2,1)} %q.9, bf16[512,512]{1,0:T(8,128)(2,1)} %get-tuple-element.96.g, bf16[512,512]{1,0:T(8,128)(2,1)} %copy-done.3, bf16[512,512]{1,0:T(8,128)(2,1)} %copy-done.4, ...), custom_call_target="tpu_custom_call" | custom-call | tf_op jit(solution)/shard_map/pallas_call | solution.py:56
  158.2 0.6 copy-done
  158.8 1.9 collective-permute-start.13
  160.7 1.9 collective-permute-start.14
  162.7 11.2 %all-to-all-start.3 = ((bf16[32,16,128]{2,1,0:T(8,128)(2,1)}), bf16[32,16,128]{2,1,0:T(8,128)(2,1)S(1)}, u32[]{:S(2)}, u32[]{:S(2)}) async-start(bf16[32,16,128]{2,1,0:T(8,128)(2,1)} %bitcast.4), calls=%async_computation.4 | async-start | bytes 262144 | tf_op jit(solution)/shard_map/all_to_all | solution.py:227
  174.0 9.9 %shard_map.102 = (bf16[512,128]{1,0:T(8,128)(2,1)}, bf16[512,128]{1,0:T(8,128)(2,1)}, bf16[512,128]{1,0:T(8,128)(2,1)}, bf16[512,128]{1,0:T(8,128)(2,1)}, bf16[5...) custom-call(s32[3]{0:T(128)S(1)} %pad_add_fusion.place, ...), custom_call_target="tpu_custom_call" | custom-call | tf_op jit(solution)/shard_map/pallas_call | solution.py:56
  183.9 1.5 collective-permute-start.16
  185.3 2.4 %collective-permute-start.17 = (bf16[512,128]{1,0:T(8,128)(2,1)}, bf16[512,128]{1,0:T(8,128)(2,1)S(1)}, u32[]{:S(2)}, u32[]{:S(2)}) collective-permute-start(bf16[512,128]{1,0:T(8,128)(2,1)} %get-tuple-element.121), channel_id=1, source_target_pairs={{0,16},{8,24},{16,32},{24,40},{32,48},{40,56},{48,0},{56,8},{64,80... | collective-permute-start | bytes 393224 | tf_op jit(solution)/shard_map/ppermute | solution.py:338
  187.7 3.1 %all-to-all-done.3.x = bf16[32,16,128]{2,1,0:T(8,128)(2,1)S(1)} async-done(((bf16[32,16,128]{2,1,0:T(8,128)(2,1)}), bf16[32,16,128]{2,1,0:T(8,128)(2,1)S(1)}, u32[]{:S(2)}, u32[]{:S(2)}) %all-to-all-start.3) | async-done | bytes 131104 | tf_op jit(solution)/shard_map/all_to_all | solution.py:227
  190.8 0.7 copy-done.14
  191.4 1.6 shard_map.98
  193.0 6.8 %all-to-all-start.4 = ((bf16[32,16,128]{2,1,0:T(8,128)(2,1)}), bf16[32,16,128]{2,1,0:T(8,128)(2,1)S(1)}, u32[]{:S(2)}, u32[]{:S(2)}) async-start(bf16[32,16,128]{2,1,0:T(8,128)(2,1)} %shard_map.98), calls=%async_computation.5 | async-start | bytes 262144 | tf_op jit(solution)/shard_map/all_to_all | solution.py:234
  199.8 3.3 %collective-permute-start.18 = (bf16[512,128]{1,0:T(8,128)(2,1)}, bf16[512,128]{1,0:T(8,128)(2,1)S(1)}, u32[]{:S(2)}, u32[]{:S(2)}) collective-permute-start(bf16[512,128]{1,0:T(8,128)(2,1)} %get-tuple-element.122), channel_id=1, source_target_pairs={{0,24},{8,32},{16,40},{24,48},{32,56},{40,0},{48,8},{56,16},{64,88... | collective-permute-start | bytes 393224 | tf_op jit(solution)/shard_map/ppermute | solution.py:338
  203.2 2.7 %collective-permute-start.19 = (bf16[512,128]{1,0:T(8,128)(2,1)}, bf16[512,128]{1,0:T(8,128)(2,1)S(1)}, u32[]{:S(2)}, u32[]{:S(2)}) collective-permute-start(bf16[512,128]{1,0:T(8,128)(2,1)} %get-tuple-element.123), channel_id=1, source_target_pairs={{0,32},{8,40},{16,48},{24,56},{32,0},{40,8},{48,16},{56,24},{64,96... | collective-permute-start | bytes 393224 | tf_op jit(solution)/shard_map/ppermute | solution.py:338
  205.9 4.5 %collective-permute-start.20 = (bf16[512,128]{1,0:T(8,128)(2,1)}, bf16[512,128]{1,0:T(8,128)(2,1)S(1)}, u32[]{:S(2)}, u32[]{:S(2)}) collective-permute-start(bf16[512,128]{1,0:T(8,128)(2,1)} %get-tuple-element.124), channel_id=1, source_target_pairs={{0,40},{8,48},{16,56},{24,0},{32,8},{40,16},{48,24},{56,32},{64,10... | collective-permute-start | bytes 393224 | tf_op jit(solution)/shard_map/ppermute | solution.py:338
  210.9 0.6 collective-permute-start.22
  211.4 8.0 %shard_map.100 = (bf16[512,512]{1,0:T(8,128)(2,1)}, f32[512,512]{1,0:T(8,128)}, f32[512,512]{1,0:T(8,128)}) custom-call(bf16[512,512]{1,0:T(8,128)(2,1)} %q.9, bf16[512,512]{1,0:T(8,128)(2,1)} %k.7, bf16[512,512]{1,0:T(8,128)(2,1)} %v.7, bf16[512,512]{1,0:T(8,128)(2,1)} %get-tuple-element.96.g, bf16[512,512]{1,0:T(8,128)(2,1)} %get-tuple-element.93.gl, ...), custom_call_target="tpu_custom_call" | custom-call | tf_op jit(solution)/shard_map/pallas_call | solution.py:56
  219.5 0.6 copy-done.13
  220.1 4.4 %shard_map.101 = (bf16[512,512]{1,0:T(8,128)(2,1)}, bf16[512,512]{1,0:T(8,128)(2,1)}) custom-call(bf16[512,512]{1,0:T(8,128)(2,1)} %k.7, bf16[512,512]{1,0:T(8,128)(2,1)} %v.7, bf16[4,128,128]{2,1,0:T(8,128)(2,1)} %bitcast.8, f32[512,512]{1,0:T(8,128)} %get-tuple-element.102.dk, f32[512,512]{1,0:T(8,128)} %get-tuple-element.103.dv, ...), custom_call_target="tpu_custom_call" | custom-call | tf_op jit(solution)/shard_map/pallas_call | solution.py:56
  224.6 2.4 %collective-permute-done.21 = bf16[512,128]{1,0:T(8,128)(2,1)S(1)} collective-permute-done((bf16[512,128]{1,0:T(8,128)(2,1)}, bf16[512,128]{1,0:T(8,128)(2,1)S(1)}, u32[]{:S(2)}, u32[]{:S(2)}) %collective-permute-start.21) | collective-permute-done | bytes 131104 | tf_op jit(solution)/shard_map/ppermute | solution.py:338
  226.9 1.9 collective-permute-done.22
  228.8 0.8 add_multiply_fusion
  (66 shorter events, 2.0 us)
Async XLA Ops:
  7.2 127.7 %all-gather.2.cloned.1.call-start = ((), (), s32[]{:S(2)}) async-start(), calls=%async_computation.6 | async-start | bytes 4325376 | tf_op jit(solution)/shard_map/all_gather | solution.py:370
  7.9 32.5 %collective-permute-start.4 = (bf16[512,512]{1,0:T(8,128)(2,1)}, bf16[512,512]{1,0:T(8,128)(2,1)S(1)}, u32[]{:S(2)}, u32[]{:S(2)}) collective-permute-start(bf16[512,512]{1,0:T(8,128)(2,1)} %refs_0_.1), channel_id=1, source_target_pairs={{0,6},{1,7},{2,0},{3,1},{4,2},{5,3},{6,4},{7,5},{8,14},{9,15},{10,... | collective-permute-start | bytes 1572872 | tf_op jit(solution)/shard_map/ppermute | solution.py:328
  14.4 20.4 %all-to-all-start = ((bf16[32,16,128]{2,1,0:T(8,128)(2,1)}), bf16[32,16,128]{2,1,0:T(8,128)(2,1)S(1)}, u32[]{:S(2)}, u32[]{:S(2)}) async-start(bf16[32,16,128]{2,1,0:T(8,128)(2,1)} %bitcast.1), calls=%async_computation | async-start | bytes 262144 | tf_op jit(solution)/shard_map/all_to_all | solution.py:227
  26.0 65.6 %collective-permute-start.3 = (bf16[512,512]{1,0:T(8,128)(2,1)}, bf16[512,512]{1,0:T(8,128)(2,1)S(1)}, u32[]{:S(2)}, u32[]{:S(2)}) collective-permute-start(bf16[512,512]{1,0:T(8,128)(2,1)} %refs_0_.1), channel_id=1, source_target_pairs={{0,4},{1,5},{2,6},{3,7},{4,0},{5,1},{6,2},{7,3},{8,12},{9,13},{10,... | collective-permute-start | bytes 1572872 | tf_op jit(solution)/shard_map/ppermute | solution.py:328
  26.9 64.7 %collective-permute-start.2 = (bf16[512,512]{1,0:T(8,128)(2,1)}, bf16[512,512]{1,0:T(8,128)(2,1)S(1)}, u32[]{:S(2)}, u32[]{:S(2)}) collective-permute-start(bf16[512,512]{1,0:T(8,128)(2,1)} %refs_0_.1), channel_id=1, source_target_pairs={{0,2},{1,3},{2,4},{3,5},{4,6},{5,7},{6,0},{7,1},{8,10},{9,11},{10,... | collective-permute-start | bytes 1572872 | tf_op jit(solution)/shard_map/ppermute | solution.py:328
  34.8 9.7 %copy-start.15 = (bf16[32,16,128]{2,1,0:T(8,128)(2,1)}, bf16[32,16,128]{2,1,0:T(8,128)(2,1)S(1)}, u32[]{:S(2)}) copy-start(bf16[32,16,128]{2,1,0:T(8,128)(2,1)S(1)} %all-to-all-done.x) | copy-start | bytes 393220
  34.8 56.7 %collective-permute-start = (bf16[512,512]{1,0:T(8,128)(2,1)}, bf16[512,512]{1,0:T(8,128)(2,1)S(1)}, u32[]{:S(2)}, u32[]{:S(2)}) collective-permute-start(bf16[512,512]{1,0:T(8,128)(2,1)} %k.7), channel_id=1, source_target_pairs={{0,8},{8,16},{16,24},{24,32},{32,40},{40,48},{48,56},{56,64},{64,7... | collective-permute-start | bytes 1572872 | tf_op jit(solution)/shard_map/ppermute | solution.py:302
  37.8 53.8 %collective-permute-start.1 = (bf16[512,512]{1,0:T(8,128)(2,1)}, bf16[512,512]{1,0:T(8,128)(2,1)S(1)}, u32[]{:S(2)}, u32[]{:S(2)}) collective-permute-start(bf16[512,512]{1,0:T(8,128)(2,1)} %v.7), channel_id=1, source_target_pairs={{0,8},{8,16},{16,24},{24,32},{32,40},{40,48},{48,56},{56,64},{64,7... | collective-permute-start | bytes 1572872 | tf_op jit(solution)/shard_map/ppermute | solution.py:302
  40.4 5.7 %copy-start.10 = (bf16[512,512]{1,0:T(8,128)(2,1)}, bf16[512,512]{1,0:T(8,128)(2,1)S(1)}, u32[]{:S(2)}) copy-start(bf16[512,512]{1,0:T(8,128)(2,1)S(1)} %collective-permute-done.4.refs_3_) | copy-start | bytes 1572868
  40.4 51.2 %collective-permute-start.5 = (bf16[512,512]{1,0:T(8,128)(2,1)}, bf16[512,512]{1,0:T(8,128)(2,1)S(1)}, u32[]{:S(2)}, u32[]{:S(2)}) collective-permute-start(bf16[512,512]{1,0:T(8,128)(2,1)} %refs_0_.1), channel_id=1, source_target_pairs={{0,0},{1,1},{2,64},{3,65},{4,128},{5,129},{6,192},{7,193},{8,8},{9... | collective-permute-start | bytes 1572872 | tf_op jit(solution)/shard_map/ppermute | solution.py:351
  46.1 45.4 %all-to-all-start.1 = ((bf16[32,16,128]{2,1,0:T(8,128)(2,1)}), bf16[32,16,128]{2,1,0:T(8,128)(2,1)S(1)}, u32[]{:S(2)}, u32[]{:S(2)}) async-start(bf16[32,16,128]{2,1,0:T(8,128)(2,1)} %shard_map.93), calls=%async_computation.1 | async-start | bytes 262144 | tf_op jit(solution)/shard_map/all_to_all | solution.py:234
  91.6 10.3 %copy-start.5 = (bf16[32,16,128]{2,1,0:T(8,128)(2,1)}, bf16[32,16,128]{2,1,0:T(8,128)(2,1)S(1)}, u32[]{:S(2)}) copy-start(bf16[32,16,128]{2,1,0:T(8,128)(2,1)S(1)} %all-to-all-done.1) | copy-start | bytes 393220
  91.6 16.9 %copy-start.11 = (bf16[512,512]{1,0:T(8,128)(2,1)}, bf16[512,512]{1,0:T(8,128)(2,1)S(1)}, u32[]{:S(2)}) copy-start(bf16[512,512]{1,0:T(8,128)(2,1)S(1)} %collective-permute-done.3.refs_2_) | copy-start | bytes 1572868
  91.6 15.3 %copy-start.12 = (bf16[512,512]{1,0:T(8,128)(2,1)}, bf16[512,512]{1,0:T(8,128)(2,1)S(1)}, u32[]{:S(2)}) copy-start(bf16[512,512]{1,0:T(8,128)(2,1)S(1)} %collective-permute-done.2.refs_1_) | copy-start | bytes 1572868
  91.6 0.8 copy-start.3
  91.6 1.0 copy-start.4
  106.3 0.6 copy-start.1
  108.4 3.8 %copy-start.7 = (bf16[512,512]{1,0:T(8,128)(2,1)S(1)}, bf16[512,512]{1,0:T(8,128)(2,1)}, u32[]{:S(2)}) copy-start(bf16[512,512]{1,0:T(8,128)(2,1)} %get-tuple-element.115.refs_0_) | copy-start | bytes 1572868
  108.4 7.3 %copy-start.6 = (bf16[512,512]{1,0:T(8,128)(2,1)S(1)}, bf16[512,512]{1,0:T(8,128)(2,1)}, u32[]{:S(2)}) copy-start(bf16[512,512]{1,0:T(8,128)(2,1)} %refs_0_.1) | copy-start | bytes 1572868
  108.4 26.5 %all-to-all-start.2 = ((bf16[4,512,512]{2,1,0:T(8,128)(2,1)}), bf16[4,512,512]{2,1,0:T(8,128)(2,1)S(1)}, u32[]{:S(2)}, u32[]{:S(2)}) async-start(bf16[4,512,512]{2,1,0:T(8,128)(2,1)} %broadcast_in_dim.2), calls=%async_computation.2 | async-start | bytes 4194304 | tf_op jit(solution)/shard_map/all_to_all | solution.py:310
  112.2 117.5 %reduce-scatter.2.cloned.1.call-start = ((), (), s32[]{:S(2)}) async-start(), calls=%async_computation.7 | async-start | bytes 4718592 | tf_op jit(solution)/shard_map/reduce_scatter | solution.py:429
  112.2 12.1 %collective-permute-start.8 = (bf16[512,512]{1,0:T(8,128)(2,1)S(1)}, bf16[512,512]{1,0:T(8,128)(2,1)S(1)}, u32[]{:S(2)}, u32[]{:S(2)}) collective-permute-start(bf16[512,512]{1,0:T(8,128)(2,1)S(1)} %copy-done.7), channel_id=1, source_target_pairs={{0,192},{8,200},{16,208},{24,216},{32,224},{40,232},{48,240},{56,2... | collective-permute-start | bytes 1572872 | tf_op jit(solution)/shard_map/ppermute | solution.py:319
  112.6 15.7 %collective-permute-start.7 = (bf16[512,512]{1,0:T(8,128)(2,1)S(1)}, bf16[512,512]{1,0:T(8,128)(2,1)S(1)}, u32[]{:S(2)}, u32[]{:S(2)}) collective-permute-start(bf16[512,512]{1,0:T(8,128)(2,1)S(1)} %copy-done.7), channel_id=1, source_target_pairs={{0,128},{8,136},{16,144},{24,152},{32,160},{40,168},{48,176},{56,1... | collective-permute-start | bytes 1572872 | tf_op jit(solution)/shard_map/ppermute | solution.py:319
  115.7 19.2 %collective-permute-start.9 = (bf16[512,512]{1,0:T(8,128)(2,1)S(1)}, bf16[512,512]{1,0:T(8,128)(2,1)}, u32[]{:S(2)}, u32[]{:S(2)}) collective-permute-start(bf16[512,512]{1,0:T(8,128)(2,1)S(1)} %copy-done.6), channel_id=1, source_target_pairs={{0,1},{1,0},{2,3},{3,2},{4,5},{5,4},{6,7},{7,6},{8,9},{9,8},{10,11... | collective-permute-start | bytes 1572872 | tf_op jit(solution)/shard_map/ppermute | solution.py:334
  115.7 19.2 %collective-permute-start.6 = (bf16[512,512]{1,0:T(8,128)(2,1)S(1)}, bf16[512,512]{1,0:T(8,128)(2,1)}, u32[]{:S(2)}, u32[]{:S(2)}) collective-permute-start(bf16[512,512]{1,0:T(8,128)(2,1)S(1)} %copy-done.7), channel_id=1, source_target_pairs={{0,64},{8,72},{16,80},{24,88},{32,96},{40,104},{48,112},{56,120},{... | collective-permute-start | bytes 1572872 | tf_op jit(solution)/shard_map/ppermute | solution.py:319
  115.8 19.1 %collective-permute-start.10 = (bf16[512,512]{1,0:T(8,128)(2,1)}, bf16[512,512]{1,0:T(8,128)(2,1)}, u32[]{:S(2)}, u32[]{:S(2)}) collective-permute-start(bf16[512,512]{1,0:T(8,128)(2,1)} %copy-done.12), channel_id=1, source_target_pairs={{0,1},{1,0},{2,3},{3,2},{4,5},{5,4},{6,7},{7,6},{8,9},{9,8},{10,11... | collective-permute-start | bytes 1572872 | tf_op jit(solution)/shard_map/ppermute | solution.py:334
  124.3 4.0 %copy-start.8 = (bf16[512,512]{1,0:T(8,128)(2,1)}, bf16[512,512]{1,0:T(8,128)(2,1)S(1)}, u32[]{:S(2)}) copy-start(bf16[512,512]{1,0:T(8,128)(2,1)S(1)} %collective-permute-done.8.refs_3_) | copy-start | bytes 1572868
  124.3 10.6 %collective-permute-start.11 = (bf16[512,512]{1,0:T(8,128)(2,1)}, bf16[512,512]{1,0:T(8,128)(2,1)}, u32[]{:S(2)}, u32[]{:S(2)}) collective-permute-start(bf16[512,512]{1,0:T(8,128)(2,1)} %copy-done.11), channel_id=1, source_target_pairs={{0,1},{1,0},{2,3},{3,2},{4,5},{5,4},{6,7},{7,6},{8,9},{9,8},{10,11... | collective-permute-start | bytes 1572872 | tf_op jit(solution)/shard_map/ppermute | solution.py:334
  128.3 0.8 copy-start.9
  129.1 5.8 %collective-permute-start.12 = (bf16[512,512]{1,0:T(8,128)(2,1)}, bf16[512,512]{1,0:T(8,128)(2,1)}, u32[]{:S(2)}, u32[]{:S(2)}) collective-permute-start(bf16[512,512]{1,0:T(8,128)(2,1)} %copy-done.10), channel_id=1, source_target_pairs={{0,1},{1,0},{2,3},{3,2},{4,5},{5,4},{6,7},{7,6},{8,9},{9,8},{10,11... | collective-permute-start | bytes 1572872 | tf_op jit(solution)/shard_map/ppermute | solution.py:334
  134.9 13.0 %copy-start.2 = (bf16[4,512,512]{2,1,0:T(8,128)(2,1)}, bf16[4,512,512]{2,1,0:T(8,128)(2,1)S(1)}, u32[]{:S(2)}) copy-start(bf16[4,512,512]{2,1,0:T(8,128)(2,1)S(1)} %all-to-all-done.2.mine) | copy-start | bytes 6291460
  147.9 26.1 %collective-permute-start.15 = (bf16[4,512,512]{2,1,0:T(8,128)(2,1)S(1)}, bf16[4,512,512]{2,1,0:T(8,128)(2,1)}, u32[]{:S(2)}, u32[]{:S(2)}) collective-permute-start(bf16[4,512,512]{2,1,0:T(8,128)(2,1)S(1)} %all-to-all-done.2.mine), channel_id=1, source_target_pairs={{0,1},{1,0},{2,3},{3,2},{4,5},{5,4},{6,7},{7,6},{8,9},{9,8},{10,11... | collective-permute-start | bytes 6291464 | tf_op jit(solution)/shard_map/ppermute | solution.py:334
  158.8 44.3 %collective-permute-start.13 = (bf16[448,512]{1,0:T(8,128)(2,1)}, bf16[448,512]{1,0:T(8,128)(2,1)S(1)}, u32[]{:S(2)}, u32[]{:S(2)}) collective-permute-start(bf16[448,512]{1,0:T(8,128)(2,1)} %get-tuple-element.104), channel_id=1, source_target_pairs={{8,0},{16,8},{24,16},{32,24},{40,32},{48,40},{56,48},{64,56},{72,6... | collective-permute-start | bytes 1376264 | tf_op jit(solution)/shard_map/ppermute | solution.py:302
  160.7 45.1 %collective-permute-start.14 = (bf16[448,512]{1,0:T(8,128)(2,1)}, bf16[448,512]{1,0:T(8,128)(2,1)S(1)}, u32[]{:S(2)}, u32[]{:S(2)}) collective-permute-start(bf16[448,512]{1,0:T(8,128)(2,1)} %get-tuple-element.105), channel_id=1, source_target_pairs={{8,0},{16,8},{24,16},{32,24},{40,32},{48,40},{56,48},{64,56},{72,6... | collective-permute-start | bytes 1376264 | tf_op jit(solution)/shard_map/ppermute | solution.py:302
  162.7 28.1 %all-to-all-start.3 = ((bf16[32,16,128]{2,1,0:T(8,128)(2,1)}), bf16[32,16,128]{2,1,0:T(8,128)(2,1)S(1)}, u32[]{:S(2)}, u32[]{:S(2)}) async-start(bf16[32,16,128]{2,1,0:T(8,128)(2,1)} %bitcast.4), calls=%async_computation.4 | async-start | bytes 262144 | tf_op jit(solution)/shard_map/all_to_all | solution.py:227
  183.9 26.4 %collective-permute-start.16 = (bf16[512,128]{1,0:T(8,128)(2,1)}, bf16[512,128]{1,0:T(8,128)(2,1)S(1)}, u32[]{:S(2)}, u32[]{:S(2)}) collective-permute-start(bf16[512,128]{1,0:T(8,128)(2,1)} %get-tuple-element.120), channel_id=1, source_target_pairs={{0,8},{8,16},{16,24},{24,32},{32,40},{40,48},{48,56},{56,0},{64,72... | collective-permute-start | bytes 393224 | tf_op jit(solution)/shard_map/ppermute | solution.py:338
  185.3 25.5 %collective-permute-start.17 = (bf16[512,128]{1,0:T(8,128)(2,1)}, bf16[512,128]{1,0:T(8,128)(2,1)S(1)}, u32[]{:S(2)}, u32[]{:S(2)}) collective-permute-start(bf16[512,128]{1,0:T(8,128)(2,1)} %get-tuple-element.121), channel_id=1, source_target_pairs={{0,16},{8,24},{16,32},{24,40},{32,48},{40,56},{48,0},{56,8},{64,80... | collective-permute-start | bytes 393224 | tf_op jit(solution)/shard_map/ppermute | solution.py:338
  190.8 0.7 copy-start.14
  193.0 26.4 %all-to-all-start.4 = ((bf16[32,16,128]{2,1,0:T(8,128)(2,1)}), bf16[32,16,128]{2,1,0:T(8,128)(2,1)S(1)}, u32[]{:S(2)}, u32[]{:S(2)}) async-start(bf16[32,16,128]{2,1,0:T(8,128)(2,1)} %shard_map.98), calls=%async_computation.5 | async-start | bytes 262144 | tf_op jit(solution)/shard_map/all_to_all | solution.py:234
  199.8 24.7 %collective-permute-start.18 = (bf16[512,128]{1,0:T(8,128)(2,1)}, bf16[512,128]{1,0:T(8,128)(2,1)S(1)}, u32[]{:S(2)}, u32[]{:S(2)}) collective-permute-start(bf16[512,128]{1,0:T(8,128)(2,1)} %get-tuple-element.122), channel_id=1, source_target_pairs={{0,24},{8,32},{16,40},{24,48},{32,56},{40,0},{48,8},{56,16},{64,88... | collective-permute-start | bytes 393224 | tf_op jit(solution)/shard_map/ppermute | solution.py:338
  203.2 16.3 %copy-start.16 = (bf16[448,512]{1,0:T(8,128)(2,1)}, bf16[448,512]{1,0:T(8,128)(2,1)S(1)}, u32[]{:S(2)}) copy-start(bf16[448,512]{1,0:T(8,128)(2,1)S(1)} %collective-permute-done.13.rk) | copy-start | bytes 1376260
  203.2 21.4 %collective-permute-start.19 = (bf16[512,128]{1,0:T(8,128)(2,1)}, bf16[512,128]{1,0:T(8,128)(2,1)S(1)}, u32[]{:S(2)}, u32[]{:S(2)}) collective-permute-start(bf16[512,128]{1,0:T(8,128)(2,1)} %get-tuple-element.123), channel_id=1, source_target_pairs={{0,32},{8,40},{16,48},{24,56},{32,0},{40,8},{48,16},{56,24},{64,96... | collective-permute-start | bytes 393224 | tf_op jit(solution)/shard_map/ppermute | solution.py:338
  205.9 13.6 %copy-start.17 = (bf16[448,512]{1,0:T(8,128)(2,1)}, bf16[448,512]{1,0:T(8,128)(2,1)S(1)}, u32[]{:S(2)}) copy-start(bf16[448,512]{1,0:T(8,128)(2,1)S(1)} %collective-permute-done.14.rv) | copy-start | bytes 1376260
  205.9 18.7 %collective-permute-start.20 = (bf16[512,128]{1,0:T(8,128)(2,1)}, bf16[512,128]{1,0:T(8,128)(2,1)S(1)}, u32[]{:S(2)}, u32[]{:S(2)}) collective-permute-start(bf16[512,128]{1,0:T(8,128)(2,1)} %get-tuple-element.124), channel_id=1, source_target_pairs={{0,40},{8,48},{16,56},{24,0},{32,8},{40,16},{48,24},{56,32},{64,10... | collective-permute-start | bytes 393224 | tf_op jit(solution)/shard_map/ppermute | solution.py:338
  210.3 16.6 %collective-permute-start.21 = (bf16[512,128]{1,0:T(8,128)(2,1)}, bf16[512,128]{1,0:T(8,128)(2,1)S(1)}, u32[]{:S(2)}, u32[]{:S(2)}) collective-permute-start(bf16[512,128]{1,0:T(8,128)(2,1)} %get-tuple-element.125), channel_id=1, source_target_pairs={{0,48},{8,56},{16,0},{24,8},{32,16},{40,24},{48,32},{56,40},{64,11... | collective-permute-start | bytes 393224 | tf_op jit(solution)/shard_map/ppermute | solution.py:338
  210.9 17.9 %collective-permute-start.22 = (bf16[512,128]{1,0:T(8,128)(2,1)}, bf16[512,128]{1,0:T(8,128)(2,1)S(1)}, u32[]{:S(2)}, u32[]{:S(2)}) collective-permute-start(bf16[512,128]{1,0:T(8,128)(2,1)} %get-tuple-element.126), channel_id=1, source_target_pairs={{0,56},{8,0},{16,8},{24,16},{32,24},{40,32},{48,40},{56,48},{64,12... | collective-permute-start | bytes 393224 | tf_op jit(solution)/shard_map/ppermute | solution.py:338
  219.5 0.7 copy-start.13
  220.1 8.7 %copy-start.18 = (bf16[512,128]{1,0:T(8,128)(2,1)S(1)}, bf16[512,128]{1,0:T(8,128)(2,1)}, u32[]{:S(2)}) copy-start(bf16[512,128]{1,0:T(8,128)(2,1)} %get-tuple-element.119) | copy-start | bytes 393220
  (1 other events, 0.6 us)
Sparse Core Ops, SparseCore 0:
  10.5 105.9 all-gather.1
  148.0 39.1 reduce-scatter.1

commit v6 on v5

--- a/solution.py
+++ b/solution.py
@@ -372,13 +372,10 @@
     local = call(
         sums_kernel, heads, [col, col], st, shape((heads, DH, DH), BF16), flops=2 * mm // 4
     )(keys, values)
-    before, _, sent = carry_states(local, False, (), (keys, values, grad_y))
-    kh, vh, turned_grad = shifted(sent[0], 1), shifted(sent[1], 1), turn_xy(sent[2])
-    before, kh, vh, hopped, turned_grad = lax.optimization_barrier(
-        (before, kh, vh, hopped, turned_grad)
-    )
-    grads = [grad_y] + hopped
-    grads = grads + [swap_core(g) for g in grads]
+    local, k_out, v_out = lax.optimization_barrier((local, keys, values))
+    kh, vh = shifted(k_out, 1), shifted(v_out, 1)
+    before, grad_out, _ = carry_states(local, False, grad_y)
+    turned_grad = turn_xy(grad_out)
 
     sq = large((heads, rows, rows), BF16)
     flat_t = large((width, rows), F32)
@@ -410,52 +407,14 @@
         size=5 << 20,
     )(queries, before, window, intra)
 
-    turned_grad, mixed_t = lax.optimization_barrier((turned_grad, mixed_t))
+    turned_grad, hopped, mixed_t = lax.optimization_barrier((turned_grad, hopped, mixed_t))
     mine = spread(turned_grad, "head", X_GROUPS)
     across_y = [mixed_t] + [hop_y(mixed_t, by) for by in range(1, YS)]
-    mine, across_y, full_w = lax.optimization_barrier((mine, across_y, full_w))
+    mine, across_y = lax.optimization_barrier((mine, across_y))
+    grads = [grad_y] + hopped
+    grads = grads + [swap_core(g) for g in grads]
     other = swap_core(mine)
     fixed = pl.BlockSpec((rows, width), lambda *_: (0, 0))
-    by_block = pl.BlockSpec((rows, width), lambda t, head: (0, block_id(t, head)))
-    partial_value, grad_mixed = call(
-        project_kernel,
-        2 * XS,
-        [fixed, by_block] + [fixed] * (2 * XS),
-        [by_block, fixed],
-        [large((rows, 2 * XS * width), BF16), large((rows, width), BF16)],
-        scratch=[pltpu.VMEM((rows, width), F32)],
-        prefetch=1,
-    )(head, mixed, full_w, *grads)
-    mixer_result = lax.psum_scatter(partial_value, "head", scatter_dimension=1, tiled=True)
-
-    grad_lin, local_back = call(
-        lin_kernel,
-        heads,
-        [col, col, turned, line],
-        [col, st],
-        [large((rows, width), BF16), shape((heads, DH, DH), BF16)],
-        flops=mm // 4,
-        size=3 << 20,
-    )(queries, grad_mixed, normed, inverse)
-    local_back, g_far = lax.optimization_barrier((local_back, grad_mixed))
-    edge_grad = large((edge, width), BF16)
-    dq_far, far_k, far_v, delta = call(
-        far_kernel,
-        heads,
-        [col, col, col, col, tri, turned],
-        [turned, columns(edge), columns(edge), line],
-        [flat_t, edge_grad, edge_grad, shape((heads, 1, rows), F32)],
-        scratch=[pltpu.VMEM((rows, rows), BF16)],
-        flops=8 * mm // 8,
-        size=8 << 20,
-    )(queries, g_far, kh, vh, far, window)
-    back_k, back_v = shifted(far_k, -1), shifted(far_v, -1)
-
-    later, grad_lin, _ = carry_states(local_back, True, grad_lin)
-
-    across_y, mine, other, local_back = lax.optimization_barrier(
-        (across_y, mine, other, local_back)
-    )
     parts = call(
         sens_kernel,
         (2, YS),
@@ -479,6 +438,44 @@
         scratch=[pltpu.VMEM((width, rows), F32)],
         prefetch=1,
     )(place, mine, other, *across_y)
+    parts, full_w = lax.optimization_barrier((parts, full_w))
+    by_block = pl.BlockSpec((rows, width), lambda t, head: (0, block_id(t, head)))
+    partial_value, grad_mixed = call(
+        project_kernel,
+        2 * XS,
+        [fixed, by_block] + [fixed] * (2 * XS),
+        [by_block, fixed],
+        [large((rows, 2 * XS * width), BF16), large((rows, width), BF16)],
+        scratch=[pltpu.VMEM((rows, width), F32)],
+        prefetch=1,
+    )(head, mixed, full_w, *grads)
+    mixer_result = lax.psum_scatter(partial_value, "head", scatter_dimension=1, tiled=True)
+
+    grad_lin, local_back = call(
+        lin_kernel,
+        heads,
+        [col, col, turned, line],
+        [col, st],
+        [large((rows, width), BF16), shape((heads, DH, DH), BF16)],
+        flops=mm // 4,
+        size=3 << 20,
+    )(queries, grad_mixed, normed, inverse)
+    local_back, g_far = lax.optimization_barrier((local_back, grad_mixed))
+    edge_grad = large((edge, width), BF16)
+    dq_far, far_k, far_v, delta = call(
+        far_kernel,
+        heads,
+        [col, col, col, col, tri, turned],
+        [turned, columns(edge), columns(edge), line],
+        [flat_t, edge_grad, edge_grad, shape((heads, 1, rows), F32)],
+        scratch=[pltpu.VMEM((rows, rows), BF16)],
+        flops=8 * mm // 8,
+        size=8 << 20,
+    )(queries, g_far, kh, vh, far, window)
+    back_k, back_v = shifted(far_k, -1), shifted(far_v, -1)
+
+    later, grad_lin, _ = carry_states(local_back, True, grad_lin)
+
     total = parts[0].astype(F32)
     for by in range(1, ZS):
         total = total + hop_z(parts[by], by).astype(F32)

time: 239 us -> 240 us (level)
  waiting for transfers between devices: 71.1 us -> 57.4 us
  starting transfers between devices: 78.2 us -> 90 us
  local copies, waits for them, and re-layouts: 5.84 us -> 8.89 us
    all_to_all x2, waiting for transfers between devices: 38.2 us -> 0.01 us  [carry_states(): lax.all_to_all(done, 'seq', 0, 0).reshape(local.shape)]
    ppermute x7, waiting for transfers between devices: 4.26 us -> 18.3 us  [hop_z(): lax.ppermute(shard, 'seq', [(y * ZS + z, y * ZS + (z + by) % ZS) for y in...]
    ppermute x3, waiting for transfers between devices: 17.8 us -> 29.3 us  [hop_y(): lax.ppermute(shard, 'seq', [(y * ZS + z, (y + by) % YS * ZS + z) for y in...]
    all_to_all x2, waiting for transfers between devices: 10.1 us -> 3.2 us  [carry_states(): met = lax.all_to_all(pieces, 'seq', 0, 0)]
    ppermute x4, starting transfers between devices: 9.38 us -> 15.1 us  [shifted(): return lax.ppermute(shard, 'seq', pairs)]
    all_to_all x2, starting transfers between devices: 22.8 us -> 17.8 us  [carry_states(): met = lax.all_to_all(pieces, 'seq', 0, 0)]
    all_to_all x1, starting transfers between devices: 3.74 us -> 7.38 us  [exchange(): return lax.all_to_all(pieces, axis, 0, 0, axis_index_groups=groups)]
    all_to_all x2, starting transfers between devices: 14 us -> 17.6 us  [carry_states(): lax.all_to_all(done, 'seq', 0, 0).reshape(local.shape)]
  transfers between devices with their start and end apart: 30 -> 30, of which waited for: 8 -> 7; matrix products, arithmetic and copies ran while one was open for 1% -> 1% of each run, Pallas kernels for 22% -> 22%
where the time goes in v6:
time: 240 us; the launch traced here: 237 us
  starting transfers between devices  90 us (38%)
  Pallas kernels  65.4 us (27%)
  waiting for transfers between devices  57.4 us (24%)
  between operations  14.4 us (6%)
  local copies, waits for them, and re-layouts  8.89 us (4%)
    pallas_call x9, Pallas kernels, call(): run(*args[:prefetch], *(kept(a) for a in args[prefetch:]))  62.3 us
    ppermute x3, waiting for transfers between devices, hop_y(): lax.ppermute(shard, 'seq', [(y * ZS + z, (y + by) % YS * ZS + z) for y in...  29.3 us
    ppermute x7, waiting for transfers between devices, hop_z(): lax.ppermute(shard, 'seq', [(y * ZS + z, y * ZS + (z + by) % ZS) for y in...  18.3 us
    all_to_all x2, starting transfers between devices, carry_states(): met = lax.all_to_all(pieces, 'seq', 0, 0)  17.8 us
    all_to_all x2, starting transfers between devices, carry_states(): lax.all_to_all(done, 'seq', 0, 0).reshape(local.shape)  17.6 us
    ppermute x4, starting transfers between devices, shifted(): return lax.ppermute(shard, 'seq', pairs)  15.1 us
    ppermute x7, starting transfers between devices, hop_z(): lax.ppermute(shard, 'seq', [(y * ZS + z, y * ZS + (z + by) % ZS) for y in...  12.3 us
    unnamed x50, local copies, waits for them, and re-layouts  7.38 us
  transfers between devices with their start and end apart: 30, of which 7 were waited for; matrix products, arithmetic and copies ran while one was open for 1% of the time, Pallas kernels for 22%

profile of v6, /device:TPU:16, one launch (start us, length us, event | category | flops | bytes accessed | tf_op | source)
XLA Modules:
  0.0 237.0 jit_solution(7967800851186246387)
XLA Ops:
  7.2 0.7 all-gather.2.cloned.1.call-update
  7.9 3.7 %shard_map.92 = bf16[4,128,128]{2,1,0:T(8,128)(2,1)} custom-call(bf16[512,512]{1,0:T(8,128)(2,1)} %k.7, bf16[512,512]{1,0:T(8,128)(2,1)} %v.7), custom_call_target="tpu_custom_call" | custom-call | tf_op jit(solution)/shard_map/pallas_call | solution.py:56
  11.6 3.8 %collective-permute-start = (bf16[512,512]{1,0:T(8,128)(2,1)}, bf16[512,512]{1,0:T(8,128)(2,1)S(1)}, u32[]{:S(2)}, u32[]{:S(2)}) collective-permute-start(bf16[512,512]{1,0:T(8,128)(2,1)} %k.7), channel_id=1, source_target_pairs={{0,8},{8,16},{16,24},{24,32},{32,40},{40,48},{48,56},{56,64},{64,7... | collective-permute-start | bytes 1572872 | tf_op jit(solution)/shard_map/ppermute | solution.py:302
  15.4 10.7 %all-to-all-start = ((bf16[32,16,128]{2,1,0:T(8,128)(2,1)}), bf16[32,16,128]{2,1,0:T(8,128)(2,1)S(1)}, u32[]{:S(2)}, u32[]{:S(2)}) async-start(bf16[32,16,128]{2,1,0:T(8,128)(2,1)} %bitcast.1), calls=%async_computation | async-start | bytes 262144 | tf_op jit(solution)/shard_map/all_to_all | solution.py:227
  26.1 3.4 %collective-permute-start.1 = (bf16[512,512]{1,0:T(8,128)(2,1)}, bf16[512,512]{1,0:T(8,128)(2,1)S(1)}, u32[]{:S(2)}, u32[]{:S(2)}) collective-permute-start(bf16[512,512]{1,0:T(8,128)(2,1)} %v.7), channel_id=1, source_target_pairs={{0,8},{8,16},{16,24},{24,32},{32,40},{40,48},{48,56},{56,64},{64,7... | collective-permute-start | bytes 1572872 | tf_op jit(solution)/shard_map/ppermute | solution.py:302
  29.5 1.6 collective-permute-start.3
  31.1 2.7 %collective-permute-start.4 = (bf16[512,512]{1,0:T(8,128)(2,1)}, bf16[512,512]{1,0:T(8,128)(2,1)S(1)}, u32[]{:S(2)}, u32[]{:S(2)}) collective-permute-start(bf16[512,512]{1,0:T(8,128)(2,1)} %refs_0_.1), channel_id=1, source_target_pairs={{0,4},{1,5},{2,6},{3,7},{4,0},{5,1},{6,2},{7,3},{8,12},{9,13},{10,... | collective-permute-start | bytes 1572872 | tf_op jit(solution)/shard_map/ppermute | solution.py:328
  33.8 1.4 collective-permute-start.5
  35.2 3.2 %all-to-all-done.x = bf16[32,16,128]{2,1,0:T(8,128)(2,1)S(1)} async-done(((bf16[32,16,128]{2,1,0:T(8,128)(2,1)}), bf16[32,16,128]{2,1,0:T(8,128)(2,1)S(1)}, u32[]{:S(2)}, u32[]{:S(2)}) %all-to-all-start) | async-done | bytes 131104 | tf_op jit(solution)/shard_map/all_to_all | solution.py:227
  39.1 1.6 shard_map.93
  40.7 6.6 %collective-permute-start.2 = (bf16[512,512]{1,0:T(8,128)(2,1)}, bf16[512,512]{1,0:T(8,128)(2,1)S(1)}, u32[]{:S(2)}, u32[]{:S(2)}) collective-permute-start(bf16[512,512]{1,0:T(8,128)(2,1)} %refs_0_.1), channel_id=1, source_target_pairs={{0,0},{1,1},{2,64},{3,65},{4,128},{5,129},{6,192},{7,193},{8,8},{9... | collective-permute-start | bytes 1572872 | tf_op jit(solution)/shard_map/ppermute | solution.py:351
  47.3 7.8 %all-to-all-start.1 = ((bf16[32,16,128]{2,1,0:T(8,128)(2,1)}), bf16[32,16,128]{2,1,0:T(8,128)(2,1)S(1)}, u32[]{:S(2)}, u32[]{:S(2)}) async-start(bf16[32,16,128]{2,1,0:T(8,128)(2,1)} %shard_map.93), calls=%async_computation.1 | async-start | bytes 262144 | tf_op jit(solution)/shard_map/all_to_all | solution.py:234
  55.1 0.8 copy-done.4
  55.9 9.3 %shard_map.94 = (bf16[4,512,512]{2,1,0:T(8,128)(2,1)}, bf16[4,512,512]{2,1,0:T(8,128)(2,1)}, bf16[4,512,512]{2,1,0:T(8,128)(2,1)}, f32[512,512]{1,0:T(8,128)}, f32[512,512]{1,0:T(8,128)}) custom-call(s32[1]{0:T(128)} %bitcast.3.place, bf16[512,512]{1,0:T(8,128)(2,1)} %q.9, bf16[512,512]{1,0:T(8,128)(2,1)} %k.7, bf16[512,512]{1,0:T(8,128)(2,1)} %v.7, ...), custom_call_target="tpu_custom_call" | custom-call | tf_op jit(solution)/shard_map/pallas_call | solution.py:56
  65.8 4.4 %shard_map.95 = (f32[512,512]{1,0:T(8,128)}, f32[4,1,512]{2,1,0:T(1,128)S(1)}, bf16[512,512]{1,0:T(8,128)(2,1)}, bf16[512,512]{1,0:T(8,128)(2,1)}) custom-call(bf16[512,512]{1,0:T(8,128)(2,1)} %q.9, bf16[4,128,128]{2,1,0:T(8,128)(2,1)} %bitcast.6, f32[512,512]{1,0:T(8,128)} %get-tuple-element.71.window, f32[512,512]{1,0:T(8,128)} %get-tuple-element.72.intra), custom_call_target="tpu_custom_call" | custom-call | tf_op jit(solution)/shard_map/pallas_call | solution.py:56
  70.8 2.8 %collective-permute-done.2 = bf16[512,512]{1,0:T(8,128)(2,1)S(1)} collective-permute-done((bf16[512,512]{1,0:T(8,128)(2,1)}, bf16[512,512]{1,0:T(8,128)(2,1)S(1)}, u32[]{:S(2)}, u32[]{:S(2)}) %collective-permute-start.2) | collective-permute-done | bytes 524320 | tf_op jit(solution)/shard_map/ppermute | solution.py:351
  73.6 1.5 broadcast_in_dim.2
  75.2 7.4 %all-to-all-start.2 = ((bf16[4,512,512]{2,1,0:T(8,128)(2,1)}), bf16[4,512,512]{2,1,0:T(8,128)(2,1)S(1)}, u32[]{:S(2)}, u32[]{:S(2)}) async-start(bf16[4,512,512]{2,1,0:T(8,128)(2,1)} %broadcast_in_dim.2), calls=%async_computation.2 | async-start | bytes 4194304 | tf_op jit(solution)/shard_map/all_to_all | solution.py:310
  82.5 1.3 collective-permute-start.6
  83.9 2.4 %collective-permute-start.7 = (bf16[512,512]{1,0:T(8,128)(2,1)}, bf16[512,512]{1,0:T(8,128)(2,1)S(1)}, u32[]{:S(2)}, u32[]{:S(2)}) collective-permute-start(bf16[512,512]{1,0:T(8,128)(2,1)} %get-tuple-element.79.refs_0_), channel_id=1, source_target_pairs={{0,128},{8,136},{16,144},{24,152},{32,160},{40,168},{48,176},{56,1... | collective-permute-start | bytes 1572872 | tf_op jit(solution)/shard_map/ppermute | solution.py:319
  86.3 2.5 %collective-permute-start.8 = (bf16[512,512]{1,0:T(8,128)(2,1)}, bf16[512,512]{1,0:T(8,128)(2,1)}, u32[]{:S(2)}, u32[]{:S(2)}) collective-permute-start(bf16[512,512]{1,0:T(8,128)(2,1)} %get-tuple-element.79.refs_0_), channel_id=1, source_target_pairs={{0,192},{8,200},{16,208},{24,216},{32,224},{40,232},{48,240},{56,2... | collective-permute-start | bytes 1572872 | tf_op jit(solution)/shard_map/ppermute | solution.py:319
  88.8 29.3 %collective-permute-done.6.refs_1_ = bf16[512,512]{1,0:T(8,128)(2,1)S(1)} collective-permute-done((bf16[512,512]{1,0:T(8,128)(2,1)}, bf16[512,512]{1,0:T(8,128)(2,1)S(1)}, u32[]{:S(2)}, u32[]{:S(2)}) %collective-permute-start.6) | collective-permute-done | bytes 524320 | tf_op jit(solution)/shard_map/ppermute | solution.py:319
  118.1 0.8 copy-done.10
  118.9 0.8 copy-done.11
  121.0 3.1 %collective-permute-done.9.other = bf16[4,512,512]{2,1,0:T(8,128)(2,1)} collective-permute-done((bf16[4,512,512]{2,1,0:T(8,128)(2,1)S(1)}, bf16[4,512,512]{2,1,0:T(8,128)(2,1)}, u32[]{:S(2)}, u32[]{:S(2)}) %collective-permute-start.9) | collective-permute-done | bytes 2097184 | tf_op jit(solution)/shard_map/ppermute | solution.py:334
  124.1 9.8 %shard_map.96 = (bf16[512,128]{1,0:T(8,128)(2,1)}, bf16[512,128]{1,0:T(8,128)(2,1)}, bf16[512,128]{1,0:T(8,128)(2,1)}, bf16[512,128]{1,0:T(8,128)(2,1)}, bf16[51...) custom-call(s32[3]{0:T(128)S(1)} %pad_add_fusion.place, ...), custom_call_target="tpu_custom_call" | custom-call | tf_op jit(solution)/shard_map/pallas_call | solution.py:56
  133.9 12.3 %shard_map.97 = (bf16[512,4096]{1,0:T(8,128)(2,1)}, bf16[512,512]{1,0:T(8,128)(2,1)}) custom-call(s32[1]{0:T(128)} %bitcast.head, bf16[512,512]{1,0:T(8,128)(2,1)} %get-tuple-element.73.mixed, bf16[512,4096]{1,0:T(8,128)(2,1)} %all-gather.2.cloned.1.call-done.w, bf16[512,512]{1,0:T(8,128)(2,1)} %refs_0_.1, bf16[512,512]{1,0:T(8,128)(2,1)} %copy-done.7, ...), custom_call_target="tpu_custom_call" | custom-call | tf_op jit(solution)/shard_map/pallas_call | solution.py:56
  146.2 0.9 copy-done.24
  147.1 1.4 collective-permute-start.16
  148.5 3.3 %collective-permute-start.17 = (bf16[512,128]{1,0:T(8,128)(2,1)S(1)}, bf16[512,128]{1,0:T(8,128)(2,1)S(1)}, u32[]{:S(2)}, u32[]{:S(2)}) collective-permute-start(bf16[512,128]{1,0:T(8,128)(2,1)S(1)} %copy-done.23), channel_id=1, source_target_pairs={{0,16},{8,24},{16,32},{24,40},{32,48},{40,56},{48,0},{56,8},{64,80... | collective-permute-start | bytes 393224 | tf_op jit(solution)/shard_map/ppermute | solution.py:338
  151.8 0.8 collective-permute-start.18
  152.6 3.3 %collective-permute-start.19 = (bf16[512,128]{1,0:T(8,128)(2,1)S(1)}, bf16[512,128]{1,0:T(8,128)(2,1)S(1)}, u32[]{:S(2)}, u32[]{:S(2)}) collective-permute-start(bf16[512,128]{1,0:T(8,128)(2,1)S(1)} %copy-done.21), channel_id=1, source_target_pairs={{0,32},{8,40},{16,48},{24,56},{32,0},{40,8},{48,16},{56,24},{64,96... | collective-permute-start | bytes 393224 | tf_op jit(solution)/shard_map/ppermute | solution.py:338
  155.8 4.2 %shard_map.98 = (bf16[512,512]{1,0:T(8,128)(2,1)}, bf16[4,128,128]{2,1,0:T(8,128)(2,1)}) custom-call(bf16[512,512]{1,0:T(8,128)(2,1)} %q.9, bf16[512,512]{1,0:T(8,128)(2,1)} %get-tuple-element.105.g, f32[512,512]{1,0:T(8,128)} %get-tuple-element.97.normed, f32[4,1,512]{2,1,0:T(1,128)} %copy-done), custom_call_target="tpu_custom_call" | custom-call | tf_op jit(solution)/shard_map/pallas_call | solution.py:56
  160.1 7.1 %all-to-all-start.3 = ((bf16[32,16,128]{2,1,0:T(8,128)(2,1)}), bf16[32,16,128]{2,1,0:T(8,128)(2,1)S(1)}, u32[]{:S(2)}, u32[]{:S(2)}) async-start(bf16[32,16,128]{2,1,0:T(8,128)(2,1)} %bitcast.4), calls=%async_computation.4 | async-start | bytes 262144 | tf_op jit(solution)/shard_map/all_to_all | solution.py:227
  167.2 6.2 %shard_map.100 = (f32[512,512]{1,0:T(8,128)}, bf16[448,512]{1,0:T(8,128)(2,1)}, bf16[448,512]{1,0:T(8,128)(2,1)}, f32[4,1,512]{2,1,0:T(1,128)S(1)}) custom-call(bf16[512,512]{1,0:T(8,128)(2,1)} %q.9, bf16[512,512]{1,0:T(8,128)(2,1)} %get-tuple-element.105.g, bf16[512,512]{1,0:T(8,128)(2,1)} %copy-done.3, bf16[512,512]{1,0:T(8,128)(2,1)} %copy-done.4, ...), custom_call_target="tpu_custom_call" | custom-call | tf_op jit(solution)/shard_map/pallas_call | solution.py:56
  174.0 4.6 %collective-permute-start.14 = (bf16[448,512]{1,0:T(8,128)(2,1)}, bf16[448,512]{1,0:T(8,128)(2,1)S(1)}, u32[]{:S(2)}, u32[]{:S(2)}) collective-permute-start(bf16[448,512]{1,0:T(8,128)(2,1)} %get-tuple-element.113), channel_id=1, source_target_pairs={{8,0},{16,8},{24,16},{32,24},{40,32},{48,40},{56,48},{64,56},{72,6... | collective-permute-start | bytes 1376264 | tf_op jit(solution)/shard_map/ppermute | solution.py:302
  178.6 3.4 %collective-permute-start.15 = (bf16[448,512]{1,0:T(8,128)(2,1)}, bf16[448,512]{1,0:T(8,128)(2,1)S(1)}, u32[]{:S(2)}, u32[]{:S(2)}) collective-permute-start(bf16[448,512]{1,0:T(8,128)(2,1)} %get-tuple-element.114), channel_id=1, source_target_pairs={{8,0},{16,8},{24,16},{32,24},{40,32},{48,40},{56,48},{64,56},{72,6... | collective-permute-start | bytes 1376264 | tf_op jit(solution)/shard_map/ppermute | solution.py:302
  182.0 2.4 %collective-permute-start.20 = (bf16[512,128]{1,0:T(8,128)(2,1)S(1)}, bf16[512,128]{1,0:T(8,128)(2,1)S(1)}, u32[]{:S(2)}, u32[]{:S(2)}) collective-permute-start(bf16[512,128]{1,0:T(8,128)(2,1)S(1)} %copy-done.20), channel_id=1, source_target_pairs={{0,40},{8,48},{16,56},{24,0},{32,8},{40,16},{48,24},{56,32},{64,10... | collective-permute-start | bytes 393224 | tf_op jit(solution)/shard_map/ppermute | solution.py:338
  185.6 0.7 copy-done.13
  186.3 1.6 shard_map.99
  187.9 9.8 %all-to-all-start.4 = ((bf16[32,16,128]{2,1,0:T(8,128)(2,1)}), bf16[32,16,128]{2,1,0:T(8,128)(2,1)S(1)}, u32[]{:S(2)}, u32[]{:S(2)}) async-start(bf16[32,16,128]{2,1,0:T(8,128)(2,1)} %shard_map.99), calls=%async_computation.5 | async-start | bytes 262144 | tf_op jit(solution)/shard_map/all_to_all | solution.py:234
  197.6 13.8 %collective-permute-done.20 = bf16[512,128]{1,0:T(8,128)(2,1)S(1)} collective-permute-done((bf16[512,128]{1,0:T(8,128)(2,1)S(1)}, bf16[512,128]{1,0:T(8,128)(2,1)S(1)}, u32[]{:S(2)}, u32[]{:S(2)}) %collective-permute-start.20) | collective-permute-done | bytes 131104 | tf_op jit(solution)/shard_map/ppermute | solution.py:338
  211.4 2.8 %collective-permute-done.21 = bf16[512,128]{1,0:T(8,128)(2,1)S(1)} collective-permute-done((bf16[512,128]{1,0:T(8,128)(2,1)S(1)}, bf16[512,128]{1,0:T(8,128)(2,1)S(1)}, u32[]{:S(2)}, u32[]{:S(2)}) %collective-permute-start.21) | collective-permute-done | bytes 131104 | tf_op jit(solution)/shard_map/ppermute | solution.py:338
  214.2 1.7 collective-permute-done.22
  215.9 0.8 add_multiply_fusion
  216.8 8.0 %shard_map.101 = (bf16[512,512]{1,0:T(8,128)(2,1)}, f32[512,512]{1,0:T(8,128)}, f32[512,512]{1,0:T(8,128)}) custom-call(bf16[512,512]{1,0:T(8,128)(2,1)} %q.9, bf16[512,512]{1,0:T(8,128)(2,1)} %k.7, bf16[512,512]{1,0:T(8,128)(2,1)} %v.7, bf16[512,512]{1,0:T(8,128)(2,1)} %get-tuple-element.105.g, bf16[512,512]{1,0:T(8,128)(2,1)} %get-tuple-element.102.gl, ...), custom_call_target="tpu_custom_call" | custom-call | tf_op jit(solution)/shard_map/pallas_call | solution.py:56
  224.8 0.8 copy-done.15
  225.8 4.4 %shard_map.102 = (bf16[512,512]{1,0:T(8,128)(2,1)}, bf16[512,512]{1,0:T(8,128)(2,1)}) custom-call(bf16[512,512]{1,0:T(8,128)(2,1)} %k.7, bf16[512,512]{1,0:T(8,128)(2,1)} %v.7, bf16[4,128,128]{2,1,0:T(8,128)(2,1)} %bitcast.8, f32[512,512]{1,0:T(8,128)} %get-tuple-element.111.dk, f32[512,512]{1,0:T(8,128)} %get-tuple-element.112.dv, ...), custom_call_target="tpu_custom_call" | custom-call | tf_op jit(solution)/shard_map/pallas_call | solution.py:56
  (78 shorter events, 5.3 us)
Async XLA Ops:
  7.2 126.7 %all-gather.2.cloned.1.call-start = ((), (), s32[]{:S(2)}) async-start(), calls=%async_computation.6 | async-start | bytes 4325376 | tf_op jit(solution)/shard_map/all_gather | solution.py:370
  11.6 29.1 %collective-permute-start = (bf16[512,512]{1,0:T(8,128)(2,1)}, bf16[512,512]{1,0:T(8,128)(2,1)S(1)}, u32[]{:S(2)}, u32[]{:S(2)}) collective-permute-start(bf16[512,512]{1,0:T(8,128)(2,1)} %k.7), channel_id=1, source_target_pairs={{0,8},{8,16},{16,24},{24,32},{32,40},{40,48},{48,56},{56,64},{64,7... | collective-permute-start | bytes 1572872 | tf_op jit(solution)/shard_map/ppermute | solution.py:302
  15.4 23.0 %all-to-all-start = ((bf16[32,16,128]{2,1,0:T(8,128)(2,1)}), bf16[32,16,128]{2,1,0:T(8,128)(2,1)S(1)}, u32[]{:S(2)}, u32[]{:S(2)}) async-start(bf16[32,16,128]{2,1,0:T(8,128)(2,1)} %bitcast.1), calls=%async_computation | async-start | bytes 262144 | tf_op jit(solution)/shard_map/all_to_all | solution.py:227
  26.1 29.0 %collective-permute-start.1 = (bf16[512,512]{1,0:T(8,128)(2,1)}, bf16[512,512]{1,0:T(8,128)(2,1)S(1)}, u32[]{:S(2)}, u32[]{:S(2)}) collective-permute-start(bf16[512,512]{1,0:T(8,128)(2,1)} %v.7), channel_id=1, source_target_pairs={{0,8},{8,16},{16,24},{24,32},{32,40},{40,48},{48,56},{56,64},{64,7... | collective-permute-start | bytes 1572872 | tf_op jit(solution)/shard_map/ppermute | solution.py:302
  29.5 41.3 %collective-permute-start.3 = (bf16[512,512]{1,0:T(8,128)(2,1)}, bf16[512,512]{1,0:T(8,128)(2,1)S(1)}, u32[]{:S(2)}, u32[]{:S(2)}) collective-permute-start(bf16[512,512]{1,0:T(8,128)(2,1)} %refs_0_.1), channel_id=1, source_target_pairs={{0,2},{1,3},{2,4},{3,5},{4,6},{5,7},{6,0},{7,1},{8,10},{9,11},{10,... | collective-permute-start | bytes 1572872 | tf_op jit(solution)/shard_map/ppermute | solution.py:328
  31.1 39.7 %collective-permute-start.4 = (bf16[512,512]{1,0:T(8,128)(2,1)}, bf16[512,512]{1,0:T(8,128)(2,1)S(1)}, u32[]{:S(2)}, u32[]{:S(2)}) collective-permute-start(bf16[512,512]{1,0:T(8,128)(2,1)} %refs_0_.1), channel_id=1, source_target_pairs={{0,4},{1,5},{2,6},{3,7},{4,0},{5,1},{6,2},{7,3},{8,12},{9,13},{10,... | collective-permute-start | bytes 1572872 | tf_op jit(solution)/shard_map/ppermute | solution.py:328
  33.8 37.0 %collective-permute-start.5 = (bf16[512,512]{1,0:T(8,128)(2,1)}, bf16[512,512]{1,0:T(8,128)(2,1)S(1)}, u32[]{:S(2)}, u32[]{:S(2)}) collective-permute-start(bf16[512,512]{1,0:T(8,128)(2,1)} %refs_0_.1), channel_id=1, source_target_pairs={{0,6},{1,7},{2,0},{3,1},{4,2},{5,3},{6,4},{7,5},{8,14},{9,15},{10,... | collective-permute-start | bytes 1572872 | tf_op jit(solution)/shard_map/ppermute | solution.py:328
  40.7 14.4 %copy-start.3 = (bf16[512,512]{1,0:T(8,128)(2,1)}, bf16[512,512]{1,0:T(8,128)(2,1)S(1)}, u32[]{:S(2)}) copy-start(bf16[512,512]{1,0:T(8,128)(2,1)S(1)} %collective-permute-done.kw) | copy-start | bytes 1572868
  40.7 33.0 %collective-permute-start.2 = (bf16[512,512]{1,0:T(8,128)(2,1)}, bf16[512,512]{1,0:T(8,128)(2,1)S(1)}, u32[]{:S(2)}, u32[]{:S(2)}) collective-permute-start(bf16[512,512]{1,0:T(8,128)(2,1)} %refs_0_.1), channel_id=1, source_target_pairs={{0,0},{1,1},{2,64},{3,65},{4,128},{5,129},{6,192},{7,193},{8,8},{9... | collective-permute-start | bytes 1572872 | tf_op jit(solution)/shard_map/ppermute | solution.py:351
  47.3 17.9 %all-to-all-start.1 = ((bf16[32,16,128]{2,1,0:T(8,128)(2,1)}), bf16[32,16,128]{2,1,0:T(8,128)(2,1)S(1)}, u32[]{:S(2)}, u32[]{:S(2)}) async-start(bf16[32,16,128]{2,1,0:T(8,128)(2,1)} %shard_map.93), calls=%async_computation.1 | async-start | bytes 262144 | tf_op jit(solution)/shard_map/all_to_all | solution.py:234
  70.8 49.5 %copy-start.7 = (bf16[512,512]{1,0:T(8,128)(2,1)}, bf16[512,512]{1,0:T(8,128)(2,1)S(1)}, u32[]{:S(2)}) copy-start(bf16[512,512]{1,0:T(8,128)(2,1)S(1)} %collective-permute-done.3.refs_1_) | copy-start | bytes 1572868
  70.8 4.4 %copy-start.8 = (bf16[512,512]{1,0:T(8,128)(2,1)}, bf16[512,512]{1,0:T(8,128)(2,1)S(1)}, u32[]{:S(2)}) copy-start(bf16[512,512]{1,0:T(8,128)(2,1)S(1)} %collective-permute-done.4.refs_2_) | copy-start | bytes 1572868
  70.8 4.3 %copy-start.9 = (bf16[512,512]{1,0:T(8,128)(2,1)}, bf16[512,512]{1,0:T(8,128)(2,1)S(1)}, u32[]{:S(2)}) copy-start(bf16[512,512]{1,0:T(8,128)(2,1)S(1)} %collective-permute-done.5.refs_3_) | copy-start | bytes 1572868
  75.1 44.7 %copy-start.6 = (bf16[512,512]{1,0:T(8,128)(2,1)S(1)}, bf16[512,512]{1,0:T(8,128)(2,1)}, u32[]{:S(2)}) copy-start(bf16[512,512]{1,0:T(8,128)(2,1)} %refs_0_.1) | copy-start | bytes 1572868
  75.2 44.6 %all-to-all-start.2 = ((bf16[4,512,512]{2,1,0:T(8,128)(2,1)}), bf16[4,512,512]{2,1,0:T(8,128)(2,1)S(1)}, u32[]{:S(2)}, u32[]{:S(2)}) async-start(bf16[4,512,512]{2,1,0:T(8,128)(2,1)} %broadcast_in_dim.2), calls=%async_computation.2 | async-start | bytes 4194304 | tf_op jit(solution)/shard_map/all_to_all | solution.py:310
  82.5 147.6 %reduce-scatter.2.cloned.1.call-start = ((), (), s32[]{:S(2)}) async-start(), calls=%async_computation.7 | async-start | bytes 4718592 | tf_op jit(solution)/shard_map/reduce_scatter | solution.py:452
  82.5 35.6 %collective-permute-start.6 = (bf16[512,512]{1,0:T(8,128)(2,1)}, bf16[512,512]{1,0:T(8,128)(2,1)S(1)}, u32[]{:S(2)}, u32[]{:S(2)}) collective-permute-start(bf16[512,512]{1,0:T(8,128)(2,1)} %get-tuple-element.79.refs_0_), channel_id=1, source_target_pairs={{0,64},{8,72},{16,80},{24,88},{32,96},{40,104},{48,112},{56,120},{... | collective-permute-start | bytes 1572872 | tf_op jit(solution)/shard_map/ppermute | solution.py:319
  83.9 34.2 %collective-permute-start.7 = (bf16[512,512]{1,0:T(8,128)(2,1)}, bf16[512,512]{1,0:T(8,128)(2,1)S(1)}, u32[]{:S(2)}, u32[]{:S(2)}) collective-permute-start(bf16[512,512]{1,0:T(8,128)(2,1)} %get-tuple-element.79.refs_0_), channel_id=1, source_target_pairs={{0,128},{8,136},{16,144},{24,152},{32,160},{40,168},{48,176},{56,1... | collective-permute-start | bytes 1572872 | tf_op jit(solution)/shard_map/ppermute | solution.py:319
  86.3 33.4 %collective-permute-start.8 = (bf16[512,512]{1,0:T(8,128)(2,1)}, bf16[512,512]{1,0:T(8,128)(2,1)}, u32[]{:S(2)}, u32[]{:S(2)}) collective-permute-start(bf16[512,512]{1,0:T(8,128)(2,1)} %get-tuple-element.79.refs_0_), channel_id=1, source_target_pairs={{0,192},{8,200},{16,208},{24,216},{32,224},{40,232},{48,240},{56,2... | collective-permute-start | bytes 1572872 | tf_op jit(solution)/shard_map/ppermute | solution.py:319
  118.9 0.8 copy-start.11
  119.7 4.4 %copy-start.2 = (bf16[4,512,512]{2,1,0:T(8,128)(2,1)}, bf16[4,512,512]{2,1,0:T(8,128)(2,1)S(1)}, u32[]{:S(2)}) copy-start(bf16[4,512,512]{2,1,0:T(8,128)(2,1)S(1)} %all-to-all-done.2.mine) | copy-start | bytes 6291460
  119.7 4.4 %collective-permute-start.9 = (bf16[4,512,512]{2,1,0:T(8,128)(2,1)S(1)}, bf16[4,512,512]{2,1,0:T(8,128)(2,1)}, u32[]{:S(2)}, u32[]{:S(2)}) collective-permute-start(bf16[4,512,512]{2,1,0:T(8,128)(2,1)S(1)} %all-to-all-done.2.mine), channel_id=1, source_target_pairs={{0,1},{1,0},{2,3},{3,2},{4,5},{5,4},{6,7},{7,6},{8,9},{9,8},{10,11... | collective-permute-start | bytes 6291464 | tf_op jit(solution)/shard_map/ppermute | solution.py:334
  119.8 14.1 %collective-permute-start.10 = (bf16[512,512]{1,0:T(8,128)(2,1)S(1)}, bf16[512,512]{1,0:T(8,128)(2,1)}, u32[]{:S(2)}, u32[]{:S(2)}) collective-permute-start(bf16[512,512]{1,0:T(8,128)(2,1)S(1)} %copy-done.6), channel_id=1, source_target_pairs={{0,1},{1,0},{2,3},{3,2},{4,5},{5,4},{6,7},{7,6},{8,9},{9,8},{10,11... | collective-permute-start | bytes 1572872 | tf_op jit(solution)/shard_map/ppermute | solution.py:334
  120.3 13.6 %collective-permute-start.11 = (bf16[512,512]{1,0:T(8,128)(2,1)S(1)}, bf16[512,512]{1,0:T(8,128)(2,1)}, u32[]{:S(2)}, u32[]{:S(2)}) collective-permute-start(bf16[512,512]{1,0:T(8,128)(2,1)S(1)} %collective-permute-done.3.refs_1_), channel_id=1, source_target_pairs={{0,1},{1,0},{2,3},{3,2},{4,5},{5,4},{6,7},{7,6},{8,9},{9,8},{10,11... | collective-permute-start | bytes 1572872 | tf_op jit(solution)/shard_map/ppermute | solution.py:334
  120.4 13.5 %collective-permute-start.12 = (bf16[512,512]{1,0:T(8,128)(2,1)}, bf16[512,512]{1,0:T(8,128)(2,1)}, u32[]{:S(2)}, u32[]{:S(2)}) collective-permute-start(bf16[512,512]{1,0:T(8,128)(2,1)} %copy-done.8), channel_id=1, source_target_pairs={{0,1},{1,0},{2,3},{3,2},{4,5},{5,4},{6,7},{7,6},{8,9},{9,8},{10,11... | collective-permute-start | bytes 1572872 | tf_op jit(solution)/shard_map/ppermute | solution.py:334
  120.8 13.1 %collective-permute-start.13 = (bf16[512,512]{1,0:T(8,128)(2,1)}, bf16[512,512]{1,0:T(8,128)(2,1)}, u32[]{:S(2)}, u32[]{:S(2)}) collective-permute-start(bf16[512,512]{1,0:T(8,128)(2,1)} %copy-done.9), channel_id=1, source_target_pairs={{0,1},{1,0},{2,3},{3,2},{4,5},{5,4},{6,7},{7,6},{8,9},{9,8},{10,11... | collective-permute-start | bytes 1572872 | tf_op jit(solution)/shard_map/ppermute | solution.py:334
  146.2 0.9 copy-start.24
  146.2 2.3 copy-start.23
  146.2 5.6 %copy-start.22 = (bf16[512,128]{1,0:T(8,128)(2,1)S(1)}, bf16[512,128]{1,0:T(8,128)(2,1)}, u32[]{:S(2)}) copy-start(bf16[512,128]{1,0:T(8,128)(2,1)} %get-tuple-element.120) | copy-start | bytes 393220
  146.2 6.4 %copy-start.21 = (bf16[512,128]{1,0:T(8,128)(2,1)S(1)}, bf16[512,128]{1,0:T(8,128)(2,1)}, u32[]{:S(2)}) copy-start(bf16[512,128]{1,0:T(8,128)(2,1)} %get-tuple-element.121) | copy-start | bytes 393220
  147.1 31.5 %collective-permute-start.16 = (bf16[512,128]{1,0:T(8,128)(2,1)S(1)}, bf16[512,128]{1,0:T(8,128)(2,1)S(1)}, u32[]{:S(2)}, u32[]{:S(2)}) collective-permute-start(bf16[512,128]{1,0:T(8,128)(2,1)S(1)} %copy-done.24), channel_id=1, source_target_pairs={{0,8},{8,16},{16,24},{24,32},{32,40},{40,48},{48,56},{56,0},{64,72... | collective-permute-start | bytes 393224 | tf_op jit(solution)/shard_map/ppermute | solution.py:338
  148.5 33.5 %collective-permute-start.17 = (bf16[512,128]{1,0:T(8,128)(2,1)S(1)}, bf16[512,128]{1,0:T(8,128)(2,1)S(1)}, u32[]{:S(2)}, u32[]{:S(2)}) collective-permute-start(bf16[512,128]{1,0:T(8,128)(2,1)S(1)} %copy-done.23), channel_id=1, source_target_pairs={{0,16},{8,24},{16,32},{24,40},{32,48},{40,56},{48,0},{56,8},{64,80... | collective-permute-start | bytes 393224 | tf_op jit(solution)/shard_map/ppermute | solution.py:338
  151.8 32.7 %collective-permute-start.18 = (bf16[512,128]{1,0:T(8,128)(2,1)S(1)}, bf16[512,128]{1,0:T(8,128)(2,1)S(1)}, u32[]{:S(2)}, u32[]{:S(2)}) collective-permute-start(bf16[512,128]{1,0:T(8,128)(2,1)S(1)} %copy-done.22), channel_id=1, source_target_pairs={{0,24},{8,32},{16,40},{24,48},{32,56},{40,0},{48,8},{56,16},{64,88... | collective-permute-start | bytes 393224 | tf_op jit(solution)/shard_map/ppermute | solution.py:338
  152.6 32.4 %collective-permute-start.19 = (bf16[512,128]{1,0:T(8,128)(2,1)S(1)}, bf16[512,128]{1,0:T(8,128)(2,1)S(1)}, u32[]{:S(2)}, u32[]{:S(2)}) collective-permute-start(bf16[512,128]{1,0:T(8,128)(2,1)S(1)} %copy-done.21), channel_id=1, source_target_pairs={{0,32},{8,40},{16,48},{24,56},{32,0},{40,8},{48,16},{56,24},{64,96... | collective-permute-start | bytes 393224 | tf_op jit(solution)/shard_map/ppermute | solution.py:338
  160.1 25.5 %all-to-all-start.3 = ((bf16[32,16,128]{2,1,0:T(8,128)(2,1)}), bf16[32,16,128]{2,1,0:T(8,128)(2,1)S(1)}, u32[]{:S(2)}, u32[]{:S(2)}) async-start(bf16[32,16,128]{2,1,0:T(8,128)(2,1)} %bitcast.4), calls=%async_computation.4 | async-start | bytes 262144 | tf_op jit(solution)/shard_map/all_to_all | solution.py:227
  167.2 14.8 %copy-start.20 = (bf16[512,128]{1,0:T(8,128)(2,1)S(1)}, bf16[512,128]{1,0:T(8,128)(2,1)}, u32[]{:S(2)}) copy-start(bf16[512,128]{1,0:T(8,128)(2,1)} %get-tuple-element.122) | copy-start | bytes 393220
  167.2 17.3 %copy-start.19 = (bf16[512,128]{1,0:T(8,128)(2,1)S(1)}, bf16[512,128]{1,0:T(8,128)(2,1)}, u32[]{:S(2)}) copy-start(bf16[512,128]{1,0:T(8,128)(2,1)} %get-tuple-element.123) | copy-start | bytes 393220
  167.2 17.8 %copy-start.18 = (bf16[512,128]{1,0:T(8,128)(2,1)S(1)}, bf16[512,128]{1,0:T(8,128)(2,1)}, u32[]{:S(2)}) copy-start(bf16[512,128]{1,0:T(8,128)(2,1)} %get-tuple-element.124) | copy-start | bytes 393220
  167.2 48.7 %copy-start.17 = (bf16[512,128]{1,0:T(8,128)(2,1)S(1)}, bf16[512,128]{1,0:T(8,128)(2,1)}, u32[]{:S(2)}) copy-start(bf16[512,128]{1,0:T(8,128)(2,1)} %get-tuple-element.117) | copy-start | bytes 393220
  174.0 50.7 %collective-permute-start.14 = (bf16[448,512]{1,0:T(8,128)(2,1)}, bf16[448,512]{1,0:T(8,128)(2,1)S(1)}, u32[]{:S(2)}, u32[]{:S(2)}) collective-permute-start(bf16[448,512]{1,0:T(8,128)(2,1)} %get-tuple-element.113), channel_id=1, source_target_pairs={{8,0},{16,8},{24,16},{32,24},{40,32},{48,40},{56,48},{64,56},{72,6... | collective-permute-start | bytes 1376264 | tf_op jit(solution)/shard_map/ppermute | solution.py:302
  178.6 46.2 %collective-permute-start.15 = (bf16[448,512]{1,0:T(8,128)(2,1)}, bf16[448,512]{1,0:T(8,128)(2,1)S(1)}, u32[]{:S(2)}, u32[]{:S(2)}) collective-permute-start(bf16[448,512]{1,0:T(8,128)(2,1)} %get-tuple-element.114), channel_id=1, source_target_pairs={{8,0},{16,8},{24,16},{32,24},{40,32},{48,40},{56,48},{64,56},{72,6... | collective-permute-start | bytes 1376264 | tf_op jit(solution)/shard_map/ppermute | solution.py:302
  182.0 29.4 %collective-permute-start.20 = (bf16[512,128]{1,0:T(8,128)(2,1)S(1)}, bf16[512,128]{1,0:T(8,128)(2,1)S(1)}, u32[]{:S(2)}, u32[]{:S(2)}) collective-permute-start(bf16[512,128]{1,0:T(8,128)(2,1)S(1)} %copy-done.20), channel_id=1, source_target_pairs={{0,40},{8,48},{16,56},{24,0},{32,8},{40,16},{48,24},{56,32},{64,10... | collective-permute-start | bytes 393224 | tf_op jit(solution)/shard_map/ppermute | solution.py:338
  184.5 29.8 %collective-permute-start.21 = (bf16[512,128]{1,0:T(8,128)(2,1)S(1)}, bf16[512,128]{1,0:T(8,128)(2,1)S(1)}, u32[]{:S(2)}, u32[]{:S(2)}) collective-permute-start(bf16[512,128]{1,0:T(8,128)(2,1)S(1)} %copy-done.19), channel_id=1, source_target_pairs={{0,48},{8,56},{16,0},{24,8},{32,16},{40,24},{48,32},{56,40},{64,11... | collective-permute-start | bytes 393224 | tf_op jit(solution)/shard_map/ppermute | solution.py:338
  185.0 30.9 %collective-permute-start.22 = (bf16[512,128]{1,0:T(8,128)(2,1)S(1)}, bf16[512,128]{1,0:T(8,128)(2,1)S(1)}, u32[]{:S(2)}, u32[]{:S(2)}) collective-permute-start(bf16[512,128]{1,0:T(8,128)(2,1)S(1)} %copy-done.18), channel_id=1, source_target_pairs={{0,56},{8,0},{16,8},{24,16},{32,24},{40,32},{48,40},{56,48},{64,12... | collective-permute-start | bytes 393224 | tf_op jit(solution)/shard_map/ppermute | solution.py:338
  187.9 37.0 %all-to-all-start.4 = ((bf16[32,16,128]{2,1,0:T(8,128)(2,1)}), bf16[32,16,128]{2,1,0:T(8,128)(2,1)S(1)}, u32[]{:S(2)}, u32[]{:S(2)}) async-start(bf16[32,16,128]{2,1,0:T(8,128)(2,1)} %shard_map.99), calls=%async_computation.5 | async-start | bytes 262144 | tf_op jit(solution)/shard_map/all_to_all | solution.py:234
  224.8 0.8 copy-start.15
  224.8 0.9 copy-start.16
  224.8 1.0 copy-start.12
  (7 other events, 4.7 us)
Sparse Core Ops, SparseCore 0:
  10.5 110.7 all-gather.1
  146.4 41.3 reduce-scatter.1

commit v7 on v6

--- a/solution.py
+++ b/solution.py
@@ -144,7 +144,7 @@
     mixed[...] = out.T.astype(BF16)
 
 
-def far_kernel(q, g, kw, vw, far, window, dq, dk, dv, delta, ds):
+def far_kernel(q, g, kw, vw, far, window, dq, back, delta, ds):
     g_t = flip(g[...])
     d = jnp.sum(g_t * window[...], axis=0, keepdims=True)
     delta[0] = d
@@ -160,11 +160,11 @@
         dk_j = nn(ds[lo:hi, 0:hi], q[0:hi, :]).astype(BF16)
         dv_j = nn(far[0, lo:hi, 0:hi], g[0:hi, :]).astype(BF16)
         if j == 0:
-            dk[0 : hi - BLOCK, :] = dk_j[BLOCK:]
-            dv[0 : hi - BLOCK, :] = dv_j[BLOCK:]
+            back[0 : hi - BLOCK, :] = dk_j[BLOCK:]
+            back[EDGE : EDGE + hi - BLOCK, :] = dv_j[BLOCK:]
         else:
-            dk[lo - BLOCK : hi - BLOCK, :] = dk_j
-            dv[lo - BLOCK : hi - BLOCK, :] = dv_j
+            back[lo - BLOCK : hi - BLOCK, :] = dk_j
+            back[EDGE + lo - BLOCK : EDGE + hi - BLOCK, :] = dv_j
 
 
 def lin_kernel(q, g, normed, inverse, grad_lin, sums):
@@ -374,7 +374,7 @@
     )(keys, values)
     local, k_out, v_out = lax.optimization_barrier((local, keys, values))
     kh, vh = shifted(k_out, 1), shifted(v_out, 1)
-    before, grad_out, _ = carry_states(local, False, grad_y)
+    before, (grad_out, kh, vh, hopped), _ = carry_states(local, False, (grad_y, kh, vh, hopped))
     turned_grad = turn_xy(grad_out)
 
     sq = large((heads, rows, rows), BF16)
@@ -391,7 +391,8 @@
         prefetch=1,
     )(seq, queries, keys, values, kh, vh)
 
-    before, window = lax.optimization_barrier((before, window))
+    before, window, turned_grad = lax.optimization_barrier((before, window, turned_grad))
+    mine = spread(turned_grad, "head", X_GROUPS)
     normed, inverse, mixed_t, mixed = call(
         mixed_kernel,
         heads,
@@ -407,8 +408,7 @@
         size=5 << 20,
     )(queries, before, window, intra)
 
-    turned_grad, hopped, mixed_t = lax.optimization_barrier((turned_grad, hopped, mixed_t))
-    mine = spread(turned_grad, "head", X_GROUPS)
+    hopped, mixed_t = lax.optimization_barrier((hopped, mixed_t))
     across_y = [mixed_t] + [hop_y(mixed_t, by) for by in range(1, YS)]
     mine, across_y = lax.optimization_barrier((mine, across_y))
     grads = [grad_y] + hopped
@@ -461,25 +461,22 @@
         size=3 << 20,
     )(queries, grad_mixed, normed, inverse)
     local_back, g_far = lax.optimization_barrier((local_back, grad_mixed))
-    edge_grad = large((edge, width), BF16)
-    dq_far, far_k, far_v, delta = call(
+    dq_far, back, delta = call(
         far_kernel,
         heads,
         [col, col, col, col, tri, turned],
-        [turned, columns(edge), columns(edge), line],
-        [flat_t, edge_grad, edge_grad, shape((heads, 1, rows), F32)],
+        [turned, columns(2 * edge), line],
+        [flat_t, large((2 * edge, width), BF16), shape((heads, 1, rows), F32)],
         scratch=[pltpu.VMEM((rows, rows), BF16)],
         flops=8 * mm // 8,
         size=8 << 20,
     )(queries, g_far, kh, vh, far, window)
-    back_k, back_v = shifted(far_k, -1), shifted(far_v, -1)
-
+    back = shifted(back, -1)
+
+    parts, local_back = lax.optimization_barrier((parts, local_back))
+    sums = [parts[0]] + [hop_z(parts[by], by) for by in range(1, ZS)]
     later, grad_lin, _ = carry_states(local_back, True, grad_lin)
 
-    total = parts[0].astype(F32)
-    for by in range(1, ZS):
-        total = total + hop_z(parts[by], by).astype(F32)
-    projection_sensitivity = total * tokens_all ** (-0.5)
 
     grad_queries, near_k, near_v = call(
         near_kernel,
@@ -495,12 +492,15 @@
     grad_keys, grad_values = call(
         last_kernel,
         heads,
-        [col, col, st, col, col, columns(edge), columns(edge)],
+        [col, col, st, col, col, columns(edge), columns(edge, 1)],
         [col, col],
         [large((rows, width), BF16)] * 2,
         flops=mm // 2,
         size=5 << 20,
-    )(keys, values, later, near_k, near_v, back_k, back_v)
+    )(keys, values, later, near_k, near_v, back, back)
+    sums, grad_keys = lax.optimization_barrier((sums, grad_keys))
+    total = sum(part.astype(F32) for part in sums)
+    projection_sensitivity = total * tokens_all ** (-0.5)
     return (mixer_result, grad_queries, grad_keys, grad_values, projection_sensitivity)
 
 

time: 240 us -> 239 us (level)
  blocking collectives: 0 us -> 25.8 us
  starting transfers between devices: 90 us -> 73.5 us
  waiting for transfers between devices: 57.4 us -> 51.6 us
  local copies, waits for them, and re-layouts: 8.89 us -> 5.72 us
    all_to_all x0 -> x1, blocking collectives: none -> 25.8 us  [carry_states(): met = lax.all_to_all(pieces, 'seq', 0, 0)]
    ppermute x7, waiting for transfers between devices: 18.3 us -> 3.72 us  [hop_z(): lax.ppermute(shard, 'seq', [(y * ZS + z, y * ZS + (z + by) % ZS) for y in...]
    all_to_all x2 -> x1, waiting for transfers between devices: 3.2 us -> 13.6 us  [carry_states(): met = lax.all_to_all(pieces, 'seq', 0, 0)]
    all_to_all x2 -> x1, starting transfers between devices: 17.8 us -> 8.28 us  [carry_states(): met = lax.all_to_all(pieces, 'seq', 0, 0)]
    all_to_all x2, waiting for transfers between devices: 0.01 us -> 5.24 us  [carry_states(): lax.all_to_all(done, 'seq', 0, 0).reshape(local.shape)]
    ppermute x4 -> x3, starting transfers between devices: 15.1 us -> 10.2 us  [shifted(): return lax.ppermute(shard, 'seq', pairs)]
    ppermute x3, waiting for transfers between devices: 29.3 us -> 25.2 us  [hop_y(): lax.ppermute(shard, 'seq', [(y * ZS + z, (y + by) % YS * ZS + z) for y in...]
    all_to_all x1, starting transfers between devices: 7.38 us -> 3.66 us  [exchange(): return lax.all_to_all(pieces, axis, 0, 0, axis_index_groups=groups)]
  transfers between devices with their start and end apart: 30 -> 28, of which waited for: 7 -> 6; matrix products, arithmetic and copies ran while one was open for 1% -> 1% of each run, Pallas kernels for 22% -> 22%
where the time goes in v7:
time: 239 us; the launch traced here: 237 us
  starting transfers between devices  73.5 us (31%)
  Pallas kernels  64.7 us (27%)
  waiting for transfers between devices  51.6 us (22%)
  blocking collectives  25.8 us (11%)
  between operations  14.4 us (6%)
  local copies, waits for them, and re-layouts  5.72 us (2%)
    pallas_call x9, Pallas kernels, call(): run(*args[:prefetch], *(kept(a) for a in args[prefetch:]))  61.5 us
    all_to_all x1, blocking collectives, carry_states(): met = lax.all_to_all(pieces, 'seq', 0, 0)  25.8 us
    ppermute x3, waiting for transfers between devices, hop_y(): lax.ppermute(shard, 'seq', [(y * ZS + z, (y + by) % YS * ZS + z) for y in...  25.2 us
    all_to_all x2, starting transfers between devices, carry_states(): lax.all_to_all(done, 'seq', 0, 0).reshape(local.shape)  16.5 us
    ppermute x7, starting transfers between devices, hop_z(): lax.ppermute(shard, 'seq', [(y * ZS + z, y * ZS + (z + by) % ZS) for y in...  15.6 us
    all_to_all x1, waiting for transfers between devices, carry_states(): met = lax.all_to_all(pieces, 'seq', 0, 0)  13.6 us
    ppermute x3, starting transfers between devices, shifted(): return lax.ppermute(shard, 'seq', pairs)  10.2 us
    all_to_all x1, starting transfers between devices, carry_states(): met = lax.all_to_all(pieces, 'seq', 0, 0)  8.28 us
  transfers between devices with their start and end apart: 28, of which 6 were waited for; matrix products, arithmetic and copies ran while one was open for 1% of the time, Pallas kernels for 22%

profile of v7, /device:TPU:16, one launch (start us, length us, event | category | flops | bytes accessed | tf_op | source)
XLA Modules:
  0.0 236.6 jit_solution(7619261082438498506)
XLA Ops:
  7.2 0.7 all-gather.2.cloned.1.call-update
  7.9 2.7 %shard_map.92 = bf16[4,128,128]{2,1,0:T(8,128)(2,1)S(1)} custom-call(bf16[512,512]{1,0:T(8,128)(2,1)} %k.7, bf16[512,512]{1,0:T(8,128)(2,1)} %v.7), custom_call_target="tpu_custom_call" | custom-call | tf_op jit(solution)/shard_map/pallas_call | solution.py:56
  10.6 3.8 %collective-permute-start = (bf16[512,512]{1,0:T(8,128)(2,1)}, bf16[512,512]{1,0:T(8,128)(2,1)S(1)}, u32[]{:S(2)}, u32[]{:S(2)}) collective-permute-start(bf16[512,512]{1,0:T(8,128)(2,1)} %k.7), channel_id=1, source_target_pairs={{0,8},{8,16},{16,24},{24,32},{32,40},{40,48},{48,56},{56,64},{64,7... | collective-permute-start | bytes 1572872 | tf_op jit(solution)/shard_map/ppermute | solution.py:302
  14.5 3.8 %collective-permute-start.1 = (bf16[512,512]{1,0:T(8,128)(2,1)}, bf16[512,512]{1,0:T(8,128)(2,1)S(1)}, u32[]{:S(2)}, u32[]{:S(2)}) collective-permute-start(bf16[512,512]{1,0:T(8,128)(2,1)} %v.7), channel_id=1, source_target_pairs={{0,8},{8,16},{16,24},{24,32},{32,40},{40,48},{48,56},{56,64},{64,7... | collective-permute-start | bytes 1572872 | tf_op jit(solution)/shard_map/ppermute | solution.py:302
  18.3 1.6 collective-permute-start.2
  19.9 2.7 %collective-permute-start.3 = (bf16[512,512]{1,0:T(8,128)(2,1)}, bf16[512,512]{1,0:T(8,128)(2,1)S(1)}, u32[]{:S(2)}, u32[]{:S(2)}) collective-permute-start(bf16[512,512]{1,0:T(8,128)(2,1)} %refs_0_.1), channel_id=1, source_target_pairs={{0,4},{1,5},{2,6},{3,7},{4,0},{5,1},{6,2},{7,3},{8,12},{9,13},{10,... | collective-permute-start | bytes 1572872 | tf_op jit(solution)/shard_map/ppermute | solution.py:328
  22.6 1.4 collective-permute-start.4
  24.0 25.8 %all_to_all.25.x = bf16[32,16,128]{2,1,0:T(8,128)(2,1)} all-to-all(bf16[32,16,128]{2,1,0:T(8,128)(2,1)S(1)} %bitcast.6), channel_id=1, replica_groups=mesh['seq'=32,'head'=8] {'seq'}, dimensions={0} | all-to-all | bytes 262144 | tf_op jit(solution)/shard_map/all_to_all | solution.py:227
  49.8 1.6 shard_map.93
  51.5 6.8 %collective-permute-start.5 = (bf16[512,512]{1,0:T(8,128)(2,1)}, bf16[512,512]{1,0:T(8,128)(2,1)S(1)}, u32[]{:S(2)}, u32[]{:S(2)}) collective-permute-start(bf16[512,512]{1,0:T(8,128)(2,1)} %refs_0_.1), channel_id=1, source_target_pairs={{0,0},{1,1},{2,64},{3,65},{4,128},{5,129},{6,192},{7,193},{8,8},{9... | collective-permute-start | bytes 1572872 | tf_op jit(solution)/shard_map/ppermute | solution.py:351
  58.3 6.8 %all-to-all-start.1 = ((bf16[32,16,128]{2,1,0:T(8,128)(2,1)}), bf16[32,16,128]{2,1,0:T(8,128)(2,1)S(1)}, u32[]{:S(2)}, u32[]{:S(2)}) async-start(bf16[32,16,128]{2,1,0:T(8,128)(2,1)} %shard_map.93), calls=%async_computation.1 | async-start | bytes 262144 | tf_op jit(solution)/shard_map/all_to_all | solution.py:234
  65.1 9.3 %shard_map.94 = (bf16[4,512,512]{2,1,0:T(8,128)(2,1)}, bf16[4,512,512]{2,1,0:T(8,128)(2,1)}, bf16[4,512,512]{2,1,0:T(8,128)(2,1)}, f32[512,512]{1,0:T(8,128)}, f32[512,512]{1,0:T(8,128)}) custom-call(s32[1]{0:T(128)} %bitcast.3.place, bf16[512,512]{1,0:T(8,128)(2,1)} %q.9, bf16[512,512]{1,0:T(8,128)(2,1)} %k.7, bf16[512,512]{1,0:T(8,128)(2,1)} %v.7, ...), custom_call_target="tpu_custom_call" | custom-call | tf_op jit(solution)/shard_map/pallas_call | solution.py:56
  74.4 5.2 %all-to-all-done.1 = bf16[32,16,128]{2,1,0:T(8,128)(2,1)S(1)} async-done(((bf16[32,16,128]{2,1,0:T(8,128)(2,1)}), bf16[32,16,128]{2,1,0:T(8,128)(2,1)S(1)}, u32[]{:S(2)}, u32[]{:S(2)}) %all-to-all-start.1) | async-done | bytes 131104 | tf_op jit(solution)/shard_map/all_to_all | solution.py:234
  79.7 1.5 broadcast_in_dim.2
  81.2 3.7 %all-to-all-start.2 = ((bf16[4,512,512]{2,1,0:T(8,128)(2,1)}), bf16[4,512,512]{2,1,0:T(8,128)(2,1)S(1)}, u32[]{:S(2)}, u32[]{:S(2)}) async-start(bf16[4,512,512]{2,1,0:T(8,128)(2,1)} %broadcast_in_dim.2), calls=%async_computation.2 | async-start | bytes 4194304 | tf_op jit(solution)/shard_map/all_to_all | solution.py:310
  84.9 4.5 %shard_map.95 = (f32[512,512]{1,0:T(8,128)}, f32[4,1,512]{2,1,0:T(1,128)S(1)}, bf16[512,512]{1,0:T(8,128)(2,1)}, bf16[512,512]{1,0:T(8,128)(2,1)}) custom-call(bf16[512,512]{1,0:T(8,128)(2,1)} %q.9, bf16[4,128,128]{2,1,0:T(8,128)(2,1)} %bitcast.7, f32[512,512]{1,0:T(8,128)} %get-tuple-element.96.window, f32[512,512]{1,0:T(8,128)} %get-tuple-element.97.intra), custom_call_target="tpu_custom_call" | custom-call | tf_op jit(solution)/shard_map/pallas_call | solution.py:56
  89.4 0.6 copy-done
  90.0 1.6 collective-permute-start.6
  91.6 1.5 collective-permute-start.7
  93.1 2.4 %collective-permute-start.8 = (bf16[512,512]{1,0:T(8,128)(2,1)}, bf16[512,512]{1,0:T(8,128)(2,1)}, u32[]{:S(2)}, u32[]{:S(2)}) collective-permute-start(bf16[512,512]{1,0:T(8,128)(2,1)} %get-tuple-element.106.refs_0_), channel_id=1, source_target_pairs={{0,192},{8,200},{16,208},{24,216},{32,224},{40,232},{48,240},{56,2... | collective-permute-start | bytes 1572872 | tf_op jit(solution)/shard_map/ppermute | solution.py:319
  95.5 25.2 %collective-permute-done.6.refs_1_ = bf16[512,512]{1,0:T(8,128)(2,1)S(1)} collective-permute-done((bf16[512,512]{1,0:T(8,128)(2,1)}, bf16[512,512]{1,0:T(8,128)(2,1)S(1)}, u32[]{:S(2)}, u32[]{:S(2)}) %collective-permute-start.6) | collective-permute-done | bytes 524320 | tf_op jit(solution)/shard_map/ppermute | solution.py:319
  120.7 0.8 copy-done.12
  121.5 0.8 copy-done.13
  123.6 3.1 %collective-permute-done.9.other = bf16[4,512,512]{2,1,0:T(8,128)(2,1)} collective-permute-done((bf16[4,512,512]{2,1,0:T(8,128)(2,1)S(1)}, bf16[4,512,512]{2,1,0:T(8,128)(2,1)}, u32[]{:S(2)}, u32[]{:S(2)}) %collective-permute-start.9) | collective-permute-done | bytes 2097184 | tf_op jit(solution)/shard_map/ppermute | solution.py:334
  126.7 9.8 %shard_map.96 = (bf16[512,128]{1,0:T(8,128)(2,1)}, bf16[512,128]{1,0:T(8,128)(2,1)}, bf16[512,128]{1,0:T(8,128)(2,1)}, bf16[512,128]{1,0:T(8,128)(2,1)}, bf16[51...) custom-call(s32[3]{0:T(128)S(1)} %pad_add_fusion.place, ...), custom_call_target="tpu_custom_call" | custom-call | tf_op jit(solution)/shard_map/pallas_call | solution.py:56
  136.6 12.4 %shard_map.97 = (bf16[512,4096]{1,0:T(8,128)(2,1)}, bf16[512,512]{1,0:T(8,128)(2,1)}) custom-call(s32[1]{0:T(128)} %bitcast.head, bf16[512,512]{1,0:T(8,128)(2,1)} %get-tuple-element.98.mixed, bf16[512,4096]{1,0:T(8,128)(2,1)} %all-gather.2.cloned.1.call-done.w, bf16[512,512]{1,0:T(8,128)(2,1)} %refs_0_.1, bf16[512,512]{1,0:T(8,128)(2,1)} %copy-done.8, ...), custom_call_target="tpu_custom_call" | custom-call | tf_op jit(solution)/shard_map/pallas_call | solution.py:56
  149.0 4.2 %shard_map.98 = (bf16[512,512]{1,0:T(8,128)(2,1)}, bf16[4,128,128]{2,1,0:T(8,128)(2,1)}) custom-call(bf16[512,512]{1,0:T(8,128)(2,1)} %q.9, bf16[512,512]{1,0:T(8,128)(2,1)} %get-tuple-element.141.g, f32[512,512]{1,0:T(8,128)} %get-tuple-element.132.normed, f32[4,1,512]{2,1,0:T(1,128)} %copy-done), custom_call_target="tpu_custom_call" | custom-call | tf_op jit(solution)/shard_map/pallas_call | solution.py:56
  153.3 6.2 %shard_map.100 = (f32[512,512]{1,0:T(8,128)}, bf16[896,512]{1,0:T(8,128)(2,1)}, f32[4,1,512]{2,1,0:T(1,128)S(1)}) custom-call(bf16[512,512]{1,0:T(8,128)(2,1)} %q.9, bf16[512,512]{1,0:T(8,128)(2,1)} %get-tuple-element.141.g, bf16[512,512]{1,0:T(8,128)(2,1)} %copy-done.4, bf16[512,512]{1,0:T(8,128)(2,1)} %copy-done.5, ...), custom_call_target="tpu_custom_call" | custom-call | tf_op jit(solution)/shard_map/pallas_call | solution.py:56
  159.5 0.6 copy-done.1
  160.1 2.5 %collective-permute-start.21 = (bf16[896,512]{1,0:T(8,128)(2,1)}, bf16[896,512]{1,0:T(8,128)(2,1)S(1)}, u32[]{:S(2)}, u32[]{:S(2)}) collective-permute-start(bf16[896,512]{1,0:T(8,128)(2,1)} %get-tuple-element.157), channel_id=1, source_target_pairs={{8,0},{16,8},{24,16},{32,24},{40,32},{48,40},{56,48},{64,56},{72,6... | collective-permute-start | bytes 2752520 | tf_op jit(solution)/shard_map/ppermute | solution.py:302
  162.6 8.3 %all-to-all-start.3 = ((bf16[32,16,128]{2,1,0:T(8,128)(2,1)}), bf16[32,16,128]{2,1,0:T(8,128)(2,1)S(1)}, u32[]{:S(2)}, u32[]{:S(2)}) async-start(bf16[32,16,128]{2,1,0:T(8,128)(2,1)} %bitcast.4), calls=%async_computation.4 | async-start | bytes 262144 | tf_op jit(solution)/shard_map/all_to_all | solution.py:227
  170.9 1.5 collective-permute-start.14
  172.4 2.4 collective-permute-start.15
  174.8 13.6 %all-to-all-done.3.x = bf16[32,16,128]{2,1,0:T(8,128)(2,1)S(1)} async-done(((bf16[32,16,128]{2,1,0:T(8,128)(2,1)}), bf16[32,16,128]{2,1,0:T(8,128)(2,1)S(1)}, u32[]{:S(2)}, u32[]{:S(2)}) %all-to-all-start.3) | async-done | bytes 131104 | tf_op jit(solution)/shard_map/all_to_all | solution.py:227
  188.4 0.7 copy-done.15
  189.1 1.6 shard_map.99
  190.7 9.7 %all-to-all-start.4 = ((bf16[32,16,128]{2,1,0:T(8,128)(2,1)}), bf16[32,16,128]{2,1,0:T(8,128)(2,1)S(1)}, u32[]{:S(2)}, u32[]{:S(2)}) async-start(bf16[32,16,128]{2,1,0:T(8,128)(2,1)} %shard_map.99), calls=%async_computation.5 | async-start | bytes 262144 | tf_op jit(solution)/shard_map/all_to_all | solution.py:234
  200.4 3.3 %collective-permute-start.16 = (bf16[512,128]{1,0:T(8,128)(2,1)S(1)}, bf16[512,128]{1,0:T(8,128)(2,1)S(1)}, u32[]{:S(2)}, u32[]{:S(2)}) collective-permute-start(bf16[512,128]{1,0:T(8,128)(2,1)S(1)} %copy-done.21), channel_id=1, source_target_pairs={{0,24},{8,32},{16,40},{24,48},{32,56},{40,0},{48,8},{56,16},{64,88... | collective-permute-start | bytes 393224 | tf_op jit(solution)/shard_map/ppermute | solution.py:338
  203.7 2.7 %collective-permute-start.17 = (bf16[512,128]{1,0:T(8,128)(2,1)S(1)}, bf16[512,128]{1,0:T(8,128)(2,1)S(1)}, u32[]{:S(2)}, u32[]{:S(2)}) collective-permute-start(bf16[512,128]{1,0:T(8,128)(2,1)S(1)} %copy-done.20), channel_id=1, source_target_pairs={{0,32},{8,40},{16,48},{24,56},{32,0},{40,8},{48,16},{56,24},{64,96... | collective-permute-start | bytes 393224 | tf_op jit(solution)/shard_map/ppermute | solution.py:338
  206.4 4.5 %collective-permute-start.18 = (bf16[512,128]{1,0:T(8,128)(2,1)S(1)}, bf16[512,128]{1,0:T(8,128)(2,1)S(1)}, u32[]{:S(2)}, u32[]{:S(2)}) collective-permute-start(bf16[512,128]{1,0:T(8,128)(2,1)S(1)} %copy-done.19), channel_id=1, source_target_pairs={{0,40},{8,48},{16,56},{24,0},{32,8},{40,16},{48,24},{56,32},{64,10... | collective-permute-start | bytes 393224 | tf_op jit(solution)/shard_map/ppermute | solution.py:338
  210.9 0.6 collective-permute-start.19
  211.5 0.6 collective-permute-start.20
  212.1 8.0 %shard_map.101 = (bf16[512,512]{1,0:T(8,128)(2,1)}, f32[512,512]{1,0:T(8,128)}, f32[512,512]{1,0:T(8,128)}) custom-call(bf16[512,512]{1,0:T(8,128)(2,1)} %q.9, bf16[512,512]{1,0:T(8,128)(2,1)} %k.7, bf16[512,512]{1,0:T(8,128)(2,1)} %v.7, bf16[512,512]{1,0:T(8,128)(2,1)} %get-tuple-element.141.g, bf16[512,512]{1,0:T(8,128)(2,1)} %get-tuple-element.138.gl, ...), custom_call_target="tpu_custom_call" | custom-call | tf_op jit(solution)/shard_map/pallas_call | solution.py:56
  220.1 0.6 copy-done.14
  220.8 4.4 %shard_map.102 = (bf16[512,512]{1,0:T(8,128)(2,1)}, bf16[512,512]{1,0:T(8,128)(2,1)}) custom-call(bf16[512,512]{1,0:T(8,128)(2,1)} %k.7, bf16[512,512]{1,0:T(8,128)(2,1)} %v.7, bf16[4,128,128]{2,1,0:T(8,128)(2,1)} %bitcast.9, f32[512,512]{1,0:T(8,128)} %get-tuple-element.155.dk, f32[512,512]{1,0:T(8,128)} %get-tuple-element.156.dv, ...), custom_call_target="tpu_custom_call" | custom-call | tf_op jit(solution)/shard_map/pallas_call | solution.py:56
  225.2 1.8 collective-permute-done.19
  227.0 1.9 collective-permute-done.20
  228.9 0.8 add_multiply_fusion
  (73 shorter events, 1.5 us)
Async XLA Ops:
  7.2 129.4 %all-gather.2.cloned.1.call-start = ((), (), s32[]{:S(2)}) async-start(), calls=%async_computation.6 | async-start | bytes 4325376 | tf_op jit(solution)/shard_map/all_gather | solution.py:370
  10.6 40.8 %collective-permute-start = (bf16[512,512]{1,0:T(8,128)(2,1)}, bf16[512,512]{1,0:T(8,128)(2,1)S(1)}, u32[]{:S(2)}, u32[]{:S(2)}) collective-permute-start(bf16[512,512]{1,0:T(8,128)(2,1)} %k.7), channel_id=1, source_target_pairs={{0,8},{8,16},{16,24},{24,32},{32,40},{40,48},{48,56},{56,64},{64,7... | collective-permute-start | bytes 1572872 | tf_op jit(solution)/shard_map/ppermute | solution.py:302
  14.5 37.0 %collective-permute-start.1 = (bf16[512,512]{1,0:T(8,128)(2,1)}, bf16[512,512]{1,0:T(8,128)(2,1)S(1)}, u32[]{:S(2)}, u32[]{:S(2)}) collective-permute-start(bf16[512,512]{1,0:T(8,128)(2,1)} %v.7), channel_id=1, source_target_pairs={{0,8},{8,16},{16,24},{24,32},{32,40},{40,48},{48,56},{56,64},{64,7... | collective-permute-start | bytes 1572872 | tf_op jit(solution)/shard_map/ppermute | solution.py:302
  18.3 33.1 %collective-permute-start.2 = (bf16[512,512]{1,0:T(8,128)(2,1)}, bf16[512,512]{1,0:T(8,128)(2,1)S(1)}, u32[]{:S(2)}, u32[]{:S(2)}) collective-permute-start(bf16[512,512]{1,0:T(8,128)(2,1)} %refs_0_.1), channel_id=1, source_target_pairs={{0,2},{1,3},{2,4},{3,5},{4,6},{5,7},{6,0},{7,1},{8,10},{9,11},{10,... | collective-permute-start | bytes 1572872 | tf_op jit(solution)/shard_map/ppermute | solution.py:328
  19.9 31.6 %collective-permute-start.3 = (bf16[512,512]{1,0:T(8,128)(2,1)}, bf16[512,512]{1,0:T(8,128)(2,1)S(1)}, u32[]{:S(2)}, u32[]{:S(2)}) collective-permute-start(bf16[512,512]{1,0:T(8,128)(2,1)} %refs_0_.1), channel_id=1, source_target_pairs={{0,4},{1,5},{2,6},{3,7},{4,0},{5,1},{6,2},{7,3},{8,12},{9,13},{10,... | collective-permute-start | bytes 1572872 | tf_op jit(solution)/shard_map/ppermute | solution.py:328
  22.6 28.9 %collective-permute-start.4 = (bf16[512,512]{1,0:T(8,128)(2,1)}, bf16[512,512]{1,0:T(8,128)(2,1)S(1)}, u32[]{:S(2)}, u32[]{:S(2)}) collective-permute-start(bf16[512,512]{1,0:T(8,128)(2,1)} %refs_0_.1), channel_id=1, source_target_pairs={{0,6},{1,7},{2,0},{3,1},{4,2},{5,3},{6,4},{7,5},{8,14},{9,15},{10,... | collective-permute-start | bytes 1572872 | tf_op jit(solution)/shard_map/ppermute | solution.py:328
  51.4 13.7 %copy-start.4 = (bf16[512,512]{1,0:T(8,128)(2,1)}, bf16[512,512]{1,0:T(8,128)(2,1)S(1)}, u32[]{:S(2)}) copy-start(bf16[512,512]{1,0:T(8,128)(2,1)S(1)} %collective-permute-done.kw) | copy-start | bytes 1572868
  51.4 13.7 %copy-start.5 = (bf16[512,512]{1,0:T(8,128)(2,1)}, bf16[512,512]{1,0:T(8,128)(2,1)S(1)}, u32[]{:S(2)}) copy-start(bf16[512,512]{1,0:T(8,128)(2,1)S(1)} %collective-permute-done.1.vw) | copy-start | bytes 1572868
  51.4 29.7 %copy-start.8 = (bf16[512,512]{1,0:T(8,128)(2,1)}, bf16[512,512]{1,0:T(8,128)(2,1)S(1)}, u32[]{:S(2)}) copy-start(bf16[512,512]{1,0:T(8,128)(2,1)S(1)} %collective-permute-done.2.refs_1_) | copy-start | bytes 1572868
  51.5 6.8 %copy-start.10 = (bf16[512,512]{1,0:T(8,128)(2,1)}, bf16[512,512]{1,0:T(8,128)(2,1)S(1)}, u32[]{:S(2)}) copy-start(bf16[512,512]{1,0:T(8,128)(2,1)S(1)} %collective-permute-done.3.refs_2_) | copy-start | bytes 1572868
  51.5 29.7 %copy-start.11 = (bf16[512,512]{1,0:T(8,128)(2,1)}, bf16[512,512]{1,0:T(8,128)(2,1)S(1)}, u32[]{:S(2)}) copy-start(bf16[512,512]{1,0:T(8,128)(2,1)S(1)} %collective-permute-done.4.refs_3_) | copy-start | bytes 1572868
  51.5 28.2 %collective-permute-start.5 = (bf16[512,512]{1,0:T(8,128)(2,1)}, bf16[512,512]{1,0:T(8,128)(2,1)S(1)}, u32[]{:S(2)}, u32[]{:S(2)}) collective-permute-start(bf16[512,512]{1,0:T(8,128)(2,1)} %refs_0_.1), channel_id=1, source_target_pairs={{0,0},{1,1},{2,64},{3,65},{4,128},{5,129},{6,192},{7,193},{8,8},{9... | collective-permute-start | bytes 1572872 | tf_op jit(solution)/shard_map/ppermute | solution.py:351
  58.3 21.3 %all-to-all-start.1 = ((bf16[32,16,128]{2,1,0:T(8,128)(2,1)}), bf16[32,16,128]{2,1,0:T(8,128)(2,1)S(1)}, u32[]{:S(2)}, u32[]{:S(2)}) async-start(bf16[32,16,128]{2,1,0:T(8,128)(2,1)} %shard_map.93), calls=%async_computation.1 | async-start | bytes 262144 | tf_op jit(solution)/shard_map/all_to_all | solution.py:234
  79.6 1.5 copy-start.6
  81.2 41.1 %all-to-all-start.2 = ((bf16[4,512,512]{2,1,0:T(8,128)(2,1)}), bf16[4,512,512]{2,1,0:T(8,128)(2,1)S(1)}, u32[]{:S(2)}, u32[]{:S(2)}) async-start(bf16[4,512,512]{2,1,0:T(8,128)(2,1)} %broadcast_in_dim.2), calls=%async_computation.2 | async-start | bytes 4194304 | tf_op jit(solution)/shard_map/all_to_all | solution.py:310
  84.9 37.6 %copy-start.7 = (bf16[512,512]{1,0:T(8,128)(2,1)S(1)}, bf16[512,512]{1,0:T(8,128)(2,1)}, u32[]{:S(2)}) copy-start(bf16[512,512]{1,0:T(8,128)(2,1)} %refs_0_.1) | copy-start | bytes 1572868
  84.9 38.1 %copy-start.9 = (bf16[512,512]{1,0:T(8,128)(2,1)S(1)}, bf16[512,512]{1,0:T(8,128)(2,1)}, u32[]{:S(2)}) copy-start(bf16[512,512]{1,0:T(8,128)(2,1)} %copy-done.8) | copy-start | bytes 1572868
  84.9 144.9 %reduce-scatter.2.cloned.1.call-start = ((), (), s32[]{:S(2)}) async-start(), calls=%async_computation.7 | async-start | bytes 4718592 | tf_op jit(solution)/shard_map/reduce_scatter | solution.py:452
  90.0 30.7 %collective-permute-start.6 = (bf16[512,512]{1,0:T(8,128)(2,1)}, bf16[512,512]{1,0:T(8,128)(2,1)S(1)}, u32[]{:S(2)}, u32[]{:S(2)}) collective-permute-start(bf16[512,512]{1,0:T(8,128)(2,1)} %get-tuple-element.106.refs_0_), channel_id=1, source_target_pairs={{0,64},{8,72},{16,80},{24,88},{32,96},{40,104},{48,112},{56,120},{... | collective-permute-start | bytes 1572872 | tf_op jit(solution)/shard_map/ppermute | solution.py:319
  91.6 29.1 %collective-permute-start.7 = (bf16[512,512]{1,0:T(8,128)(2,1)}, bf16[512,512]{1,0:T(8,128)(2,1)S(1)}, u32[]{:S(2)}, u32[]{:S(2)}) collective-permute-start(bf16[512,512]{1,0:T(8,128)(2,1)} %get-tuple-element.106.refs_0_), channel_id=1, source_target_pairs={{0,128},{8,136},{16,144},{24,152},{32,160},{40,168},{48,176},{56,1... | collective-permute-start | bytes 1572872 | tf_op jit(solution)/shard_map/ppermute | solution.py:319
  93.1 29.3 %collective-permute-start.8 = (bf16[512,512]{1,0:T(8,128)(2,1)}, bf16[512,512]{1,0:T(8,128)(2,1)}, u32[]{:S(2)}, u32[]{:S(2)}) collective-permute-start(bf16[512,512]{1,0:T(8,128)(2,1)} %get-tuple-element.106.refs_0_), channel_id=1, source_target_pairs={{0,192},{8,200},{16,208},{24,216},{32,224},{40,232},{48,240},{56,2... | collective-permute-start | bytes 1572872 | tf_op jit(solution)/shard_map/ppermute | solution.py:319
  120.7 0.8 copy-start.12
  121.5 0.8 copy-start.13
  122.3 4.4 %copy-start.2 = (bf16[4,512,512]{2,1,0:T(8,128)(2,1)}, bf16[4,512,512]{2,1,0:T(8,128)(2,1)S(1)}, u32[]{:S(2)}) copy-start(bf16[4,512,512]{2,1,0:T(8,128)(2,1)S(1)} %all-to-all-done.2.mine) | copy-start | bytes 6291460
  122.3 4.4 %collective-permute-start.9 = (bf16[4,512,512]{2,1,0:T(8,128)(2,1)S(1)}, bf16[4,512,512]{2,1,0:T(8,128)(2,1)}, u32[]{:S(2)}, u32[]{:S(2)}) collective-permute-start(bf16[4,512,512]{2,1,0:T(8,128)(2,1)S(1)} %all-to-all-done.2.mine), channel_id=1, source_target_pairs={{0,1},{1,0},{2,3},{3,2},{4,5},{5,4},{6,7},{7,6},{8,9},{9,8},{10,11... | collective-permute-start | bytes 6291464 | tf_op jit(solution)/shard_map/ppermute | solution.py:334
  122.5 14.1 %collective-permute-start.10 = (bf16[512,512]{1,0:T(8,128)(2,1)S(1)}, bf16[512,512]{1,0:T(8,128)(2,1)}, u32[]{:S(2)}, u32[]{:S(2)}) collective-permute-start(bf16[512,512]{1,0:T(8,128)(2,1)S(1)} %copy-done.7), channel_id=1, source_target_pairs={{0,1},{1,0},{2,3},{3,2},{4,5},{5,4},{6,7},{7,6},{8,9},{9,8},{10,11... | collective-permute-start | bytes 1572872 | tf_op jit(solution)/shard_map/ppermute | solution.py:334
  122.9 13.6 %collective-permute-start.11 = (bf16[512,512]{1,0:T(8,128)(2,1)S(1)}, bf16[512,512]{1,0:T(8,128)(2,1)}, u32[]{:S(2)}, u32[]{:S(2)}) collective-permute-start(bf16[512,512]{1,0:T(8,128)(2,1)S(1)} %copy-done.9), channel_id=1, source_target_pairs={{0,1},{1,0},{2,3},{3,2},{4,5},{5,4},{6,7},{7,6},{8,9},{9,8},{10,11... | collective-permute-start | bytes 1572872 | tf_op jit(solution)/shard_map/ppermute | solution.py:334
  123.1 13.5 %collective-permute-start.12 = (bf16[512,512]{1,0:T(8,128)(2,1)}, bf16[512,512]{1,0:T(8,128)(2,1)}, u32[]{:S(2)}, u32[]{:S(2)}) collective-permute-start(bf16[512,512]{1,0:T(8,128)(2,1)} %copy-done.10), channel_id=1, source_target_pairs={{0,1},{1,0},{2,3},{3,2},{4,5},{5,4},{6,7},{7,6},{8,9},{9,8},{10,11... | collective-permute-start | bytes 1572872 | tf_op jit(solution)/shard_map/ppermute | solution.py:334
  123.5 13.1 %collective-permute-start.13 = (bf16[512,512]{1,0:T(8,128)(2,1)}, bf16[512,512]{1,0:T(8,128)(2,1)}, u32[]{:S(2)}, u32[]{:S(2)}) collective-permute-start(bf16[512,512]{1,0:T(8,128)(2,1)} %copy-done.11), channel_id=1, source_target_pairs={{0,1},{1,0},{2,3},{3,2},{4,5},{5,4},{6,7},{7,6},{8,9},{9,8},{10,11... | collective-permute-start | bytes 1572872 | tf_op jit(solution)/shard_map/ppermute | solution.py:334
  153.2 17.7 %copy-start.23 = (bf16[512,128]{1,0:T(8,128)(2,1)S(1)}, bf16[512,128]{1,0:T(8,128)(2,1)}, u32[]{:S(2)}) copy-start(bf16[512,128]{1,0:T(8,128)(2,1)} %get-tuple-element.147) | copy-start | bytes 393220
  153.2 19.2 %copy-start.22 = (bf16[512,128]{1,0:T(8,128)(2,1)S(1)}, bf16[512,128]{1,0:T(8,128)(2,1)}, u32[]{:S(2)}) copy-start(bf16[512,128]{1,0:T(8,128)(2,1)} %get-tuple-element.148) | copy-start | bytes 393220
  153.2 47.2 %copy-start.21 = (bf16[512,128]{1,0:T(8,128)(2,1)S(1)}, bf16[512,128]{1,0:T(8,128)(2,1)}, u32[]{:S(2)}) copy-start(bf16[512,128]{1,0:T(8,128)(2,1)} %get-tuple-element.149) | copy-start | bytes 393220
  153.2 50.5 %copy-start.20 = (bf16[512,128]{1,0:T(8,128)(2,1)S(1)}, bf16[512,128]{1,0:T(8,128)(2,1)}, u32[]{:S(2)}) copy-start(bf16[512,128]{1,0:T(8,128)(2,1)} %get-tuple-element.150) | copy-start | bytes 393220
  153.2 53.2 %copy-start.19 = (bf16[512,128]{1,0:T(8,128)(2,1)S(1)}, bf16[512,128]{1,0:T(8,128)(2,1)}, u32[]{:S(2)}) copy-start(bf16[512,128]{1,0:T(8,128)(2,1)} %get-tuple-element.151) | copy-start | bytes 393220
  153.2 57.7 %copy-start.18 = (bf16[512,128]{1,0:T(8,128)(2,1)S(1)}, bf16[512,128]{1,0:T(8,128)(2,1)}, u32[]{:S(2)}) copy-start(bf16[512,128]{1,0:T(8,128)(2,1)} %get-tuple-element.152) | copy-start | bytes 393220
  153.2 58.2 %copy-start.17 = (bf16[512,128]{1,0:T(8,128)(2,1)S(1)}, bf16[512,128]{1,0:T(8,128)(2,1)}, u32[]{:S(2)}) copy-start(bf16[512,128]{1,0:T(8,128)(2,1)} %get-tuple-element.153) | copy-start | bytes 393220
  160.1 51.4 %collective-permute-start.21 = (bf16[896,512]{1,0:T(8,128)(2,1)}, bf16[896,512]{1,0:T(8,128)(2,1)S(1)}, u32[]{:S(2)}, u32[]{:S(2)}) collective-permute-start(bf16[896,512]{1,0:T(8,128)(2,1)} %get-tuple-element.157), channel_id=1, source_target_pairs={{8,0},{16,8},{24,16},{32,24},{40,32},{48,40},{56,48},{64,56},{72,6... | collective-permute-start | bytes 2752520 | tf_op jit(solution)/shard_map/ppermute | solution.py:302
  162.6 25.8 %all-to-all-start.3 = ((bf16[32,16,128]{2,1,0:T(8,128)(2,1)}), bf16[32,16,128]{2,1,0:T(8,128)(2,1)S(1)}, u32[]{:S(2)}, u32[]{:S(2)}) async-start(bf16[32,16,128]{2,1,0:T(8,128)(2,1)} %bitcast.4), calls=%async_computation.4 | async-start | bytes 262144 | tf_op jit(solution)/shard_map/all_to_all | solution.py:227
  170.9 35.6 %collective-permute-start.14 = (bf16[512,128]{1,0:T(8,128)(2,1)S(1)}, bf16[512,128]{1,0:T(8,128)(2,1)S(1)}, u32[]{:S(2)}, u32[]{:S(2)}) collective-permute-start(bf16[512,128]{1,0:T(8,128)(2,1)S(1)} %copy-done.23), channel_id=1, source_target_pairs={{0,8},{8,16},{16,24},{24,32},{32,40},{40,48},{48,56},{56,0},{64,72... | collective-permute-start | bytes 393224 | tf_op jit(solution)/shard_map/ppermute | solution.py:338
  172.4 38.5 %collective-permute-start.15 = (bf16[512,128]{1,0:T(8,128)(2,1)S(1)}, bf16[512,128]{1,0:T(8,128)(2,1)S(1)}, u32[]{:S(2)}, u32[]{:S(2)}) collective-permute-start(bf16[512,128]{1,0:T(8,128)(2,1)S(1)} %copy-done.22), channel_id=1, source_target_pairs={{0,16},{8,24},{16,32},{24,40},{32,48},{40,56},{48,0},{56,8},{64,80... | collective-permute-start | bytes 393224 | tf_op jit(solution)/shard_map/ppermute | solution.py:338
  190.7 29.4 %all-to-all-start.4 = ((bf16[32,16,128]{2,1,0:T(8,128)(2,1)}), bf16[32,16,128]{2,1,0:T(8,128)(2,1)S(1)}, u32[]{:S(2)}, u32[]{:S(2)}) async-start(bf16[32,16,128]{2,1,0:T(8,128)(2,1)} %shard_map.99), calls=%async_computation.5 | async-start | bytes 262144 | tf_op jit(solution)/shard_map/all_to_all | solution.py:234
  200.4 24.8 %collective-permute-start.16 = (bf16[512,128]{1,0:T(8,128)(2,1)S(1)}, bf16[512,128]{1,0:T(8,128)(2,1)S(1)}, u32[]{:S(2)}, u32[]{:S(2)}) collective-permute-start(bf16[512,128]{1,0:T(8,128)(2,1)S(1)} %copy-done.21), channel_id=1, source_target_pairs={{0,24},{8,32},{16,40},{24,48},{32,56},{40,0},{48,8},{56,16},{64,88... | collective-permute-start | bytes 393224 | tf_op jit(solution)/shard_map/ppermute | solution.py:338
  203.7 21.4 %collective-permute-start.17 = (bf16[512,128]{1,0:T(8,128)(2,1)S(1)}, bf16[512,128]{1,0:T(8,128)(2,1)S(1)}, u32[]{:S(2)}, u32[]{:S(2)}) collective-permute-start(bf16[512,128]{1,0:T(8,128)(2,1)S(1)} %copy-done.20), channel_id=1, source_target_pairs={{0,32},{8,40},{16,48},{24,56},{32,0},{40,8},{48,16},{56,24},{64,96... | collective-permute-start | bytes 393224 | tf_op jit(solution)/shard_map/ppermute | solution.py:338
  206.4 18.8 %collective-permute-start.18 = (bf16[512,128]{1,0:T(8,128)(2,1)S(1)}, bf16[512,128]{1,0:T(8,128)(2,1)S(1)}, u32[]{:S(2)}, u32[]{:S(2)}) collective-permute-start(bf16[512,128]{1,0:T(8,128)(2,1)S(1)} %copy-done.19), channel_id=1, source_target_pairs={{0,40},{8,48},{16,56},{24,0},{32,8},{40,16},{48,24},{56,32},{64,10... | collective-permute-start | bytes 393224 | tf_op jit(solution)/shard_map/ppermute | solution.py:338
  210.9 16.1 %collective-permute-start.19 = (bf16[512,128]{1,0:T(8,128)(2,1)S(1)}, bf16[512,128]{1,0:T(8,128)(2,1)S(1)}, u32[]{:S(2)}, u32[]{:S(2)}) collective-permute-start(bf16[512,128]{1,0:T(8,128)(2,1)S(1)} %copy-done.18), channel_id=1, source_target_pairs={{0,48},{8,56},{16,0},{24,8},{32,16},{40,24},{48,32},{56,40},{64,11... | collective-permute-start | bytes 393224 | tf_op jit(solution)/shard_map/ppermute | solution.py:338
  211.5 8.6 %copy-start.3 = (bf16[896,512]{1,0:T(8,128)(2,1)}, bf16[896,512]{1,0:T(8,128)(2,1)S(1)}, u32[]{:S(2)}) copy-start(bf16[896,512]{1,0:T(8,128)(2,1)S(1)} %collective-permute-done.21.rk.rv) | copy-start | bytes 2752516
  211.5 17.4 %collective-permute-start.20 = (bf16[512,128]{1,0:T(8,128)(2,1)S(1)}, bf16[512,128]{1,0:T(8,128)(2,1)S(1)}, u32[]{:S(2)}, u32[]{:S(2)}) collective-permute-start(bf16[512,128]{1,0:T(8,128)(2,1)S(1)} %copy-done.17), channel_id=1, source_target_pairs={{0,56},{8,0},{16,8},{24,16},{32,24},{40,32},{48,40},{56,48},{64,12... | collective-permute-start | bytes 393224 | tf_op jit(solution)/shard_map/ppermute | solution.py:338
  220.8 8.2 %copy-start.16 = (bf16[512,128]{1,0:T(8,128)(2,1)S(1)}, bf16[512,128]{1,0:T(8,128)(2,1)}, u32[]{:S(2)}) copy-start(bf16[512,128]{1,0:T(8,128)(2,1)} %get-tuple-element.161) | copy-start | bytes 393220
  (4 other events, 2.5 us)
Sparse Core Ops, SparseCore 0:
  10.5 106.7 all-gather.1
  149.1 40.5 reduce-scatter.1

commit v8 on v5

--- a/solution.py
+++ b/solution.py
@@ -144,7 +144,7 @@
     mixed[...] = out.T.astype(BF16)
 
 
-def far_kernel(q, g, kw, vw, far, window, dq, dk, dv, delta, ds):
+def far_kernel(q, g, kw, vw, far, window, dq, back, delta, ds):
     g_t = flip(g[...])
     d = jnp.sum(g_t * window[...], axis=0, keepdims=True)
     delta[0] = d
@@ -160,11 +160,11 @@
         dk_j = nn(ds[lo:hi, 0:hi], q[0:hi, :]).astype(BF16)
         dv_j = nn(far[0, lo:hi, 0:hi], g[0:hi, :]).astype(BF16)
         if j == 0:
-            dk[0 : hi - BLOCK, :] = dk_j[BLOCK:]
-            dv[0 : hi - BLOCK, :] = dv_j[BLOCK:]
+            back[0 : hi - BLOCK, :] = dk_j[BLOCK:]
+            back[EDGE : EDGE + hi - BLOCK, :] = dv_j[BLOCK:]
         else:
-            dk[lo - BLOCK : hi - BLOCK, :] = dk_j
-            dv[lo - BLOCK : hi - BLOCK, :] = dv_j
+            back[lo - BLOCK : hi - BLOCK, :] = dk_j
+            back[EDGE + lo - BLOCK : EDGE + hi - BLOCK, :] = dv_j
 
 
 def lin_kernel(q, g, normed, inverse, grad_lin, sums):
@@ -372,13 +372,10 @@
     local = call(
         sums_kernel, heads, [col, col], st, shape((heads, DH, DH), BF16), flops=2 * mm // 4
     )(keys, values)
-    before, _, sent = carry_states(local, False, (), (keys, values, grad_y))
-    kh, vh, turned_grad = shifted(sent[0], 1), shifted(sent[1], 1), turn_xy(sent[2])
-    before, kh, vh, hopped, turned_grad = lax.optimization_barrier(
-        (before, kh, vh, hopped, turned_grad)
-    )
-    grads = [grad_y] + hopped
-    grads = grads + [swap_core(g) for g in grads]
+    local, k_out, v_out = lax.optimization_barrier((local, keys, values))
+    kh, vh = shifted(k_out, 1), shifted(v_out, 1)
+    before, grad_out, _ = carry_states(local, False, grad_y)
+    turned_grad = turn_xy(grad_out)
 
     sq = large((heads, rows, rows), BF16)
     flat_t = large((width, rows), F32)
@@ -394,7 +391,6 @@
         prefetch=1,
     )(seq, queries, keys, values, kh, vh)
 
-    before, window = lax.optimization_barrier((before, window))
     normed, inverse, mixed_t, mixed = call(
         mixed_kernel,
         heads,
@@ -410,11 +406,14 @@
         size=5 << 20,
     )(queries, before, window, intra)
 
-    turned_grad, mixed_t = lax.optimization_barrier((turned_grad, mixed_t))
+    turned_grad, hopped, mixed_t = lax.optimization_barrier((turned_grad, hopped, mixed_t))
     mine = spread(turned_grad, "head", X_GROUPS)
     across_y = [mixed_t] + [hop_y(mixed_t, by) for by in range(1, YS)]
-    mine, across_y, full_w = lax.optimization_barrier((mine, across_y, full_w))
+    grads = [grad_y] + hopped
+    grads = grads + [swap_core(g) for g in grads]
+    mine, across_y = lax.optimization_barrier((mine, across_y))
     other = swap_core(mine)
+    mine, other, across_y, full_w = lax.optimization_barrier((mine, other, across_y, full_w))
     fixed = pl.BlockSpec((rows, width), lambda *_: (0, 0))
     by_block = pl.BlockSpec((rows, width), lambda t, head: (0, block_id(t, head)))
     partial_value, grad_mixed = call(
@@ -438,23 +437,20 @@
         size=3 << 20,
     )(queries, grad_mixed, normed, inverse)
     local_back, g_far = lax.optimization_barrier((local_back, grad_mixed))
-    edge_grad = large((edge, width), BF16)
-    dq_far, far_k, far_v, delta = call(
+    dq_far, back, delta = call(
         far_kernel,
         heads,
         [col, col, col, col, tri, turned],
-        [turned, columns(edge), columns(edge), line],
-        [flat_t, edge_grad, edge_grad, shape((heads, 1, rows), F32)],
+        [turned, columns(2 * edge), line],
+        [flat_t, large((2 * edge, width), BF16), shape((heads, 1, rows), F32)],
         scratch=[pltpu.VMEM((rows, rows), BF16)],
         flops=8 * mm // 8,
         size=8 << 20,
     )(queries, g_far, kh, vh, far, window)
-    back_k, back_v = shifted(far_k, -1), shifted(far_v, -1)
-
-    later, grad_lin, _ = carry_states(local_back, True, grad_lin)
-
-    across_y, mine, other, local_back = lax.optimization_barrier(
-        (across_y, mine, other, local_back)
+    back = shifted(back, -1)
+
+    mine, other, across_y, local_back = lax.optimization_barrier(
+        (mine, other, across_y, local_back)
     )
     parts = call(
         sens_kernel,
@@ -479,10 +475,9 @@
         scratch=[pltpu.VMEM((width, rows), F32)],
         prefetch=1,
     )(place, mine, other, *across_y)
-    total = parts[0].astype(F32)
-    for by in range(1, ZS):
-        total = total + hop_z(parts[by], by).astype(F32)
-    projection_sensitivity = total * tokens_all ** (-0.5)
+    sums = [parts[0]] + [hop_z(parts[by], by) for by in range(1, ZS)]
+    later, grad_lin, _ = carry_states(local_back, True, grad_lin)
+
 
     grad_queries, near_k, near_v = call(
         near_kernel,
@@ -498,12 +493,15 @@
     grad_keys, grad_values = call(
         last_kernel,
         heads,
-        [col, col, st, col, col, columns(edge), columns(edge)],
+        [col, col, st, col, col, columns(edge), columns(edge, 1)],
         [col, col],
         [large((rows, width), BF16)] * 2,
         flops=mm // 2,
         size=5 << 20,
-    )(keys, values, later, near_k, near_v, back_k, back_v)
+    )(keys, values, later, near_k, near_v, back, back)
+    sums, grad_keys = lax.optimization_barrier((sums, grad_keys))
+    total = sum(part.astype(F32) for part in sums)
+    projection_sensitivity = total * tokens_all ** (-0.5)
     return (mixer_result, grad_queries, grad_keys, grad_values, projection_sensitivity)
 
 

time: 239 us -> 230 us (0.962)
  waiting for transfers between devices: 71.1 us -> 50.8 us
  starting transfers between devices: 78.2 us -> 88.9 us
    all_to_all x2, waiting for transfers between devices: 38.2 us -> 0.01 us  [carry_states(): lax.all_to_all(done, 'seq', 0, 0).reshape(local.shape)]
    ppermute x3, waiting for transfers between devices: 17.8 us -> 28.1 us  [hop_y(): lax.ppermute(shard, 'seq', [(y * ZS + z, (y + by) % YS * ZS + z) for y in...]
    ppermute x5, waiting for transfers between devices: 0.01 us -> 6.37 us  [swap_core(): return lax.ppermute(shard, 'head', [(i, i ^ 1) for i in range(2 * XS)])]
    ppermute x1, waiting for transfers between devices: 0.01 us -> 4.56 us  [turn_xy(): return lax.ppermute(shard, ('seq', 'head'), pairs)]
    all_to_all x2, starting transfers between devices: 22.8 us -> 18.4 us  [carry_states(): met = lax.all_to_all(pieces, 'seq', 0, 0)]
    ppermute x4 -> x3, starting transfers between devices: 9.38 us -> 13.7 us  [shifted(): return lax.ppermute(shard, 'seq', pairs)]
    ppermute x3, starting transfers between devices: 3.55 us -> 6.92 us  [hop_y(): lax.ppermute(shard, 'seq', [(y * ZS + z, (y + by) % YS * ZS + z) for y in...]
    all_to_all x2, waiting for transfers between devices: 10.1 us -> 6.84 us  [carry_states(): met = lax.all_to_all(pieces, 'seq', 0, 0)]
  transfers between devices with their start and end apart: 30 -> 29, of which waited for: 8 -> 11; matrix products, arithmetic and copies ran while one was open for 1% -> 1% of each run, Pallas kernels for 22% -> 23%
where the time goes in v8:
time: 230 us; the launch traced here: 228 us
  starting transfers between devices  88.9 us (39%)
  Pallas kernels  65.3 us (28%)
  waiting for transfers between devices  50.8 us (22%)
  between operations  14.3 us (6%)
  local copies, waits for them, and re-layouts  7.47 us (3%)
    pallas_call x9, Pallas kernels, call(): run(*args[:prefetch], *(kept(a) for a in args[prefetch:]))  62.1 us
    ppermute x3, waiting for transfers between devices, hop_y(): lax.ppermute(shard, 'seq', [(y * ZS + z, (y + by) % YS * ZS + z) for y in...  28.1 us
    all_to_all x2, starting transfers between devices, carry_states(): met = lax.all_to_all(pieces, 'seq', 0, 0)  18.4 us
    all_to_all x2, starting transfers between devices, carry_states(): lax.all_to_all(done, 'seq', 0, 0).reshape(local.shape)  17.2 us
    ppermute x7, starting transfers between devices, hop_z(): lax.ppermute(shard, 'seq', [(y * ZS + z, y * ZS + (z + by) % ZS) for y in...  15.4 us
    ppermute x3, starting transfers between devices, shifted(): return lax.ppermute(shard, 'seq', pairs)  13.7 us
    ppermute x3, starting transfers between devices, hop_y(): lax.ppermute(shard, 'seq', [(y * ZS + z, (y + by) % YS * ZS + z) for y in...  6.92 us
    all_to_all x2, waiting for transfers between devices, carry_states(): met = lax.all_to_all(pieces, 'seq', 0, 0)  6.84 us
  transfers between devices with their start and end apart: 29, of which 11 were waited for; matrix products, arithmetic and copies ran while one was open for 1% of the time, Pallas kernels for 23%

profile of v8, /device:TPU:16, one launch (start us, length us, event | category | flops | bytes accessed | tf_op | source)
XLA Modules:
  0.0 227.7 jit_solution(15313424860293422411)
XLA Ops:
  7.2 0.7 all-gather.2.cloned.1.call-update
  7.9 3.7 %shard_map.92 = bf16[4,128,128]{2,1,0:T(8,128)(2,1)} custom-call(bf16[512,512]{1,0:T(8,128)(2,1)} %k.7, bf16[512,512]{1,0:T(8,128)(2,1)} %v.7), custom_call_target="tpu_custom_call" | custom-call | tf_op jit(solution)/shard_map/pallas_call | solution.py:56
  11.6 3.8 %collective-permute-start = (bf16[512,512]{1,0:T(8,128)(2,1)}, bf16[512,512]{1,0:T(8,128)(2,1)S(1)}, u32[]{:S(2)}, u32[]{:S(2)}) collective-permute-start(bf16[512,512]{1,0:T(8,128)(2,1)} %k.7), channel_id=1, source_target_pairs={{0,8},{8,16},{16,24},{24,32},{32,40},{40,48},{48,56},{56,64},{64,7... | collective-permute-start | bytes 1572872 | tf_op jit(solution)/shard_map/ppermute | solution.py:302
  15.4 10.7 %all-to-all-start = ((bf16[32,16,128]{2,1,0:T(8,128)(2,1)}), bf16[32,16,128]{2,1,0:T(8,128)(2,1)S(1)}, u32[]{:S(2)}, u32[]{:S(2)}) async-start(bf16[32,16,128]{2,1,0:T(8,128)(2,1)} %bitcast.1), calls=%async_computation | async-start | bytes 262144 | tf_op jit(solution)/shard_map/all_to_all | solution.py:227
  26.1 3.4 %collective-permute-start.1 = (bf16[512,512]{1,0:T(8,128)(2,1)}, bf16[512,512]{1,0:T(8,128)(2,1)S(1)}, u32[]{:S(2)}, u32[]{:S(2)}) collective-permute-start(bf16[512,512]{1,0:T(8,128)(2,1)} %v.7), channel_id=1, source_target_pairs={{0,8},{8,16},{16,24},{24,32},{32,40},{40,48},{48,56},{56,64},{64,7... | collective-permute-start | bytes 1572872 | tf_op jit(solution)/shard_map/ppermute | solution.py:302
  29.5 2.8 %collective-permute-start.5 = (bf16[512,512]{1,0:T(8,128)(2,1)}, bf16[512,512]{1,0:T(8,128)(2,1)S(1)}, u32[]{:S(2)}, u32[]{:S(2)}) collective-permute-start(bf16[512,512]{1,0:T(8,128)(2,1)} %refs_0_.1), channel_id=1, source_target_pairs={{0,6},{1,7},{2,0},{3,1},{4,2},{5,3},{6,4},{7,5},{8,14},{9,15},{10,... | collective-permute-start | bytes 1572872 | tf_op jit(solution)/shard_map/ppermute | solution.py:328
  32.3 0.8 collective-permute-start.4
  33.1 0.9 collective-permute-start.3
  34.0 4.4 %all-to-all-done.x = bf16[32,16,128]{2,1,0:T(8,128)(2,1)S(1)} async-done(((bf16[32,16,128]{2,1,0:T(8,128)(2,1)}), bf16[32,16,128]{2,1,0:T(8,128)(2,1)S(1)}, u32[]{:S(2)}, u32[]{:S(2)}) %all-to-all-start) | async-done | bytes 131104 | tf_op jit(solution)/shard_map/all_to_all | solution.py:227
  38.4 0.7 copy-done.17
  39.1 1.6 shard_map.93
  40.7 6.6 %collective-permute-start.2 = (bf16[512,512]{1,0:T(8,128)(2,1)}, bf16[512,512]{1,0:T(8,128)(2,1)S(1)}, u32[]{:S(2)}, u32[]{:S(2)}) collective-permute-start(bf16[512,512]{1,0:T(8,128)(2,1)} %refs_0_.1), channel_id=1, source_target_pairs={{0,0},{1,1},{2,64},{3,65},{4,128},{5,129},{6,192},{7,193},{8,8},{9... | collective-permute-start | bytes 1572872 | tf_op jit(solution)/shard_map/ppermute | solution.py:351
  47.3 7.8 %all-to-all-start.1 = ((bf16[32,16,128]{2,1,0:T(8,128)(2,1)}), bf16[32,16,128]{2,1,0:T(8,128)(2,1)S(1)}, u32[]{:S(2)}, u32[]{:S(2)}) async-start(bf16[32,16,128]{2,1,0:T(8,128)(2,1)} %shard_map.93), calls=%async_computation.1 | async-start | bytes 262144 | tf_op jit(solution)/shard_map/all_to_all | solution.py:234
  55.1 0.8 copy-done.5
  55.9 9.3 %shard_map.94 = (bf16[4,512,512]{2,1,0:T(8,128)(2,1)}, bf16[4,512,512]{2,1,0:T(8,128)(2,1)}, bf16[4,512,512]{2,1,0:T(8,128)(2,1)}, f32[512,512]{1,0:T(8,128)}, f32[512,512]{1,0:T(8,128)}) custom-call(s32[1]{0:T(128)} %bitcast.3.place, bf16[512,512]{1,0:T(8,128)(2,1)} %q.9, bf16[512,512]{1,0:T(8,128)(2,1)} %k.7, bf16[512,512]{1,0:T(8,128)(2,1)} %v.7, ...), custom_call_target="tpu_custom_call" | custom-call | tf_op jit(solution)/shard_map/pallas_call | solution.py:56
  65.2 0.6 copy-done.6
  65.8 4.4 %shard_map.95 = (f32[512,512]{1,0:T(8,128)}, f32[4,1,512]{2,1,0:T(1,128)S(1)}, bf16[512,512]{1,0:T(8,128)(2,1)}, bf16[512,512]{1,0:T(8,128)(2,1)}) custom-call(bf16[512,512]{1,0:T(8,128)(2,1)} %q.9, bf16[4,128,128]{2,1,0:T(8,128)(2,1)} %bitcast.6, f32[512,512]{1,0:T(8,128)} %get-tuple-element.80.window, f32[512,512]{1,0:T(8,128)} %get-tuple-element.81.intra), custom_call_target="tpu_custom_call" | custom-call | tf_op jit(solution)/shard_map/pallas_call | solution.py:56
  70.9 4.6 %collective-permute-done.2 = bf16[512,512]{1,0:T(8,128)(2,1)S(1)} collective-permute-done((bf16[512,512]{1,0:T(8,128)(2,1)}, bf16[512,512]{1,0:T(8,128)(2,1)S(1)}, u32[]{:S(2)}, u32[]{:S(2)}) %collective-permute-start.2) | collective-permute-done | bytes 524320 | tf_op jit(solution)/shard_map/ppermute | solution.py:351
  75.4 1.5 broadcast_in_dim.2
  77.0 4.9 %all-to-all-start.2 = ((bf16[4,512,512]{2,1,0:T(8,128)(2,1)}), bf16[4,512,512]{2,1,0:T(8,128)(2,1)S(1)}, u32[]{:S(2)}, u32[]{:S(2)}) async-start(bf16[4,512,512]{2,1,0:T(8,128)(2,1)} %broadcast_in_dim.2), calls=%async_computation.2 | async-start | bytes 4194304 | tf_op jit(solution)/shard_map/all_to_all | solution.py:310
  81.8 3.5 %collective-permute-start.8 = (bf16[512,512]{1,0:T(8,128)(2,1)S(1)}, bf16[512,512]{1,0:T(8,128)(2,1)S(1)}, u32[]{:S(2)}, u32[]{:S(2)}) collective-permute-start(bf16[512,512]{1,0:T(8,128)(2,1)S(1)} %copy-done.8), channel_id=1, source_target_pairs={{0,192},{8,200},{16,208},{24,216},{32,224},{40,232},{48,240},{56,2... | collective-permute-start | bytes 1572872 | tf_op jit(solution)/shard_map/ppermute | solution.py:319
  85.4 3.4 %collective-permute-start.7 = (bf16[512,512]{1,0:T(8,128)(2,1)S(1)}, bf16[512,512]{1,0:T(8,128)(2,1)S(1)}, u32[]{:S(2)}, u32[]{:S(2)}) collective-permute-start(bf16[512,512]{1,0:T(8,128)(2,1)S(1)} %copy-done.8), channel_id=1, source_target_pairs={{0,128},{8,136},{16,144},{24,152},{32,160},{40,168},{48,176},{56,1... | collective-permute-start | bytes 1572872 | tf_op jit(solution)/shard_map/ppermute | solution.py:319
  88.8 17.7 %collective-permute-done.8.refs_3_ = bf16[512,512]{1,0:T(8,128)(2,1)S(1)} collective-permute-done((bf16[512,512]{1,0:T(8,128)(2,1)S(1)}, bf16[512,512]{1,0:T(8,128)(2,1)S(1)}, u32[]{:S(2)}, u32[]{:S(2)}) %collective-permute-start.8) | collective-permute-done | bytes 524320 | tf_op jit(solution)/shard_map/ppermute | solution.py:319
  107.2 0.8 copy-done.10
  108.1 10.2 %collective-permute-done.6.refs_1_ = bf16[512,512]{1,0:T(8,128)(2,1)} collective-permute-done((bf16[512,512]{1,0:T(8,128)(2,1)S(1)}, bf16[512,512]{1,0:T(8,128)(2,1)}, u32[]{:S(2)}, u32[]{:S(2)}) %collective-permute-start.6) | collective-permute-done | bytes 524320 | tf_op jit(solution)/shard_map/ppermute | solution.py:319
  119.4 5.1 %collective-permute-done.9.other = bf16[4,512,512]{2,1,0:T(8,128)(2,1)} collective-permute-done((bf16[4,512,512]{2,1,0:T(8,128)(2,1)S(1)}, bf16[4,512,512]{2,1,0:T(8,128)(2,1)}, u32[]{:S(2)}, u32[]{:S(2)}) %collective-permute-start.9) | collective-permute-done | bytes 2097184 | tf_op jit(solution)/shard_map/ppermute | solution.py:334
  125.0 0.7 collective-permute-done.13.refs_7_
  125.7 12.2 %shard_map.96 = (bf16[512,4096]{1,0:T(8,128)(2,1)}, bf16[512,512]{1,0:T(8,128)(2,1)}) custom-call(s32[1]{0:T(128)} %bitcast.head, bf16[512,512]{1,0:T(8,128)(2,1)} %get-tuple-element.82.mixed, bf16[512,4096]{1,0:T(8,128)(2,1)} %all-gather.2.cloned.1.call-done.w, bf16[512,512]{1,0:T(8,128)(2,1)} %refs_0_.1, bf16[512,512]{1,0:T(8,128)(2,1)} %copy-done.13, ...), custom_call_target="tpu_custom_call" | custom-call | tf_op jit(solution)/shard_map/pallas_call | solution.py:56
  138.0 4.2 %shard_map.97 = (bf16[512,512]{1,0:T(8,128)(2,1)}, bf16[4,128,128]{2,1,0:T(8,128)(2,1)}) custom-call(bf16[512,512]{1,0:T(8,128)(2,1)} %q.9, bf16[512,512]{1,0:T(8,128)(2,1)} %get-tuple-element.113.g, f32[512,512]{1,0:T(8,128)} %get-tuple-element.104.normed, f32[4,1,512]{2,1,0:T(1,128)} %copy-done.1), custom_call_target="tpu_custom_call" | custom-call | tf_op jit(solution)/shard_map/pallas_call | solution.py:56
  142.2 6.1 %shard_map.99 = (f32[512,512]{1,0:T(8,128)}, bf16[896,512]{1,0:T(8,128)(2,1)}, f32[4,1,512]{2,1,0:T(1,128)S(1)}) custom-call(bf16[512,512]{1,0:T(8,128)(2,1)} %q.9, bf16[512,512]{1,0:T(8,128)(2,1)} %get-tuple-element.113.g, bf16[512,512]{1,0:T(8,128)(2,1)} %copy-done.4, bf16[512,512]{1,0:T(8,128)(2,1)} %copy-done.5, ...), custom_call_target="tpu_custom_call" | custom-call | tf_op jit(solution)/shard_map/pallas_call | solution.py:56
  148.8 6.5 %collective-permute-start.21 = (bf16[896,512]{1,0:T(8,128)(2,1)}, bf16[896,512]{1,0:T(8,128)(2,1)S(1)}, u32[]{:S(2)}, u32[]{:S(2)}) collective-permute-start(bf16[896,512]{1,0:T(8,128)(2,1)} %get-tuple-element.135), channel_id=1, source_target_pairs={{8,0},{16,8},{24,16},{32,24},{40,32},{48,40},{56,48},{64,56},{72,6... | collective-permute-start | bytes 2752520 | tf_op jit(solution)/shard_map/ppermute | solution.py:302
  155.4 7.7 %all-to-all-start.3 = ((bf16[32,16,128]{2,1,0:T(8,128)(2,1)}), bf16[32,16,128]{2,1,0:T(8,128)(2,1)S(1)}, u32[]{:S(2)}, u32[]{:S(2)}) async-start(bf16[32,16,128]{2,1,0:T(8,128)(2,1)} %bitcast.4), calls=%async_computation.4 | async-start | bytes 262144 | tf_op jit(solution)/shard_map/all_to_all | solution.py:227
  163.2 9.9 %shard_map.101 = (bf16[512,128]{1,0:T(8,128)(2,1)}, bf16[512,128]{1,0:T(8,128)(2,1)}, bf16[512,128]{1,0:T(8,128)(2,1)}, bf16[512,128]{1,0:T(8,128)(2,1)}, bf16[5...) custom-call(s32[3]{0:T(128)S(1)} %pad_add_fusion.place, ...), custom_call_target="tpu_custom_call" | custom-call | tf_op jit(solution)/shard_map/pallas_call | solution.py:56
  173.1 1.5 collective-permute-start.14
  174.6 2.3 %collective-permute-start.15 = (bf16[512,128]{1,0:T(8,128)(2,1)}, bf16[512,128]{1,0:T(8,128)(2,1)S(1)}, u32[]{:S(2)}, u32[]{:S(2)}) collective-permute-start(bf16[512,128]{1,0:T(8,128)(2,1)} %get-tuple-element.126), channel_id=1, source_target_pairs={{0,16},{8,24},{16,32},{24,40},{32,48},{40,56},{48,0},{56,8},{64,80... | collective-permute-start | bytes 393224 | tf_op jit(solution)/shard_map/ppermute | solution.py:338
  176.9 2.4 %all-to-all-done.3.x = bf16[32,16,128]{2,1,0:T(8,128)(2,1)S(1)} async-done(((bf16[32,16,128]{2,1,0:T(8,128)(2,1)}), bf16[32,16,128]{2,1,0:T(8,128)(2,1)S(1)}, u32[]{:S(2)}, u32[]{:S(2)}) %all-to-all-start.3) | async-done | bytes 131104 | tf_op jit(solution)/shard_map/all_to_all | solution.py:227
  179.4 0.7 copy-done.16
  180.0 1.6 shard_map.98
  181.6 9.4 %all-to-all-start.4 = ((bf16[32,16,128]{2,1,0:T(8,128)(2,1)}), bf16[32,16,128]{2,1,0:T(8,128)(2,1)S(1)}, u32[]{:S(2)}, u32[]{:S(2)}) async-start(bf16[32,16,128]{2,1,0:T(8,128)(2,1)} %shard_map.98), calls=%async_computation.5 | async-start | bytes 262144 | tf_op jit(solution)/shard_map/all_to_all | solution.py:234
  191.1 3.3 %collective-permute-start.16 = (bf16[512,128]{1,0:T(8,128)(2,1)}, bf16[512,128]{1,0:T(8,128)(2,1)S(1)}, u32[]{:S(2)}, u32[]{:S(2)}) collective-permute-start(bf16[512,128]{1,0:T(8,128)(2,1)} %get-tuple-element.127), channel_id=1, source_target_pairs={{0,24},{8,32},{16,40},{24,48},{32,56},{40,0},{48,8},{56,16},{64,88... | collective-permute-start | bytes 393224 | tf_op jit(solution)/shard_map/ppermute | solution.py:338
  194.4 2.7 %collective-permute-start.17 = (bf16[512,128]{1,0:T(8,128)(2,1)}, bf16[512,128]{1,0:T(8,128)(2,1)S(1)}, u32[]{:S(2)}, u32[]{:S(2)}) collective-permute-start(bf16[512,128]{1,0:T(8,128)(2,1)} %get-tuple-element.128), channel_id=1, source_target_pairs={{0,32},{8,40},{16,48},{24,56},{32,0},{40,8},{48,16},{56,24},{64,96... | collective-permute-start | bytes 393224 | tf_op jit(solution)/shard_map/ppermute | solution.py:338
  197.1 4.5 %collective-permute-start.18 = (bf16[512,128]{1,0:T(8,128)(2,1)}, bf16[512,128]{1,0:T(8,128)(2,1)S(1)}, u32[]{:S(2)}, u32[]{:S(2)}) collective-permute-start(bf16[512,128]{1,0:T(8,128)(2,1)} %get-tuple-element.129), channel_id=1, source_target_pairs={{0,40},{8,48},{16,56},{24,0},{32,8},{40,16},{48,24},{56,32},{64,10... | collective-permute-start | bytes 393224 | tf_op jit(solution)/shard_map/ppermute | solution.py:338
  202.7 8.0 %shard_map.100 = (bf16[512,512]{1,0:T(8,128)(2,1)}, f32[512,512]{1,0:T(8,128)}, f32[512,512]{1,0:T(8,128)}) custom-call(bf16[512,512]{1,0:T(8,128)(2,1)} %q.9, bf16[512,512]{1,0:T(8,128)(2,1)} %k.7, bf16[512,512]{1,0:T(8,128)(2,1)} %v.7, bf16[512,512]{1,0:T(8,128)(2,1)} %get-tuple-element.113.g, bf16[512,512]{1,0:T(8,128)(2,1)} %get-tuple-element.110.gl, ...), custom_call_target="tpu_custom_call" | custom-call | tf_op jit(solution)/shard_map/pallas_call | solution.py:56
  210.7 0.6 copy-done.15
  211.4 4.4 %shard_map.102 = (bf16[512,512]{1,0:T(8,128)(2,1)}, bf16[512,512]{1,0:T(8,128)(2,1)}) custom-call(bf16[512,512]{1,0:T(8,128)(2,1)} %k.7, bf16[512,512]{1,0:T(8,128)(2,1)} %v.7, bf16[4,128,128]{2,1,0:T(8,128)(2,1)} %bitcast.8, f32[512,512]{1,0:T(8,128)} %get-tuple-element.133.dk, f32[512,512]{1,0:T(8,128)} %get-tuple-element.134.dv, ...), custom_call_target="tpu_custom_call" | custom-call | tf_op jit(solution)/shard_map/pallas_call | solution.py:56
  215.8 2.3 collective-permute-done.19
  218.1 1.9 collective-permute-done.20
  220.0 0.8 add_multiply_fusion
  (64 shorter events, 4.9 us)
Async XLA Ops:
  7.2 117.3 %all-gather.2.cloned.1.call-start = ((), (), s32[]{:S(2)}) async-start(), calls=%async_computation.6 | async-start | bytes 4325376 | tf_op jit(solution)/shard_map/all_gather | solution.py:370
  11.6 29.1 %collective-permute-start = (bf16[512,512]{1,0:T(8,128)(2,1)}, bf16[512,512]{1,0:T(8,128)(2,1)S(1)}, u32[]{:S(2)}, u32[]{:S(2)}) collective-permute-start(bf16[512,512]{1,0:T(8,128)(2,1)} %k.7), channel_id=1, source_target_pairs={{0,8},{8,16},{16,24},{24,32},{32,40},{40,48},{48,56},{56,64},{64,7... | collective-permute-start | bytes 1572872 | tf_op jit(solution)/shard_map/ppermute | solution.py:302
  15.4 23.0 %all-to-all-start = ((bf16[32,16,128]{2,1,0:T(8,128)(2,1)}), bf16[32,16,128]{2,1,0:T(8,128)(2,1)S(1)}, u32[]{:S(2)}, u32[]{:S(2)}) async-start(bf16[32,16,128]{2,1,0:T(8,128)(2,1)} %bitcast.1), calls=%async_computation | async-start | bytes 262144 | tf_op jit(solution)/shard_map/all_to_all | solution.py:227
  26.1 29.0 %collective-permute-start.1 = (bf16[512,512]{1,0:T(8,128)(2,1)}, bf16[512,512]{1,0:T(8,128)(2,1)S(1)}, u32[]{:S(2)}, u32[]{:S(2)}) collective-permute-start(bf16[512,512]{1,0:T(8,128)(2,1)} %v.7), channel_id=1, source_target_pairs={{0,8},{8,16},{16,24},{24,32},{32,40},{40,48},{48,56},{56,64},{64,7... | collective-permute-start | bytes 1572872 | tf_op jit(solution)/shard_map/ppermute | solution.py:302
  29.5 41.3 %collective-permute-start.5 = (bf16[512,512]{1,0:T(8,128)(2,1)}, bf16[512,512]{1,0:T(8,128)(2,1)S(1)}, u32[]{:S(2)}, u32[]{:S(2)}) collective-permute-start(bf16[512,512]{1,0:T(8,128)(2,1)} %refs_0_.1), channel_id=1, source_target_pairs={{0,6},{1,7},{2,0},{3,1},{4,2},{5,3},{6,4},{7,5},{8,14},{9,15},{10,... | collective-permute-start | bytes 1572872 | tf_op jit(solution)/shard_map/ppermute | solution.py:328
  32.3 38.5 %collective-permute-start.4 = (bf16[512,512]{1,0:T(8,128)(2,1)}, bf16[512,512]{1,0:T(8,128)(2,1)S(1)}, u32[]{:S(2)}, u32[]{:S(2)}) collective-permute-start(bf16[512,512]{1,0:T(8,128)(2,1)} %refs_0_.1), channel_id=1, source_target_pairs={{0,4},{1,5},{2,6},{3,7},{4,0},{5,1},{6,2},{7,3},{8,12},{9,13},{10,... | collective-permute-start | bytes 1572872 | tf_op jit(solution)/shard_map/ppermute | solution.py:328
  33.1 37.7 %collective-permute-start.3 = (bf16[512,512]{1,0:T(8,128)(2,1)}, bf16[512,512]{1,0:T(8,128)(2,1)S(1)}, u32[]{:S(2)}, u32[]{:S(2)}) collective-permute-start(bf16[512,512]{1,0:T(8,128)(2,1)} %refs_0_.1), channel_id=1, source_target_pairs={{0,2},{1,3},{2,4},{3,5},{4,6},{5,7},{6,0},{7,1},{8,10},{9,11},{10,... | collective-permute-start | bytes 1572872 | tf_op jit(solution)/shard_map/ppermute | solution.py:328
  38.4 0.7 copy-start.17
  40.7 14.4 %copy-start.4 = (bf16[512,512]{1,0:T(8,128)(2,1)}, bf16[512,512]{1,0:T(8,128)(2,1)S(1)}, u32[]{:S(2)}) copy-start(bf16[512,512]{1,0:T(8,128)(2,1)S(1)} %collective-permute-done.kw) | copy-start | bytes 1572868
  40.7 34.8 %collective-permute-start.2 = (bf16[512,512]{1,0:T(8,128)(2,1)}, bf16[512,512]{1,0:T(8,128)(2,1)S(1)}, u32[]{:S(2)}, u32[]{:S(2)}) collective-permute-start(bf16[512,512]{1,0:T(8,128)(2,1)} %refs_0_.1), channel_id=1, source_target_pairs={{0,0},{1,1},{2,64},{3,65},{4,128},{5,129},{6,192},{7,193},{8,8},{9... | collective-permute-start | bytes 1572872 | tf_op jit(solution)/shard_map/ppermute | solution.py:351
  47.3 17.9 %all-to-all-start.1 = ((bf16[32,16,128]{2,1,0:T(8,128)(2,1)}), bf16[32,16,128]{2,1,0:T(8,128)(2,1)S(1)}, u32[]{:S(2)}, u32[]{:S(2)}) async-start(bf16[32,16,128]{2,1,0:T(8,128)(2,1)} %shard_map.93), calls=%async_computation.1 | async-start | bytes 262144 | tf_op jit(solution)/shard_map/all_to_all | solution.py:234
  55.1 0.8 copy-start.5
  65.2 0.7 copy-start.6
  70.2 0.6 copy-start.1
  70.8 6.1 %copy-start.11 = (bf16[512,512]{1,0:T(8,128)(2,1)}, bf16[512,512]{1,0:T(8,128)(2,1)S(1)}, u32[]{:S(2)}) copy-start(bf16[512,512]{1,0:T(8,128)(2,1)S(1)} %collective-permute-done.5.refs_3_) | copy-start | bytes 1572868
  70.8 4.6 %copy-start.12 = (bf16[512,512]{1,0:T(8,128)(2,1)}, bf16[512,512]{1,0:T(8,128)(2,1)S(1)}, u32[]{:S(2)}) copy-start(bf16[512,512]{1,0:T(8,128)(2,1)S(1)} %collective-permute-done.4.refs_2_) | copy-start | bytes 1572868
  70.9 4.6 %copy-start.13 = (bf16[512,512]{1,0:T(8,128)(2,1)}, bf16[512,512]{1,0:T(8,128)(2,1)S(1)}, u32[]{:S(2)}) copy-start(bf16[512,512]{1,0:T(8,128)(2,1)S(1)} %collective-permute-done.3.refs_1_) | copy-start | bytes 1572868
  77.0 4.9 %copy-start.8 = (bf16[512,512]{1,0:T(8,128)(2,1)S(1)}, bf16[512,512]{1,0:T(8,128)(2,1)}, u32[]{:S(2)}) copy-start(bf16[512,512]{1,0:T(8,128)(2,1)} %get-tuple-element.120.refs_0_) | copy-start | bytes 1572868
  77.0 41.3 %copy-start.7 = (bf16[512,512]{1,0:T(8,128)(2,1)S(1)}, bf16[512,512]{1,0:T(8,128)(2,1)}, u32[]{:S(2)}) copy-start(bf16[512,512]{1,0:T(8,128)(2,1)} %refs_0_.1) | copy-start | bytes 1572868
  77.0 41.3 %all-to-all-start.2 = ((bf16[4,512,512]{2,1,0:T(8,128)(2,1)}), bf16[4,512,512]{2,1,0:T(8,128)(2,1)S(1)}, u32[]{:S(2)}, u32[]{:S(2)}) async-start(bf16[4,512,512]{2,1,0:T(8,128)(2,1)} %broadcast_in_dim.2), calls=%async_computation.2 | async-start | bytes 4194304 | tf_op jit(solution)/shard_map/all_to_all | solution.py:310
  81.8 139.0 %reduce-scatter.2.cloned.1.call-start = ((), (), s32[]{:S(2)}) async-start(), calls=%async_computation.7 | async-start | bytes 4718592 | tf_op jit(solution)/shard_map/reduce_scatter | solution.py:428
  81.8 24.6 %collective-permute-start.8 = (bf16[512,512]{1,0:T(8,128)(2,1)S(1)}, bf16[512,512]{1,0:T(8,128)(2,1)S(1)}, u32[]{:S(2)}, u32[]{:S(2)}) collective-permute-start(bf16[512,512]{1,0:T(8,128)(2,1)S(1)} %copy-done.8), channel_id=1, source_target_pairs={{0,192},{8,200},{16,208},{24,216},{32,224},{40,232},{48,240},{56,2... | collective-permute-start | bytes 1572872 | tf_op jit(solution)/shard_map/ppermute | solution.py:319
  85.4 21.4 %collective-permute-start.7 = (bf16[512,512]{1,0:T(8,128)(2,1)S(1)}, bf16[512,512]{1,0:T(8,128)(2,1)S(1)}, u32[]{:S(2)}, u32[]{:S(2)}) collective-permute-start(bf16[512,512]{1,0:T(8,128)(2,1)S(1)} %copy-done.8), channel_id=1, source_target_pairs={{0,128},{8,136},{16,144},{24,152},{32,160},{40,168},{48,176},{56,1... | collective-permute-start | bytes 1572872 | tf_op jit(solution)/shard_map/ppermute | solution.py:319
  88.8 29.5 %collective-permute-start.6 = (bf16[512,512]{1,0:T(8,128)(2,1)S(1)}, bf16[512,512]{1,0:T(8,128)(2,1)}, u32[]{:S(2)}, u32[]{:S(2)}) collective-permute-start(bf16[512,512]{1,0:T(8,128)(2,1)S(1)} %copy-done.8), channel_id=1, source_target_pairs={{0,64},{8,72},{16,80},{24,88},{32,96},{40,104},{48,112},{56,120},{... | collective-permute-start | bytes 1572872 | tf_op jit(solution)/shard_map/ppermute | solution.py:319
  106.4 0.8 copy-start.9
  107.2 0.8 copy-start.10
  118.2 19.7 %copy-start.2 = (bf16[4,512,512]{2,1,0:T(8,128)(2,1)}, bf16[4,512,512]{2,1,0:T(8,128)(2,1)S(1)}, u32[]{:S(2)}) copy-start(bf16[4,512,512]{2,1,0:T(8,128)(2,1)S(1)} %all-to-all-done.2.mine) | copy-start | bytes 6291460
  118.2 6.3 %collective-permute-start.9 = (bf16[4,512,512]{2,1,0:T(8,128)(2,1)S(1)}, bf16[4,512,512]{2,1,0:T(8,128)(2,1)}, u32[]{:S(2)}, u32[]{:S(2)}) collective-permute-start(bf16[4,512,512]{2,1,0:T(8,128)(2,1)S(1)} %all-to-all-done.2.mine), channel_id=1, source_target_pairs={{0,1},{1,0},{2,3},{3,2},{4,5},{5,4},{6,7},{7,6},{8,9},{9,8},{10,11... | collective-permute-start | bytes 6291464 | tf_op jit(solution)/shard_map/ppermute | solution.py:334
  118.3 6.3 %collective-permute-start.10 = (bf16[512,512]{1,0:T(8,128)(2,1)S(1)}, bf16[512,512]{1,0:T(8,128)(2,1)S(1)}, u32[]{:S(2)}, u32[]{:S(2)}) collective-permute-start(bf16[512,512]{1,0:T(8,128)(2,1)S(1)} %copy-done.7), channel_id=1, source_target_pairs={{0,1},{1,0},{2,3},{3,2},{4,5},{5,4},{6,7},{7,6},{8,9},{9,8},{10,11... | collective-permute-start | bytes 1572872 | tf_op jit(solution)/shard_map/ppermute | solution.py:334
  118.8 5.8 %collective-permute-start.11 = (bf16[512,512]{1,0:T(8,128)(2,1)}, bf16[512,512]{1,0:T(8,128)(2,1)}, u32[]{:S(2)}, u32[]{:S(2)}) collective-permute-start(bf16[512,512]{1,0:T(8,128)(2,1)} %copy-done.13), channel_id=1, source_target_pairs={{0,1},{1,0},{2,3},{3,2},{4,5},{5,4},{6,7},{7,6},{8,9},{9,8},{10,11... | collective-permute-start | bytes 1572872 | tf_op jit(solution)/shard_map/ppermute | solution.py:334
  118.9 6.1 %collective-permute-start.12 = (bf16[512,512]{1,0:T(8,128)(2,1)}, bf16[512,512]{1,0:T(8,128)(2,1)}, u32[]{:S(2)}, u32[]{:S(2)}) collective-permute-start(bf16[512,512]{1,0:T(8,128)(2,1)} %copy-done.12), channel_id=1, source_target_pairs={{0,1},{1,0},{2,3},{3,2},{4,5},{5,4},{6,7},{7,6},{8,9},{9,8},{10,11... | collective-permute-start | bytes 1572872 | tf_op jit(solution)/shard_map/ppermute | solution.py:334
  119.3 6.5 %collective-permute-start.13 = (bf16[512,512]{1,0:T(8,128)(2,1)}, bf16[512,512]{1,0:T(8,128)(2,1)}, u32[]{:S(2)}, u32[]{:S(2)}) collective-permute-start(bf16[512,512]{1,0:T(8,128)(2,1)} %copy-done.11), channel_id=1, source_target_pairs={{0,1},{1,0},{2,3},{3,2},{4,5},{5,4},{6,7},{7,6},{8,9},{9,8},{10,11... | collective-permute-start | bytes 1572872 | tf_op jit(solution)/shard_map/ppermute | solution.py:334
  124.5 1.2 copy-start.14
  148.2 0.6 copy-start
  148.8 53.3 %collective-permute-start.21 = (bf16[896,512]{1,0:T(8,128)(2,1)}, bf16[896,512]{1,0:T(8,128)(2,1)S(1)}, u32[]{:S(2)}, u32[]{:S(2)}) collective-permute-start(bf16[896,512]{1,0:T(8,128)(2,1)} %get-tuple-element.135), channel_id=1, source_target_pairs={{8,0},{16,8},{24,16},{32,24},{40,32},{48,40},{56,48},{64,56},{72,6... | collective-permute-start | bytes 2752520 | tf_op jit(solution)/shard_map/ppermute | solution.py:302
  155.4 24.0 %all-to-all-start.3 = ((bf16[32,16,128]{2,1,0:T(8,128)(2,1)}), bf16[32,16,128]{2,1,0:T(8,128)(2,1)S(1)}, u32[]{:S(2)}, u32[]{:S(2)}) async-start(bf16[32,16,128]{2,1,0:T(8,128)(2,1)} %bitcast.4), calls=%async_computation.4 | async-start | bytes 262144 | tf_op jit(solution)/shard_map/all_to_all | solution.py:227
  173.1 24.0 %collective-permute-start.14 = (bf16[512,128]{1,0:T(8,128)(2,1)}, bf16[512,128]{1,0:T(8,128)(2,1)S(1)}, u32[]{:S(2)}, u32[]{:S(2)}) collective-permute-start(bf16[512,128]{1,0:T(8,128)(2,1)} %get-tuple-element.125), channel_id=1, source_target_pairs={{0,8},{8,16},{16,24},{24,32},{32,40},{40,48},{48,56},{56,0},{64,72... | collective-permute-start | bytes 393224 | tf_op jit(solution)/shard_map/ppermute | solution.py:338
  174.6 27.0 %collective-permute-start.15 = (bf16[512,128]{1,0:T(8,128)(2,1)}, bf16[512,128]{1,0:T(8,128)(2,1)S(1)}, u32[]{:S(2)}, u32[]{:S(2)}) collective-permute-start(bf16[512,128]{1,0:T(8,128)(2,1)} %get-tuple-element.126), channel_id=1, source_target_pairs={{0,16},{8,24},{16,32},{24,40},{32,48},{40,56},{48,0},{56,8},{64,80... | collective-permute-start | bytes 393224 | tf_op jit(solution)/shard_map/ppermute | solution.py:338
  179.4 0.7 copy-start.16
  181.6 29.1 %all-to-all-start.4 = ((bf16[32,16,128]{2,1,0:T(8,128)(2,1)}), bf16[32,16,128]{2,1,0:T(8,128)(2,1)S(1)}, u32[]{:S(2)}, u32[]{:S(2)}) async-start(bf16[32,16,128]{2,1,0:T(8,128)(2,1)} %shard_map.98), calls=%async_computation.5 | async-start | bytes 262144 | tf_op jit(solution)/shard_map/all_to_all | solution.py:234
  191.1 24.7 %collective-permute-start.16 = (bf16[512,128]{1,0:T(8,128)(2,1)}, bf16[512,128]{1,0:T(8,128)(2,1)S(1)}, u32[]{:S(2)}, u32[]{:S(2)}) collective-permute-start(bf16[512,128]{1,0:T(8,128)(2,1)} %get-tuple-element.127), channel_id=1, source_target_pairs={{0,24},{8,32},{16,40},{24,48},{32,56},{40,0},{48,8},{56,16},{64,88... | collective-permute-start | bytes 393224 | tf_op jit(solution)/shard_map/ppermute | solution.py:338
  194.4 21.4 %collective-permute-start.17 = (bf16[512,128]{1,0:T(8,128)(2,1)}, bf16[512,128]{1,0:T(8,128)(2,1)S(1)}, u32[]{:S(2)}, u32[]{:S(2)}) collective-permute-start(bf16[512,128]{1,0:T(8,128)(2,1)} %get-tuple-element.128), channel_id=1, source_target_pairs={{0,32},{8,40},{16,48},{24,56},{32,0},{40,8},{48,16},{56,24},{64,96... | collective-permute-start | bytes 393224 | tf_op jit(solution)/shard_map/ppermute | solution.py:338
  197.1 18.7 %collective-permute-start.18 = (bf16[512,128]{1,0:T(8,128)(2,1)}, bf16[512,128]{1,0:T(8,128)(2,1)S(1)}, u32[]{:S(2)}, u32[]{:S(2)}) collective-permute-start(bf16[512,128]{1,0:T(8,128)(2,1)} %get-tuple-element.129), channel_id=1, source_target_pairs={{0,40},{8,48},{16,56},{24,0},{32,8},{40,16},{48,24},{56,32},{64,10... | collective-permute-start | bytes 393224 | tf_op jit(solution)/shard_map/ppermute | solution.py:338
  201.6 16.5 %collective-permute-start.19 = (bf16[512,128]{1,0:T(8,128)(2,1)}, bf16[512,128]{1,0:T(8,128)(2,1)S(1)}, u32[]{:S(2)}, u32[]{:S(2)}) collective-permute-start(bf16[512,128]{1,0:T(8,128)(2,1)} %get-tuple-element.130), channel_id=1, source_target_pairs={{0,48},{8,56},{16,0},{24,8},{32,16},{40,24},{48,32},{56,40},{64,11... | collective-permute-start | bytes 393224 | tf_op jit(solution)/shard_map/ppermute | solution.py:338
  202.1 8.6 %copy-start.3 = (bf16[896,512]{1,0:T(8,128)(2,1)}, bf16[896,512]{1,0:T(8,128)(2,1)S(1)}, u32[]{:S(2)}) copy-start(bf16[896,512]{1,0:T(8,128)(2,1)S(1)} %collective-permute-done.21.rk.rv) | copy-start | bytes 2752516
  202.1 17.9 %collective-permute-start.20 = (bf16[512,128]{1,0:T(8,128)(2,1)}, bf16[512,128]{1,0:T(8,128)(2,1)S(1)}, u32[]{:S(2)}, u32[]{:S(2)}) collective-permute-start(bf16[512,128]{1,0:T(8,128)(2,1)} %get-tuple-element.131), channel_id=1, source_target_pairs={{0,56},{8,0},{16,8},{24,16},{32,24},{40,32},{48,40},{56,48},{64,12... | collective-permute-start | bytes 393224 | tf_op jit(solution)/shard_map/ppermute | solution.py:338
  210.7 0.7 copy-start.15
  211.4 8.7 %copy-start.18 = (bf16[512,128]{1,0:T(8,128)(2,1)S(1)}, bf16[512,128]{1,0:T(8,128)(2,1)}, u32[]{:S(2)}) copy-start(bf16[512,128]{1,0:T(8,128)(2,1)} %get-tuple-element.139) | copy-start | bytes 393220
Sparse Core Ops, SparseCore 0:
  10.5 107.5 all-gather.1
  138.1 44.2 reduce-scatter.1

commit v9 on v8

--- a/solution.py
+++ b/solution.py
@@ -409,11 +409,11 @@
     turned_grad, hopped, mixed_t = lax.optimization_barrier((turned_grad, hopped, mixed_t))
     mine = spread(turned_grad, "head", X_GROUPS)
     across_y = [mixed_t] + [hop_y(mixed_t, by) for by in range(1, YS)]
-    grads = [grad_y] + hopped
+    mine, first, hopped = lax.optimization_barrier((mine, grad_y, hopped))
+    grads = [first] + hopped
     grads = grads + [swap_core(g) for g in grads]
-    mine, across_y = lax.optimization_barrier((mine, across_y))
+    mine, across_y, full_w = lax.optimization_barrier((mine, across_y, full_w))
     other = swap_core(mine)
-    mine, other, across_y, full_w = lax.optimization_barrier((mine, other, across_y, full_w))
     fixed = pl.BlockSpec((rows, width), lambda *_: (0, 0))
     by_block = pl.BlockSpec((rows, width), lambda t, head: (0, block_id(t, head)))
     partial_value, grad_mixed = call(

time: 230 us -> 226 us (0.983); the launches traced: 228 us -> 221 us
  waiting for transfers between devices: 50.8 us -> 41.6 us
  starting transfers between devices: 88.9 us -> 91.6 us
    all_to_all x1, waiting for transfers between devices: 0.01 us -> 19.9 us  [exchange(): return lax.all_to_all(pieces, axis, 0, 0, axis_index_groups=groups)]
    ppermute x3, waiting for transfers between devices: 28.1 us -> 8.39 us  [hop_y(): lax.ppermute(shard, 'seq', [(y * ZS + z, (y + by) % YS * ZS + z) for y in...]
    ppermute x5, waiting for transfers between devices: 6.37 us -> 0.01 us  [swap_core(): return lax.ppermute(shard, 'head', [(i, i ^ 1) for i in range(2 * XS)])]
    all_to_all x2, waiting for transfers between devices: 6.84 us -> 3.62 us  [carry_states(): met = lax.all_to_all(pieces, 'seq', 0, 0)]
    all_to_all x1, starting transfers between devices: 4.87 us -> 7.5 us  [exchange(): return lax.all_to_all(pieces, axis, 0, 0, axis_index_groups=groups)]
    all_gather x1, waiting for transfers between devices: 0.01 us -> 2.6 us  [shards(): full_w = lax.all_gather(w_out, 'seq', axis=1, tiled=True)]
    ppermute x1, waiting for transfers between devices: 4.56 us -> 2.13 us  [turn_xy(): return lax.ppermute(shard, ('seq', 'head'), pairs)]
    unnamed x38 -> x34, local copies, waits for them, and re-layouts: 5.94 us -> 5.96 us
  transfers between devices with their start and end apart: 29 -> 29, of which waited for: 11 -> 8; matrix products, arithmetic and copies ran while one was open for 1% -> 1% of each run, Pallas kernels for 23% -> 24%
where the time goes in v9:
time: 226 us; the launch traced here: 221 us
  starting transfers between devices  91.6 us (41%)
  Pallas kernels  65.4 us (29%)
  waiting for transfers between devices  41.6 us (18%)
  between operations  14.3 us (6%)
  local copies, waits for them, and re-layouts  7.42 us (3%)
    pallas_call x9, Pallas kernels, call(): run(*args[:prefetch], *(kept(a) for a in args[prefetch:]))  62.2 us
    all_to_all x1, waiting for transfers between devices, exchange(): return lax.all_to_all(pieces, axis, 0, 0, axis_index_groups=groups)  19.9 us
    all_to_all x2, starting transfers between devices, carry_states(): met = lax.all_to_all(pieces, 'seq', 0, 0)  19.5 us
    all_to_all x2, starting transfers between devices, carry_states(): lax.all_to_all(done, 'seq', 0, 0).reshape(local.shape)  16.5 us
    ppermute x7, starting transfers between devices, hop_z(): lax.ppermute(shard, 'seq', [(y * ZS + z, y * ZS + (z + by) % ZS) for y in...  15.4 us
    ppermute x3, starting transfers between devices, shifted(): return lax.ppermute(shard, 'seq', pairs)  11.9 us
    ppermute x3, waiting for transfers between devices, hop_y(): lax.ppermute(shard, 'seq', [(y * ZS + z, (y + by) % YS * ZS + z) for y in...  8.39 us
    all_to_all x1, starting transfers between devices, exchange(): return lax.all_to_all(pieces, axis, 0, 0, axis_index_groups=groups)  7.5 us
  transfers between devices with their start and end apart: 29, of which 8 were waited for; matrix products, arithmetic and copies ran while one was open for 1% of the time, Pallas kernels for 24%

profile of v9, /device:TPU:16, one launch (start us, length us, event | category | flops | bytes accessed | tf_op | source)
XLA Modules:
  0.0 221.2 jit_solution(9185401520266227957)
XLA Ops:
  7.2 0.7 all-gather.2.cloned.1.call-update
  7.9 3.7 %shard_map.92 = bf16[4,128,128]{2,1,0:T(8,128)(2,1)} custom-call(bf16[512,512]{1,0:T(8,128)(2,1)} %k.7, bf16[512,512]{1,0:T(8,128)(2,1)} %v.7), custom_call_target="tpu_custom_call" | custom-call | tf_op jit(solution)/shard_map/pallas_call | solution.py:56
  11.6 3.8 %collective-permute-start = (bf16[512,512]{1,0:T(8,128)(2,1)}, bf16[512,512]{1,0:T(8,128)(2,1)S(1)}, u32[]{:S(2)}, u32[]{:S(2)}) collective-permute-start(bf16[512,512]{1,0:T(8,128)(2,1)} %k.7), channel_id=1, source_target_pairs={{0,8},{8,16},{16,24},{24,32},{32,40},{40,48},{48,56},{56,64},{64,7... | collective-permute-start | bytes 1572872 | tf_op jit(solution)/shard_map/ppermute | solution.py:302
  15.4 10.7 %all-to-all-start = ((bf16[32,16,128]{2,1,0:T(8,128)(2,1)}), bf16[32,16,128]{2,1,0:T(8,128)(2,1)S(1)}, u32[]{:S(2)}, u32[]{:S(2)}) async-start(bf16[32,16,128]{2,1,0:T(8,128)(2,1)} %bitcast.1), calls=%async_computation | async-start | bytes 262144 | tf_op jit(solution)/shard_map/all_to_all | solution.py:227
  26.1 3.4 %collective-permute-start.1 = (bf16[512,512]{1,0:T(8,128)(2,1)}, bf16[512,512]{1,0:T(8,128)(2,1)S(1)}, u32[]{:S(2)}, u32[]{:S(2)}) collective-permute-start(bf16[512,512]{1,0:T(8,128)(2,1)} %v.7), channel_id=1, source_target_pairs={{0,8},{8,16},{16,24},{24,32},{32,40},{40,48},{48,56},{56,64},{64,7... | collective-permute-start | bytes 1572872 | tf_op jit(solution)/shard_map/ppermute | solution.py:302
  29.5 3.1 %collective-permute-start.4 = (bf16[512,512]{1,0:T(8,128)(2,1)}, bf16[512,512]{1,0:T(8,128)(2,1)S(1)}, u32[]{:S(2)}, u32[]{:S(2)}) collective-permute-start(bf16[512,512]{1,0:T(8,128)(2,1)} %refs_0_), channel_id=1, source_target_pairs={{0,4},{1,5},{2,6},{3,7},{4,0},{5,1},{6,2},{7,3},{8,12},{9,13},{10,... | collective-permute-start | bytes 1572872 | tf_op jit(solution)/shard_map/ppermute | solution.py:328
  33.2 2.6 %collective-permute-start.5 = (bf16[512,512]{1,0:T(8,128)(2,1)}, bf16[512,512]{1,0:T(8,128)(2,1)S(1)}, u32[]{:S(2)}, u32[]{:S(2)}) collective-permute-start(bf16[512,512]{1,0:T(8,128)(2,1)} %refs_0_), channel_id=1, source_target_pairs={{0,6},{1,7},{2,0},{3,1},{4,2},{5,3},{6,4},{7,5},{8,14},{9,15},{10,... | collective-permute-start | bytes 1572872 | tf_op jit(solution)/shard_map/ppermute | solution.py:328
  35.8 2.6 %all-to-all-done.x = bf16[32,16,128]{2,1,0:T(8,128)(2,1)S(1)} async-done(((bf16[32,16,128]{2,1,0:T(8,128)(2,1)}), bf16[32,16,128]{2,1,0:T(8,128)(2,1)S(1)}, u32[]{:S(2)}, u32[]{:S(2)}) %all-to-all-start) | async-done | bytes 131104 | tf_op jit(solution)/shard_map/all_to_all | solution.py:227
  38.4 0.7 copy-done.15
  39.1 1.6 shard_map.93
  40.7 6.6 %collective-permute-start.2 = (bf16[512,512]{1,0:T(8,128)(2,1)}, bf16[512,512]{1,0:T(8,128)(2,1)S(1)}, u32[]{:S(2)}, u32[]{:S(2)}) collective-permute-start(bf16[512,512]{1,0:T(8,128)(2,1)} %refs_0_), channel_id=1, source_target_pairs={{0,0},{1,1},{2,64},{3,65},{4,128},{5,129},{6,192},{7,193},{8,8},{9... | collective-permute-start | bytes 1572872 | tf_op jit(solution)/shard_map/ppermute | solution.py:351
  47.3 7.8 %all-to-all-start.1 = ((bf16[32,16,128]{2,1,0:T(8,128)(2,1)}), bf16[32,16,128]{2,1,0:T(8,128)(2,1)S(1)}, u32[]{:S(2)}, u32[]{:S(2)}) async-start(bf16[32,16,128]{2,1,0:T(8,128)(2,1)} %shard_map.93), calls=%async_computation.1 | async-start | bytes 262144 | tf_op jit(solution)/shard_map/all_to_all | solution.py:234
  55.1 0.8 copy-done.6
  55.9 9.3 %shard_map.94 = (bf16[4,512,512]{2,1,0:T(8,128)(2,1)}, bf16[4,512,512]{2,1,0:T(8,128)(2,1)}, bf16[4,512,512]{2,1,0:T(8,128)(2,1)}, f32[512,512]{1,0:T(8,128)}, f32[512,512]{1,0:T(8,128)}) custom-call(s32[1]{0:T(128)} %bitcast.3.place, bf16[512,512]{1,0:T(8,128)(2,1)} %q.9, bf16[512,512]{1,0:T(8,128)(2,1)} %k.7, bf16[512,512]{1,0:T(8,128)(2,1)} %v.7, ...), custom_call_target="tpu_custom_call" | custom-call | tf_op jit(solution)/shard_map/pallas_call | solution.py:56
  65.2 0.6 copy-done.7
  65.8 4.4 %shard_map.95 = (f32[512,512]{1,0:T(8,128)}, f32[4,1,512]{2,1,0:T(1,128)S(1)}, bf16[512,512]{1,0:T(8,128)(2,1)}, bf16[512,512]{1,0:T(8,128)(2,1)}) custom-call(bf16[512,512]{1,0:T(8,128)(2,1)} %q.9, bf16[4,128,128]{2,1,0:T(8,128)(2,1)} %bitcast.6, f32[512,512]{1,0:T(8,128)} %get-tuple-element.79.window, f32[512,512]{1,0:T(8,128)} %get-tuple-element.80.intra), custom_call_target="tpu_custom_call" | custom-call | tf_op jit(solution)/shard_map/pallas_call | solution.py:56
  70.9 2.1 collective-permute-done.2
  73.0 1.5 broadcast_in_dim.2
  74.5 7.5 %all-to-all-start.2 = ((bf16[4,512,512]{2,1,0:T(8,128)(2,1)}), bf16[4,512,512]{2,1,0:T(8,128)(2,1)S(1)}, u32[]{:S(2)}, u32[]{:S(2)}) async-start(bf16[4,512,512]{2,1,0:T(8,128)(2,1)} %broadcast_in_dim.2), calls=%async_computation.2 | async-start | bytes 4194304 | tf_op jit(solution)/shard_map/all_to_all | solution.py:310
  82.0 2.2 %collective-permute-start.8 = (bf16[512,512]{1,0:T(8,128)(2,1)S(1)}, bf16[512,512]{1,0:T(8,128)(2,1)}, u32[]{:S(2)}, u32[]{:S(2)}) collective-permute-start(bf16[512,512]{1,0:T(8,128)(2,1)S(1)} %copy-done.9), channel_id=1, source_target_pairs={{0,192},{8,200},{16,208},{24,216},{32,224},{40,232},{48,240},{56,2... | collective-permute-start | bytes 1572872 | tf_op jit(solution)/shard_map/ppermute | solution.py:319
  84.2 2.0 collective-permute-start.7
  86.2 2.4 %collective-permute-start.6 = (bf16[512,512]{1,0:T(8,128)(2,1)S(1)}, bf16[512,512]{1,0:T(8,128)(2,1)}, u32[]{:S(2)}, u32[]{:S(2)}) collective-permute-start(bf16[512,512]{1,0:T(8,128)(2,1)S(1)} %copy-done.9), channel_id=1, source_target_pairs={{0,64},{8,72},{16,80},{24,88},{32,96},{40,104},{48,112},{56,120},{... | collective-permute-start | bytes 1572872 | tf_op jit(solution)/shard_map/ppermute | solution.py:319
  88.7 19.9 %all-to-all-done.2.mine = bf16[4,512,512]{2,1,0:T(8,128)(2,1)S(1)} async-done(((bf16[4,512,512]{2,1,0:T(8,128)(2,1)}), bf16[4,512,512]{2,1,0:T(8,128)(2,1)S(1)}, u32[]{:S(2)}, u32[]{:S(2)}) %all-to-all-start.2) | async-done | bytes 2097184 | tf_op jit(solution)/shard_map/all_to_all | solution.py:310
  109.6 8.4 %collective-permute-done.6.refs_1_ = bf16[512,512]{1,0:T(8,128)(2,1)} collective-permute-done((bf16[512,512]{1,0:T(8,128)(2,1)S(1)}, bf16[512,512]{1,0:T(8,128)(2,1)}, u32[]{:S(2)}, u32[]{:S(2)}) %collective-permute-start.6) | collective-permute-done | bytes 524320 | tf_op jit(solution)/shard_map/ppermute | solution.py:319
  118.0 2.6 %all-gather.2.cloned.1.call-done.w = bf16[512,4096]{1,0:T(8,128)(2,1)} async-done(((bf16[512,128]{1,0:T(8,128)(2,1)}), bf16[512,4096]{1,0:T(8,128)(2,1)}) %all-gather.2.cloned.1.call-update) | async-done | bytes 4194320 | tf_op jit(solution)/shard_map/all_gather | solution.py:370
  120.6 12.2 %shard_map.96 = (bf16[512,4096]{1,0:T(8,128)(2,1)}, bf16[512,512]{1,0:T(8,128)(2,1)}) custom-call(s32[1]{0:T(128)} %bitcast.head, bf16[512,512]{1,0:T(8,128)(2,1)} %get-tuple-element.81.mixed, bf16[512,4096]{1,0:T(8,128)(2,1)} %all-gather.2.cloned.1.call-done.w, bf16[512,512]{1,0:T(8,128)(2,1)} %refs_0_, bf16[512,512]{1,0:T(8,128)(2,1)} %copy-done.11, ...), custom_call_target="tpu_custom_call" | custom-call | tf_op jit(solution)/shard_map/pallas_call | solution.py:56
  132.9 4.2 %shard_map.97 = (bf16[512,512]{1,0:T(8,128)(2,1)}, bf16[4,128,128]{2,1,0:T(8,128)(2,1)}) custom-call(bf16[512,512]{1,0:T(8,128)(2,1)} %q.9, bf16[512,512]{1,0:T(8,128)(2,1)} %get-tuple-element.111.g, f32[512,512]{1,0:T(8,128)} %get-tuple-element.102.normed, f32[4,1,512]{2,1,0:T(1,128)} %copy-done.1), custom_call_target="tpu_custom_call" | custom-call | tf_op jit(solution)/shard_map/pallas_call | solution.py:56
  137.1 6.1 %shard_map.99 = (f32[512,512]{1,0:T(8,128)}, bf16[896,512]{1,0:T(8,128)(2,1)}, f32[4,1,512]{2,1,0:T(1,128)S(1)}) custom-call(bf16[512,512]{1,0:T(8,128)(2,1)} %q.9, bf16[512,512]{1,0:T(8,128)(2,1)} %get-tuple-element.111.g, bf16[512,512]{1,0:T(8,128)(2,1)} %copy-done.5, bf16[512,512]{1,0:T(8,128)(2,1)} %copy-done.6, ...), custom_call_target="tpu_custom_call" | custom-call | tf_op jit(solution)/shard_map/pallas_call | solution.py:56
  143.2 0.6 copy-done
  143.8 4.7 %collective-permute-start.21 = (bf16[896,512]{1,0:T(8,128)(2,1)}, bf16[896,512]{1,0:T(8,128)(2,1)S(1)}, u32[]{:S(2)}, u32[]{:S(2)}) collective-permute-start(bf16[896,512]{1,0:T(8,128)(2,1)} %get-tuple-element.133), channel_id=1, source_target_pairs={{8,0},{16,8},{24,16},{32,24},{40,32},{48,40},{56,48},{64,56},{72,6... | collective-permute-start | bytes 2752520 | tf_op jit(solution)/shard_map/ppermute | solution.py:302
  148.6 1.4 copy-done.4
  149.9 8.7 %all-to-all-start.3 = ((bf16[32,16,128]{2,1,0:T(8,128)(2,1)}), bf16[32,16,128]{2,1,0:T(8,128)(2,1)S(1)}, u32[]{:S(2)}, u32[]{:S(2)}) async-start(bf16[32,16,128]{2,1,0:T(8,128)(2,1)} %bitcast.4), calls=%async_computation.4 | async-start | bytes 262144 | tf_op jit(solution)/shard_map/all_to_all | solution.py:227
  158.8 10.0 %shard_map.101 = (bf16[512,128]{1,0:T(8,128)(2,1)}, bf16[512,128]{1,0:T(8,128)(2,1)}, bf16[512,128]{1,0:T(8,128)(2,1)}, bf16[512,128]{1,0:T(8,128)(2,1)}, bf16[5...) custom-call(s32[3]{0:T(128)S(1)} %pad_add_fusion.place, ...), custom_call_target="tpu_custom_call" | custom-call | tf_op jit(solution)/shard_map/pallas_call | solution.py:56
  168.7 1.5 collective-permute-start.14
  170.2 2.4 %collective-permute-start.15 = (bf16[512,128]{1,0:T(8,128)(2,1)}, bf16[512,128]{1,0:T(8,128)(2,1)S(1)}, u32[]{:S(2)}, u32[]{:S(2)}) collective-permute-start(bf16[512,128]{1,0:T(8,128)(2,1)} %get-tuple-element.124), channel_id=1, source_target_pairs={{0,16},{8,24},{16,32},{24,40},{32,48},{40,56},{48,0},{56,8},{64,80... | collective-permute-start | bytes 393224 | tf_op jit(solution)/shard_map/ppermute | solution.py:338
  172.6 1.0 all-to-all-done.3.x
  173.6 0.7 copy-done.14
  174.3 1.6 shard_map.98
  175.9 8.7 %all-to-all-start.4 = ((bf16[32,16,128]{2,1,0:T(8,128)(2,1)}), bf16[32,16,128]{2,1,0:T(8,128)(2,1)S(1)}, u32[]{:S(2)}, u32[]{:S(2)}) async-start(bf16[32,16,128]{2,1,0:T(8,128)(2,1)} %shard_map.98), calls=%async_computation.5 | async-start | bytes 262144 | tf_op jit(solution)/shard_map/all_to_all | solution.py:234
  184.6 3.3 %collective-permute-start.16 = (bf16[512,128]{1,0:T(8,128)(2,1)}, bf16[512,128]{1,0:T(8,128)(2,1)S(1)}, u32[]{:S(2)}, u32[]{:S(2)}) collective-permute-start(bf16[512,128]{1,0:T(8,128)(2,1)} %get-tuple-element.125), channel_id=1, source_target_pairs={{0,24},{8,32},{16,40},{24,48},{32,56},{40,0},{48,8},{56,16},{64,88... | collective-permute-start | bytes 393224 | tf_op jit(solution)/shard_map/ppermute | solution.py:338
  187.9 2.7 %collective-permute-start.17 = (bf16[512,128]{1,0:T(8,128)(2,1)}, bf16[512,128]{1,0:T(8,128)(2,1)S(1)}, u32[]{:S(2)}, u32[]{:S(2)}) collective-permute-start(bf16[512,128]{1,0:T(8,128)(2,1)} %get-tuple-element.126), channel_id=1, source_target_pairs={{0,32},{8,40},{16,48},{24,56},{32,0},{40,8},{48,16},{56,24},{64,96... | collective-permute-start | bytes 393224 | tf_op jit(solution)/shard_map/ppermute | solution.py:338
  190.6 4.5 %collective-permute-start.18 = (bf16[512,128]{1,0:T(8,128)(2,1)}, bf16[512,128]{1,0:T(8,128)(2,1)S(1)}, u32[]{:S(2)}, u32[]{:S(2)}) collective-permute-start(bf16[512,128]{1,0:T(8,128)(2,1)} %get-tuple-element.127), channel_id=1, source_target_pairs={{0,40},{8,48},{16,56},{24,0},{32,8},{40,16},{48,24},{56,32},{64,10... | collective-permute-start | bytes 393224 | tf_op jit(solution)/shard_map/ppermute | solution.py:338
  196.2 8.0 %shard_map.100 = (bf16[512,512]{1,0:T(8,128)(2,1)}, f32[512,512]{1,0:T(8,128)}, f32[512,512]{1,0:T(8,128)}) custom-call(bf16[512,512]{1,0:T(8,128)(2,1)} %q.9, bf16[512,512]{1,0:T(8,128)(2,1)} %k.7, bf16[512,512]{1,0:T(8,128)(2,1)} %v.7, bf16[512,512]{1,0:T(8,128)(2,1)} %get-tuple-element.111.g, bf16[512,512]{1,0:T(8,128)(2,1)} %get-tuple-element.108.gl, ...), custom_call_target="tpu_custom_call" | custom-call | tf_op jit(solution)/shard_map/pallas_call | solution.py:56
  204.2 0.6 copy-done.13
  204.9 4.4 %shard_map.102 = (bf16[512,512]{1,0:T(8,128)(2,1)}, bf16[512,512]{1,0:T(8,128)(2,1)}) custom-call(bf16[512,512]{1,0:T(8,128)(2,1)} %k.7, bf16[512,512]{1,0:T(8,128)(2,1)} %v.7, bf16[4,128,128]{2,1,0:T(8,128)(2,1)} %bitcast.8, f32[512,512]{1,0:T(8,128)} %get-tuple-element.131.dk, f32[512,512]{1,0:T(8,128)} %get-tuple-element.132.dv, ...), custom_call_target="tpu_custom_call" | custom-call | tf_op jit(solution)/shard_map/pallas_call | solution.py:56
  209.3 2.3 %collective-permute-done.19 = bf16[512,128]{1,0:T(8,128)(2,1)S(1)} collective-permute-done((bf16[512,128]{1,0:T(8,128)(2,1)}, bf16[512,128]{1,0:T(8,128)(2,1)S(1)}, u32[]{:S(2)}, u32[]{:S(2)}) %collective-permute-start.19) | collective-permute-done | bytes 131104 | tf_op jit(solution)/shard_map/ppermute | solution.py:338
  211.6 1.9 collective-permute-done.20
  213.5 0.8 add_multiply_fusion
  (60 shorter events, 3.7 us)
Async XLA Ops:
  7.2 113.4 %all-gather.2.cloned.1.call-start = ((), (), s32[]{:S(2)}) async-start(), calls=%async_computation.6 | async-start | bytes 4325376 | tf_op jit(solution)/shard_map/all_gather | solution.py:370
  11.6 29.1 %collective-permute-start = (bf16[512,512]{1,0:T(8,128)(2,1)}, bf16[512,512]{1,0:T(8,128)(2,1)S(1)}, u32[]{:S(2)}, u32[]{:S(2)}) collective-permute-start(bf16[512,512]{1,0:T(8,128)(2,1)} %k.7), channel_id=1, source_target_pairs={{0,8},{8,16},{16,24},{24,32},{32,40},{40,48},{48,56},{56,64},{64,7... | collective-permute-start | bytes 1572872 | tf_op jit(solution)/shard_map/ppermute | solution.py:302
  15.4 23.0 %all-to-all-start = ((bf16[32,16,128]{2,1,0:T(8,128)(2,1)}), bf16[32,16,128]{2,1,0:T(8,128)(2,1)S(1)}, u32[]{:S(2)}, u32[]{:S(2)}) async-start(bf16[32,16,128]{2,1,0:T(8,128)(2,1)} %bitcast.1), calls=%async_computation | async-start | bytes 262144 | tf_op jit(solution)/shard_map/all_to_all | solution.py:227
  26.1 29.0 %collective-permute-start.1 = (bf16[512,512]{1,0:T(8,128)(2,1)}, bf16[512,512]{1,0:T(8,128)(2,1)S(1)}, u32[]{:S(2)}, u32[]{:S(2)}) collective-permute-start(bf16[512,512]{1,0:T(8,128)(2,1)} %v.7), channel_id=1, source_target_pairs={{0,8},{8,16},{16,24},{24,32},{32,40},{40,48},{48,56},{56,64},{64,7... | collective-permute-start | bytes 1572872 | tf_op jit(solution)/shard_map/ppermute | solution.py:302
  29.5 41.3 %collective-permute-start.4 = (bf16[512,512]{1,0:T(8,128)(2,1)}, bf16[512,512]{1,0:T(8,128)(2,1)S(1)}, u32[]{:S(2)}, u32[]{:S(2)}) collective-permute-start(bf16[512,512]{1,0:T(8,128)(2,1)} %refs_0_), channel_id=1, source_target_pairs={{0,4},{1,5},{2,6},{3,7},{4,0},{5,1},{6,2},{7,3},{8,12},{9,13},{10,... | collective-permute-start | bytes 1572872 | tf_op jit(solution)/shard_map/ppermute | solution.py:328
  32.6 38.2 %collective-permute-start.3 = (bf16[512,512]{1,0:T(8,128)(2,1)}, bf16[512,512]{1,0:T(8,128)(2,1)S(1)}, u32[]{:S(2)}, u32[]{:S(2)}) collective-permute-start(bf16[512,512]{1,0:T(8,128)(2,1)} %refs_0_), channel_id=1, source_target_pairs={{0,2},{1,3},{2,4},{3,5},{4,6},{5,7},{6,0},{7,1},{8,10},{9,11},{10,... | collective-permute-start | bytes 1572872 | tf_op jit(solution)/shard_map/ppermute | solution.py:328
  33.2 37.7 %collective-permute-start.5 = (bf16[512,512]{1,0:T(8,128)(2,1)}, bf16[512,512]{1,0:T(8,128)(2,1)S(1)}, u32[]{:S(2)}, u32[]{:S(2)}) collective-permute-start(bf16[512,512]{1,0:T(8,128)(2,1)} %refs_0_), channel_id=1, source_target_pairs={{0,6},{1,7},{2,0},{3,1},{4,2},{5,3},{6,4},{7,5},{8,14},{9,15},{10,... | collective-permute-start | bytes 1572872 | tf_op jit(solution)/shard_map/ppermute | solution.py:328
  38.4 0.7 copy-start.15
  40.7 14.4 %copy-start.5 = (bf16[512,512]{1,0:T(8,128)(2,1)}, bf16[512,512]{1,0:T(8,128)(2,1)S(1)}, u32[]{:S(2)}) copy-start(bf16[512,512]{1,0:T(8,128)(2,1)S(1)} %collective-permute-done.kw) | copy-start | bytes 1572868
  40.7 32.3 %collective-permute-start.2 = (bf16[512,512]{1,0:T(8,128)(2,1)}, bf16[512,512]{1,0:T(8,128)(2,1)S(1)}, u32[]{:S(2)}, u32[]{:S(2)}) collective-permute-start(bf16[512,512]{1,0:T(8,128)(2,1)} %refs_0_), channel_id=1, source_target_pairs={{0,0},{1,1},{2,64},{3,65},{4,128},{5,129},{6,192},{7,193},{8,8},{9... | collective-permute-start | bytes 1572872 | tf_op jit(solution)/shard_map/ppermute | solution.py:351
  47.3 17.9 %all-to-all-start.1 = ((bf16[32,16,128]{2,1,0:T(8,128)(2,1)}), bf16[32,16,128]{2,1,0:T(8,128)(2,1)S(1)}, u32[]{:S(2)}, u32[]{:S(2)}) async-start(bf16[32,16,128]{2,1,0:T(8,128)(2,1)} %shard_map.93), calls=%async_computation.1 | async-start | bytes 262144 | tf_op jit(solution)/shard_map/all_to_all | solution.py:234
  55.1 0.8 copy-start.6
  65.2 0.7 copy-start.7
  70.2 0.6 copy-start.1
  70.8 3.6 %copy-start.10 = (bf16[512,512]{1,0:T(8,128)(2,1)}, bf16[512,512]{1,0:T(8,128)(2,1)S(1)}, u32[]{:S(2)}) copy-start(bf16[512,512]{1,0:T(8,128)(2,1)S(1)} %collective-permute-done.4.refs_2_) | copy-start | bytes 1572868
  70.8 3.6 %copy-start.11 = (bf16[512,512]{1,0:T(8,128)(2,1)}, bf16[512,512]{1,0:T(8,128)(2,1)S(1)}, u32[]{:S(2)}) copy-start(bf16[512,512]{1,0:T(8,128)(2,1)S(1)} %collective-permute-done.3.refs_1_) | copy-start | bytes 1572868
  70.9 3.6 %copy-start.12 = (bf16[512,512]{1,0:T(8,128)(2,1)}, bf16[512,512]{1,0:T(8,128)(2,1)S(1)}, u32[]{:S(2)}) copy-start(bf16[512,512]{1,0:T(8,128)(2,1)S(1)} %collective-permute-done.5.refs_3_) | copy-start | bytes 1572868
  74.5 7.5 %copy-start.9 = (bf16[512,512]{1,0:T(8,128)(2,1)S(1)}, bf16[512,512]{1,0:T(8,128)(2,1)}, u32[]{:S(2)}) copy-start(bf16[512,512]{1,0:T(8,128)(2,1)} %get-tuple-element.118.refs_0_) | copy-start | bytes 1572868
  74.5 34.1 %copy-start.8 = (bf16[512,512]{1,0:T(8,128)(2,1)S(1)}, bf16[512,512]{1,0:T(8,128)(2,1)}, u32[]{:S(2)}) copy-start(bf16[512,512]{1,0:T(8,128)(2,1)} %refs_0_) | copy-start | bytes 1572868
  74.5 34.1 %all-to-all-start.2 = ((bf16[4,512,512]{2,1,0:T(8,128)(2,1)}), bf16[4,512,512]{2,1,0:T(8,128)(2,1)S(1)}, u32[]{:S(2)}, u32[]{:S(2)}) async-start(bf16[4,512,512]{2,1,0:T(8,128)(2,1)} %broadcast_in_dim.2), calls=%async_computation.2 | async-start | bytes 4194304 | tf_op jit(solution)/shard_map/all_to_all | solution.py:310
  82.0 132.4 %reduce-scatter.2.cloned.1.call-start = ((), (), s32[]{:S(2)}) async-start(), calls=%async_computation.7 | async-start | bytes 4718592 | tf_op jit(solution)/shard_map/reduce_scatter | solution.py:428
  82.0 27.1 %collective-permute-start.8 = (bf16[512,512]{1,0:T(8,128)(2,1)S(1)}, bf16[512,512]{1,0:T(8,128)(2,1)}, u32[]{:S(2)}, u32[]{:S(2)}) collective-permute-start(bf16[512,512]{1,0:T(8,128)(2,1)S(1)} %copy-done.9), channel_id=1, source_target_pairs={{0,192},{8,200},{16,208},{24,216},{32,224},{40,232},{48,240},{56,2... | collective-permute-start | bytes 1572872 | tf_op jit(solution)/shard_map/ppermute | solution.py:319
  84.2 24.9 %collective-permute-start.7 = (bf16[512,512]{1,0:T(8,128)(2,1)S(1)}, bf16[512,512]{1,0:T(8,128)(2,1)}, u32[]{:S(2)}, u32[]{:S(2)}) collective-permute-start(bf16[512,512]{1,0:T(8,128)(2,1)S(1)} %copy-done.9), channel_id=1, source_target_pairs={{0,128},{8,136},{16,144},{24,152},{32,160},{40,168},{48,176},{56,1... | collective-permute-start | bytes 1572872 | tf_op jit(solution)/shard_map/ppermute | solution.py:319
  86.2 31.7 %collective-permute-start.6 = (bf16[512,512]{1,0:T(8,128)(2,1)S(1)}, bf16[512,512]{1,0:T(8,128)(2,1)}, u32[]{:S(2)}, u32[]{:S(2)}) collective-permute-start(bf16[512,512]{1,0:T(8,128)(2,1)S(1)} %copy-done.9), channel_id=1, source_target_pairs={{0,64},{8,72},{16,80},{24,88},{32,96},{40,104},{48,112},{56,120},{... | collective-permute-start | bytes 1572872 | tf_op jit(solution)/shard_map/ppermute | solution.py:319
  108.5 24.3 %copy-start.2 = (bf16[4,512,512]{2,1,0:T(8,128)(2,1)}, bf16[4,512,512]{2,1,0:T(8,128)(2,1)S(1)}, u32[]{:S(2)}) copy-start(bf16[4,512,512]{2,1,0:T(8,128)(2,1)S(1)} %all-to-all-done.2.mine) | copy-start | bytes 6291460
  108.5 12.0 %collective-permute-start.9 = (bf16[512,512]{1,0:T(8,128)(2,1)S(1)}, bf16[512,512]{1,0:T(8,128)(2,1)}, u32[]{:S(2)}, u32[]{:S(2)}) collective-permute-start(bf16[512,512]{1,0:T(8,128)(2,1)S(1)} %copy-done.8), channel_id=1, source_target_pairs={{0,1},{1,0},{2,3},{3,2},{4,5},{5,4},{6,7},{7,6},{8,9},{9,8},{10,11... | collective-permute-start | bytes 1572872 | tf_op jit(solution)/shard_map/ppermute | solution.py:334
  108.6 12.0 %collective-permute-start.10 = (bf16[512,512]{1,0:T(8,128)(2,1)}, bf16[512,512]{1,0:T(8,128)(2,1)}, u32[]{:S(2)}, u32[]{:S(2)}) collective-permute-start(bf16[512,512]{1,0:T(8,128)(2,1)} %copy-done.11), channel_id=1, source_target_pairs={{0,1},{1,0},{2,3},{3,2},{4,5},{5,4},{6,7},{7,6},{8,9},{9,8},{10,11... | collective-permute-start | bytes 1572872 | tf_op jit(solution)/shard_map/ppermute | solution.py:334
  109.1 11.5 %collective-permute-start.11 = (bf16[512,512]{1,0:T(8,128)(2,1)}, bf16[512,512]{1,0:T(8,128)(2,1)}, u32[]{:S(2)}, u32[]{:S(2)}) collective-permute-start(bf16[512,512]{1,0:T(8,128)(2,1)} %copy-done.10), channel_id=1, source_target_pairs={{0,1},{1,0},{2,3},{3,2},{4,5},{5,4},{6,7},{7,6},{8,9},{9,8},{10,11... | collective-permute-start | bytes 1572872 | tf_op jit(solution)/shard_map/ppermute | solution.py:334
  109.2 11.4 %collective-permute-start.12 = (bf16[512,512]{1,0:T(8,128)(2,1)}, bf16[512,512]{1,0:T(8,128)(2,1)}, u32[]{:S(2)}, u32[]{:S(2)}) collective-permute-start(bf16[512,512]{1,0:T(8,128)(2,1)} %copy-done.12), channel_id=1, source_target_pairs={{0,1},{1,0},{2,3},{3,2},{4,5},{5,4},{6,7},{7,6},{8,9},{9,8},{10,11... | collective-permute-start | bytes 1572872 | tf_op jit(solution)/shard_map/ppermute | solution.py:334
  132.8 15.7 %collective-permute-start.13 = (bf16[4,512,512]{2,1,0:T(8,128)(2,1)S(1)}, bf16[4,512,512]{2,1,0:T(8,128)(2,1)S(1)}, u32[]{:S(2)}, u32[]{:S(2)}) collective-permute-start(bf16[4,512,512]{2,1,0:T(8,128)(2,1)S(1)} %all-to-all-done.2.mine), channel_id=1, source_target_pairs={{0,1},{1,0},{2,3},{3,2},{4,5},{5,4},{6,7},{7,6},{8,9},{9,8},{10,11... | collective-permute-start | bytes 6291464 | tf_op jit(solution)/shard_map/ppermute | solution.py:334
  143.2 0.6 copy-start
  143.8 46.8 %collective-permute-start.21 = (bf16[896,512]{1,0:T(8,128)(2,1)}, bf16[896,512]{1,0:T(8,128)(2,1)S(1)}, u32[]{:S(2)}, u32[]{:S(2)}) collective-permute-start(bf16[896,512]{1,0:T(8,128)(2,1)} %get-tuple-element.133), channel_id=1, source_target_pairs={{8,0},{16,8},{24,16},{32,24},{40,32},{48,40},{56,48},{64,56},{72,6... | collective-permute-start | bytes 2752520 | tf_op jit(solution)/shard_map/ppermute | solution.py:302
  148.6 1.4 copy-start.4
  149.9 23.7 %all-to-all-start.3 = ((bf16[32,16,128]{2,1,0:T(8,128)(2,1)}), bf16[32,16,128]{2,1,0:T(8,128)(2,1)S(1)}, u32[]{:S(2)}, u32[]{:S(2)}) async-start(bf16[32,16,128]{2,1,0:T(8,128)(2,1)} %bitcast.4), calls=%async_computation.4 | async-start | bytes 262144 | tf_op jit(solution)/shard_map/all_to_all | solution.py:227
  168.7 26.3 %collective-permute-start.14 = (bf16[512,128]{1,0:T(8,128)(2,1)}, bf16[512,128]{1,0:T(8,128)(2,1)S(1)}, u32[]{:S(2)}, u32[]{:S(2)}) collective-permute-start(bf16[512,128]{1,0:T(8,128)(2,1)} %get-tuple-element.123), channel_id=1, source_target_pairs={{0,8},{8,16},{16,24},{24,32},{32,40},{40,48},{48,56},{56,0},{64,72... | collective-permute-start | bytes 393224 | tf_op jit(solution)/shard_map/ppermute | solution.py:338
  170.2 25.4 %collective-permute-start.15 = (bf16[512,128]{1,0:T(8,128)(2,1)}, bf16[512,128]{1,0:T(8,128)(2,1)S(1)}, u32[]{:S(2)}, u32[]{:S(2)}) collective-permute-start(bf16[512,128]{1,0:T(8,128)(2,1)} %get-tuple-element.124), channel_id=1, source_target_pairs={{0,16},{8,24},{16,32},{24,40},{32,48},{40,56},{48,0},{56,8},{64,80... | collective-permute-start | bytes 393224 | tf_op jit(solution)/shard_map/ppermute | solution.py:338
  173.6 0.7 copy-start.14
  175.9 28.3 %all-to-all-start.4 = ((bf16[32,16,128]{2,1,0:T(8,128)(2,1)}), bf16[32,16,128]{2,1,0:T(8,128)(2,1)S(1)}, u32[]{:S(2)}, u32[]{:S(2)}) async-start(bf16[32,16,128]{2,1,0:T(8,128)(2,1)} %shard_map.98), calls=%async_computation.5 | async-start | bytes 262144 | tf_op jit(solution)/shard_map/all_to_all | solution.py:234
  184.6 24.7 %collective-permute-start.16 = (bf16[512,128]{1,0:T(8,128)(2,1)}, bf16[512,128]{1,0:T(8,128)(2,1)S(1)}, u32[]{:S(2)}, u32[]{:S(2)}) collective-permute-start(bf16[512,128]{1,0:T(8,128)(2,1)} %get-tuple-element.125), channel_id=1, source_target_pairs={{0,24},{8,32},{16,40},{24,48},{32,56},{40,0},{48,8},{56,16},{64,88... | collective-permute-start | bytes 393224 | tf_op jit(solution)/shard_map/ppermute | solution.py:338
  187.9 21.4 %collective-permute-start.17 = (bf16[512,128]{1,0:T(8,128)(2,1)}, bf16[512,128]{1,0:T(8,128)(2,1)S(1)}, u32[]{:S(2)}, u32[]{:S(2)}) collective-permute-start(bf16[512,128]{1,0:T(8,128)(2,1)} %get-tuple-element.126), channel_id=1, source_target_pairs={{0,32},{8,40},{16,48},{24,56},{32,0},{40,8},{48,16},{56,24},{64,96... | collective-permute-start | bytes 393224 | tf_op jit(solution)/shard_map/ppermute | solution.py:338
  190.6 13.6 %copy-start.3 = (bf16[896,512]{1,0:T(8,128)(2,1)}, bf16[896,512]{1,0:T(8,128)(2,1)S(1)}, u32[]{:S(2)}) copy-start(bf16[896,512]{1,0:T(8,128)(2,1)S(1)} %collective-permute-done.21.rk.rv) | copy-start | bytes 2752516
  190.6 18.7 %collective-permute-start.18 = (bf16[512,128]{1,0:T(8,128)(2,1)}, bf16[512,128]{1,0:T(8,128)(2,1)S(1)}, u32[]{:S(2)}, u32[]{:S(2)}) collective-permute-start(bf16[512,128]{1,0:T(8,128)(2,1)} %get-tuple-element.127), channel_id=1, source_target_pairs={{0,40},{8,48},{16,56},{24,0},{32,8},{40,16},{48,24},{56,32},{64,10... | collective-permute-start | bytes 393224 | tf_op jit(solution)/shard_map/ppermute | solution.py:338
  195.1 16.5 %collective-permute-start.19 = (bf16[512,128]{1,0:T(8,128)(2,1)}, bf16[512,128]{1,0:T(8,128)(2,1)S(1)}, u32[]{:S(2)}, u32[]{:S(2)}) collective-permute-start(bf16[512,128]{1,0:T(8,128)(2,1)} %get-tuple-element.128), channel_id=1, source_target_pairs={{0,48},{8,56},{16,0},{24,8},{32,16},{40,24},{48,32},{56,40},{64,11... | collective-permute-start | bytes 393224 | tf_op jit(solution)/shard_map/ppermute | solution.py:338
  195.6 17.9 %collective-permute-start.20 = (bf16[512,128]{1,0:T(8,128)(2,1)}, bf16[512,128]{1,0:T(8,128)(2,1)S(1)}, u32[]{:S(2)}, u32[]{:S(2)}) collective-permute-start(bf16[512,128]{1,0:T(8,128)(2,1)} %get-tuple-element.129), channel_id=1, source_target_pairs={{0,56},{8,0},{16,8},{24,16},{32,24},{40,32},{48,40},{56,48},{64,12... | collective-permute-start | bytes 393224 | tf_op jit(solution)/shard_map/ppermute | solution.py:338
  204.2 0.7 copy-start.13
  204.9 8.7 %copy-start.16 = (bf16[512,128]{1,0:T(8,128)(2,1)S(1)}, bf16[512,128]{1,0:T(8,128)(2,1)}, u32[]{:S(2)}) copy-start(bf16[512,128]{1,0:T(8,128)(2,1)} %get-tuple-element.137) | copy-start | bytes 393220
Sparse Core Ops, SparseCore 0:
  10.5 110.0 all-gather.1
  132.9 42.8 reduce-scatter.1
